TPU v7x, 256 devices: a whole 4x4x8 slice. The times are simulated.
256 devices in a mesh: row: 8 (over y, core), col: 32 (over x, z).
Axes of the slice: x: 4, y: 4, z: 8, core: 2. Of those that a mesh axis runs over, the one named last changes fastest.
Arguments:
- features: bfloat16 [64, 1024, 512], P('row', 'col'), may hold values from -6 to 6
- kernel: float32 [7, 7, 512], replicated, may hold values from -0.875 to 0.875
- gain: float32 [512], replicated, may hold values from 0.1 to 1.9
- w_expand: bfloat16 [512, 2048], replicated, may hold values from -0.25 to 0.25
- w_reduce: bfloat16 [2048, 512], replicated, may hold values from -0.125 to 0.125
- layer_scale: float32 [512], replicated, may hold values from 0.25 to 2
- cotangent: bfloat16 [64, 1024, 512], P('row', 'col'), may hold values from -6 to 6
Outputs:
- grad_features: bfloat16 [64, 1024, 512], P('row', 'col')
- grad_kernel: float32 [7, 7, 512], replicated
- scaled_gain_gradient: float32 [512], replicated
- grad_scale: float32 [512], replicated
- grad_expand: float32 [512, 2048], P(('row', 'col'))
- grad_reduce: float32 [2048, 512], P(('row', 'col'))
All inputs are finite; a program needn't handle non-finite values.
Results may differ from a plain program's by a relative error of at most 0.013.
Values may be sent and summed in bfloat16 or wider, within the bound.
No kernel may reach another device: no remote copies, remote signals or barrier semaphores. Data moves between devices by JAX's collectives and lax.ppermute only.
A program may use at most 64 MiB of HBM per device.

v0:
```python
import math

import jax
import jax.numpy as jnp
from jax import lax
from jax.sharding import PartitionSpec as P

ROOT_TWO = math.sqrt(2.0)
INV_ROOT_TWO_PI = 1.0 / math.sqrt(2.0 * math.pi)


def extended(block, sides, width):
    for axis, dim in sides:
        count = lax.axis_size(axis)
        forward = [(i, i + 1) for i in range(count - 1)]
        backward = [(target, source) for source, target in forward]
        low = lax.ppermute(
            lax.slice_in_dim(block, block.shape[dim] - width, None, axis=dim), axis, forward
        )
        high = lax.ppermute(lax.slice_in_dim(block, 0, width, axis=dim), axis, backward)
        block = jnp.concatenate([low, block, high], axis=dim)
    return block


def gelu(value):
    return 0.5 * value * (1.0 + lax.erf(value / ROOT_TWO))


def gelu_slope(value):
    return (
        0.5 * (1.0 + lax.erf(value / ROOT_TWO))
        + value * jnp.exp(-0.5 * value * value) * INV_ROOT_TWO_PI
    )


def depthwise(padded, kernel, map_height, map_width, flip):
    total = jnp.zeros((map_height, map_width, padded.shape[2]), jnp.float32)
    side = kernel.shape[0]
    for first in range(side):
        for second in range(side):
            row_off = side - 1 - first if flip else first
            col_off = side - 1 - second if flip else second
            total = (
                total
                + kernel[first, second]
                * padded[row_off : row_off + map_height, col_off : col_off + map_width]
            )
    return total


def input_border(field, reach):
    return extended(field, (("row", 0), ("col", 1)), reach)


def grad_border(field, reach):
    return extended(field.astype(jnp.bfloat16), (("row", 0), ("col", 1)), reach).astype(field.dtype)


def outer_term(left, right):
    return lax.dot_general(
        left, right, (((0,), (0,)), ((), ())), preferred_element_type=jnp.float32
    )


def shards(features, kernel, gain, w_expand, w_reduce, layer_scale, cotangent):
    map_height, map_width, channel_total = features.shape
    reach = kernel.shape[0] // 2
    n_row = lax.axis_size("row")
    n_col = lax.axis_size("col")
    multiplier = 1.0 / math.sqrt(map_height * map_width * n_row * n_col)
    xpad = input_border(features, reach).astype(jnp.float32)
    conv = depthwise(xpad, kernel, map_height, map_width, False)
    centered_input = conv - jnp.mean(conv, axis=-1, keepdims=True)
    inverse_deviation = lax.rsqrt(
        jnp.mean(centered_input * centered_input, axis=-1, keepdims=True) + 1e-06
    )
    standardized_input = centered_input * inverse_deviation
    normalized_input = (
        (standardized_input * gain)
        .astype(jnp.bfloat16)
        .reshape(map_height * map_width, channel_total)
    )
    pre = jnp.dot(normalized_input, w_expand, preferred_element_type=jnp.float32)
    act = gelu(pre).astype(jnp.bfloat16)
    branch = jnp.dot(act, w_reduce, preferred_element_type=jnp.float32)
    gflt = cotangent.astype(jnp.float32).reshape(map_height * map_width, channel_total)
    dbranch = (gflt * layer_scale).astype(jnp.bfloat16)
    dscale = jnp.sum(gflt * branch, axis=0)
    dact = jnp.dot(dbranch, w_reduce.T, preferred_element_type=jnp.float32)
    dpre = (dact * gelu_slope(pre)).astype(jnp.bfloat16)
    dreduce = lax.psum_scatter(
        outer_term(act, dbranch), ("row", "col"), scatter_dimension=0, tiled=True
    )
    dexpand = lax.psum_scatter(
        outer_term(normalized_input, dpre), ("row", "col"), scatter_dimension=0, tiled=True
    )
    normalized_gradient = jnp.dot(dpre, w_expand.T, preferred_element_type=jnp.float32).reshape(
        map_height, map_width, channel_total
    )
    gain_gradient = jnp.sum(normalized_gradient * standardized_input, axis=(0, 1))
    rescaled_output = normalized_gradient * gain
    conv_gradient = inverse_deviation * (
        rescaled_output
        - jnp.mean(rescaled_output, axis=-1, keepdims=True)
        - standardized_input
        * jnp.mean(rescaled_output * standardized_input, axis=-1, keepdims=True)
    )
    side = kernel.shape[0]
    pieces = []
    for first in range(side):
        for second in range(side):
            pieces.append(
                jnp.sum(
                    conv_gradient * xpad[first : first + map_height, second : second + map_width],
                    axis=(0, 1),
                )
            )
    dkernel = jnp.stack(pieces).reshape(side, side, channel_total)
    dpad = grad_border(conv_gradient, reach)
    back = depthwise(dpad, kernel, map_height, map_width, True)
    grad_features = (cotangent.astype(jnp.float32) + back).astype(jnp.bfloat16)
    total_kernel, total_gain, total_scale = lax.psum(
        (dkernel, gain_gradient, dscale), ("row", "col")
    )
    return (
        grad_features,
        total_kernel * multiplier,
        total_gain * multiplier,
        total_scale * multiplier,
        dexpand * multiplier,
        dreduce * multiplier,
    )


def solution(mesh):
    placed = (P("row", "col", None), P(), P(), P(), P(), P(), P("row", "col", None))
    return jax.shard_map(
        shards,
        mesh=mesh,
        in_specs=placed,
        out_specs=(
            P("row", "col", None),
            P(),
            P(),
            P(),
            P(("row", "col"), None),
            P(("row", "col"), None),
        ),
        check_vma=False,
    )
```

profile of v0, /device:TPU:2, one launch (start us, length us, event | category | flops | bytes accessed | tf_op | source)
XLA Modules:
  0.0 1594.0 jit_solution(5805933053119316306)
XLA Ops:
  7.2 1.1 fusion.60
  8.3 1.7 collective-permute-start
  10.1 1.3 collective-permute-start.1
  11.4 1.2 fusion.61
  16.1 7.7 collective-permute-start.3
  23.8 1.9 collective-permute-start.2
  25.7 1.5 fusion.63
  27.4 4.6 collective-permute-done.2
  32.2 5.1 fusion.57
  38.1 1.9 multiply_convert_fusion
  40.0 1.3 fusion
  43.0 3.3 multiply_reduce_fusion.1
  46.3 1.6 multiply_reduce_fusion.19
  47.8 1.3 multiply_reduce_fusion.37
  49.5 2.7 fusion.64
  52.5 1.6 stack.199
  54.9 1.1 copy-done.2
  56.1 3.7 fusion.65
  60.4 1.3 collective-permute-start.5
  61.7 4.2 collective-permute-start.4
  65.9 2.9 fusion.5
  68.8 77.4 %all-reduce.1 = (f32[512]{0:T(512)S(1)}, f32[512]{0:T(512)S(1)}) all-reduce(f32[512]{0:T(512)} %get-tuple-element.55, f32[512]{0:T(512)} %fusion.5), channel_id=1, replica_groups=mesh['row'=8,'col'=32] {'row','col'}, use_global_device_ids=true, to_apply=%region_55.0 | all-reduce | flops 1024 | bytes 8192 | tf_op jit(solution)/shard_map/psum | solution.py:122
  147.1 5.5 collective-permute-start.7
  152.6 1.9 collective-permute-start.6
  155.1 5.7 collective-permute-done.6
  160.8 1.1 maximum_convert_fusion.1
  162.0 5.7 fusion.8
  167.6 157.1 %all-reduce.5.cloned.1.call-done = (f32[7,7,512]{2,1,0:T(8,128)}, f32[512,2048]{1,0:T(8,128)}) async-done(((f32[7,7,512]{2,1,0:T(8,128)}, f32[512,2048]{1,0:T(8,128)}), (f32[7,7,512]{2,1,0:T(8,128)}, f32[512,2048]{1,0:T(8,128)})) %all-reduce.5.cloned.1.call-update) | async-done | bytes 4294672 | tf_op jit(solution)/shard_map/psum | solution.py:122
  324.7 1.5 dynamic-slice_multiply_fusion
  326.2 1.6 broadcast_multiply_fusion
  327.8 1258.1 %reduce-scatter.2.cloned.1.call-done = f32[8,512]{1,0:T(8,128)} async-done(((f32[2048,512]{1,0:T(8,128)}), f32[8,512]{1,0:T(8,128)}) %reduce-scatter.2.cloned.1.call-update) | async-done | bytes 16400 | tf_op jit(solution)/shard_map/reduce_scatter | solution.py:91
  1585.8 1.3 broadcast_multiply_fusion.1
  (209 shorter events, 8.7 us)
Async XLA Ops:
  7.2 30.9 %copy-start = (bf16[512,2048]{1,0:T(8,128)(2,1)S(1)}, bf16[512,2048]{1,0:T(8,128)(2,1)}, u32[]{:S(2)}) copy-start(bf16[512,2048]{1,0:T(8,128)(2,1)} %param.10) | copy-start | bytes 6291460
  7.2 317.6 %all-reduce.5.cloned.1.call-start = ((), (), s32[]{:S(2)}) async-start(), calls=%async_computation.2 | async-start | bytes 8617984 | tf_op jit(solution)/shard_map/psum | solution.py:122
  8.3 6.7 collective-permute-start
  10.1 5.9 collective-permute-start.1
  12.6 24.7 %copy-start.11 = (f32[1,1,512]{2,1,0:T(1,128)}, f32[1,1,512]{2,1,0:T(1,128)S(1)}, u32[]{:S(2)}) copy-start(f32[1,1,512]{2,1,0:T(1,128)S(1)} %get-tuple-element.82) | copy-start | bytes 6148
  12.6 24.7 %copy-start.13 = (f32[1,1,512]{2,1,0:T(1,128)}, f32[1,1,512]{2,1,0:T(1,128)S(1)}, u32[]{:S(2)}) copy-start(f32[1,1,512]{2,1,0:T(1,128)S(1)} %get-tuple-element.83) | copy-start | bytes 6148
  12.6 24.7 %copy-start.15 = (f32[1,1,512]{2,1,0:T(1,128)}, f32[1,1,512]{2,1,0:T(1,128)S(1)}, u32[]{:S(2)}) copy-start(f32[1,1,512]{2,1,0:T(1,128)S(1)} %get-tuple-element.84) | copy-start | bytes 6148
  12.6 24.7 %copy-start.17 = (f32[1,1,512]{2,1,0:T(1,128)}, f32[1,1,512]{2,1,0:T(1,128)S(1)}, u32[]{:S(2)}) copy-start(f32[1,1,512]{2,1,0:T(1,128)S(1)} %get-tuple-element.85) | copy-start | bytes 6148
  12.6 24.7 %copy-start.18 = (f32[1,1,512]{2,1,0:T(1,128)}, f32[1,1,512]{2,1,0:T(1,128)S(1)}, u32[]{:S(2)}) copy-start(f32[1,1,512]{2,1,0:T(1,128)S(1)} %get-tuple-element.86) | copy-start | bytes 6148
  12.6 24.7 %copy-start.19 = (f32[1,1,512]{2,1,0:T(1,128)}, f32[1,1,512]{2,1,0:T(1,128)S(1)}, u32[]{:S(2)}) copy-start(f32[1,1,512]{2,1,0:T(1,128)S(1)} %get-tuple-element.87) | copy-start | bytes 6148
  12.6 24.7 %copy-start.20 = (f32[1,1,512]{2,1,0:T(1,128)}, f32[1,1,512]{2,1,0:T(1,128)S(1)}, u32[]{:S(2)}) copy-start(f32[1,1,512]{2,1,0:T(1,128)S(1)} %get-tuple-element.88) | copy-start | bytes 6148
  12.6 24.7 %copy-start.21 = (f32[1,1,512]{2,1,0:T(1,128)}, f32[1,1,512]{2,1,0:T(1,128)S(1)}, u32[]{:S(2)}) copy-start(f32[1,1,512]{2,1,0:T(1,128)S(1)} %get-tuple-element.89) | copy-start | bytes 6148
  12.7 24.7 %copy-start.22 = (f32[1,1,512]{2,1,0:T(1,128)}, f32[1,1,512]{2,1,0:T(1,128)S(1)}, u32[]{:S(2)}) copy-start(f32[1,1,512]{2,1,0:T(1,128)S(1)} %get-tuple-element.90) | copy-start | bytes 6148
  12.7 24.7 %copy-start.23 = (f32[1,1,512]{2,1,0:T(1,128)}, f32[1,1,512]{2,1,0:T(1,128)S(1)}, u32[]{:S(2)}) copy-start(f32[1,1,512]{2,1,0:T(1,128)S(1)} %get-tuple-element.91) | copy-start | bytes 6148
  13.7 26.3 %copy-start.6 = (bf16[256,512]{1,0:T(8,128)(2,1)}, bf16[256,512]{1,0:T(8,128)(2,1)S(1)}, u32[]{:S(2)}) copy-start(bf16[256,512]{1,0:T(8,128)(2,1)S(1)} %fusion.56) | copy-start | bytes 786436
  14.8 22.6 %copy-start.24 = (f32[1,1,512]{2,1,0:T(1,128)}, f32[1,1,512]{2,1,0:T(1,128)S(1)}, u32[]{:S(2)}) copy-start(f32[1,1,512]{2,1,0:T(1,128)S(1)} %get-tuple-element.92) | copy-start | bytes 6148
  14.8 22.6 %copy-start.25 = (f32[1,1,512]{2,1,0:T(1,128)}, f32[1,1,512]{2,1,0:T(1,128)S(1)}, u32[]{:S(2)}) copy-start(f32[1,1,512]{2,1,0:T(1,128)S(1)} %get-tuple-element.93) | copy-start | bytes 6148
  14.8 22.6 %copy-start.26 = (f32[1,1,512]{2,1,0:T(1,128)}, f32[1,1,512]{2,1,0:T(1,128)S(1)}, u32[]{:S(2)}) copy-start(f32[1,1,512]{2,1,0:T(1,128)S(1)} %get-tuple-element.94) | copy-start | bytes 6148
  14.8 22.6 %copy-start.27 = (f32[1,1,512]{2,1,0:T(1,128)}, f32[1,1,512]{2,1,0:T(1,128)S(1)}, u32[]{:S(2)}) copy-start(f32[1,1,512]{2,1,0:T(1,128)S(1)} %get-tuple-element.95) | copy-start | bytes 6148
  14.8 22.6 %copy-start.28 = (f32[1,1,512]{2,1,0:T(1,128)}, f32[1,1,512]{2,1,0:T(1,128)S(1)}, u32[]{:S(2)}) copy-start(f32[1,1,512]{2,1,0:T(1,128)S(1)} %get-tuple-element.96) | copy-start | bytes 6148
  14.8 22.6 %copy-start.29 = (f32[1,1,512]{2,1,0:T(1,128)}, f32[1,1,512]{2,1,0:T(1,128)S(1)}, u32[]{:S(2)}) copy-start(f32[1,1,512]{2,1,0:T(1,128)S(1)} %get-tuple-element.97) | copy-start | bytes 6148
  14.9 22.6 %copy-start.30 = (f32[1,1,512]{2,1,0:T(1,128)}, f32[1,1,512]{2,1,0:T(1,128)S(1)}, u32[]{:S(2)}) copy-start(f32[1,1,512]{2,1,0:T(1,128)S(1)} %get-tuple-element.98) | copy-start | bytes 6148
  16.1 11.3 collective-permute-start.3
  23.8 8.2 collective-permute-start.2
  54.9 1531.0 %reduce-scatter.2.cloned.1.call-start = ((), (), s32[]{:S(2)}) async-start(), calls=%async_computation.1 | async-start | bytes 4210688 | tf_op jit(solution)/shard_map/reduce_scatter | solution.py:91
  60.4 85.8 %collective-permute-start.5 = (bf16[3,32,512]{2,1,0:T(8,128)(2,1)}, bf16[3,32,512]{2,1,0:T(8,128)(2,1)S(1)}, u32[]{:S(2)}, u32[]{:S(2)}) collective-permute-start(bf16[3,32,512]{2,1,0:T(8,128)(2,1)} %get-tuple-element.70), channel_id=1, source_target_pairs={{32,0},{64,32},{96,64},{128,96},{160,128},{192,160},{224,192},{33,... | collective-permute-start | bytes 294920 | tf_op jit(solution)/shard_map/ppermute | solution.py:20
  61.7 84.5 %collective-permute-start.4 = (bf16[3,32,512]{2,1,0:T(8,128)(2,1)}, bf16[3,32,512]{2,1,0:T(8,128)(2,1)}, u32[]{:S(2)}, u32[]{:S(2)}) collective-permute-start(bf16[3,32,512]{2,1,0:T(8,128)(2,1)} %get-tuple-element.69), channel_id=1, source_target_pairs={{0,32},{32,64},{64,96},{96,128},{128,160},{160,192},{192,224},{1,3... | collective-permute-start | bytes 294920 | tf_op jit(solution)/shard_map/ppermute | solution.py:17
  68.8 93.1 %copy-start.12 = (f32[1,1,512]{2,1,0:T(1,128)S(1)}, f32[1,1,512]{2,1,0:T(1,128)}, u32[]{:S(2)}) copy-start(f32[1,1,512]{2,1,0:T(1,128)} %copy-done.11) | copy-start | bytes 6148
  68.8 93.1 %copy-start.14 = (f32[1,1,512]{2,1,0:T(1,128)S(1)}, f32[1,1,512]{2,1,0:T(1,128)}, u32[]{:S(2)}) copy-start(f32[1,1,512]{2,1,0:T(1,128)} %copy-done.13) | copy-start | bytes 6148
  68.8 93.1 %copy-start.16 = (f32[1,1,512]{2,1,0:T(1,128)S(1)}, f32[1,1,512]{2,1,0:T(1,128)}, u32[]{:S(2)}) copy-start(f32[1,1,512]{2,1,0:T(1,128)} %copy-done.15) | copy-start | bytes 6148
  147.1 8.0 collective-permute-start.7
  152.6 8.2 collective-permute-start.6
  (68 other events, 497.8 us)
Sparse Core Ops, SparseCore 0:
  55.0 269.7 all-reduce.4
  327.4 1258.3 reduce-scatter.1
where the time goes:
time: 1610 us; the launch traced here: 1590 us
  waiting for transfers between devices  1430 us (89%)
  blocking collectives  77.4 us (5%)
  other arithmetic  26.1 us (2%)
  starting transfers between devices  25.7 us (2%)
    reduce_scatter x1, waiting for transfers between devices, shards(): lax.psum_scatter(outer_term(act, dbranch), ('row', 'col'), scatter_dimens...  1260 us
    psum x1, waiting for transfers between devices, shards(): lax.psum((dkernel, gain_gradient, dscale), ('row', 'col'))  157 us
    psum x1, blocking collectives, shards(): lax.psum((dkernel, gain_gradient, dscale), ('row', 'col'))  77.4 us
  transfers between devices with their start and end apart: 10, of which 4 were waited for; matrix products, arithmetic and copies ran while one was open for 2% of the time, Pallas kernels for 0%

commit v1 on v0

v1 whole, which is shorter than its diff:
```python
import functools
import math

import jax
import jax.numpy as jnp
from jax import lax
from jax.experimental import pallas as pl
from jax.experimental.pallas import tpu as pltpu
from jax.sharding import Mesh
from jax.sharding import PartitionSpec as P

Y, CORE, X, Z = 4, 2, 4, 8
ROW, COL = ("y", "core"), ("x", "z")
INV_ROOT_TWO = 1.0 / math.sqrt(2.0)
INV_ROOT_TWO_PI = 1.0 / math.sqrt(2.0 * math.pi)
LANES = 128
LEFT = 8
SMALL = 64

NN = (((1,), (0,)), ((), ()))
NT = (((1,), (1,)), ((), ()))


def product(left, right, dims):
    return lax.dot_general(left, right, dims, preferred_element_type=jnp.float32)


def fill(padded, field, up, down, left, right, reach):
    height, width, channels = field.shape
    for block in range(channels // LANES):
        lanes = pl.ds(block * LANES, LANES)
        own = pl.ds(LEFT, width)
        padded[block, pl.ds(0, reach), own, :] = up[:, :, lanes].astype(jnp.float32)
        padded[block, pl.ds(reach, height), own, :] = field[:, :, lanes].astype(jnp.float32)
        padded[block, pl.ds(reach + height, reach), own, :] = down[:, :, lanes].astype(jnp.float32)
        padded[block, :, pl.ds(LEFT - reach, reach), :] = left[:, :, lanes].astype(jnp.float32)
        padded[block, :, pl.ds(LEFT + width, reach), :] = right[:, :, lanes].astype(jnp.float32)


def depthwise(padded, taps, block, first_col, height, side):
    reach = side // 2
    totals = [None] * height
    for second in range(side):
        columns = pl.ds(LEFT - reach + first_col + second, 8)
        rows = [padded[block, row, columns, :] for row in range(height + side - 1)]
        for first in range(side):
            weight = taps[block, pl.ds(first * side + second, 1), :]
            for row in range(height):
                term = weight * rows[row + first]
                totals[row] = term if totals[row] is None else totals[row] + term
    return totals


def forward_kernel(
    core_ref, field, up, down, left, right, taps, gain, expand_t, reduce, scale, cotangent,
    sent, kept, dpre_out, xhat_out, rstd_out, padded, dscale_out,
    conv, normed, dbranch, turned, chosen, expand_v, reduce_v, sems,
):
    core = core_ref[0]
    copies = [
        pltpu.make_async_copy(expand_t, expand_v, sems.at[0]),
        pltpu.make_async_copy(reduce, reduce_v, sems.at[1]),
    ]
    for copy in copies:
        copy.start()
    height, width, channels = field.shape
    blocks = channels // LANES
    side = 7
    fill(padded, field, up, down, left, right, side // 2)

    def conv_block(block, _):
        for first_col in range(0, width, 8):
            for row, total in enumerate(depthwise(padded, taps, block, first_col, height, side)):
                conv[block, pl.ds(row * width + first_col, 8), :] = total
        return 0

    lax.fori_loop(0, blocks, conv_block, 0)
    for row in range(height):
        pixels = pl.ds(row * width, width)
        values = [conv[block, pixels, :] for block in range(blocks)]
        mean = jnp.sum(sum(values), axis=-1, keepdims=True) / channels
        values = [value - mean for value in values]
        spread = jnp.sum(sum(value * value for value in values), axis=-1, keepdims=True) / channels
        rstd = lax.rsqrt(spread + 1e-06)
        rstd_out[pixels, :] = jnp.broadcast_to(rstd, (width, LANES))
        for block, value in enumerate(values):
            lanes = pl.ds(block * LANES, LANES)
            xhat = value * rstd
            xhat_out[block, pixels, :] = xhat
            normed[pixels, lanes] = (xhat * gain[:, lanes]).astype(jnp.bfloat16)
        dbranch[pixels, :] = (cotangent[row].astype(jnp.float32) * scale[...]).astype(jnp.bfloat16)
    turned[...] = normed[...].T
    part = channels // (Y * CORE)
    for y in range(Y):
        for own in range(CORE):
            owner = core if own else 1 - core
            chosen[pl.ds((own * Y + y) * part, part), :] = turned[
                pl.ds(pl.multiple_of((y * CORE + owner) * part, part), part), :
            ]
    dscale_out[...] = jnp.zeros_like(dscale_out)
    for copy in copies:
        copy.wait()
    step = reduce_v.shape[0] // (Y * CORE)
    per_x = step // X
    part_x = part // X
    wide = channels // step

    def hidden_block(y, _):
        for own, target in ((0, sent), (1, kept)):
            owner = core if own else 1 - core
            chunk = y * CORE + owner
            hidden = pl.ds(pl.multiple_of(chunk * step, step), step)
            pre = product(expand_v[hidden, :], normed[...], NT)
            dact = product(reduce_v[hidden, :], dbranch[...], NT)
            half = 0.5 * (1.0 + lax.erf(pre * INV_ROOT_TWO))
            slope = half + pre * jnp.exp(-0.5 * pre * pre) * INV_ROOT_TWO_PI
            act = (pre * half).astype(jnp.bfloat16)
            dpre = (dact * slope).astype(jnp.bfloat16)
            dpre_out[hidden, :] = dpre
            share = product(act, dbranch[...], NN)
            weighed = share * reduce_v[hidden, :].astype(jnp.float32)
            dscale_out[...] += jnp.sum(weighed.reshape(step // 8, 8, channels), axis=0)
            for x in range(X):
                target[y * X + x, pl.ds(0, per_x), :] = share[x * per_x : (x + 1) * per_x].astype(
                    jnp.bfloat16
                )
            share = product(chosen[...], dpre, NT).astype(jnp.bfloat16)
            rows = pl.ds(pl.multiple_of(per_x + (chunk // wide) * part_x, part_x), part_x)
            lanes = pl.ds(pl.multiple_of((chunk % wide) * step, step), step)
            for place in range(Y * X):
                for back, goal in ((0, sent), (1, kept)):
                    first = back * Y * part + place * part_x
                    goal[place, rows, lanes] = share[first : first + part_x]
        return 0

    lax.fori_loop(0, Y, hidden_block, 0)


def backward_kernel(
    multiplier, dpre, expand, xhat, rstd, padded, gain, dscale, scale, dconv_out, small, dconv
):
    height, width, channels = dconv_out.shape
    blocks = channels // LANES
    side = 7
    for block in range(blocks):
        lanes = pl.ds(block * LANES, LANES)
        dconv[block] = product(expand[lanes, :], dpre[...], NN).T
        small[block] = jnp.zeros_like(small[block])
    sums = [jnp.zeros((width, LANES), jnp.float32)] * blocks
    for row in range(height):
        pixels = pl.ds(row * width, width)
        grads = [dconv[block, pixels, :] for block in range(blocks)]
        hats = [xhat[block, pixels, :] for block in range(blocks)]
        sums = [total + grad * hat for total, grad, hat in zip(sums, grads, hats)]
        grads = [grad * gain[:, pl.ds(block * LANES, LANES)] for block, grad in enumerate(grads)]
        mean = jnp.sum(sum(grads), axis=-1, keepdims=True) / channels
        slant = sum(grad * hat for grad, hat in zip(grads, hats))
        slant = jnp.sum(slant, axis=-1, keepdims=True) / channels
        for block in range(blocks):
            value = rstd[pixels, :] * (grads[block] - mean - hats[block] * slant)
            dconv[block, pixels, :] = value
            dconv_out[row, :, pl.ds(block * LANES, LANES)] = value.astype(jnp.bfloat16)
    taps = side * side
    for block in range(blocks):
        lanes = pl.ds(block * LANES, LANES)
        total = jnp.sum(sums[block], axis=0, keepdims=True)
        small[block, pl.ds(taps, 1), :] = total * multiplier
        total = jnp.sum(dscale[:, lanes], axis=0, keepdims=True)
        small[block, pl.ds(taps + 1, 1), :] = total / scale[:, lanes] * multiplier

    def tap_block(block, _):
        for second in range(side):
            totals = [jnp.zeros((8, LANES), jnp.float32)] * side
            for first_col in range(0, width, 8):
                grads = [
                    dconv[block, pl.ds(row * width + first_col, 8), :] for row in range(height)
                ]
                columns = pl.ds(LEFT - side // 2 + first_col + second, 8)
                for row in range(height + side - 1):
                    value = padded[block, row, columns, :]
                    for first in range(max(0, row - height + 1), min(side, row + 1)):
                        totals[first] = totals[first] + grads[row - first] * value
            for first, total in enumerate(totals):
                total = jnp.sum(total, axis=0, keepdims=True) * multiplier
                small[block, pl.ds(first * side + second, 1), :] = total
        return 0

    lax.fori_loop(0, blocks, tap_block, 0)


def feature_kernel(field, up, down, left, right, taps, cotangent, out, padded):
    height, width, channels = field.shape
    side = 7
    fill(padded, field, up, down, left, right, side // 2)
    for block in range(channels // LANES):
        lanes = pl.ds(block * LANES, LANES)
        for first_col in range(0, width, 8):
            columns = pl.ds(first_col, 8)
            for row, total in enumerate(depthwise(padded, taps, block, first_col, height, side)):
                total = total + cotangent[row, columns, lanes].astype(jnp.float32)
                out[row, columns, lanes] = total.astype(jnp.bfloat16)


VMEM = pl.BlockSpec(memory_space=pltpu.VMEM)
ANY = pl.BlockSpec(memory_space=pl.ANY)
SMEM = pl.BlockSpec(memory_space=pltpu.SMEM)
PARAMS = pltpu.CompilerParams(vmem_limit_bytes=40 << 20)


def shifted(value, axes, by):
    count = lax.axis_size(axes)
    pairs = [(i, i + by) for i in range(count) if 0 <= i + by < count]
    return lax.ppermute(value, axes, pairs)


def borders(field, reach):
    up = shifted(field[-reach:], ROW, 1)
    down = shifted(field[:reach], ROW, -1)
    left, right = (
        jnp.concatenate([part[:, columns] for part in (up, field, down)])
        for columns in (slice(-reach, None), slice(0, reach))
    )
    return up, down, shifted(left, COL, 1), shifted(right, COL, -1)


def exchanged(chunks, axes):
    return lax.all_to_all(chunks, axes, 0, 0, tiled=True)


def summed(chunks):
    return jnp.sum(chunks.astype(jnp.float32), axis=0)


def everywhere(small):
    chunks = exchanged(small.reshape(Y * CORE * X, 8, LANES), ("y", "core", "x"))
    part = summed(chunks)
    part = summed(exchanged(jnp.broadcast_to(part, (Z, *part.shape)), "z"))
    full = exchanged(jnp.broadcast_to(part, (Y * CORE * X, *part.shape)), ("y", "core", "x"))
    return full.reshape(small.shape)


def shards(features, kernel, gain, w_expand, w_reduce, layer_scale, cotangent):
    height, width, channels = features.shape
    hidden = w_reduce.shape[0]
    side = kernel.shape[0]
    taps_total = side * side
    reach = side // 2
    blocks = channels // LANES
    pixels = height * width
    multiplier = 1.0 / math.sqrt(pixels * lax.axis_size(ROW) * lax.axis_size(COL))
    taps = kernel.reshape(taps_total, blocks, LANES).transpose(1, 0, 2)
    flipped = taps[:, ::-1]
    gain_row = gain.reshape(1, channels)
    scale_row = layer_scale.reshape(1, channels)
    core = lax.axis_index("core").reshape(1)
    places = Y * X
    rows = hidden // (Y * CORE * X)
    f32, bf16 = jnp.float32, jnp.bfloat16
    shape = jax.ShapeDtypeStruct
    padded_shape = (blocks, height + side - 1, LEFT + width + 8, LANES)

    sent, kept, dpre, xhat, rstd, padded, dscale = pl.pallas_call(
        forward_kernel,
        name="forward",
        in_specs=[SMEM] + [VMEM] * 7 + [ANY] * 2 + [VMEM] * 2,
        out_specs=[VMEM] * 7,
        out_shape=[
            shape((places, 2 * rows, channels), bf16),
            shape((places, 2 * rows, channels), bf16),
            shape((hidden, pixels), bf16),
            shape((blocks, pixels, LANES), f32),
            shape((pixels, LANES), f32),
            shape(padded_shape, f32),
            shape((8, channels), f32),
        ],
        scratch_shapes=[
            pltpu.VMEM((blocks, pixels, LANES), f32),
            pltpu.VMEM((pixels, channels), bf16),
            pltpu.VMEM((pixels, channels), bf16),
            pltpu.VMEM((channels, pixels), bf16),
            pltpu.VMEM((channels, pixels), bf16),
            pltpu.VMEM((hidden, channels), bf16),
            pltpu.VMEM((hidden, channels), bf16),
            pltpu.SemaphoreType.DMA((2,)),
        ],
        compiler_params=PARAMS,
    )(
        core, features, *borders(features, reach), taps, gain_row, w_expand.T, w_reduce,
        scale_row, cotangent,
    )

    came = lax.ppermute(sent, "core", [(0, 1), (1, 0)])
    chip = (kept.astype(f32) + came.astype(f32)).astype(bf16)
    plane = summed(exchanged(chip, ("y", "x")))
    first = plane[:rows].reshape(Z, -1, channels)
    second = plane[rows:].reshape(hidden // channels, Z, -1, channels).transpose(1, 2, 0, 3)
    second = second.reshape(Z, -1, channels)
    line = jnp.concatenate([first, second], axis=1).astype(bf16)
    own = summed(exchanged(line, "z")) * multiplier
    dreduce = own[: rows // Z]
    dexpand = own[rows // Z :].reshape(-1, hidden)

    dconv, small = pl.pallas_call(
        functools.partial(backward_kernel, multiplier),
        name="backward",
        in_specs=[VMEM] * 8,
        out_specs=[VMEM] * 2,
        out_shape=[
            shape((height, width, channels), bf16),
            shape((blocks, SMALL, LANES), f32),
        ],
        scratch_shapes=[pltpu.VMEM((blocks, pixels, LANES), f32)],
        compiler_params=PARAMS,
    )(dpre, w_expand, xhat, rstd, padded, gain_row, dscale, scale_row)

    small = everywhere(small).transpose(1, 0, 2).reshape(SMALL, channels)
    grad_features = pl.pallas_call(
        feature_kernel,
        name="features",
        in_specs=[VMEM] * 7,
        out_specs=VMEM,
        out_shape=shape((height, width, channels), bf16),
        scratch_shapes=[pltpu.VMEM(padded_shape, f32)],
        compiler_params=PARAMS,
    )(dconv, *borders(dconv, reach), flipped, cotangent)
    return (
        grad_features,
        small[:taps_total].reshape(side, side, channels),
        small[taps_total],
        small[taps_total + 1],
        dexpand,
        dreduce,
    )


def solution(mesh):
    pixels = P(ROW, COL, None)
    return jax.shard_map(
        shards,
        mesh=Mesh(mesh.devices.reshape(Y, CORE, X, Z), (*ROW, *COL)),
        in_specs=(pixels, P(), P(), P(), P(), P(), pixels),
        out_specs=(pixels, P(), P(), P(), P((*ROW, *COL), None), P((*ROW, *COL), None)),
        check_vma=False,
    )
```

time: 1610 us -> 131 us (0.08)
  waiting for transfers between devices: 1430 us -> 37.7 us
  blocking collectives: 77.4 us -> 14 us
  other arithmetic: 26.1 us -> 4.79 us
  starting transfers between devices: 25.7 us -> 46.1 us
    reduce_scatter x1 -> x0, waiting for transfers between devices: 1260 us -> none  [shards(): lax.psum_scatter(outer_term(act, dbranch), ('row', 'col'), scatter_dimens...]
    psum x1 -> x0, waiting for transfers between devices: 157 us -> none  [shards(): lax.psum((dkernel, gain_gradient, dscale), ('row', 'col'))]
    psum x1 -> x0, blocking collectives: 77.4 us -> none  [shards(): lax.psum((dkernel, gain_gradient, dscale), ('row', 'col'))]
    all_to_all x0 -> x4, waiting for transfers between devices: none -> 29.6 us  [exchanged(): return lax.all_to_all(chunks, axes, 0, 0, tiled=True)]
    all_to_all x0 -> x4, starting transfers between devices: none -> 23.2 us  [exchanged(): return lax.all_to_all(chunks, axes, 0, 0, tiled=True)]
  transfers between devices with their start and end apart: 10 -> 13, of which waited for: 4 -> 7; matrix products, arithmetic and copies ran while one was open for 2% -> 9% of each run, Pallas kernels for 0% -> 4%
where the time goes in v1:
time: 131 us; the launch traced here: 130 us
  starting transfers between devices  46.1 us (35%)
  waiting for transfers between devices  37.7 us (29%)
  blocking collectives  14 us (11%)
  Pallas kernels  13.7 us (10%)
  local copies, waits for them, and re-layouts  12.7 us (10%)
  other arithmetic  4.79 us (4%)
    all_to_all x4, waiting for transfers between devices, exchanged(): return lax.all_to_all(chunks, axes, 0, 0, tiled=True)  29.6 us
    all_to_all x4, starting transfers between devices, exchanged(): return lax.all_to_all(chunks, axes, 0, 0, tiled=True)  23.2 us
    ppermute x8, starting transfers between devices, shifted(): return lax.ppermute(value, axes, pairs)  21.1 us
    all_to_all x1, blocking collectives, exchanged(): return lax.all_to_all(chunks, axes, 0, 0, tiled=True)  14 us
    pallas_call x1, Pallas kernels, shards(): pl.pallas_call(forward_kernel, name='forward', in_specs=[SMEM] + [VMEM] *...  8.33 us
    ppermute x8, waiting for transfers between devices, shifted(): return lax.ppermute(value, axes, pairs)  8.19 us
    unnamed x17, local copies, waits for them, and re-layouts  5.89 us
    convert_element_type x1, other arithmetic, shards(): chip = (kept.astype(f32) + came.astype(f32)).astype(bf16)  3.58 us
  transfers between devices with their start and end apart: 13, of which 7 were waited for; matrix products, arithmetic and copies ran while one was open for 9% of the time, Pallas kernels for 4%

profile of v1, /device:TPU:2, one launch (start us, length us, event | category | flops | bytes accessed | tf_op | source)
XLA Modules:
  0.0 130.2 jit_solution(17123828131195418498)
XLA Ops:
  0.6 1.0 fusion.3
  1.6 1.7 %collective-permute-start = (bf16[3,32,512]{2,1,0:T(8,128)(2,1)S(1)}, bf16[3,32,512]{2,1,0:T(8,128)(2,1)S(1)}, u32[]{:S(2)}, u32[]{:S(2)}) collective-permute-start(bf16[3,32,512]{2,1,0:T(8,128)(2,1)S(1)} %get-tuple-element.31), channel_id=1, source_target_pairs={{0,32},{32,64},{64,96},{96,128},{128,160},{160,192},{192,224},{1,3... | collective-permute-start | bytes 294920 | tf_op jit(solution)/shard_map/ppermute | solution.py:213
  3.3 1.3 collective-permute-start.1
  4.6 0.9 fusion.2
  5.6 2.3 %collective-permute-done.1.down = bf16[3,32,512]{2,1,0:T(8,128)(2,1)S(1)} collective-permute-done((bf16[3,32,512]{2,1,0:T(8,128)(2,1)S(1)}, bf16[3,32,512]{2,1,0:T(8,128)(2,1)S(1)}, u32[]{:S(2)}, u32[]{:S(2)}) %collective-permute-start.1) | collective-permute-done | bytes 98336 | tf_op jit(solution)/shard_map/ppermute | solution.py:213
  8.0 7.7 %collective-permute-start.3 = (bf16[14,3,512]{2,1,0:T(4,128)(2,1)S(1)}, bf16[14,3,512]{2,1,0:T(4,128)(2,1)S(1)}, u32[]{:S(2)}, u32[]{:S(2)}) collective-permute-start(bf16[14,3,512]{2,1,0:T(4,128)(2,1)S(1)} %pad_maximum_fusion.2), channel_id=1, source_target_pairs={{1,0},{2,1},{3,2},{4,3},{5,4},{6,5},{7,6},{8,7},{9,8},{10,9},{11,1... | collective-permute-start | bytes 129032 | tf_op jit(solution)/shard_map/ppermute | solution.py:213
  15.8 1.9 %collective-permute-start.2 = (bf16[14,3,512]{2,1,0:T(4,128)(2,1)S(1)}, bf16[14,3,512]{2,1,0:T(4,128)(2,1)S(1)}, u32[]{:S(2)}, u32[]{:S(2)}) collective-permute-start(bf16[14,3,512]{2,1,0:T(4,128)(2,1)S(1)} %pad_maximum_fusion.1), channel_id=1, source_target_pairs={{0,1},{1,2},{2,3},{3,4},{4,5},{5,6},{6,7},{7,8},{8,9},{9,10},{10,1... | collective-permute-start | bytes 129032 | tf_op jit(solution)/shard_map/ppermute | solution.py:213
  17.7 0.9 reshape.56
  18.7 2.9 %copy.22 = bf16[512,2048]{0,1:T(8,128)(2,1)S(1)} copy(bf16[512,2048]{1,0:T(8,128)(2,1)} %expand.1) | data formatting | bytes 4194304 | tf_op args[3]
  21.6 2.3 %collective-permute-done.2.left = bf16[14,3,512]{2,1,0:T(4,128)(2,1)S(1)} collective-permute-done((bf16[14,3,512]{2,1,0:T(4,128)(2,1)S(1)}, bf16[14,3,512]{2,1,0:T(4,128)(2,1)S(1)}, u32[]{:S(2)}, u32[]{:S(2)}) %collective-permute-start.2) | collective-permute-done | bytes 43040 | tf_op jit(solution)/shard_map/ppermute | solution.py:213
  24.0 1.6 %copy-done.3 = bf16[2048,512]{1,0:T(8,128)(2,1)S(1)} copy-done((bf16[2048,512]{1,0:T(8,128)(2,1)S(1)}, bf16[2048,512]{1,0:T(8,128)(2,1)}, u32[]{:S(2)}) %copy-start.3) | copy-done | bytes 2097176
  25.6 8.3 %forward.1 = (bf16[16,128,512]{2,1,0:T(8,128)(2,1)}, bf16[16,128,512]{2,1,0:T(8,128)(2,1)S(1)}, bf16[2048,256]{1,0:T(8,128)(2,1)S(1)}, f32[4,256,128]{2,1,0:T(8,...) custom-call(s32[1]{0:T(128)} %bitcast.core_ref, ...), custom_call_target="tpu_custom_call" | custom-call | tf_op jit(solution)/shard_map/forward/pallas_call | solution.py:262
  33.9 1.4 %copy-done.1 = bf16[16,128,512]{2,1,0:T(8,128)(2,1)} copy-done((bf16[16,128,512]{2,1,0:T(8,128)(2,1)}, bf16[16,128,512]{2,1,0:T(8,128)(2,1)S(1)}, u32[]{:S(2)}) %copy-start.1) | copy-done | bytes 2097176
  35.3 1.8 %collective-permute-start.8 = (bf16[16,128,512]{2,1,0:T(8,128)(2,1)}, bf16[16,128,512]{2,1,0:T(8,128)(2,1)}, u32[]{:S(2)}, u32[]{:S(2)}) collective-permute-start(bf16[16,128,512]{2,1,0:T(8,128)(2,1)} %get-tuple-element.23), channel_id=1, source_target_pairs={{0,32},{32,0},{1,33},{33,1},{2,34},{34,2},{3,35},{35,3},{4,36},{36... | collective-permute-start | bytes 6291464 | tf_op jit(solution)/shard_map/ppermute | solution.py:292
  37.1 2.9 %backward.1 = (bf16[8,32,512]{2,1,0:T(8,128)(2,1)S(1)}, f32[4,64,128]{2,1,0:T(8,128)S(1)}) custom-call(bf16[2048,256]{1,0:T(8,128)(2,1)S(1)} %get-tuple-element.15.dpre, bf16[512,2048]{1,0:T(8,128)(2,1)S(1)} %copy-done, f32[4,256,128]{2,1,0:T(8,128)S(1)} %get-tuple-element.16.xhat, f32[256,128]{1,0:T(8,128)S(1)} %get-tuple-element.17.rstd, ...), custom_call_target="tpu_custom_call" | custom-call | tf_op jit(solution)/shard_map/backward/pallas_call | solution.py:303
  40.0 14.0 %all_to_all.25 = f32[32,8,128]{2,1,0:T(8,128)S(1)} all-to-all(f32[32,8,128]{2,1,0:T(8,128)S(1)} %bitcast.20), channel_id=1, replica_groups=mesh['y'=4,'core'=2,'x'=4,'z'=8] {'y','core','x'}, dimensions={0} | all-to-all | bytes 262144 | tf_op jit(solution)/shard_map/all_to_all | solution.py:227
  54.7 3.5 %all-to-all-start.1 = ((f32[8,8,128]{2,1,0:T(8,128)}), f32[8,8,128]{2,1,0:T(8,128)S(1)}, u32[]{:S(2)}, u32[]{:S(2)}) async-start(f32[8,8,128]{2,1,0:T(8,128)} %broadcast_in_dim.6), calls=%async_computation.1 | async-start | bytes 65536 | tf_op jit(solution)/shard_map/all_to_all | solution.py:227
  58.2 3.6 %add_convert_fusion = bf16[16,128,512]{2,1,0:T(8,128)(2,1)} fusion(bf16[16,128,512]{2,1,0:T(8,128)(2,1)} %collective-permute-done.8, bf16[16,128,512]{2,1,0:T(8,128)(2,1)S(1)} %copy-done.2), kind=kLoop, calls=%fused_computation | loop fusion | flops 4194304 | bytes 6291456 | tf_op jit(solution)/shard_map/convert_element_type | solution.py:293
  61.8 4.4 %all-to-all-done.1 = f32[8,8,128]{2,1,0:T(8,128)S(1)} async-done(((f32[8,8,128]{2,1,0:T(8,128)}), f32[8,8,128]{2,1,0:T(8,128)S(1)}, u32[]{:S(2)}, u32[]{:S(2)}) %all-to-all-start.1) | async-done | bytes 32800 | tf_op jit(solution)/shard_map/all_to_all | solution.py:227
  66.2 5.1 %all-to-all-start.3 = ((bf16[16,128,512]{2,1,0:T(8,128)(2,1)}), bf16[16,128,512]{2,1,0:T(8,128)(2,1)S(1)}, u32[]{:S(2)}, u32[]{:S(2)}) async-start(bf16[16,128,512]{2,1,0:T(8,128)(2,1)} %add_convert_fusion), calls=%async_computation.3 | async-start | bytes 4194304 | tf_op jit(solution)/shard_map/all_to_all | solution.py:227
  71.4 1.3 collective-permute-start.4
  72.7 1.3 collective-permute-start.5
  74.0 3.6 %collective-permute-done.5.down = bf16[3,32,512]{2,1,0:T(8,128)(2,1)S(1)} collective-permute-done((bf16[3,32,512]{2,1,0:T(8,128)(2,1)S(1)}, bf16[3,32,512]{2,1,0:T(8,128)(2,1)S(1)}, u32[]{:S(2)}, u32[]{:S(2)}) %collective-permute-start.5) | collective-permute-done | bytes 98336 | tf_op jit(solution)/shard_map/ppermute | solution.py:213
  77.7 2.3 %collective-permute-start.7 = (bf16[14,3,512]{2,1,0:T(4,128)(2,1)S(1)}, bf16[14,3,512]{2,1,0:T(4,128)(2,1)S(1)}, u32[]{:S(2)}, u32[]{:S(2)}) collective-permute-start(bf16[14,3,512]{2,1,0:T(4,128)(2,1)S(1)} %pad_maximum_fusion.4), channel_id=1, source_target_pairs={{1,0},{2,1},{3,2},{4,3},{5,4},{6,5},{7,6},{8,7},{9,8},{10,9},{11,1... | collective-permute-start | bytes 129032 | tf_op jit(solution)/shard_map/ppermute | solution.py:213
  80.0 3.5 %collective-permute-start.6 = (bf16[14,3,512]{2,1,0:T(4,128)(2,1)S(1)}, bf16[14,3,512]{2,1,0:T(4,128)(2,1)S(1)}, u32[]{:S(2)}, u32[]{:S(2)}) collective-permute-start(bf16[14,3,512]{2,1,0:T(4,128)(2,1)S(1)} %pad_maximum_fusion.3), channel_id=1, source_target_pairs={{0,1},{1,2},{2,3},{3,4},{4,5},{5,6},{6,7},{7,8},{8,9},{9,10},{10,1... | collective-permute-start | bytes 129032 | tf_op jit(solution)/shard_map/ppermute | solution.py:213
  83.6 14.2 %all-to-all-done.3 = bf16[16,128,512]{2,1,0:T(8,128)(2,1)S(1)} async-done(((bf16[16,128,512]{2,1,0:T(8,128)(2,1)}), bf16[16,128,512]{2,1,0:T(8,128)(2,1)S(1)}, u32[]{:S(2)}, u32[]{:S(2)}) %all-to-all-start.3) | async-done | bytes 2097184 | tf_op jit(solution)/shard_map/all_to_all | solution.py:227
  98.4 10.6 %all-to-all-start.2 = ((f32[32,8,128]{2,1,0:T(8,128)}), f32[32,8,128]{2,1,0:T(8,128)S(1)}, u32[]{:S(2)}, u32[]{:S(2)}) async-start(f32[32,8,128]{2,1,0:T(8,128)} %broadcast_in_dim.7), calls=%async_computation.2 | async-start | bytes 262144 | tf_op jit(solution)/shard_map/all_to_all | solution.py:227
  110.1 5.3 %all-to-all-done.2 = f32[32,8,128]{2,1,0:T(8,128)S(1)} async-done(((f32[32,8,128]{2,1,0:T(8,128)}), f32[32,8,128]{2,1,0:T(8,128)S(1)}, u32[]{:S(2)}, u32[]{:S(2)}) %all-to-all-start.2) | async-done | bytes 131104 | tf_op jit(solution)/shard_map/all_to_all | solution.py:227
  115.5 3.9 %all-to-all-start.4 = ((bf16[8,16,512]{2,1,0:T(8,128)(2,1)}), bf16[8,16,512]{2,1,0:T(8,128)(2,1)S(1)}, u32[]{:S(2)}, u32[]{:S(2)}) async-start(bf16[8,16,512]{2,1,0:T(8,128)(2,1)} %pad_maximum_fusion), calls=%async_computation.4 | async-start | bytes 262144 | tf_op jit(solution)/shard_map/all_to_all | solution.py:227
  119.5 2.5 %features.1 = bf16[8,32,512]{2,1,0:T(8,128)(2,1)} custom-call(bf16[8,32,512]{2,1,0:T(8,128)(2,1)S(1)} %get-tuple-element.20.field, bf16[3,32,512]{2,1,0:T(8,128)(2,1)S(1)} %collective-permute-done.4.up, bf16[3,32,512]{2,1,0:T(8,128)(2,1)S(1)} %collective-permute-done.5.down, bf16[14,3,512]{2,1,0:T(4,128)(2,1)S(1)} %collective-permute-done.6.left, ...), custom_call_target="tpu_custom_call" | custom-call | tf_op jit(solution)/shard_map/features/pallas_call | solution.py:317
  122.0 0.7 reshape.61
  123.3 5.6 %all-to-all-done.4 = bf16[8,16,512]{2,1,0:T(8,128)(2,1)S(1)} async-done(((bf16[8,16,512]{2,1,0:T(8,128)(2,1)}), bf16[8,16,512]{2,1,0:T(8,128)(2,1)S(1)}, u32[]{:S(2)}, u32[]{:S(2)}) %all-to-all-start.4) | async-done | bytes 131104 | tf_op jit(solution)/shard_map/all_to_all | solution.py:227
  (49 shorter events, 4.6 us)
Async XLA Ops:
  1.6 4.0 %collective-permute-start = (bf16[3,32,512]{2,1,0:T(8,128)(2,1)S(1)}, bf16[3,32,512]{2,1,0:T(8,128)(2,1)S(1)}, u32[]{:S(2)}, u32[]{:S(2)}) collective-permute-start(bf16[3,32,512]{2,1,0:T(8,128)(2,1)S(1)} %get-tuple-element.31), channel_id=1, source_target_pairs={{0,32},{32,64},{64,96},{96,128},{128,160},{160,192},{192,224},{1,3... | collective-permute-start | bytes 294920 | tf_op jit(solution)/shard_map/ppermute | solution.py:213
  3.3 4.6 %collective-permute-start.1 = (bf16[3,32,512]{2,1,0:T(8,128)(2,1)S(1)}, bf16[3,32,512]{2,1,0:T(8,128)(2,1)S(1)}, u32[]{:S(2)}, u32[]{:S(2)}) collective-permute-start(bf16[3,32,512]{2,1,0:T(8,128)(2,1)S(1)} %get-tuple-element.30), channel_id=1, source_target_pairs={{32,0},{64,32},{96,64},{128,96},{160,128},{192,160},{224,192},{33,... | collective-permute-start | bytes 294920 | tf_op jit(solution)/shard_map/ppermute | solution.py:213
  8.0 13.7 %collective-permute-start.3 = (bf16[14,3,512]{2,1,0:T(4,128)(2,1)S(1)}, bf16[14,3,512]{2,1,0:T(4,128)(2,1)S(1)}, u32[]{:S(2)}, u32[]{:S(2)}) collective-permute-start(bf16[14,3,512]{2,1,0:T(4,128)(2,1)S(1)} %pad_maximum_fusion.2), channel_id=1, source_target_pairs={{1,0},{2,1},{3,2},{4,3},{5,4},{6,5},{7,6},{8,7},{9,8},{10,9},{11,1... | collective-permute-start | bytes 129032 | tf_op jit(solution)/shard_map/ppermute | solution.py:213
  15.8 8.2 %collective-permute-start.2 = (bf16[14,3,512]{2,1,0:T(4,128)(2,1)S(1)}, bf16[14,3,512]{2,1,0:T(4,128)(2,1)S(1)}, u32[]{:S(2)}, u32[]{:S(2)}) collective-permute-start(bf16[14,3,512]{2,1,0:T(4,128)(2,1)S(1)} %pad_maximum_fusion.1), channel_id=1, source_target_pairs={{0,1},{1,2},{2,3},{3,4},{4,5},{5,6},{6,7},{7,8},{8,9},{9,10},{10,1... | collective-permute-start | bytes 129032 | tf_op jit(solution)/shard_map/ppermute | solution.py:213
  18.7 5.3 %copy-start.4 = (bf16[8,32,512]{2,1,0:T(8,128)(2,1)S(1)}, bf16[8,32,512]{2,1,0:T(8,128)(2,1)}, u32[]{:S(2)}) copy-start(bf16[8,32,512]{2,1,0:T(8,128)(2,1)} %cotangent.3) | copy-start | bytes 786436
  18.7 5.3 %copy-start.5 = (bf16[8,32,512]{2,1,0:T(8,128)(2,1)S(1)}, bf16[8,32,512]{2,1,0:T(8,128)(2,1)}, u32[]{:S(2)}) copy-start(bf16[8,32,512]{2,1,0:T(8,128)(2,1)} %field.1) | copy-start | bytes 786436
  18.7 5.3 %copy-start.6 = (f32[512]{0:T(512)S(1)}, f32[512]{0:T(512)}, u32[]{:S(2)}) copy-start(f32[512]{0:T(512)} %param.9) | copy-start | bytes 6148
  18.7 5.3 %copy-start.7 = (f32[512]{0:T(512)S(1)}, f32[512]{0:T(512)}, u32[]{:S(2)}) copy-start(f32[512]{0:T(512)} %param.12) | copy-start | bytes 6148
  24.0 1.6 %copy-start.3 = (bf16[2048,512]{1,0:T(8,128)(2,1)S(1)}, bf16[2048,512]{1,0:T(8,128)(2,1)}, u32[]{:S(2)}) copy-start(bf16[2048,512]{1,0:T(8,128)(2,1)} %reduce.2) | copy-start | bytes 6291460
  25.6 11.5 %copy-start = (bf16[512,2048]{1,0:T(8,128)(2,1)S(1)}, bf16[512,2048]{1,0:T(8,128)(2,1)}, u32[]{:S(2)}) copy-start(bf16[512,2048]{1,0:T(8,128)(2,1)} %expand.1) | copy-start | bytes 6291460
  33.9 1.4 %copy-start.1 = (bf16[16,128,512]{2,1,0:T(8,128)(2,1)}, bf16[16,128,512]{2,1,0:T(8,128)(2,1)S(1)}, u32[]{:S(2)}) copy-start(bf16[16,128,512]{2,1,0:T(8,128)(2,1)S(1)} %get-tuple-element.22) | copy-start | bytes 6291460
  35.3 23.0 %collective-permute-start.8 = (bf16[16,128,512]{2,1,0:T(8,128)(2,1)}, bf16[16,128,512]{2,1,0:T(8,128)(2,1)}, u32[]{:S(2)}, u32[]{:S(2)}) collective-permute-start(bf16[16,128,512]{2,1,0:T(8,128)(2,1)} %get-tuple-element.23), channel_id=1, source_target_pairs={{0,32},{32,0},{1,33},{33,1},{2,34},{34,2},{3,35},{35,3},{4,36},{36... | collective-permute-start | bytes 6291464 | tf_op jit(solution)/shard_map/ppermute | solution.py:292
  37.1 21.2 %copy-start.2 = (bf16[16,128,512]{2,1,0:T(8,128)(2,1)S(1)}, bf16[16,128,512]{2,1,0:T(8,128)(2,1)}, u32[]{:S(2)}) copy-start(bf16[16,128,512]{2,1,0:T(8,128)(2,1)} %copy-done.1) | copy-start | bytes 6291460
  54.7 11.6 %all-to-all-start.1 = ((f32[8,8,128]{2,1,0:T(8,128)}), f32[8,8,128]{2,1,0:T(8,128)S(1)}, u32[]{:S(2)}, u32[]{:S(2)}) async-start(f32[8,8,128]{2,1,0:T(8,128)} %broadcast_in_dim.6), calls=%async_computation.1 | async-start | bytes 65536 | tf_op jit(solution)/shard_map/all_to_all | solution.py:227
  66.2 31.5 %all-to-all-start.3 = ((bf16[16,128,512]{2,1,0:T(8,128)(2,1)}), bf16[16,128,512]{2,1,0:T(8,128)(2,1)S(1)}, u32[]{:S(2)}, u32[]{:S(2)}) async-start(bf16[16,128,512]{2,1,0:T(8,128)(2,1)} %add_convert_fusion), calls=%async_computation.3 | async-start | bytes 4194304 | tf_op jit(solution)/shard_map/all_to_all | solution.py:227
  71.4 2.6 %collective-permute-start.4 = (bf16[3,32,512]{2,1,0:T(8,128)(2,1)S(1)}, bf16[3,32,512]{2,1,0:T(8,128)(2,1)S(1)}, u32[]{:S(2)}, u32[]{:S(2)}) collective-permute-start(bf16[3,32,512]{2,1,0:T(8,128)(2,1)S(1)} %get-tuple-element.27), channel_id=1, source_target_pairs={{0,32},{32,64},{64,96},{96,128},{128,160},{160,192},{192,224},{1,3... | collective-permute-start | bytes 294920 | tf_op jit(solution)/shard_map/ppermute | solution.py:213
  72.7 4.9 %collective-permute-start.5 = (bf16[3,32,512]{2,1,0:T(8,128)(2,1)S(1)}, bf16[3,32,512]{2,1,0:T(8,128)(2,1)S(1)}, u32[]{:S(2)}, u32[]{:S(2)}) collective-permute-start(bf16[3,32,512]{2,1,0:T(8,128)(2,1)S(1)} %get-tuple-element.26), channel_id=1, source_target_pairs={{32,0},{64,32},{96,64},{128,96},{160,128},{192,160},{224,192},{33,... | collective-permute-start | bytes 294920 | tf_op jit(solution)/shard_map/ppermute | solution.py:213
  77.7 41.8 %collective-permute-start.7 = (bf16[14,3,512]{2,1,0:T(4,128)(2,1)S(1)}, bf16[14,3,512]{2,1,0:T(4,128)(2,1)S(1)}, u32[]{:S(2)}, u32[]{:S(2)}) collective-permute-start(bf16[14,3,512]{2,1,0:T(4,128)(2,1)S(1)} %pad_maximum_fusion.4), channel_id=1, source_target_pairs={{1,0},{2,1},{3,2},{4,3},{5,4},{6,5},{7,6},{8,7},{9,8},{10,9},{11,1... | collective-permute-start | bytes 129032 | tf_op jit(solution)/shard_map/ppermute | solution.py:213
  80.0 39.4 %collective-permute-start.6 = (bf16[14,3,512]{2,1,0:T(4,128)(2,1)S(1)}, bf16[14,3,512]{2,1,0:T(4,128)(2,1)S(1)}, u32[]{:S(2)}, u32[]{:S(2)}) collective-permute-start(bf16[14,3,512]{2,1,0:T(4,128)(2,1)S(1)} %pad_maximum_fusion.3), channel_id=1, source_target_pairs={{0,1},{1,2},{2,3},{3,4},{4,5},{5,6},{6,7},{7,8},{8,9},{9,10},{10,1... | collective-permute-start | bytes 129032 | tf_op jit(solution)/shard_map/ppermute | solution.py:213
  98.4 17.1 %all-to-all-start.2 = ((f32[32,8,128]{2,1,0:T(8,128)}), f32[32,8,128]{2,1,0:T(8,128)S(1)}, u32[]{:S(2)}, u32[]{:S(2)}) async-start(f32[32,8,128]{2,1,0:T(8,128)} %broadcast_in_dim.7), calls=%async_computation.2 | async-start | bytes 262144 | tf_op jit(solution)/shard_map/all_to_all | solution.py:227
  115.5 13.4 %all-to-all-start.4 = ((bf16[8,16,512]{2,1,0:T(8,128)(2,1)}), bf16[8,16,512]{2,1,0:T(8,128)(2,1)S(1)}, u32[]{:S(2)}, u32[]{:S(2)}) async-start(bf16[8,16,512]{2,1,0:T(8,128)(2,1)} %pad_maximum_fusion), calls=%async_computation.4 | async-start | bytes 262144 | tf_op jit(solution)/shard_map/all_to_all | solution.py:227

commit v2 on v1

--- a/solution.py
+++ b/solution.py
@@ -19,6 +19,7 @@
 
 NN = (((1,), (0,)), ((), ()))
 NT = (((1,), (1,)), ((), ()))
+TN = (((0,), (0,)), ((), ()))
 
 
 def product(left, right, dims):
@@ -52,13 +53,13 @@
 
 
 def forward_kernel(
-    core_ref, field, up, down, left, right, taps, gain, expand_t, reduce, scale, cotangent,
+    core_ref, field, up, down, left, right, taps, gain, expand, reduce, scale, cotangent,
     sent, kept, dpre_out, xhat_out, rstd_out, padded, dscale_out,
     conv, normed, dbranch, turned, chosen, expand_v, reduce_v, sems,
 ):
     core = core_ref[0]
     copies = [
-        pltpu.make_async_copy(expand_t, expand_v, sems.at[0]),
+        pltpu.make_async_copy(expand, expand_v, sems.at[0]),
         pltpu.make_async_copy(reduce, reduce_v, sems.at[1]),
     ]
     for copy in copies:
@@ -110,21 +111,21 @@
             owner = core if own else 1 - core
             chunk = y * CORE + owner
             hidden = pl.ds(pl.multiple_of(chunk * step, step), step)
-            pre = product(expand_v[hidden, :], normed[...], NT)
-            dact = product(reduce_v[hidden, :], dbranch[...], NT)
+            pre = product(normed[...], expand_v[:, hidden], NN)
+            dact = product(dbranch[...], reduce_v[hidden, :], NT)
             half = 0.5 * (1.0 + lax.erf(pre * INV_ROOT_TWO))
             slope = half + pre * jnp.exp(-0.5 * pre * pre) * INV_ROOT_TWO_PI
             act = (pre * half).astype(jnp.bfloat16)
             dpre = (dact * slope).astype(jnp.bfloat16)
-            dpre_out[hidden, :] = dpre
-            share = product(act, dbranch[...], NN)
+            dpre_out[:, hidden] = dpre
+            share = product(act, dbranch[...], TN)
             weighed = share * reduce_v[hidden, :].astype(jnp.float32)
             dscale_out[...] += jnp.sum(weighed.reshape(step // 8, 8, channels), axis=0)
             for x in range(X):
                 target[y * X + x, pl.ds(0, per_x), :] = share[x * per_x : (x + 1) * per_x].astype(
                     jnp.bfloat16
                 )
-            share = product(chosen[...], dpre, NT).astype(jnp.bfloat16)
+            share = product(chosen[...], dpre, NN).astype(jnp.bfloat16)
             rows = pl.ds(pl.multiple_of(per_x + (chunk // wide) * part_x, part_x), part_x)
             lanes = pl.ds(pl.multiple_of((chunk % wide) * step, step), step)
             for place in range(Y * X):
@@ -142,10 +143,9 @@
     height, width, channels = dconv_out.shape
     blocks = channels // LANES
     side = 7
+    dnormed = product(dpre[...], expand[...], NT)
     for block in range(blocks):
-        lanes = pl.ds(block * LANES, LANES)
-        dconv[block] = product(expand[lanes, :], dpre[...], NN).T
-        small[block] = jnp.zeros_like(small[block])
+        dconv[block] = dnormed[:, block * LANES : (block + 1) * LANES]
     sums = [jnp.zeros((width, LANES), jnp.float32)] * blocks
     for row in range(height):
         pixels = pl.ds(row * width, width)
@@ -161,14 +161,18 @@
             dconv[block, pixels, :] = value
             dconv_out[row, :, pl.ds(block * LANES, LANES)] = value.astype(jnp.bfloat16)
     taps = side * side
+    small[pl.ds(taps + 2, SMALL - taps - 2), :] = jnp.zeros(
+        (SMALL - taps - 2, channels), jnp.float32
+    )
     for block in range(blocks):
         lanes = pl.ds(block * LANES, LANES)
         total = jnp.sum(sums[block], axis=0, keepdims=True)
-        small[block, pl.ds(taps, 1), :] = total * multiplier
+        small[pl.ds(taps, 1), lanes] = total * multiplier
         total = jnp.sum(dscale[:, lanes], axis=0, keepdims=True)
-        small[block, pl.ds(taps + 1, 1), :] = total / scale[:, lanes] * multiplier
+        small[pl.ds(taps + 1, 1), lanes] = total / scale[:, lanes] * multiplier
 
     def tap_block(block, _):
+        lanes = pl.ds(pl.multiple_of(block * LANES, LANES), LANES)
         for second in range(side):
             totals = [jnp.zeros((8, LANES), jnp.float32)] * side
             for first_col in range(0, width, 8):
@@ -182,7 +186,7 @@
                         totals[first] = totals[first] + grads[row - first] * value
             for first, total in enumerate(totals):
                 total = jnp.sum(total, axis=0, keepdims=True) * multiplier
-                small[block, pl.ds(first * side + second, 1), :] = total
+                small[pl.ds(first * side + second, 1), lanes] = total
         return 0
 
     lax.fori_loop(0, blocks, tap_block, 0)
@@ -201,10 +205,55 @@
                 out[row, columns, lanes] = total.astype(jnp.bfloat16)
 
 
+def merge_kernel(kept, came, small, small_came, out):
+    rows = kept.shape[1]
+    out[:, pl.ds(0, rows), :] = (
+        kept[...].astype(jnp.float32) + came[...].astype(jnp.float32)
+    ).astype(jnp.bfloat16)
+    total = small[...] + small_came[...]
+    high = total.astype(jnp.bfloat16)
+    low = (total - high.astype(jnp.float32)).astype(jnp.bfloat16)
+    out[:, pl.ds(rows, 2 * total.shape[1]), :] = jnp.concatenate([high, low], axis=1)
+
+
+def plane_kernel(chunks, out, total):
+    total[...] = jnp.sum(chunks[...].astype(jnp.float32), axis=0)
+    rows = total.shape[0] - 8
+    each = rows // 2 // Z
+    wide = rows // 2 // (2 * Z)
+    small = total[pl.ds(rows, 4), :] + total[pl.ds(rows + 4, 4), :]
+    high = small.astype(jnp.bfloat16).astype(jnp.float32)
+    for z in range(Z):
+        parts = [total[pl.ds(z * each, each), :]]
+        parts += [
+            total[pl.ds(rows // 2 + q * 2 * Z + 2 * z, 2), :] for q in range(wide)
+        ]
+        out[z] = jnp.concatenate([*parts, high, small - high]).astype(jnp.bfloat16)
+
+
+def line_kernel(multiplier, chunks, dreduce, dexpand, small):
+    total = jnp.sum(chunks[...].astype(jnp.float32), axis=0)
+    each, channels = dreduce.shape
+    dreduce[...] = total[:each] * multiplier
+    for q in range(dexpand.shape[1] // channels):
+        first = each + 2 * q
+        dexpand[:, pl.ds(q * channels, channels)] = total[first : first + 2] * multiplier
+    part = total[2 * each : 2 * each + 4] + total[2 * each + 4 :]
+    small[...] = jnp.broadcast_to(part[None], small.shape)
+
+
+def small_kernel(full, dkernel, dgain, dscale):
+    side = dkernel.shape[0]
+    for place in range(side * side):
+        dkernel[place // side, pl.ds(place % side, 1), :] = full[place // 4, pl.ds(place % 4, 1), :]
+    for place, out in ((side * side, dgain), (side * side + 1, dscale)):
+        out[...] = full[place // 4, pl.ds(place % 4, 1), :]
+
+
 VMEM = pl.BlockSpec(memory_space=pltpu.VMEM)
-ANY = pl.BlockSpec(memory_space=pl.ANY)
+HBM = pl.BlockSpec(memory_space=pltpu.HBM)
 SMEM = pl.BlockSpec(memory_space=pltpu.SMEM)
-PARAMS = pltpu.CompilerParams(vmem_limit_bytes=40 << 20)
+PARAMS = pltpu.CompilerParams(vmem_limit_bytes=24 << 20)
 
 
 def shifted(value, axes, by):
@@ -225,18 +274,6 @@
 
 def exchanged(chunks, axes):
     return lax.all_to_all(chunks, axes, 0, 0, tiled=True)
-
-
-def summed(chunks):
-    return jnp.sum(chunks.astype(jnp.float32), axis=0)
-
-
-def everywhere(small):
-    chunks = exchanged(small.reshape(Y * CORE * X, 8, LANES), ("y", "core", "x"))
-    part = summed(chunks)
-    part = summed(exchanged(jnp.broadcast_to(part, (Z, *part.shape)), "z"))
-    full = exchanged(jnp.broadcast_to(part, (Y * CORE * X, *part.shape)), ("y", "core", "x"))
-    return full.reshape(small.shape)
 
 
 def shards(features, kernel, gain, w_expand, w_reduce, layer_scale, cotangent):
@@ -262,12 +299,12 @@
     sent, kept, dpre, xhat, rstd, padded, dscale = pl.pallas_call(
         forward_kernel,
         name="forward",
-        in_specs=[SMEM] + [VMEM] * 7 + [ANY] * 2 + [VMEM] * 2,
+        in_specs=[SMEM] + [VMEM] * 7 + [HBM] * 2 + [VMEM] * 2,
         out_specs=[VMEM] * 7,
         out_shape=[
             shape((places, 2 * rows, channels), bf16),
             shape((places, 2 * rows, channels), bf16),
-            shape((hidden, pixels), bf16),
+            shape((pixels, hidden), bf16),
             shape((blocks, pixels, LANES), f32),
             shape((pixels, LANES), f32),
             shape(padded_shape, f32),
@@ -279,27 +316,21 @@
             pltpu.VMEM((pixels, channels), bf16),
             pltpu.VMEM((channels, pixels), bf16),
             pltpu.VMEM((channels, pixels), bf16),
-            pltpu.VMEM((hidden, channels), bf16),
+            pltpu.VMEM((channels, hidden), bf16),
             pltpu.VMEM((hidden, channels), bf16),
             pltpu.SemaphoreType.DMA((2,)),
         ],
         compiler_params=PARAMS,
     )(
-        core, features, *borders(features, reach), taps, gain_row, w_expand.T, w_reduce,
+        core, features, *borders(features, reach), taps, gain_row,
+        pltpu.with_memory_space_constraint(w_expand, pltpu.HBM),
+        pltpu.with_memory_space_constraint(w_reduce, pltpu.HBM),
+
         scale_row, cotangent,
     )
 
-    came = lax.ppermute(sent, "core", [(0, 1), (1, 0)])
-    chip = (kept.astype(f32) + came.astype(f32)).astype(bf16)
-    plane = summed(exchanged(chip, ("y", "x")))
-    first = plane[:rows].reshape(Z, -1, channels)
-    second = plane[rows:].reshape(hidden // channels, Z, -1, channels).transpose(1, 2, 0, 3)
-    second = second.reshape(Z, -1, channels)
-    line = jnp.concatenate([first, second], axis=1).astype(bf16)
-    own = summed(exchanged(line, "z")) * multiplier
-    dreduce = own[: rows // Z]
-    dexpand = own[rows // Z :].reshape(-1, hidden)
-
+    swap = [(0, 1), (1, 0)]
+    came = lax.ppermute(sent, "core", swap)
     dconv, small = pl.pallas_call(
         functools.partial(backward_kernel, multiplier),
         name="backward",
@@ -307,13 +338,59 @@
         out_specs=[VMEM] * 2,
         out_shape=[
             shape((height, width, channels), bf16),
-            shape((blocks, SMALL, LANES), f32),
+            shape((SMALL, channels), f32),
         ],
         scratch_shapes=[pltpu.VMEM((blocks, pixels, LANES), f32)],
         compiler_params=PARAMS,
     )(dpre, w_expand, xhat, rstd, padded, gain_row, dscale, scale_row)
 
-    small = everywhere(small).transpose(1, 0, 2).reshape(SMALL, channels)
+    small_came = lax.ppermute(small, "core", swap)
+    each = SMALL // places
+    whole = 2 * rows + 2 * each
+    chip = pl.pallas_call(
+        merge_kernel,
+        name="merge",
+        grid=(Y,),
+        in_specs=[pl.BlockSpec((X, 2 * rows, channels), lambda i: (i, 0, 0))] * 2
+        + [pl.BlockSpec((X, each, channels), lambda i: (i, 0, 0))] * 2,
+        out_specs=pl.BlockSpec((X, whole, channels), lambda i: (i, 0, 0)),
+        out_shape=shape((places, whole, channels), bf16),
+        compiler_params=PARAMS,
+    )(
+        kept, came, small.reshape(places, each, channels),
+        small_came.reshape(places, each, channels),
+    )
+    chip, dconv = lax.optimization_barrier((chip, dconv))
+    chunks, edges = lax.optimization_barrier((exchanged(chip, ("y", "x")), borders(dconv, reach)))
+    line = pl.pallas_call(
+        plane_kernel,
+        name="plane",
+        in_specs=[VMEM],
+        out_specs=VMEM,
+        out_shape=shape((Z, 2 * rows // Z + 2 * each, channels), bf16),
+        scratch_shapes=[pltpu.VMEM((whole, channels), f32)],
+        compiler_params=PARAMS,
+    )(chunks)
+    dreduce, dexpand, part = pl.pallas_call(
+        functools.partial(line_kernel, multiplier),
+        name="line",
+        in_specs=[VMEM],
+        out_specs=[VMEM] * 3,
+        out_shape=[
+            shape((rows // Z, channels), f32),
+            shape((channels * rows // Z // hidden, hidden), f32),
+            shape((places, each, channels), f32),
+        ],
+        compiler_params=PARAMS,
+    )(exchanged(line, "z"))
+    dkernel, dgain, dscale = pl.pallas_call(
+        small_kernel,
+        name="small",
+        in_specs=[VMEM],
+        out_specs=[VMEM] * 3,
+        out_shape=[shape((side, side, channels), f32)] + [shape((1, channels), f32)] * 2,
+        compiler_params=PARAMS,
+    )(exchanged(part, ("y", "x")))
     grad_features = pl.pallas_call(
         feature_kernel,
         name="features",
@@ -322,12 +399,12 @@
         out_shape=shape((height, width, channels), bf16),
         scratch_shapes=[pltpu.VMEM(padded_shape, f32)],
         compiler_params=PARAMS,
-    )(dconv, *borders(dconv, reach), flipped, cotangent)
+    )(dconv, *edges, flipped, cotangent)
     return (
         grad_features,
-        small[:taps_total].reshape(side, side, channels),
-        small[taps_total],
-        small[taps_total + 1],
+        dkernel,
+        dgain.reshape(channels),
+        dscale.reshape(channels),
         dexpand,
         dreduce,
     )

time: 131 us -> 121 us (0.924)
  local copies, waits for them, and re-layouts: 12.7 us -> 6.3 us
  Pallas kernels: 13.7 us -> 19.7 us
  other arithmetic: 4.79 us -> 0.19 us
  waiting for transfers between devices: 37.7 us -> 34.8 us
  blocking collectives: 14 us -> 12.2 us
    all_to_all x4 -> x2, waiting for transfers between devices: 29.6 us -> 18.4 us  [exchanged(): return lax.all_to_all(chunks, axes, 0, 0, tiled=True)]
    ppermute x8, waiting for transfers between devices: 8.19 us -> 15.1 us  [shifted(): return lax.ppermute(value, axes, pairs)]
    pallas_call x0 -> x4, Pallas kernels: none -> 5.85 us  [the longest x1 4.03 us: shards(): pl.pallas_call(merge_kernel, name='merge', grid=(Y,), in_specs=[pl.BlockS...]
    convert_element_type x1 -> x0, other arithmetic: 3.58 us -> none  [shards(): chip = (kept.astype(f32) + came.astype(f32)).astype(bf16)]
    unnamed x17 -> x12, local copies, waits for them, and re-layouts: 5.89 us -> 3.27 us
    all_to_all x1, blocking collectives: 14 us -> 12.2 us  [exchanged(): return lax.all_to_all(chunks, axes, 0, 0, tiled=True)]
    all_to_all x4 -> x2, starting transfers between devices: 23.2 us -> 22.1 us  [exchanged(): return lax.all_to_all(chunks, axes, 0, 0, tiled=True)]
  transfers between devices with their start and end apart: 13 -> 12, of which waited for: 7 -> 8; matrix products, arithmetic and copies ran while one was open for 9% -> 2% of each run, Pallas kernels for 4% -> 5%
where the time goes in v2:
time: 121 us; the launch traced here: 120 us
  starting transfers between devices  45.7 us (38%)
  waiting for transfers between devices  34.8 us (29%)
  Pallas kernels  19.7 us (16%)
  blocking collectives  12.2 us (10%)
  local copies, waits for them, and re-layouts  6.3 us (5%)
    all_to_all x2, starting transfers between devices, exchanged(): return lax.all_to_all(chunks, axes, 0, 0, tiled=True)  22.1 us
    ppermute x8, starting transfers between devices, shifted(): return lax.ppermute(value, axes, pairs)  21.7 us
    all_to_all x2, waiting for transfers between devices, exchanged(): return lax.all_to_all(chunks, axes, 0, 0, tiled=True)  18.4 us
    ppermute x8, waiting for transfers between devices, shifted(): return lax.ppermute(value, axes, pairs)  15.1 us
    all_to_all x1, blocking collectives, exchanged(): return lax.all_to_all(chunks, axes, 0, 0, tiled=True)  12.2 us
    pallas_call x1, Pallas kernels, shards(): pl.pallas_call(forward_kernel, name='forward', in_specs=[SMEM] + [VMEM] *...  8.34 us
    pallas_call x1, Pallas kernels, shards(): pl.pallas_call(merge_kernel, name='merge', grid=(Y,), in_specs=[pl.BlockS...  4.03 us
    unnamed x12, local copies, waits for them, and re-layouts  3.27 us
  transfers between devices with their start and end apart: 12, of which 8 were waited for; matrix products, arithmetic and copies ran while one was open for 2% of the time, Pallas kernels for 5%

profile of v2, /device:TPU:2, one launch (start us, length us, event | category | flops | bytes accessed | tf_op | source)
XLA Modules:
  0.0 119.8 jit_solution(13738860263569870071)
XLA Ops:
  0.6 1.0 fusion.3
  1.6 1.7 %collective-permute-start = (bf16[3,32,512]{2,1,0:T(8,128)(2,1)S(1)}, bf16[3,32,512]{2,1,0:T(8,128)(2,1)S(1)}, u32[]{:S(2)}, u32[]{:S(2)}) collective-permute-start(bf16[3,32,512]{2,1,0:T(8,128)(2,1)S(1)} %get-tuple-element.57), channel_id=1, source_target_pairs={{0,32},{32,64},{64,96},{96,128},{128,160},{160,192},{192,224},{1,3... | collective-permute-start | bytes 294920 | tf_op jit(solution)/shard_map/ppermute | solution.py:262
  3.3 1.3 %collective-permute-start.1 = (bf16[3,32,512]{2,1,0:T(8,128)(2,1)S(1)}, bf16[3,32,512]{2,1,0:T(8,128)(2,1)S(1)}, u32[]{:S(2)}, u32[]{:S(2)}) collective-permute-start(bf16[3,32,512]{2,1,0:T(8,128)(2,1)S(1)} %get-tuple-element.56), channel_id=1, source_target_pairs={{32,0},{64,32},{96,64},{128,96},{160,128},{192,160},{224,192},{33,... | collective-permute-start | bytes 294920 | tf_op jit(solution)/shard_map/ppermute | solution.py:262
  4.6 0.9 fusion.2
  5.6 2.3 %collective-permute-done.1.down = bf16[3,32,512]{2,1,0:T(8,128)(2,1)S(1)} collective-permute-done((bf16[3,32,512]{2,1,0:T(8,128)(2,1)S(1)}, bf16[3,32,512]{2,1,0:T(8,128)(2,1)S(1)}, u32[]{:S(2)}, u32[]{:S(2)}) %collective-permute-start.1) | collective-permute-done | bytes 98336 | tf_op jit(solution)/shard_map/ppermute | solution.py:262
  8.0 7.7 %collective-permute-start.3 = (bf16[14,3,512]{2,1,0:T(4,128)(2,1)S(1)}, bf16[14,3,512]{2,1,0:T(4,128)(2,1)S(1)}, u32[]{:S(2)}, u32[]{:S(2)}) collective-permute-start(bf16[14,3,512]{2,1,0:T(4,128)(2,1)S(1)} %pad_maximum_fusion.1), channel_id=1, source_target_pairs={{1,0},{2,1},{3,2},{4,3},{5,4},{6,5},{7,6},{8,7},{9,8},{10,9},{11,1... | collective-permute-start | bytes 129032 | tf_op jit(solution)/shard_map/ppermute | solution.py:262
  15.8 1.9 %collective-permute-start.2 = (bf16[14,3,512]{2,1,0:T(4,128)(2,1)S(1)}, bf16[14,3,512]{2,1,0:T(4,128)(2,1)S(1)}, u32[]{:S(2)}, u32[]{:S(2)}) collective-permute-start(bf16[14,3,512]{2,1,0:T(4,128)(2,1)S(1)} %pad_maximum_fusion), channel_id=1, source_target_pairs={{0,1},{1,2},{2,3},{3,4},{4,5},{5,6},{6,7},{7,8},{8,9},{9,10},{10,1... | collective-permute-start | bytes 129032 | tf_op jit(solution)/shard_map/ppermute | solution.py:262
  17.7 0.9 reshape.37
  18.7 5.3 %collective-permute-done.2.left = bf16[14,3,512]{2,1,0:T(4,128)(2,1)S(1)} collective-permute-done((bf16[14,3,512]{2,1,0:T(4,128)(2,1)S(1)}, bf16[14,3,512]{2,1,0:T(4,128)(2,1)S(1)}, u32[]{:S(2)}, u32[]{:S(2)}) %collective-permute-start.2) | collective-permute-done | bytes 43040 | tf_op jit(solution)/shard_map/ppermute | solution.py:262
  23.9 0.9 copy-done.1
  24.9 0.9 copy-done.3
  25.8 0.7 copy-done.4
  26.5 0.7 copy-done.5
  27.2 8.3 %forward.1 = (bf16[16,128,512]{2,1,0:T(8,128)(2,1)}, bf16[16,128,512]{2,1,0:T(8,128)(2,1)S(1)}, bf16[256,2048]{1,0:T(8,128)(2,1)S(1)}, f32[4,256,128]{2,1,0:T(8,...) custom-call(s32[1]{0:T(128)} %bitcast.core_ref, ...), custom_call_target="tpu_custom_call" | custom-call | tf_op jit(solution)/shard_map/forward/pallas_call | solution.py:299
  35.6 1.9 %collective-permute-start.4 = (bf16[16,128,512]{2,1,0:T(8,128)(2,1)}, bf16[16,128,512]{2,1,0:T(8,128)(2,1)}, u32[]{:S(2)}, u32[]{:S(2)}) collective-permute-start(bf16[16,128,512]{2,1,0:T(8,128)(2,1)} %get-tuple-element.29), channel_id=1, source_target_pairs={{0,32},{32,0},{1,33},{33,1},{2,34},{34,2},{3,35},{35,3},{4,36},{36... | collective-permute-start | bytes 6291464 | tf_op jit(solution)/shard_map/ppermute | solution.py:333
  37.4 3.0 %backward.1 = (bf16[8,32,512]{2,1,0:T(8,128)(2,1)S(1)}, f32[64,512]{1,0:T(8,128)S(1)}) custom-call(bf16[256,2048]{1,0:T(8,128)(2,1)S(1)} %get-tuple-element.30.dpre, bf16[512,2048]{1,0:T(8,128)(2,1)S(1)} %copy-done, f32[4,256,128]{2,1,0:T(8,128)S(1)} %get-tuple-element.31.xhat, f32[256,128]{1,0:T(8,128)S(1)} %get-tuple-element.32.rstd, ...), custom_call_target="tpu_custom_call" | custom-call | tf_op jit(solution)/shard_map/backward/pallas_call | solution.py:334
  40.6 1.3 %collective-permute-done.5 = f32[64,512]{1,0:T(8,128)S(1)} collective-permute-done((f32[64,512]{1,0:T(8,128)S(1)}, f32[64,512]{1,0:T(8,128)S(1)}, u32[]{:S(2)}, u32[]{:S(2)}) %collective-permute-start.5) | collective-permute-done | bytes 131104 | tf_op jit(solution)/shard_map/ppermute | solution.py:347
  42.0 4.0 %merge.1 = bf16[16,136,512]{2,1,0:T(8,128)(2,1)} custom-call(bf16[16,128,512]{2,1,0:T(8,128)(2,1)S(1)} %get-tuple-element.28.kept, bf16[16,128,512]{2,1,0:T(8,128)(2,1)} %collective-permute-done.4.came, f32[16,4,512]{2,1,0:T(4,128)S(1)} %reshape.40.small, f32[16,4,512]{2,1,0:T(4,128)S(1)} %reshape.41.small_came), custom_call_target="tpu_custom_call" | custom-call | tf_op jit(solution)/shard_map/merge/pallas_call | solution.py:350
  46.0 7.7 %all-to-all-start = ((bf16[16,136,512]{2,1,0:T(8,128)(2,1)}), bf16[16,136,512]{2,1,0:T(8,128)(2,1)S(1)}, u32[]{:S(2)}, u32[]{:S(2)}) async-start(bf16[16,136,512]{2,1,0:T(8,128)(2,1)} %merge.1), calls=%async_computation | async-start | bytes 4456448 | tf_op jit(solution)/shard_map/all_to_all | solution.py:276
  53.8 1.8 %collective-permute-start.6 = (bf16[3,32,512]{2,1,0:T(8,128)(2,1)S(1)}, bf16[3,32,512]{2,1,0:T(8,128)(2,1)S(1)}, u32[]{:S(2)}, u32[]{:S(2)}) collective-permute-start(bf16[3,32,512]{2,1,0:T(8,128)(2,1)S(1)} %get-tuple-element.53), channel_id=1, source_target_pairs={{0,32},{32,64},{64,96},{96,128},{128,160},{160,192},{192,224},{1,3... | collective-permute-start | bytes 294920 | tf_op jit(solution)/shard_map/ppermute | solution.py:262
  55.6 1.3 %collective-permute-start.7 = (bf16[3,32,512]{2,1,0:T(8,128)(2,1)S(1)}, bf16[3,32,512]{2,1,0:T(8,128)(2,1)S(1)}, u32[]{:S(2)}, u32[]{:S(2)}) collective-permute-start(bf16[3,32,512]{2,1,0:T(8,128)(2,1)S(1)} %get-tuple-element.52), channel_id=1, source_target_pairs={{32,0},{64,32},{96,64},{128,96},{160,128},{192,160},{224,192},{33,... | collective-permute-start | bytes 294920 | tf_op jit(solution)/shard_map/ppermute | solution.py:262
  57.0 3.2 %collective-permute-done.7.down = bf16[3,32,512]{2,1,0:T(8,128)(2,1)S(1)} collective-permute-done((bf16[3,32,512]{2,1,0:T(8,128)(2,1)S(1)}, bf16[3,32,512]{2,1,0:T(8,128)(2,1)S(1)}, u32[]{:S(2)}, u32[]{:S(2)}) %collective-permute-start.7) | collective-permute-done | bytes 98336 | tf_op jit(solution)/shard_map/ppermute | solution.py:262
  60.2 1.9 %collective-permute-start.9 = (bf16[14,3,512]{2,1,0:T(4,128)(2,1)S(1)}, bf16[14,3,512]{2,1,0:T(4,128)(2,1)S(1)}, u32[]{:S(2)}, u32[]{:S(2)}) collective-permute-start(bf16[14,3,512]{2,1,0:T(4,128)(2,1)S(1)} %pad_maximum_fusion.3), channel_id=1, source_target_pairs={{1,0},{2,1},{3,2},{4,3},{5,4},{6,5},{7,6},{8,7},{9,8},{10,9},{11,1... | collective-permute-start | bytes 129032 | tf_op jit(solution)/shard_map/ppermute | solution.py:262
  62.2 3.9 %collective-permute-start.8 = (bf16[14,3,512]{2,1,0:T(4,128)(2,1)S(1)}, bf16[14,3,512]{2,1,0:T(4,128)(2,1)S(1)}, u32[]{:S(2)}, u32[]{:S(2)}) collective-permute-start(bf16[14,3,512]{2,1,0:T(4,128)(2,1)S(1)} %pad_maximum_fusion.2), channel_id=1, source_target_pairs={{0,1},{1,2},{2,3},{3,4},{4,5},{5,6},{6,7},{7,8},{8,9},{9,10},{10,1... | collective-permute-start | bytes 129032 | tf_op jit(solution)/shard_map/ppermute | solution.py:262
  66.3 4.2 %collective-permute-done.8.left = bf16[14,3,512]{2,1,0:T(4,128)(2,1)S(1)} collective-permute-done((bf16[14,3,512]{2,1,0:T(4,128)(2,1)S(1)}, bf16[14,3,512]{2,1,0:T(4,128)(2,1)S(1)}, u32[]{:S(2)}, u32[]{:S(2)}) %collective-permute-start.8) | collective-permute-done | bytes 43040 | tf_op jit(solution)/shard_map/ppermute | solution.py:262
  70.5 14.3 %all-to-all-done.chunks = bf16[16,136,512]{2,1,0:T(8,128)(2,1)S(1)} async-done(((bf16[16,136,512]{2,1,0:T(8,128)(2,1)}), bf16[16,136,512]{2,1,0:T(8,128)(2,1)S(1)}, u32[]{:S(2)}, u32[]{:S(2)}) %all-to-all-start) | async-done | bytes 2228256 | tf_op jit(solution)/shard_map/all_to_all | solution.py:276
  85.2 12.2 %all_to_all.15.chunks = bf16[8,24,512]{2,1,0:T(8,128)(2,1)S(1)} all-to-all(bf16[8,24,512]{2,1,0:T(8,128)(2,1)S(1)} %plane.1), channel_id=1, replica_groups=mesh['y'=4,'core'=2,'x'=4,'z'=8] {'z'}, dimensions={0} | all-to-all | bytes 393216 | tf_op jit(solution)/shard_map/all_to_all | solution.py:276
  97.4 0.7 line.1
  98.1 14.4 %all-to-all-start.2 = ((f32[16,4,512]{2,1,0:T(4,128)}), f32[16,4,512]{2,1,0:T(4,128)S(1)}, u32[]{:S(2)}, u32[]{:S(2)}) async-start(f32[16,4,512]{2,1,0:T(4,128)} %get-tuple-element.44), calls=%async_computation.2 | async-start | bytes 262144 | tf_op jit(solution)/shard_map/all_to_all | solution.py:276
  112.5 2.5 %features.1 = bf16[8,32,512]{2,1,0:T(8,128)(2,1)} custom-call(bf16[8,32,512]{2,1,0:T(8,128)(2,1)S(1)} %get-tuple-element.37.field, bf16[3,32,512]{2,1,0:T(8,128)(2,1)S(1)} %collective-permute-done.6.up, bf16[3,32,512]{2,1,0:T(8,128)(2,1)S(1)} %collective-permute-done.7.down, bf16[14,3,512]{2,1,0:T(4,128)(2,1)S(1)} %collective-permute-done.8.left, ...), custom_call_target="tpu_custom_call" | custom-call | tf_op jit(solution)/shard_map/features/pallas_call | solution.py:394
  115.0 4.1 %all-to-all-done.2.full = f32[16,4,512]{2,1,0:T(4,128)S(1)} async-done(((f32[16,4,512]{2,1,0:T(4,128)}), f32[16,4,512]{2,1,0:T(4,128)S(1)}, u32[]{:S(2)}, u32[]{:S(2)}) %all-to-all-start.2) | async-done | bytes 131104 | tf_op jit(solution)/shard_map/all_to_all | solution.py:276
  119.1 0.7 small.1
  (29 shorter events, 1.2 us)
Async XLA Ops:
  1.6 4.0 %collective-permute-start = (bf16[3,32,512]{2,1,0:T(8,128)(2,1)S(1)}, bf16[3,32,512]{2,1,0:T(8,128)(2,1)S(1)}, u32[]{:S(2)}, u32[]{:S(2)}) collective-permute-start(bf16[3,32,512]{2,1,0:T(8,128)(2,1)S(1)} %get-tuple-element.57), channel_id=1, source_target_pairs={{0,32},{32,64},{64,96},{96,128},{128,160},{160,192},{192,224},{1,3... | collective-permute-start | bytes 294920 | tf_op jit(solution)/shard_map/ppermute | solution.py:262
  3.3 4.6 %collective-permute-start.1 = (bf16[3,32,512]{2,1,0:T(8,128)(2,1)S(1)}, bf16[3,32,512]{2,1,0:T(8,128)(2,1)S(1)}, u32[]{:S(2)}, u32[]{:S(2)}) collective-permute-start(bf16[3,32,512]{2,1,0:T(8,128)(2,1)S(1)} %get-tuple-element.56), channel_id=1, source_target_pairs={{32,0},{64,32},{96,64},{128,96},{160,128},{192,160},{224,192},{33,... | collective-permute-start | bytes 294920 | tf_op jit(solution)/shard_map/ppermute | solution.py:262
  8.0 10.7 %collective-permute-start.3 = (bf16[14,3,512]{2,1,0:T(4,128)(2,1)S(1)}, bf16[14,3,512]{2,1,0:T(4,128)(2,1)S(1)}, u32[]{:S(2)}, u32[]{:S(2)}) collective-permute-start(bf16[14,3,512]{2,1,0:T(4,128)(2,1)S(1)} %pad_maximum_fusion.1), channel_id=1, source_target_pairs={{1,0},{2,1},{3,2},{4,3},{5,4},{6,5},{7,6},{8,7},{9,8},{10,9},{11,1... | collective-permute-start | bytes 129032 | tf_op jit(solution)/shard_map/ppermute | solution.py:262
  15.8 8.2 %collective-permute-start.2 = (bf16[14,3,512]{2,1,0:T(4,128)(2,1)S(1)}, bf16[14,3,512]{2,1,0:T(4,128)(2,1)S(1)}, u32[]{:S(2)}, u32[]{:S(2)}) collective-permute-start(bf16[14,3,512]{2,1,0:T(4,128)(2,1)S(1)} %pad_maximum_fusion), channel_id=1, source_target_pairs={{0,1},{1,2},{2,3},{3,4},{4,5},{5,6},{6,7},{7,8},{8,9},{9,10},{10,1... | collective-permute-start | bytes 129032 | tf_op jit(solution)/shard_map/ppermute | solution.py:262
  23.9 1.0 copy-start.1
  24.9 0.9 copy-start.3
  25.8 0.7 copy-start.4
  26.5 0.7 copy-start.5
  27.2 10.2 %copy-start = (bf16[512,2048]{1,0:T(8,128)(2,1)S(1)}, bf16[512,2048]{1,0:T(8,128)(2,1)}, u32[]{:S(2)}) copy-start(bf16[512,2048]{1,0:T(8,128)(2,1)} %expand.3) | copy-start | bytes 6291460
  35.6 6.4 %collective-permute-start.4 = (bf16[16,128,512]{2,1,0:T(8,128)(2,1)}, bf16[16,128,512]{2,1,0:T(8,128)(2,1)}, u32[]{:S(2)}, u32[]{:S(2)}) collective-permute-start(bf16[16,128,512]{2,1,0:T(8,128)(2,1)} %get-tuple-element.29), channel_id=1, source_target_pairs={{0,32},{32,0},{1,33},{33,1},{2,34},{34,2},{3,35},{35,3},{4,36},{36... | collective-permute-start | bytes 6291464 | tf_op jit(solution)/shard_map/ppermute | solution.py:333
  40.5 1.4 %collective-permute-start.5 = (f32[64,512]{1,0:T(8,128)S(1)}, f32[64,512]{1,0:T(8,128)S(1)}, u32[]{:S(2)}, u32[]{:S(2)}) collective-permute-start(f32[64,512]{1,0:T(8,128)S(1)} %get-tuple-element.35), channel_id=1, source_target_pairs={{0,32},{32,0},{1,33},{33,1},{2,34},{34,2},{3,35},{35,3},{4,36},{36... | collective-permute-start | bytes 393224 | tf_op jit(solution)/shard_map/ppermute | solution.py:347
  46.0 38.8 %all-to-all-start = ((bf16[16,136,512]{2,1,0:T(8,128)(2,1)}), bf16[16,136,512]{2,1,0:T(8,128)(2,1)S(1)}, u32[]{:S(2)}, u32[]{:S(2)}) async-start(bf16[16,136,512]{2,1,0:T(8,128)(2,1)} %merge.1), calls=%async_computation | async-start | bytes 4456448 | tf_op jit(solution)/shard_map/all_to_all | solution.py:276
  53.7 58.8 %copy-start.2 = (bf16[8,32,512]{2,1,0:T(8,128)(2,1)S(1)}, bf16[8,32,512]{2,1,0:T(8,128)(2,1)}, u32[]{:S(2)}) copy-start(bf16[8,32,512]{2,1,0:T(8,128)(2,1)} %cotangent.3) | copy-start | bytes 786436
  53.8 3.2 %collective-permute-start.6 = (bf16[3,32,512]{2,1,0:T(8,128)(2,1)S(1)}, bf16[3,32,512]{2,1,0:T(8,128)(2,1)S(1)}, u32[]{:S(2)}, u32[]{:S(2)}) collective-permute-start(bf16[3,32,512]{2,1,0:T(8,128)(2,1)S(1)} %get-tuple-element.53), channel_id=1, source_target_pairs={{0,32},{32,64},{64,96},{96,128},{128,160},{160,192},{192,224},{1,3... | collective-permute-start | bytes 294920 | tf_op jit(solution)/shard_map/ppermute | solution.py:262
  55.6 4.5 %collective-permute-start.7 = (bf16[3,32,512]{2,1,0:T(8,128)(2,1)S(1)}, bf16[3,32,512]{2,1,0:T(8,128)(2,1)S(1)}, u32[]{:S(2)}, u32[]{:S(2)}) collective-permute-start(bf16[3,32,512]{2,1,0:T(8,128)(2,1)S(1)} %get-tuple-element.52), channel_id=1, source_target_pairs={{32,0},{64,32},{96,64},{128,96},{160,128},{192,160},{224,192},{33,... | collective-permute-start | bytes 294920 | tf_op jit(solution)/shard_map/ppermute | solution.py:262
  60.2 6.1 %collective-permute-start.9 = (bf16[14,3,512]{2,1,0:T(4,128)(2,1)S(1)}, bf16[14,3,512]{2,1,0:T(4,128)(2,1)S(1)}, u32[]{:S(2)}, u32[]{:S(2)}) collective-permute-start(bf16[14,3,512]{2,1,0:T(4,128)(2,1)S(1)} %pad_maximum_fusion.3), channel_id=1, source_target_pairs={{1,0},{2,1},{3,2},{4,3},{5,4},{6,5},{7,6},{8,7},{9,8},{10,9},{11,1... | collective-permute-start | bytes 129032 | tf_op jit(solution)/shard_map/ppermute | solution.py:262
  62.2 8.3 %collective-permute-start.8 = (bf16[14,3,512]{2,1,0:T(4,128)(2,1)S(1)}, bf16[14,3,512]{2,1,0:T(4,128)(2,1)S(1)}, u32[]{:S(2)}, u32[]{:S(2)}) collective-permute-start(bf16[14,3,512]{2,1,0:T(4,128)(2,1)S(1)} %pad_maximum_fusion.2), channel_id=1, source_target_pairs={{0,1},{1,2},{2,3},{3,4},{4,5},{5,6},{6,7},{7,8},{8,9},{9,10},{10,1... | collective-permute-start | bytes 129032 | tf_op jit(solution)/shard_map/ppermute | solution.py:262
  98.1 21.0 %all-to-all-start.2 = ((f32[16,4,512]{2,1,0:T(4,128)}), f32[16,4,512]{2,1,0:T(4,128)S(1)}, u32[]{:S(2)}, u32[]{:S(2)}) async-start(f32[16,4,512]{2,1,0:T(4,128)} %get-tuple-element.44), calls=%async_computation.2 | async-start | bytes 262144 | tf_op jit(solution)/shard_map/all_to_all | solution.py:276

commit v3 on v2

v3 whole, which is shorter than its diff:
```python
import functools
import math

import jax
import jax.numpy as jnp
from jax import lax
from jax.experimental import pallas as pl
from jax.experimental.pallas import tpu as pltpu
from jax.sharding import Mesh
from jax.sharding import PartitionSpec as P

Y, CORE, X, Z = 4, 2, 4, 8
ROW, COL = ("y", "core"), ("x", "z")
INV_ROOT_TWO = 1.0 / math.sqrt(2.0)
INV_ROOT_TWO_PI = 1.0 / math.sqrt(2.0 * math.pi)
LANES = 128
LEFT = 8
SMALL = 64

NN = (((1,), (0,)), ((), ()))
NT = (((1,), (1,)), ((), ()))
TN = (((0,), (0,)), ((), ()))


def product(left, right, dims):
    return lax.dot_general(left, right, dims, preferred_element_type=jnp.float32)


def fill(padded, field, up, down, left, right, reach):
    height, width, channels = field.shape
    for block in range(channels // LANES):
        lanes = pl.ds(block * LANES, LANES)
        own = pl.ds(LEFT, width)
        padded[block, pl.ds(0, reach), own, :] = up[:, :, lanes].astype(jnp.float32)
        padded[block, pl.ds(reach, height), own, :] = field[:, :, lanes].astype(jnp.float32)
        padded[block, pl.ds(reach + height, reach), own, :] = down[:, :, lanes].astype(jnp.float32)
        padded[block, :, pl.ds(LEFT - reach, reach), :] = left[:, :, lanes].astype(jnp.float32)
        padded[block, :, pl.ds(LEFT + width, reach), :] = right[:, :, lanes].astype(jnp.float32)


def depthwise(padded, taps, block, first_col, height, side, flip):
    reach = side // 2
    totals = [None] * height
    lanes = pl.ds(pl.multiple_of(block * LANES, LANES), LANES)
    for second in range(side):
        columns = pl.ds(LEFT - reach + first_col + second, 8)
        rows = [padded[block, row, columns, :] for row in range(height + side - 1)]
        for first in range(side):
            if flip:
                weight = taps[side - 1 - first, pl.ds(side - 1 - second, 1), lanes]
            else:
                weight = taps[first, pl.ds(second, 1), lanes]
            for row in range(height):
                term = weight * rows[row + first]
                totals[row] = term if totals[row] is None else totals[row] + term
    return totals


def forward_kernel(
    core_ref, field_h, up, down, left, right, taps_h, gain_h, expand_h, reduce_h, scale_h,
    cotangent_h,
    sent_e, kept_e, sent_r, kept_r, dpre_out, xhat_out, rstd_out, padded, rows_out,
    conv, normed, dbranch, turned, chosen, field, taps, gain, expand, reduce, scale, cotangent,
    sems,
):
    core = core_ref[0]
    copies = [
        pltpu.make_async_copy(source, target, sems.at[i])
        for i, (source, target) in enumerate(
            (
                (field_h, field),
                (taps_h, taps),
                (gain_h, gain),
                (scale_h, scale),
                (cotangent_h, cotangent),
                (expand_h, expand),
                (reduce_h, reduce),
            )
        )
    ]
    for copy in copies:
        copy.start()
    for copy in copies[:2]:
        copy.wait()
    height, width, channels = field.shape
    blocks = channels // LANES
    side = 7
    fill(padded, field, up, down, left, right, side // 2)

    def conv_block(block, _):
        for first_col in range(0, width, 8):
            for row, total in enumerate(
                depthwise(padded, taps, block, first_col, height, side, False)
            ):
                conv[block, pl.ds(row * width + first_col, 8), :] = total
        return 0

    lax.fori_loop(0, blocks, conv_block, 0)
    for copy in copies[2:5]:
        copy.wait()
    for row in range(height):
        pixels = pl.ds(row * width, width)
        values = [conv[block, pixels, :] for block in range(blocks)]
        mean = jnp.sum(sum(values), axis=-1, keepdims=True) / channels
        values = [value - mean for value in values]
        spread = jnp.sum(sum(value * value for value in values), axis=-1, keepdims=True) / channels
        rstd = lax.rsqrt(spread + 1e-06)
        rstd_out[pixels, :] = jnp.broadcast_to(rstd, (width, LANES))
        for block, value in enumerate(values):
            lanes = pl.ds(block * LANES, LANES)
            xhat = value * rstd
            xhat_out[block, pixels, :] = xhat
            normed[pixels, lanes] = (xhat * gain[:, lanes]).astype(jnp.bfloat16)
        dbranch[pixels, :] = (cotangent[row].astype(jnp.float32) * scale[...]).astype(jnp.bfloat16)
    turned[...] = normed[...].T
    part = channels // (Y * CORE)
    for y in range(Y):
        for own in range(CORE):
            owner = core if own else 1 - core
            chosen[pl.ds((own * Y + y) * part, part), :] = turned[
                pl.ds(pl.multiple_of((y * CORE + owner) * part, part), part), :
            ]
    rows_out[pl.ds(0, 8), :] = jnp.zeros((8, channels), jnp.float32)
    rows_out[pl.ds(8, 8), :] = jnp.broadcast_to(gain[...], (8, channels))
    rows_out[pl.ds(16, 8), :] = jnp.broadcast_to(scale[...], (8, channels))
    for copy in copies[5:]:
        copy.wait()
    step = reduce.shape[0] // (Y * CORE)
    per_z = step // (X * Z)
    part_x = part // X
    wide = channels // step

    def hidden_block(y, _):
        for own, target in ((0, sent_r), (1, kept_r)):
            owner = core if own else 1 - core
            chunk = y * CORE + owner
            hidden = pl.ds(pl.multiple_of(chunk * step, step), step)
            pre = product(normed[...], expand[:, hidden], NN)
            dact = product(dbranch[...], reduce[hidden, :], NT)
            half = 0.5 * (1.0 + lax.erf(pre * INV_ROOT_TWO))
            slope = half + pre * jnp.exp(-0.5 * pre * pre) * INV_ROOT_TWO_PI
            act = (pre * half).astype(jnp.bfloat16)
            dpre = (dact * slope).astype(jnp.bfloat16)
            dpre_out[:, hidden] = dpre
            share = product(act, dbranch[...], TN)
            weighed = share * reduce[hidden, :].astype(jnp.float32)
            rows_out[pl.ds(0, 8), :] += jnp.sum(weighed.reshape(step // 8, 8, channels), axis=0)
            share = share.astype(jnp.bfloat16)
            for place in range(X * Z):
                x, z = place // Z, place % Z
                target[z, y * X + x] = share[place * per_z : (place + 1) * per_z]
            share = product(chosen[...], dpre, NN).astype(jnp.bfloat16)
            rows = pl.ds(pl.multiple_of((chunk // wide) * part_x, part_x), part_x)
            lanes = pl.ds(pl.multiple_of((chunk % wide) * step, step), step)
            for place in range(Y * X):
                for back, goal in ((0, sent_e), (1, kept_e)):
                    first = back * Y * part + place * part_x
                    goal[place, rows, lanes] = share[first : first + part_x]
        return 0

    lax.fori_loop(0, Y, hidden_block, 0)


def backward_kernel(
    multiplier, dpre, expand, xhat, rstd, padded, rows, dconv_out, small, dconv
):
    height, width, channels = dconv_out.shape
    blocks = channels // LANES
    side = 7
    dnormed = product(dpre[...], expand[...], NT)
    for block in range(blocks):
        dconv[block] = dnormed[:, block * LANES : (block + 1) * LANES]
    sums = [jnp.zeros((width, LANES), jnp.float32)] * blocks
    for row in range(height):
        pixels = pl.ds(row * width, width)
        grads = [dconv[block, pixels, :] for block in range(blocks)]
        hats = [xhat[block, pixels, :] for block in range(blocks)]
        sums = [total + grad * hat for total, grad, hat in zip(sums, grads, hats)]
        grads = [grad * rows[pl.ds(8, 1), pl.ds(block * LANES, LANES)] for block, grad in enumerate(grads)]
        mean = jnp.sum(sum(grads), axis=-1, keepdims=True) / channels
        slant = sum(grad * hat for grad, hat in zip(grads, hats))
        slant = jnp.sum(slant, axis=-1, keepdims=True) / channels
        for block in range(blocks):
            value = rstd[pixels, :] * (grads[block] - mean - hats[block] * slant)
            dconv[block, pixels, :] = value
            dconv_out[row, :, pl.ds(block * LANES, LANES)] = value.astype(jnp.bfloat16)
    taps = side * side
    small[pl.ds(taps + 2, SMALL - taps - 2), :] = jnp.zeros(
        (SMALL - taps - 2, channels), jnp.float32
    )
    for block in range(blocks):
        lanes = pl.ds(block * LANES, LANES)
        total = jnp.sum(sums[block], axis=0, keepdims=True)
        small[pl.ds(taps, 1), lanes] = total * multiplier
        total = jnp.sum(rows[pl.ds(0, 8), lanes], axis=0, keepdims=True)
        small[pl.ds(taps + 1, 1), lanes] = total / rows[pl.ds(16, 1), lanes] * multiplier

    def tap_block(block, _):
        lanes = pl.ds(pl.multiple_of(block * LANES, LANES), LANES)
        for second in range(side):
            totals = [jnp.zeros((8, LANES), jnp.float32)] * side
            for first_col in range(0, width, 8):
                grads = [
                    dconv[block, pl.ds(row * width + first_col, 8), :] for row in range(height)
                ]
                columns = pl.ds(LEFT - side // 2 + first_col + second, 8)
                for row in range(height + side - 1):
                    value = padded[block, row, columns, :]
                    for first in range(max(0, row - height + 1), min(side, row + 1)):
                        totals[first] = totals[first] + grads[row - first] * value
            for first, total in enumerate(totals):
                total = jnp.sum(total, axis=0, keepdims=True) * multiplier
                small[pl.ds(first * side + second, 1), lanes] = total
        return 0

    lax.fori_loop(0, blocks, tap_block, 0)


def feature_kernel(field, up, down, left, right, taps, cotangent, out, padded):
    height, width, channels = field.shape
    side = 7
    fill(padded, field, up, down, left, right, side // 2)
    for block in range(channels // LANES):
        lanes = pl.ds(block * LANES, LANES)
        for first_col in range(0, width, 8):
            columns = pl.ds(first_col, 8)
            for row, total in enumerate(
                depthwise(padded, taps, block, first_col, height, side, True)
            ):
                total = total + cotangent[row, columns, lanes].astype(jnp.float32)
                out[row, columns, lanes] = total.astype(jnp.bfloat16)


def halves(value):
    high = value.astype(jnp.bfloat16)
    return high, (value - high.astype(jnp.float32)).astype(jnp.bfloat16)


def added(left, right):
    return (left.astype(jnp.float32) + right.astype(jnp.float32)).astype(jnp.bfloat16)


def merge_kernel(kept, came, small, small_came, out):
    rows = kept.shape[1]
    out[:, pl.ds(0, rows), :] = added(kept[...], came[...])
    total = small[...] + small_came[...]
    out[:, pl.ds(rows, 2 * total.shape[1]), :] = jnp.concatenate(halves(total), axis=1)


def join_kernel(kept, came, out):
    out[...] = added(kept[...], came[...])


def plane_kernel(chunks, out, total):
    total[...] = jnp.sum(chunks[...].astype(jnp.float32), axis=0)
    rows = total.shape[0] - 8
    small = jnp.concatenate(halves(total[pl.ds(rows, 4), :] + total[pl.ds(rows + 4, 4), :]))
    for z in range(Z):
        parts = [total[pl.ds(q * 2 * Z + 2 * z, 2), :] for q in range(rows // (2 * Z))]
        own = jnp.concatenate(parts).astype(jnp.bfloat16)
        out[z] = jnp.concatenate([own, small])


def line_kernel(multiplier, chunks, line, dexpand, out):
    total = jnp.sum(chunks[...].astype(jnp.float32), axis=0)
    each = total.shape[0] - 8
    channels = total.shape[1]
    for q in range(each // 2):
        dexpand[:, pl.ds(q * channels, channels)] = total[2 * q : 2 * q + 2] * multiplier
    small = jnp.concatenate(halves(total[each : each + 4] + total[each + 4 :]))
    for place in range(out.shape[0]):
        out[place, pl.ds(0, each), :] = line[place]
        out[place, pl.ds(each, 8), :] = small


def last_kernel(multiplier, chunks, dreduce, dkernel, dgain, dscale, full):
    each = dreduce.shape[0]
    total = jnp.sum(chunks[:, pl.ds(0, each), :].astype(jnp.float32), axis=0)
    dreduce[...] = total * multiplier
    full[...] = chunks[:, pl.ds(each, 4), :].astype(jnp.float32) + chunks[
        :, pl.ds(each + 4, 4), :
    ].astype(jnp.float32)
    side = dkernel.shape[0]
    for place in range(side * side):
        dkernel[place // side, pl.ds(place % side, 1), :] = full[place // 4, pl.ds(place % 4, 1), :]
    for place, out in ((side * side, dgain), (side * side + 1, dscale)):
        out[...] = full[place // 4, pl.ds(place % 4, 1), :]


VMEM = pl.BlockSpec(memory_space=pltpu.VMEM)
HBM = pl.BlockSpec(memory_space=pltpu.HBM)
SMEM = pl.BlockSpec(memory_space=pltpu.SMEM)
PARAMS = pltpu.CompilerParams(vmem_limit_bytes=24 << 20)


def in_hbm(value):
    return pltpu.with_memory_space_constraint(value, pltpu.HBM)


def shifted(value, axes, by):
    count = lax.axis_size(axes)
    pairs = [(i, i + by) for i in range(count) if 0 <= i + by < count]
    return lax.ppermute(value, axes, pairs)


def borders(field, reach):
    up = shifted(field[-reach:], ROW, 1)
    down = shifted(field[:reach], ROW, -1)
    left, right = (
        jnp.concatenate([part[:, columns] for part in (up, field, down)])
        for columns in (slice(-reach, None), slice(0, reach))
    )
    return up, down, shifted(left, COL, 1), shifted(right, COL, -1)


def exchanged(chunks, axes):
    return lax.all_to_all(chunks, axes, 0, 0, tiled=True)


def shards(features, kernel, gain, w_expand, w_reduce, layer_scale, cotangent):
    height, width, channels = features.shape
    hidden = w_reduce.shape[0]
    side = kernel.shape[0]
    reach = side // 2
    blocks = channels // LANES
    pixels = height * width
    multiplier = 1.0 / math.sqrt(pixels * lax.axis_size(ROW) * lax.axis_size(COL))
    gain_row = gain.reshape(1, channels)
    scale_row = layer_scale.reshape(1, channels)
    core = lax.axis_index("core").reshape(1)
    places = Y * X
    rows = hidden // (Y * CORE * X)
    f32, bf16 = jnp.float32, jnp.bfloat16
    shape = jax.ShapeDtypeStruct
    padded_shape = (blocks, height + side - 1, LEFT + width + 8, LANES)

    sent_e, kept_e, sent_r, kept_r, dpre, xhat, rstd, padded, row_sums = pl.pallas_call(
        forward_kernel,
        name="forward",
        in_specs=[SMEM, HBM] + [VMEM] * 4 + [HBM] * 6,
        out_specs=[VMEM] * 9,
        out_shape=[shape((places, rows, channels), bf16)] * 2
        + [shape((Z, places, rows // Z, channels), bf16)] * 2
        + [
            shape((pixels, hidden), bf16),
            shape((blocks, pixels, LANES), f32),
            shape((pixels, LANES), f32),
            shape(padded_shape, f32),
            shape((24, channels), f32),
        ],
        scratch_shapes=[
            pltpu.VMEM((blocks, pixels, LANES), f32),
            pltpu.VMEM((pixels, channels), bf16),
            pltpu.VMEM((pixels, channels), bf16),
            pltpu.VMEM((channels, pixels), bf16),
            pltpu.VMEM((channels, pixels), bf16),
            pltpu.VMEM(features.shape, bf16),
            pltpu.VMEM(kernel.shape, f32),
            pltpu.VMEM((1, channels), f32),
            pltpu.VMEM((channels, hidden), bf16),
            pltpu.VMEM((hidden, channels), bf16),
            pltpu.VMEM((1, channels), f32),
            pltpu.VMEM(cotangent.shape, bf16),
            pltpu.SemaphoreType.DMA((7,)),
        ],
        compiler_params=PARAMS,
    )(
        core, in_hbm(features), *borders(features, reach), in_hbm(kernel), in_hbm(gain_row),
        in_hbm(w_expand), in_hbm(w_reduce), in_hbm(scale_row), in_hbm(cotangent),
    )

    swap = [(0, 1), (1, 0)]
    came_e = lax.ppermute(sent_e, "core", swap)
    came_r = lax.ppermute(sent_r, "core", swap)
    dconv, small = pl.pallas_call(
        functools.partial(backward_kernel, multiplier),
        name="backward",
        in_specs=[VMEM] * 6,
        out_specs=[VMEM] * 2,
        out_shape=[
            shape((height, width, channels), bf16),
            shape((SMALL, channels), f32),
        ],
        scratch_shapes=[pltpu.VMEM((blocks, pixels, LANES), f32)],
        compiler_params=PARAMS,
    )(dpre, w_expand, xhat, rstd, padded, row_sums)

    small_came = lax.ppermute(small, "core", swap)
    each = SMALL // places
    whole = rows + 2 * each
    chip = pl.pallas_call(
        merge_kernel,
        name="merge",
        grid=(Y,),
        in_specs=[pl.BlockSpec((X, rows, channels), lambda i: (i, 0, 0))] * 2
        + [pl.BlockSpec((X, each, channels), lambda i: (i, 0, 0))] * 2,
        out_specs=pl.BlockSpec((X, whole, channels), lambda i: (i, 0, 0)),
        out_shape=shape((places, whole, channels), bf16),
        compiler_params=PARAMS,
    )(
        kept_e, came_e, small.reshape(places, each, channels),
        small_came.reshape(places, each, channels),
    )
    chip, dconv, kept_r = lax.optimization_barrier((chip, dconv, kept_r))
    block = pl.BlockSpec((2, places, rows // Z, channels), lambda i: (i, 0, 0, 0))
    joined = pl.pallas_call(
        join_kernel,
        name="join",
        grid=(Z // 2,),
        in_specs=[block] * 2,
        out_specs=block,
        out_shape=shape(kept_r.shape, bf16),
        compiler_params=PARAMS,
    )(kept_r, came_r)
    line = lax.psum_scatter(
        joined.reshape(Z * rows * places // Z, channels), "z", scatter_dimension=0, tiled=True
    ).reshape(places, rows // Z, channels)
    chunks, edges = lax.optimization_barrier((exchanged(chip, ("y", "x")), borders(dconv, reach)))
    chunks = pl.pallas_call(
        plane_kernel,
        name="plane",
        in_specs=[VMEM],
        out_specs=VMEM,
        out_shape=shape((Z, rows // Z + 2 * each, channels), bf16),
        scratch_shapes=[pltpu.VMEM((whole, channels), f32)],
        compiler_params=PARAMS,
    )(chunks)
    dexpand, chunks = pl.pallas_call(
        functools.partial(line_kernel, multiplier),
        name="line",
        in_specs=[VMEM] * 2,
        out_specs=[VMEM] * 2,
        out_shape=[
            shape((channels * rows // Z // hidden, hidden), f32),
            shape((places, rows // Z + 2 * each, channels), bf16),
        ],
        compiler_params=PARAMS,
    )(exchanged(chunks, "z"), line)
    dreduce, dkernel, dgain, dscale = pl.pallas_call(
        functools.partial(last_kernel, multiplier),
        name="last",
        in_specs=[VMEM],
        out_specs=[VMEM] * 4,
        out_shape=[shape((rows // Z, channels), f32), shape((side, side, channels), f32)]
        + [shape((1, channels), f32)] * 2,
        scratch_shapes=[pltpu.VMEM((places, each, channels), f32)],
        compiler_params=PARAMS,
    )(exchanged(chunks, ("y", "x")))
    grad_features = pl.pallas_call(
        feature_kernel,
        name="features",
        in_specs=[VMEM] * 7,
        out_specs=VMEM,
        out_shape=shape((height, width, channels), bf16),
        scratch_shapes=[pltpu.VMEM(padded_shape, f32)],
        compiler_params=PARAMS,
    )(dconv, *edges, kernel, cotangent)
    return (
        grad_features,
        dkernel,
        dgain.reshape(channels),
        dscale.reshape(channels),
        dexpand,
        dreduce,
    )


def solution(mesh):
    pixels = P(ROW, COL, None)
    return jax.shard_map(
        shards,
        mesh=Mesh(mesh.devices.reshape(Y, CORE, X, Z), (*ROW, *COL)),
        in_specs=(pixels, P(), P(), P(), P(), P(), pixels),
        out_specs=(pixels, P(), P(), P(), P((*ROW, *COL), None), P((*ROW, *COL), None)),
        check_vma=False,
    )
```

time: 121 us -> 125 us (1.033)
  waiting for transfers between devices: 34.8 us -> 11.9 us
  between operations: 0.86 us -> 14.2 us
  starting transfers between devices: 45.7 us -> 53.9 us
  blocking collectives: 12.2 us -> 15.5 us
  Pallas kernels: 19.7 us -> 22.5 us
    all_to_all x2, waiting for transfers between devices: 18.4 us -> 6.47 us  [exchanged(): return lax.all_to_all(chunks, axes, 0, 0, tiled=True)]
    ppermute x8, waiting for transfers between devices: 15.1 us -> 5 us  [shifted(): return lax.ppermute(value, axes, pairs)]
    ppermute x8, starting transfers between devices: 21.7 us -> 26.4 us  [shifted(): return lax.ppermute(value, axes, pairs)]
    all_to_all x2, starting transfers between devices: 22.1 us -> 25.8 us  [exchanged(): return lax.all_to_all(chunks, axes, 0, 0, tiled=True)]
    all_to_all x1, blocking collectives: 12.2 us -> 15.5 us  [exchanged(): return lax.all_to_all(chunks, axes, 0, 0, tiled=True)]
    pallas_call x2 -> x3, Pallas kernels: 9.02 us -> 11.8 us  [the longest x1 9.43 us: shards(): pl.pallas_call(forward_kernel, name='forward', in_specs=[SMEM, HBM] + [VM...]
    reshape x1, local copies, waits for them, and re-layouts: 0.04 us -> 1.6 us  [shards(): small_came.reshape(places, each, channels)]
    unnamed x12 -> x10, local copies, waits for them, and re-layouts: 3.27 us -> 1.83 us
  transfers between devices with their start and end apart: 12 -> 14, of which waited for: 8 -> 8; matrix products, arithmetic and copies ran while one was open for 2% -> 3% of each run, Pallas kernels for 5% -> 8%
where the time goes in v3:
time: 125 us; the launch traced here: 124 us
  starting transfers between devices  53.9 us (43%)
  Pallas kernels  22.5 us (18%)
  blocking collectives  15.5 us (12%)
  between operations  14.2 us (11%)
  waiting for transfers between devices  11.9 us (10%)
  local copies, waits for them, and re-layouts  6.33 us (5%)
    ppermute x8, starting transfers between devices, shifted(): return lax.ppermute(value, axes, pairs)  26.4 us
    all_to_all x2, starting transfers between devices, exchanged(): return lax.all_to_all(chunks, axes, 0, 0, tiled=True)  25.8 us
    all_to_all x1, blocking collectives, exchanged(): return lax.all_to_all(chunks, axes, 0, 0, tiled=True)  15.5 us
    pallas_call x1, Pallas kernels, shards(): pl.pallas_call(forward_kernel, name='forward', in_specs=[SMEM, HBM] + [VM...  9.43 us
    all_to_all x2, waiting for transfers between devices, exchanged(): return lax.all_to_all(chunks, axes, 0, 0, tiled=True)  6.47 us
    ppermute x8, waiting for transfers between devices, shifted(): return lax.ppermute(value, axes, pairs)  5 us
    pallas_call x1, Pallas kernels, shards(): pl.pallas_call(functools.partial(backward_kernel, multiplier), name='back...  3.72 us
    pallas_call x1, Pallas kernels, shards(): pl.pallas_call(merge_kernel, name='merge', grid=(Y,), in_specs=[pl.BlockS...  3.5 us
  transfers between devices with their start and end apart: 14, of which 8 were waited for; matrix products, arithmetic and copies ran while one was open for 3% of the time, Pallas kernels for 8%

profile of v3, /device:TPU:2, one launch (start us, length us, event | category | flops | bytes accessed | tf_op | source)
XLA Modules:
  0.0 124.4 jit_solution(15573977971939687020)
XLA Ops:
  7.2 1.0 fusion.3
  8.2 1.3 %collective-permute-start.1 = (bf16[3,32,512]{2,1,0:T(8,128)(2,1)S(1)}, bf16[3,32,512]{2,1,0:T(8,128)(2,1)S(1)}, u32[]{:S(2)}, u32[]{:S(2)}) collective-permute-start(bf16[3,32,512]{2,1,0:T(8,128)(2,1)S(1)} %get-tuple-element.62), channel_id=1, source_target_pairs={{32,0},{64,32},{96,64},{128,96},{160,128},{192,160},{224,192},{33,... | collective-permute-start | bytes 294920 | tf_op jit(solution)/shard_map/ppermute | solution.py:303
  9.5 3.0 %collective-permute-start = (bf16[3,32,512]{2,1,0:T(8,128)(2,1)S(1)}, bf16[3,32,512]{2,1,0:T(8,128)(2,1)S(1)}, u32[]{:S(2)}, u32[]{:S(2)}) collective-permute-start(bf16[3,32,512]{2,1,0:T(8,128)(2,1)S(1)} %get-tuple-element.63), channel_id=1, source_target_pairs={{0,32},{32,64},{64,96},{96,128},{128,160},{160,192},{192,224},{1,3... | collective-permute-start | bytes 294920 | tf_op jit(solution)/shard_map/ppermute | solution.py:303
  12.5 0.9 fusion.2
  13.5 3.8 %collective-permute-start.2 = (bf16[14,3,512]{2,1,0:T(4,128)(2,1)S(1)}, bf16[14,3,512]{2,1,0:T(4,128)(2,1)S(1)}, u32[]{:S(2)}, u32[]{:S(2)}) collective-permute-start(bf16[14,3,512]{2,1,0:T(4,128)(2,1)S(1)} %pad_maximum_fusion), channel_id=1, source_target_pairs={{0,1},{1,2},{2,3},{3,4},{4,5},{5,6},{6,7},{7,8},{8,9},{9,10},{10,1... | collective-permute-start | bytes 129032 | tf_op jit(solution)/shard_map/ppermute | solution.py:303
  17.4 5.8 %collective-permute-start.3 = (bf16[14,3,512]{2,1,0:T(4,128)(2,1)S(1)}, bf16[14,3,512]{2,1,0:T(4,128)(2,1)S(1)}, u32[]{:S(2)}, u32[]{:S(2)}) collective-permute-start(bf16[14,3,512]{2,1,0:T(4,128)(2,1)S(1)} %pad_maximum_fusion.1), channel_id=1, source_target_pairs={{1,0},{2,1},{3,2},{4,3},{5,4},{6,5},{7,6},{8,7},{9,8},{10,9},{11,1... | collective-permute-start | bytes 129032 | tf_op jit(solution)/shard_map/ppermute | solution.py:303
  23.4 1.6 %collective-permute-done.3.right = bf16[14,3,512]{2,1,0:T(4,128)(2,1)S(1)} collective-permute-done((bf16[14,3,512]{2,1,0:T(4,128)(2,1)S(1)}, bf16[14,3,512]{2,1,0:T(4,128)(2,1)S(1)}, u32[]{:S(2)}, u32[]{:S(2)}) %collective-permute-start.3) | collective-permute-done | bytes 43040 | tf_op jit(solution)/shard_map/ppermute | solution.py:303
  25.1 9.4 %forward.1 = (bf16[16,64,512]{2,1,0:T(8,128)(2,1)}, bf16[16,64,512]{2,1,0:T(8,128)(2,1)S(1)}, bf16[8,16,8,512]{3,2,1,0:T(8,128)(2,1)}, bf16[8,16,8,512]{3,2,1,0:...) custom-call(s32[1]{0:T(128)} %bitcast.core_ref, ...), custom_call_target="tpu_custom_call" | custom-call | tf_op jit(solution)/shard_map/forward/pallas_call | solution.py:337
  34.5 1.1 collective-permute-start.4
  35.7 3.7 %backward.1 = (bf16[8,32,512]{2,1,0:T(8,128)(2,1)S(1)}, f32[64,512]{1,0:T(8,128)}) custom-call(bf16[256,2048]{1,0:T(8,128)(2,1)S(1)} %get-tuple-element.33.dpre, bf16[512,2048]{1,0:T(8,128)(2,1)S(1)} %copy-done, f32[4,256,128]{2,1,0:T(8,128)S(1)} %get-tuple-element.34.xhat, f32[256,128]{1,0:T(8,128)S(1)} %get-tuple-element.35.rstd, ...), custom_call_target="tpu_custom_call" | custom-call | tf_op jit(solution)/shard_map/backward/pallas_call | solution.py:375
  39.4 0.4 collective-permute-start.5
  39.8 0.9 reshape.42.small
  41.2 1.6 %reshape.43.small_came = f32[16,4,512]{2,1,0:T(4,128)} reshape(f32[64,512]{1,0:T(8,128)} %collective-permute-done.5) | data formatting | bytes 262144 | tf_op jit(solution)/shard_map/reshape | solution.py:402
  42.8 0.9 copy-done.2
  43.7 3.5 %merge.1 = bf16[16,72,512]{2,1,0:T(8,128)(2,1)} custom-call(bf16[16,64,512]{2,1,0:T(8,128)(2,1)S(1)} %get-tuple-element.31.kept, bf16[16,64,512]{2,1,0:T(8,128)(2,1)} %collective-permute-done.4.came, f32[16,4,512]{2,1,0:T(4,128)S(1)} %reshape.42.small, f32[16,4,512]{2,1,0:T(4,128)S(1)} %copy-done.2), custom_call_target="tpu_custom_call" | custom-call | tf_op jit(solution)/shard_map/merge/pallas_call | solution.py:391
  47.2 1.6 %join.1 = bf16[8,16,8,512]{3,2,1,0:T(8,128)(2,1)} custom-call(bf16[8,16,8,512]{3,2,1,0:T(8,128)(2,1)S(1)} %get-tuple-element.48.kept, bf16[8,16,8,512]{3,2,1,0:T(8,128)(2,1)S(1)} %collective-permute-done.10.came), custom_call_target="tpu_custom_call" | custom-call | tf_op jit(solution)/shard_map/join/pallas_call | solution.py:406
  48.8 9.4 %all-to-all-start = ((bf16[16,72,512]{2,1,0:T(8,128)(2,1)}), bf16[16,72,512]{2,1,0:T(8,128)(2,1)S(1)}, u32[]{:S(2)}, u32[]{:S(2)}) async-start(bf16[16,72,512]{2,1,0:T(8,128)(2,1)} %merge.1), calls=%async_computation | async-start | bytes 2359296 | tf_op jit(solution)/shard_map/all_to_all | solution.py:317
  58.3 1.3 %collective-permute-start.7 = (bf16[3,32,512]{2,1,0:T(8,128)(2,1)S(1)}, bf16[3,32,512]{2,1,0:T(8,128)(2,1)S(1)}, u32[]{:S(2)}, u32[]{:S(2)}) collective-permute-start(bf16[3,32,512]{2,1,0:T(8,128)(2,1)S(1)} %get-tuple-element.58), channel_id=1, source_target_pairs={{32,0},{64,32},{96,64},{128,96},{160,128},{192,160},{224,192},{33,... | collective-permute-start | bytes 294920 | tf_op jit(solution)/shard_map/ppermute | solution.py:303
  59.7 3.2 %collective-permute-start.6 = (bf16[3,32,512]{2,1,0:T(8,128)(2,1)S(1)}, bf16[3,32,512]{2,1,0:T(8,128)(2,1)S(1)}, u32[]{:S(2)}, u32[]{:S(2)}) collective-permute-start(bf16[3,32,512]{2,1,0:T(8,128)(2,1)S(1)} %get-tuple-element.59), channel_id=1, source_target_pairs={{0,32},{32,64},{64,96},{96,128},{128,160},{160,192},{192,224},{1,3... | collective-permute-start | bytes 294920 | tf_op jit(solution)/shard_map/ppermute | solution.py:303
  62.9 0.9 collective-permute-done.6.up
  63.8 2.2 %collective-permute-start.8 = (bf16[14,3,512]{2,1,0:T(4,128)(2,1)S(1)}, bf16[14,3,512]{2,1,0:T(4,128)(2,1)S(1)}, u32[]{:S(2)}, u32[]{:S(2)}) collective-permute-start(bf16[14,3,512]{2,1,0:T(4,128)(2,1)S(1)} %pad_maximum_fusion.2), channel_id=1, source_target_pairs={{0,1},{1,2},{2,3},{3,4},{4,5},{5,6},{6,7},{7,8},{8,9},{9,10},{10,1... | collective-permute-start | bytes 129032 | tf_op jit(solution)/shard_map/ppermute | solution.py:303
  66.1 5.7 %collective-permute-start.9 = (bf16[14,3,512]{2,1,0:T(4,128)(2,1)S(1)}, bf16[14,3,512]{2,1,0:T(4,128)(2,1)S(1)}, u32[]{:S(2)}, u32[]{:S(2)}) collective-permute-start(bf16[14,3,512]{2,1,0:T(4,128)(2,1)S(1)} %pad_maximum_fusion.3), channel_id=1, source_target_pairs={{1,0},{2,1},{3,2},{4,3},{5,4},{6,5},{7,6},{8,7},{9,8},{10,9},{11,1... | collective-permute-start | bytes 129032 | tf_op jit(solution)/shard_map/ppermute | solution.py:303
  71.8 0.5 collective-permute-done.8.left
  72.4 1.8 %collective-permute-done.9.right = bf16[14,3,512]{2,1,0:T(4,128)(2,1)S(1)} collective-permute-done((bf16[14,3,512]{2,1,0:T(4,128)(2,1)S(1)}, bf16[14,3,512]{2,1,0:T(4,128)(2,1)S(1)}, u32[]{:S(2)}, u32[]{:S(2)}) %collective-permute-start.9) | collective-permute-done | bytes 43040 | tf_op jit(solution)/shard_map/ppermute | solution.py:303
  74.1 1.6 %all-to-all-done.chunks = bf16[16,72,512]{2,1,0:T(8,128)(2,1)S(1)} async-done(((bf16[16,72,512]{2,1,0:T(8,128)(2,1)}), bf16[16,72,512]{2,1,0:T(8,128)(2,1)S(1)}, u32[]{:S(2)}, u32[]{:S(2)}) %all-to-all-start) | async-done | bytes 1179680 | tf_op jit(solution)/shard_map/all_to_all | solution.py:317
  76.0 15.5 %all_to_all.15.chunks = bf16[8,16,512]{2,1,0:T(8,128)(2,1)S(1)} all-to-all(bf16[8,16,512]{2,1,0:T(8,128)(2,1)S(1)} %plane.1), channel_id=1, replica_groups=mesh['y'=4,'core'=2,'x'=4,'z'=8] {'z'}, dimensions={0} | all-to-all | bytes 262144 | tf_op jit(solution)/shard_map/all_to_all | solution.py:317
  91.5 0.9 copy-done.4
  92.4 0.7 line.1
  93.1 16.4 %all-to-all-start.2 = ((bf16[16,16,512]{2,1,0:T(8,128)(2,1)}), bf16[16,16,512]{2,1,0:T(8,128)(2,1)S(1)}, u32[]{:S(2)}, u32[]{:S(2)}) async-start(bf16[16,16,512]{2,1,0:T(8,128)(2,1)} %get-tuple-element.50), calls=%async_computation.3 | async-start | bytes 524288 | tf_op jit(solution)/shard_map/all_to_all | solution.py:317
  109.6 2.5 %features.1 = bf16[8,32,512]{2,1,0:T(8,128)(2,1)} custom-call(bf16[8,32,512]{2,1,0:T(8,128)(2,1)S(1)} %get-tuple-element.41.field, bf16[3,32,512]{2,1,0:T(8,128)(2,1)S(1)} %collective-permute-done.6.up, bf16[3,32,512]{2,1,0:T(8,128)(2,1)S(1)} %collective-permute-done.7.down, bf16[14,3,512]{2,1,0:T(4,128)(2,1)S(1)} %collective-permute-done.8.left, ...), custom_call_target="tpu_custom_call" | custom-call | tf_op jit(solution)/shard_map/features/pallas_call | solution.py:449
  112.0 4.8 %all-to-all-done.2.chunks = bf16[16,16,512]{2,1,0:T(8,128)(2,1)S(1)} async-done(((bf16[16,16,512]{2,1,0:T(8,128)(2,1)}), bf16[16,16,512]{2,1,0:T(8,128)(2,1)S(1)}, u32[]{:S(2)}, u32[]{:S(2)}) %all-to-all-start.2) | async-done | bytes 262176 | tf_op jit(solution)/shard_map/all_to_all | solution.py:317
  116.9 0.7 last.1
  (30 shorter events, 1.3 us)
Async XLA Ops:
  7.2 84.3 %reduce-scatter.2.cloned.1.call-start = ((), (), s32[]{:S(2)}) async-start(), calls=%async_computation.4 | async-start | bytes 1179648 | tf_op jit(solution)/shard_map/reduce_scatter | solution.py:415
  8.2 5.3 %collective-permute-start.1 = (bf16[3,32,512]{2,1,0:T(8,128)(2,1)S(1)}, bf16[3,32,512]{2,1,0:T(8,128)(2,1)S(1)}, u32[]{:S(2)}, u32[]{:S(2)}) collective-permute-start(bf16[3,32,512]{2,1,0:T(8,128)(2,1)S(1)} %get-tuple-element.62), channel_id=1, source_target_pairs={{32,0},{64,32},{96,64},{128,96},{160,128},{192,160},{224,192},{33,... | collective-permute-start | bytes 294920 | tf_op jit(solution)/shard_map/ppermute | solution.py:303
  9.5 4.0 %collective-permute-start = (bf16[3,32,512]{2,1,0:T(8,128)(2,1)S(1)}, bf16[3,32,512]{2,1,0:T(8,128)(2,1)S(1)}, u32[]{:S(2)}, u32[]{:S(2)}) collective-permute-start(bf16[3,32,512]{2,1,0:T(8,128)(2,1)S(1)} %get-tuple-element.63), channel_id=1, source_target_pairs={{0,32},{32,64},{64,96},{96,128},{128,160},{160,192},{192,224},{1,3... | collective-permute-start | bytes 294920 | tf_op jit(solution)/shard_map/ppermute | solution.py:303
  13.5 9.9 %collective-permute-start.2 = (bf16[14,3,512]{2,1,0:T(4,128)(2,1)S(1)}, bf16[14,3,512]{2,1,0:T(4,128)(2,1)S(1)}, u32[]{:S(2)}, u32[]{:S(2)}) collective-permute-start(bf16[14,3,512]{2,1,0:T(4,128)(2,1)S(1)} %pad_maximum_fusion), channel_id=1, source_target_pairs={{0,1},{1,2},{2,3},{3,4},{4,5},{5,6},{6,7},{7,8},{8,9},{9,10},{10,1... | collective-permute-start | bytes 129032 | tf_op jit(solution)/shard_map/ppermute | solution.py:303
  17.4 7.6 %collective-permute-start.3 = (bf16[14,3,512]{2,1,0:T(4,128)(2,1)S(1)}, bf16[14,3,512]{2,1,0:T(4,128)(2,1)S(1)}, u32[]{:S(2)}, u32[]{:S(2)}) collective-permute-start(bf16[14,3,512]{2,1,0:T(4,128)(2,1)S(1)} %pad_maximum_fusion.1), channel_id=1, source_target_pairs={{1,0},{2,1},{3,2},{4,3},{5,4},{6,5},{7,6},{8,7},{9,8},{10,9},{11,1... | collective-permute-start | bytes 129032 | tf_op jit(solution)/shard_map/ppermute | solution.py:303
  25.1 10.6 %copy-start = (bf16[512,2048]{1,0:T(8,128)(2,1)S(1)}, bf16[512,2048]{1,0:T(8,128)(2,1)}, u32[]{:S(2)}) copy-start(bf16[512,2048]{1,0:T(8,128)(2,1)} %expand.1) | copy-start | bytes 6291460
  34.5 8.3 %collective-permute-start.4 = (bf16[16,64,512]{2,1,0:T(8,128)(2,1)}, bf16[16,64,512]{2,1,0:T(8,128)(2,1)}, u32[]{:S(2)}, u32[]{:S(2)}) collective-permute-start(bf16[16,64,512]{2,1,0:T(8,128)(2,1)} %get-tuple-element.32), channel_id=1, source_target_pairs={{0,32},{32,0},{1,33},{33,1},{2,34},{34,2},{3,35},{35,3},{4,36},{36... | collective-permute-start | bytes 3145736 | tf_op jit(solution)/shard_map/ppermute | solution.py:373
  35.6 11.6 %collective-permute-start.10 = (bf16[8,16,8,512]{3,2,1,0:T(8,128)(2,1)}, bf16[8,16,8,512]{3,2,1,0:T(8,128)(2,1)S(1)}, u32[]{:S(2)}, u32[]{:S(2)}) collective-permute-start(bf16[8,16,8,512]{3,2,1,0:T(8,128)(2,1)} %get-tuple-element.49), channel_id=1, source_target_pairs={{0,32},{32,0},{1,33},{33,1},{2,34},{34,2},{3,35},{35,3},{4,36},{36... | collective-permute-start | bytes 3145736 | tf_op jit(solution)/shard_map/ppermute | solution.py:374
  39.4 1.7 %collective-permute-start.5 = (f32[64,512]{1,0:T(8,128)}, f32[64,512]{1,0:T(8,128)}, u32[]{:S(2)}, u32[]{:S(2)}) collective-permute-start(f32[64,512]{1,0:T(8,128)} %get-tuple-element.38), channel_id=1, source_target_pairs={{0,32},{32,0},{1,33},{33,1},{2,34},{34,2},{3,35},{35,3},{4,36},{36... | collective-permute-start | bytes 393224 | tf_op jit(solution)/shard_map/ppermute | solution.py:388
  42.8 0.9 copy-start.2
  48.8 27.0 %all-to-all-start = ((bf16[16,72,512]{2,1,0:T(8,128)(2,1)}), bf16[16,72,512]{2,1,0:T(8,128)(2,1)S(1)}, u32[]{:S(2)}, u32[]{:S(2)}) async-start(bf16[16,72,512]{2,1,0:T(8,128)(2,1)} %merge.1), calls=%async_computation | async-start | bytes 2359296 | tf_op jit(solution)/shard_map/all_to_all | solution.py:317
  58.3 4.5 %collective-permute-start.7 = (bf16[3,32,512]{2,1,0:T(8,128)(2,1)S(1)}, bf16[3,32,512]{2,1,0:T(8,128)(2,1)S(1)}, u32[]{:S(2)}, u32[]{:S(2)}) collective-permute-start(bf16[3,32,512]{2,1,0:T(8,128)(2,1)S(1)} %get-tuple-element.58), channel_id=1, source_target_pairs={{32,0},{64,32},{96,64},{128,96},{160,128},{192,160},{224,192},{33,... | collective-permute-start | bytes 294920 | tf_op jit(solution)/shard_map/ppermute | solution.py:303
  59.6 49.9 %copy-start.1 = (bf16[8,32,512]{2,1,0:T(8,128)(2,1)S(1)}, bf16[8,32,512]{2,1,0:T(8,128)(2,1)}, u32[]{:S(2)}) copy-start(bf16[8,32,512]{2,1,0:T(8,128)(2,1)} %cotangent.1) | copy-start | bytes 786436
  59.6 49.9 %copy-start.3 = (f32[7,7,512]{2,1,0:T(8,128)S(1)}, f32[7,7,512]{2,1,0:T(8,128)}, u32[]{:S(2)}) copy-start(f32[7,7,512]{2,1,0:T(8,128)} %taps.1) | copy-start | bytes 301060
  59.7 4.1 %collective-permute-start.6 = (bf16[3,32,512]{2,1,0:T(8,128)(2,1)S(1)}, bf16[3,32,512]{2,1,0:T(8,128)(2,1)S(1)}, u32[]{:S(2)}, u32[]{:S(2)}) collective-permute-start(bf16[3,32,512]{2,1,0:T(8,128)(2,1)S(1)} %get-tuple-element.59), channel_id=1, source_target_pairs={{0,32},{32,64},{64,96},{96,128},{128,160},{160,192},{192,224},{1,3... | collective-permute-start | bytes 294920 | tf_op jit(solution)/shard_map/ppermute | solution.py:303
  63.8 8.5 %collective-permute-start.8 = (bf16[14,3,512]{2,1,0:T(4,128)(2,1)S(1)}, bf16[14,3,512]{2,1,0:T(4,128)(2,1)S(1)}, u32[]{:S(2)}, u32[]{:S(2)}) collective-permute-start(bf16[14,3,512]{2,1,0:T(4,128)(2,1)S(1)} %pad_maximum_fusion.2), channel_id=1, source_target_pairs={{0,1},{1,2},{2,3},{3,4},{4,5},{5,6},{6,7},{7,8},{8,9},{9,10},{10,1... | collective-permute-start | bytes 129032 | tf_op jit(solution)/shard_map/ppermute | solution.py:303
  66.1 8.0 %collective-permute-start.9 = (bf16[14,3,512]{2,1,0:T(4,128)(2,1)S(1)}, bf16[14,3,512]{2,1,0:T(4,128)(2,1)S(1)}, u32[]{:S(2)}, u32[]{:S(2)}) collective-permute-start(bf16[14,3,512]{2,1,0:T(4,128)(2,1)S(1)} %pad_maximum_fusion.3), channel_id=1, source_target_pairs={{1,0},{2,1},{3,2},{4,3},{5,4},{6,5},{7,6},{8,7},{9,8},{10,9},{11,1... | collective-permute-start | bytes 129032 | tf_op jit(solution)/shard_map/ppermute | solution.py:303
  91.5 0.9 copy-start.4
  93.1 23.7 %all-to-all-start.2 = ((bf16[16,16,512]{2,1,0:T(8,128)(2,1)}), bf16[16,16,512]{2,1,0:T(8,128)(2,1)S(1)}, u32[]{:S(2)}, u32[]{:S(2)}) async-start(bf16[16,16,512]{2,1,0:T(8,128)(2,1)} %get-tuple-element.50), calls=%async_computation.3 | async-start | bytes 524288 | tf_op jit(solution)/shard_map/all_to_all | solution.py:317
Sparse Core Ops, SparseCore 0:
  48.9 42.4 reduce-scatter.1

commit v4 on v3

--- a/solution.py
+++ b/solution.py
@@ -15,7 +15,7 @@
 INV_ROOT_TWO_PI = 1.0 / math.sqrt(2.0 * math.pi)
 LANES = 128
 LEFT = 8
-SMALL = 64
+SMALL = 4
 
 NN = (((1,), (0,)), ((), ()))
 NT = (((1,), (1,)), ((), ()))
@@ -59,7 +59,7 @@
 def forward_kernel(
     core_ref, field_h, up, down, left, right, taps_h, gain_h, expand_h, reduce_h, scale_h,
     cotangent_h,
-    sent_e, kept_e, sent_r, kept_r, dpre_out, xhat_out, rstd_out, padded, rows_out,
+    sent, kept, sent_z, kept_z, dpre_out, xhat_out, rstd_out, padded, rows_out,
     conv, normed, dbranch, turned, chosen, field, taps, gain, expand, reduce, scale, cotangent,
     sems,
 ):
@@ -129,9 +129,11 @@
     per_z = step // (X * Z)
     part_x = part // X
     wide = channels // step
+    narrow = channels // 2
+    top = per_z * Z // 2
 
     def hidden_block(y, _):
-        for own, target in ((0, sent_r), (1, kept_r)):
+        for own, target, target_z in ((0, sent, sent_z), (1, kept, kept_z)):
             owner = core if own else 1 - core
             chunk = y * CORE + owner
             hidden = pl.ds(pl.multiple_of(chunk * step, step), step)
@@ -148,12 +150,18 @@
             share = share.astype(jnp.bfloat16)
             for place in range(X * Z):
                 x, z = place // Z, place % Z
-                target[z, y * X + x] = share[place * per_z : (place + 1) * per_z]
+                mine = share[place * per_z : (place + 1) * per_z]
+                target[
+                    y * X + x, pl.ds(z // 2 * per_z, per_z), pl.ds(z % 2 * narrow, narrow)
+                ] = mine[:, :narrow]
+                target_z[
+                    z, y * (X // 2) + x // 2, :, pl.ds(x % 2 * narrow, narrow)
+                ] = mine[:, narrow:]
             share = product(chosen[...], dpre, NN).astype(jnp.bfloat16)
-            rows = pl.ds(pl.multiple_of((chunk // wide) * part_x, part_x), part_x)
+            rows = pl.ds(pl.multiple_of(top + (chunk // wide) * part_x, part_x), part_x)
             lanes = pl.ds(pl.multiple_of((chunk % wide) * step, step), step)
             for place in range(Y * X):
-                for back, goal in ((0, sent_e), (1, kept_e)):
+                for back, goal in ((0, sent), (1, kept)):
                     first = back * Y * part + place * part_x
                     goal[place, rows, lanes] = share[first : first + part_x]
         return 0
@@ -162,7 +170,7 @@
 
 
 def backward_kernel(
-    multiplier, dpre, expand, xhat, rstd, padded, rows, dconv_out, small, dconv
+    multiplier, dpre, expand, xhat, rstd, padded, rows, dconv_out, out, dconv, small
 ):
     height, width, channels = dconv_out.shape
     blocks = channels // LANES
@@ -185,9 +193,8 @@
             dconv[block, pixels, :] = value
             dconv_out[row, :, pl.ds(block * LANES, LANES)] = value.astype(jnp.bfloat16)
     taps = side * side
-    small[pl.ds(taps + 2, SMALL - taps - 2), :] = jnp.zeros(
-        (SMALL - taps - 2, channels), jnp.float32
-    )
+    unused = small.shape[0] - taps - 2
+    small[pl.ds(taps + 2, unused), :] = jnp.zeros((unused, channels), jnp.float32)
     for block in range(blocks):
         lanes = pl.ds(block * LANES, LANES)
         total = jnp.sum(sums[block], axis=0, keepdims=True)
@@ -214,6 +221,9 @@
         return 0
 
     lax.fori_loop(0, blocks, tap_block, 0)
+    for place in range(out.shape[0]):
+        part = small[pl.ds(place * SMALL, SMALL), :]
+        out[place] = jnp.concatenate([part, jnp.zeros_like(part)]).astype(jnp.bfloat16)
 
 
 def feature_kernel(field, up, down, left, right, taps, cotangent, out, padded):
@@ -231,11 +241,6 @@
                 out[row, columns, lanes] = total.astype(jnp.bfloat16)
 
 
-def halves(value):
-    high = value.astype(jnp.bfloat16)
-    return high, (value - high.astype(jnp.float32)).astype(jnp.bfloat16)
-
-
 def added(left, right):
     return (left.astype(jnp.float32) + right.astype(jnp.float32)).astype(jnp.bfloat16)
 
@@ -243,48 +248,69 @@
 def merge_kernel(kept, came, small, small_came, out):
     rows = kept.shape[1]
     out[:, pl.ds(0, rows), :] = added(kept[...], came[...])
-    total = small[...] + small_came[...]
-    out[:, pl.ds(rows, 2 * total.shape[1]), :] = jnp.concatenate(halves(total), axis=1)
-
-
-def join_kernel(kept, came, out):
-    out[...] = added(kept[...], came[...])
+    out[:, pl.ds(rows, small.shape[1]), :] = added(small[...], small_came[...])
+
+
+def join_kernel(z_ref, kept, came, *outs):
+    for step, out in enumerate(outs):
+        z = lax.rem(z_ref[0] + step, Z)
+        out[...] = added(kept[z], came[z])
 
 
 def plane_kernel(chunks, out, total):
     total[...] = jnp.sum(chunks[...].astype(jnp.float32), axis=0)
-    rows = total.shape[0] - 8
-    small = jnp.concatenate(halves(total[pl.ds(rows, 4), :] + total[pl.ds(rows + 4, 4), :]))
+    each = out.shape[1] // 2
+    channels = out.shape[2]
+    narrow = channels // 2
+    top = each * Z // 2
+    small = total[pl.ds(total.shape[0] - 2 * SMALL, SMALL), :].astype(jnp.bfloat16)
+    small = jnp.concatenate([small[:, :narrow], small[:, narrow:]])
     for z in range(Z):
-        parts = [total[pl.ds(q * 2 * Z + 2 * z, 2), :] for q in range(rows // (2 * Z))]
-        own = jnp.concatenate(parts).astype(jnp.bfloat16)
-        out[z] = jnp.concatenate([own, small])
-
-
-def line_kernel(multiplier, chunks, line, dexpand, out):
+        parts = [total[pl.ds(top + q * 2 * Z + 2 * z, 2), :] for q in range(each // 2)]
+        out[z, pl.ds(0, each), :] = jnp.concatenate(parts).astype(jnp.bfloat16)
+        half = total[pl.ds(z // 2 * each, each), pl.ds(z % 2 * narrow, narrow)]
+        out[z, pl.ds(each, each), pl.ds(0, narrow)] = half.astype(jnp.bfloat16)
+        out[z, pl.ds(each, each), pl.ds(narrow, narrow)] = small
+
+
+def line_kernel(multiplier, chunks, *refs):
+    *came, dexpand, dreduce, out = refs
     total = jnp.sum(chunks[...].astype(jnp.float32), axis=0)
-    each = total.shape[0] - 8
+    each = total.shape[0] // 2
     channels = total.shape[1]
+    narrow = channels // 2
     for q in range(each // 2):
         dexpand[:, pl.ds(q * channels, channels)] = total[2 * q : 2 * q + 2] * multiplier
-    small = jnp.concatenate(halves(total[each : each + 4] + total[each + 4 :]))
+    dreduce[...] = total[each:, :narrow] * multiplier
+    small = total[each:, narrow:].astype(jnp.bfloat16)
+    line = sum(ref[...].astype(jnp.float32) for ref in came).astype(jnp.bfloat16)
     for place in range(out.shape[0]):
-        out[place, pl.ds(0, each), :] = line[place]
-        out[place, pl.ds(each, 8), :] = small
-
-
-def last_kernel(multiplier, chunks, dreduce, dkernel, dgain, dscale, full):
-    each = dreduce.shape[0]
-    total = jnp.sum(chunks[:, pl.ds(0, each), :].astype(jnp.float32), axis=0)
-    dreduce[...] = total * multiplier
-    full[...] = chunks[:, pl.ds(each, 4), :].astype(jnp.float32) + chunks[
-        :, pl.ds(each + 4, 4), :
-    ].astype(jnp.float32)
+        out[place, :, pl.ds(0, narrow)] = line[place // 2][
+            :, place % 2 * narrow : (place % 2 + 1) * narrow
+        ]
+        out[place, :, pl.ds(narrow, narrow)] = small
+
+
+def last_kernel(multiplier, chunks, half, dreduce, dkernel, dgain, dscale):
+    channels = dreduce.shape[1]
+    narrow = channels // 2
+    dreduce[:, pl.ds(0, narrow)] = half[...]
+    total = jnp.sum(chunks[:, :, pl.ds(0, narrow)].astype(jnp.float32), axis=0)
+    dreduce[:, pl.ds(narrow, narrow)] = total * multiplier
     side = dkernel.shape[0]
-    for place in range(side * side):
-        dkernel[place // side, pl.ds(place % side, 1), :] = full[place // 4, pl.ds(place % 4, 1), :]
-    for place, out in ((side * side, dgain), (side * side + 1, dscale)):
-        out[...] = full[place // 4, pl.ds(place % 4, 1), :]
+    for place in range(chunks.shape[0]):
+        part = chunks[place, :, pl.ds(narrow, narrow)].astype(jnp.float32)
+        for row in range(SMALL):
+            tap = place * SMALL + row
+            for i in range(2):
+                lanes = pl.ds(i * narrow, narrow)
+                value = part[i * SMALL + row : i * SMALL + row + 1]
+                if tap < side * side:
+                    dkernel[tap // side, pl.ds(tap % side, 1), lanes] = value
+                elif tap == side * side:
+                    dgain[:, lanes] = value
+                elif tap == side * side + 1:
+                    dscale[:, lanes] = value
 
 
 VMEM = pl.BlockSpec(memory_space=pltpu.VMEM)
@@ -334,13 +360,15 @@
     shape = jax.ShapeDtypeStruct
     padded_shape = (blocks, height + side - 1, LEFT + width + 8, LANES)
 
-    sent_e, kept_e, sent_r, kept_r, dpre, xhat, rstd, padded, row_sums = pl.pallas_call(
+    each = rows // Z
+    top = rows // 2
+    sent, kept, sent_z, kept_z, dpre, xhat, rstd, padded, row_sums = pl.pallas_call(
         forward_kernel,
         name="forward",
         in_specs=[SMEM, HBM] + [VMEM] * 4 + [HBM] * 6,
         out_specs=[VMEM] * 9,
-        out_shape=[shape((places, rows, channels), bf16)] * 2
-        + [shape((Z, places, rows // Z, channels), bf16)] * 2
+        out_shape=[shape((places, top + rows, channels), bf16)] * 2
+        + [shape((Z, places // 2, each, channels), bf16)] * 2
         + [
             shape((pixels, hidden), bf16),
             shape((blocks, pixels, LANES), f32),
@@ -370,8 +398,8 @@
     )
 
     swap = [(0, 1), (1, 0)]
-    came_e = lax.ppermute(sent_e, "core", swap)
-    came_r = lax.ppermute(sent_r, "core", swap)
+    came = lax.ppermute(sent, "core", swap)
+    came_z = lax.ppermute(sent_z, "core", swap)
     dconv, small = pl.pallas_call(
         functools.partial(backward_kernel, multiplier),
         name="backward",
@@ -379,73 +407,73 @@
         out_specs=[VMEM] * 2,
         out_shape=[
             shape((height, width, channels), bf16),
-            shape((SMALL, channels), f32),
+            shape((places, 2 * SMALL, channels), bf16),
         ],
-        scratch_shapes=[pltpu.VMEM((blocks, pixels, LANES), f32)],
+        scratch_shapes=[
+            pltpu.VMEM((blocks, pixels, LANES), f32),
+            pltpu.VMEM((places * SMALL, channels), f32),
+        ],
         compiler_params=PARAMS,
     )(dpre, w_expand, xhat, rstd, padded, row_sums)
 
     small_came = lax.ppermute(small, "core", swap)
-    each = SMALL // places
-    whole = rows + 2 * each
+    whole = top + rows + 2 * SMALL
     chip = pl.pallas_call(
         merge_kernel,
         name="merge",
         grid=(Y,),
-        in_specs=[pl.BlockSpec((X, rows, channels), lambda i: (i, 0, 0))] * 2
-        + [pl.BlockSpec((X, each, channels), lambda i: (i, 0, 0))] * 2,
+        in_specs=[pl.BlockSpec((X, top + rows, channels), lambda i: (i, 0, 0))] * 2
+        + [pl.BlockSpec((X, 2 * SMALL, channels), lambda i: (i, 0, 0))] * 2,
         out_specs=pl.BlockSpec((X, whole, channels), lambda i: (i, 0, 0)),
         out_shape=shape((places, whole, channels), bf16),
         compiler_params=PARAMS,
-    )(
-        kept_e, came_e, small.reshape(places, each, channels),
-        small_came.reshape(places, each, channels),
-    )
-    chip, dconv, kept_r = lax.optimization_barrier((chip, dconv, kept_r))
-    block = pl.BlockSpec((2, places, rows // Z, channels), lambda i: (i, 0, 0, 0))
-    joined = pl.pallas_call(
+    )(kept, came, small, small_came)
+    chip, dconv, came_z = lax.optimization_barrier((chip, dconv, came_z))
+    line = pl.pallas_call(
         join_kernel,
         name="join",
-        grid=(Z // 2,),
-        in_specs=[block] * 2,
-        out_specs=block,
-        out_shape=shape(kept_r.shape, bf16),
-        compiler_params=PARAMS,
-    )(kept_r, came_r)
-    line = lax.psum_scatter(
-        joined.reshape(Z * rows * places // Z, channels), "z", scatter_dimension=0, tiled=True
-    ).reshape(places, rows // Z, channels)
-    chunks, edges = lax.optimization_barrier((exchanged(chip, ("y", "x")), borders(dconv, reach)))
+        in_specs=[SMEM] + [VMEM] * 2,
+        out_specs=[VMEM] * Z,
+        out_shape=[shape(kept_z.shape[1:], bf16)] * Z,
+        compiler_params=PARAMS,
+    )(lax.axis_index("z").reshape(1), kept_z, came_z)
+    line = [
+        part if step == 0 else lax.ppermute(part, "z", [(i, (i + step) % Z) for i in range(Z)])
+        for step, part in enumerate(line)
+    ]
+    chunks, edges, line = lax.optimization_barrier(
+        (exchanged(chip, ("y", "x")), borders(dconv, reach), line)
+    )
     chunks = pl.pallas_call(
         plane_kernel,
         name="plane",
         in_specs=[VMEM],
         out_specs=VMEM,
-        out_shape=shape((Z, rows // Z + 2 * each, channels), bf16),
+        out_shape=shape((Z, 2 * each, channels), bf16),
         scratch_shapes=[pltpu.VMEM((whole, channels), f32)],
         compiler_params=PARAMS,
     )(chunks)
-    dexpand, chunks = pl.pallas_call(
+    dexpand, half, chunks = pl.pallas_call(
         functools.partial(line_kernel, multiplier),
         name="line",
-        in_specs=[VMEM] * 2,
-        out_specs=[VMEM] * 2,
+        in_specs=[VMEM] * (1 + Z),
+        out_specs=[VMEM] * 3,
         out_shape=[
-            shape((channels * rows // Z // hidden, hidden), f32),
-            shape((places, rows // Z + 2 * each, channels), bf16),
+            shape((channels * each // hidden, hidden), f32),
+            shape((each, channels // 2), f32),
+            shape((places, each, channels), bf16),
         ],
         compiler_params=PARAMS,
-    )(exchanged(chunks, "z"), line)
+    )(exchanged(chunks, "z"), *line)
     dreduce, dkernel, dgain, dscale = pl.pallas_call(
         functools.partial(last_kernel, multiplier),
         name="last",
-        in_specs=[VMEM],
+        in_specs=[VMEM] * 2,
         out_specs=[VMEM] * 4,
-        out_shape=[shape((rows // Z, channels), f32), shape((side, side, channels), f32)]
+        out_shape=[shape((each, channels), f32), shape((side, side, channels), f32)]
         + [shape((1, channels), f32)] * 2,
-        scratch_shapes=[pltpu.VMEM((places, each, channels), f32)],
-        compiler_params=PARAMS,
-    )(exchanged(chunks, ("y", "x")))
+        compiler_params=PARAMS,
+    )(exchanged(chunks, ("y", "x")), half)
     grad_features = pl.pallas_call(
         feature_kernel,
         name="features",

time: 125 us -> 116 us (0.928)
  starting transfers between devices: 53.9 us -> 71.8 us
  between operations: 14.2 us -> 0.9 us
  Pallas kernels: 22.5 us -> 17.7 us
  local copies, waits for them, and re-layouts: 6.33 us -> 1.98 us
  blocking collectives: 15.5 us -> 13.4 us
  waiting for transfers between devices: 11.9 us -> 9.86 us
    ppermute x2 -> x9, starting transfers between devices: 1.19 us -> 18.7 us  [the longest x7 17.5 us: shards(): lax.ppermute(part, 'z', [(i, (i + step) % Z) for i in range(Z)])]
    ppermute x8, starting transfers between devices: 26.4 us -> 35.6 us  [shifted(): return lax.ppermute(value, axes, pairs)]
    all_to_all x2, starting transfers between devices: 25.8 us -> 16.9 us  [exchanged(): return lax.all_to_all(chunks, axes, 0, 0, tiled=True)]
    reshape x2 -> x0, local copies, waits for them, and re-layouts: 2.54 us -> none  [the longest x1 1.6 us: shards(): small_came.reshape(places, each, channels)]
    all_to_all x2, waiting for transfers between devices: 6.47 us -> 4.13 us  [exchanged(): return lax.all_to_all(chunks, axes, 0, 0, tiled=True)]
    all_to_all x1, blocking collectives: 15.5 us -> 13.4 us  [exchanged(): return lax.all_to_all(chunks, axes, 0, 0, tiled=True)]
    unnamed x10 -> x6, local copies, waits for them, and re-layouts: 1.83 us -> 0.02 us
    pallas_call x1, Pallas kernels: 3.5 us -> 1.88 us  [shards(): pl.pallas_call(merge_kernel, name='merge', grid=(Y,), in_specs=[pl.BlockS...]
  transfers between devices with their start and end apart: 14 -> 20, of which waited for: 8 -> 7; matrix products, arithmetic and copies ran while one was open for 3% -> 1% of each run, Pallas kernels for 8% -> 7%
where the time goes in v4:
time: 116 us
  starting transfers between devices  71.8 us (62%)
  Pallas kernels  17.7 us (15%)
  blocking collectives  13.4 us (12%)
  waiting for transfers between devices  9.86 us (8%)
  local copies, waits for them, and re-layouts  1.98 us (2%)
    ppermute x8, starting transfers between devices, shifted(): return lax.ppermute(value, axes, pairs)  35.6 us
    ppermute x7, starting transfers between devices, shards(): lax.ppermute(part, 'z', [(i, (i + step) % Z) for i in range(Z)])  17.5 us
    all_to_all x2, starting transfers between devices, exchanged(): return lax.all_to_all(chunks, axes, 0, 0, tiled=True)  16.9 us
    all_to_all x1, blocking collectives, exchanged(): return lax.all_to_all(chunks, axes, 0, 0, tiled=True)  13.4 us
    pallas_call x1, Pallas kernels, shards(): pl.pallas_call(forward_kernel, name='forward', in_specs=[SMEM, HBM] + [VM...  8.34 us
    ppermute x8, waiting for transfers between devices, shifted(): return lax.ppermute(value, axes, pairs)  4.72 us
    all_to_all x2, waiting for transfers between devices, exchanged(): return lax.all_to_all(chunks, axes, 0, 0, tiled=True)  4.13 us
    pallas_call x1, Pallas kernels, shards(): pl.pallas_call(functools.partial(backward_kernel, multiplier), name='back...  3.1 us
  transfers between devices with their start and end apart: 20, of which 7 were waited for; matrix products, arithmetic and copies ran while one was open for 1% of the time, Pallas kernels for 7%

profile of v4, /device:TPU:2, one launch (start us, length us, event | category | flops | bytes accessed | tf_op | source)
XLA Modules:
  0.0 115.7 jit_solution(8221044256978381099)
XLA Ops:
  0.6 1.0 fusion.3
  1.6 1.3 %collective-permute-start.1 = (bf16[3,32,512]{2,1,0:T(8,128)(2,1)S(1)}, bf16[3,32,512]{2,1,0:T(8,128)(2,1)S(1)}, u32[]{:S(2)}, u32[]{:S(2)}) collective-permute-start(bf16[3,32,512]{2,1,0:T(8,128)(2,1)S(1)} %get-tuple-element.96), channel_id=1, source_target_pairs={{32,0},{64,32},{96,64},{128,96},{160,128},{192,160},{224,192},{33,... | collective-permute-start | bytes 294920 | tf_op jit(solution)/shard_map/ppermute | solution.py:329
  2.9 3.0 %collective-permute-start = (bf16[3,32,512]{2,1,0:T(8,128)(2,1)S(1)}, bf16[3,32,512]{2,1,0:T(8,128)(2,1)S(1)}, u32[]{:S(2)}, u32[]{:S(2)}) collective-permute-start(bf16[3,32,512]{2,1,0:T(8,128)(2,1)S(1)} %get-tuple-element.97), channel_id=1, source_target_pairs={{0,32},{32,64},{64,96},{96,128},{128,160},{160,192},{192,224},{1,3... | collective-permute-start | bytes 294920 | tf_op jit(solution)/shard_map/ppermute | solution.py:329
  5.9 0.9 fusion.2
  7.0 3.8 %collective-permute-start.2 = (bf16[14,3,512]{2,1,0:T(4,128)(2,1)S(1)}, bf16[14,3,512]{2,1,0:T(4,128)(2,1)S(1)}, u32[]{:S(2)}, u32[]{:S(2)}) collective-permute-start(bf16[14,3,512]{2,1,0:T(4,128)(2,1)S(1)} %pad_maximum_fusion), channel_id=1, source_target_pairs={{0,1},{1,2},{2,3},{3,4},{4,5},{5,6},{6,7},{7,8},{8,9},{9,10},{10,1... | collective-permute-start | bytes 129032 | tf_op jit(solution)/shard_map/ppermute | solution.py:329
  10.8 5.8 %collective-permute-start.3 = (bf16[14,3,512]{2,1,0:T(4,128)(2,1)S(1)}, bf16[14,3,512]{2,1,0:T(4,128)(2,1)S(1)}, u32[]{:S(2)}, u32[]{:S(2)}) collective-permute-start(bf16[14,3,512]{2,1,0:T(4,128)(2,1)S(1)} %pad_maximum_fusion.1), channel_id=1, source_target_pairs={{1,0},{2,1},{3,2},{4,3},{5,4},{6,5},{7,6},{8,7},{9,8},{10,9},{11,1... | collective-permute-start | bytes 129032 | tf_op jit(solution)/shard_map/ppermute | solution.py:329
  16.8 1.6 %collective-permute-done.3.right = bf16[14,3,512]{2,1,0:T(4,128)(2,1)S(1)} collective-permute-done((bf16[14,3,512]{2,1,0:T(4,128)(2,1)S(1)}, bf16[14,3,512]{2,1,0:T(4,128)(2,1)S(1)}, u32[]{:S(2)}, u32[]{:S(2)}) %collective-permute-start.3) | collective-permute-done | bytes 43040 | tf_op jit(solution)/shard_map/ppermute | solution.py:329
  18.5 8.3 %forward.1 = (bf16[16,96,512]{2,1,0:T(8,128)(2,1)S(1)}, bf16[16,96,512]{2,1,0:T(8,128)(2,1)S(1)}, bf16[8,8,8,512]{3,2,1,0:T(8,128)(2,1)S(1)}, bf16[8,8,8,512]{3,...) custom-call(s32[1]{0:T(128)} %bitcast.core_ref, ...), custom_call_target="tpu_custom_call" | custom-call | tf_op jit(solution)/shard_map/forward/pallas_call | solution.py:365
  26.8 1.1 collective-permute-start.4
  28.0 3.1 %backward.1 = (bf16[8,32,512]{2,1,0:T(8,128)(2,1)S(1)}, bf16[16,8,512]{2,1,0:T(8,128)(2,1)S(1)}) custom-call(bf16[256,2048]{1,0:T(8,128)(2,1)S(1)} %get-tuple-element.50.dpre, bf16[512,2048]{1,0:T(8,128)(2,1)S(1)} %copy-done, f32[4,256,128]{2,1,0:T(8,128)S(1)} %get-tuple-element.51.xhat, f32[256,128]{1,0:T(8,128)S(1)} %get-tuple-element.52.rstd, ...), custom_call_target="tpu_custom_call" | custom-call | tf_op jit(solution)/shard_map/backward/pallas_call | solution.py:403
  31.1 0.5 collective-permute-start.5
  31.6 1.0 collective-permute-done.5.small_came
  32.6 1.9 %merge.1 = bf16[16,104,512]{2,1,0:T(8,128)(2,1)} custom-call(bf16[16,96,512]{2,1,0:T(8,128)(2,1)S(1)} %get-tuple-element.48.kept, bf16[16,96,512]{2,1,0:T(8,128)(2,1)S(1)} %collective-permute-done.4.came, bf16[16,8,512]{2,1,0:T(8,128)(2,1)S(1)} %get-tuple-element.55.small, bf16[16,8,512]{2,1,0:T(8,128)(2,1)S(1)} %collective-permute-done.5.small_came), custom_call_target="tpu_custom_call" | custom-call | tf_op jit(solution)/shard_map/merge/pallas_call | solution.py:421
  34.5 9.4 %all-to-all-start = ((bf16[16,104,512]{2,1,0:T(8,128)(2,1)}), bf16[16,104,512]{2,1,0:T(8,128)(2,1)S(1)}, u32[]{:S(2)}, u32[]{:S(2)}) async-start(bf16[16,104,512]{2,1,0:T(8,128)(2,1)} %merge.1), calls=%async_computation | async-start | bytes 3407872 | tf_op jit(solution)/shard_map/all_to_all | solution.py:343
  44.0 1.3 %collective-permute-start.8 = (bf16[3,32,512]{2,1,0:T(8,128)(2,1)S(1)}, bf16[3,32,512]{2,1,0:T(8,128)(2,1)S(1)}, u32[]{:S(2)}, u32[]{:S(2)}) collective-permute-start(bf16[3,32,512]{2,1,0:T(8,128)(2,1)S(1)} %get-tuple-element.92), channel_id=1, source_target_pairs={{32,0},{64,32},{96,64},{128,96},{160,128},{192,160},{224,192},{33,... | collective-permute-start | bytes 294920 | tf_op jit(solution)/shard_map/ppermute | solution.py:329
  45.5 0.4 collective-permute-start.11
  45.9 5.7 %collective-permute-start.12 = (bf16[8,8,512]{2,1,0:T(8,128)(2,1)S(1)}, bf16[8,8,512]{2,1,0:T(8,128)(2,1)S(1)}, u32[]{:S(2)}, u32[]{:S(2)}) collective-permute-start(bf16[8,8,512]{2,1,0:T(8,128)(2,1)S(1)} %get-tuple-element.64), channel_id=1, source_target_pairs={{0,2},{1,3},{2,4},{3,5},{4,6},{5,7},{6,0},{7,1},{8,10},{9,11},{10,... | collective-permute-start | bytes 196616 | tf_op jit(solution)/shard_map/ppermute | solution.py:441
  51.5 0.7 collective-permute-start.13
  52.3 2.6 %collective-permute-start.14 = (bf16[8,8,512]{2,1,0:T(8,128)(2,1)S(1)}, bf16[8,8,512]{2,1,0:T(8,128)(2,1)S(1)}, u32[]{:S(2)}, u32[]{:S(2)}) collective-permute-start(bf16[8,8,512]{2,1,0:T(8,128)(2,1)S(1)} %get-tuple-element.66), channel_id=1, source_target_pairs={{0,4},{1,5},{2,6},{3,7},{4,0},{5,1},{6,2},{7,3},{8,12},{9,13},{10,... | collective-permute-start | bytes 196616 | tf_op jit(solution)/shard_map/ppermute | solution.py:441
  54.8 12.4 %collective-permute-start.7 = (bf16[3,32,512]{2,1,0:T(8,128)(2,1)S(1)}, bf16[3,32,512]{2,1,0:T(8,128)(2,1)S(1)}, u32[]{:S(2)}, u32[]{:S(2)}) collective-permute-start(bf16[3,32,512]{2,1,0:T(8,128)(2,1)S(1)} %get-tuple-element.93), channel_id=1, source_target_pairs={{0,32},{32,64},{64,96},{96,128},{128,160},{160,192},{192,224},{1,3... | collective-permute-start | bytes 294920 | tf_op jit(solution)/shard_map/ppermute | solution.py:329
  67.3 0.9 collective-permute-done.7.up
  68.2 4.2 %collective-permute-start.15 = (bf16[8,8,512]{2,1,0:T(8,128)(2,1)S(1)}, bf16[8,8,512]{2,1,0:T(8,128)(2,1)S(1)}, u32[]{:S(2)}, u32[]{:S(2)}) collective-permute-start(bf16[8,8,512]{2,1,0:T(8,128)(2,1)S(1)} %get-tuple-element.67), channel_id=1, source_target_pairs={{0,5},{1,6},{2,7},{3,0},{4,1},{5,2},{6,3},{7,4},{8,13},{9,14},{10,... | collective-permute-start | bytes 196616 | tf_op jit(solution)/shard_map/ppermute | solution.py:441
  72.5 4.0 %collective-permute-start.16 = (bf16[8,8,512]{2,1,0:T(8,128)(2,1)S(1)}, bf16[8,8,512]{2,1,0:T(8,128)(2,1)S(1)}, u32[]{:S(2)}, u32[]{:S(2)}) collective-permute-start(bf16[8,8,512]{2,1,0:T(8,128)(2,1)S(1)} %get-tuple-element.68), channel_id=1, source_target_pairs={{0,6},{1,7},{2,0},{3,1},{4,2},{5,3},{6,4},{7,5},{8,14},{9,15},{10,... | collective-permute-start | bytes 196616 | tf_op jit(solution)/shard_map/ppermute | solution.py:441
  76.5 3.9 %collective-permute-start.9 = (bf16[14,3,512]{2,1,0:T(4,128)(2,1)S(1)}, bf16[14,3,512]{2,1,0:T(4,128)(2,1)S(1)}, u32[]{:S(2)}, u32[]{:S(2)}) collective-permute-start(bf16[14,3,512]{2,1,0:T(4,128)(2,1)S(1)} %pad_maximum_fusion.2), channel_id=1, source_target_pairs={{0,1},{1,2},{2,3},{3,4},{4,5},{5,6},{6,7},{7,8},{8,9},{9,10},{10,1... | collective-permute-start | bytes 129032 | tf_op jit(solution)/shard_map/ppermute | solution.py:329
  80.4 4.0 %collective-permute-start.10 = (bf16[14,3,512]{2,1,0:T(4,128)(2,1)S(1)}, bf16[14,3,512]{2,1,0:T(4,128)(2,1)S(1)}, u32[]{:S(2)}, u32[]{:S(2)}) collective-permute-start(bf16[14,3,512]{2,1,0:T(4,128)(2,1)S(1)} %pad_maximum_fusion.3), channel_id=1, source_target_pairs={{1,0},{2,1},{3,2},{4,3},{5,4},{6,5},{7,6},{8,7},{9,8},{10,9},{11,1... | collective-permute-start | bytes 129032 | tf_op jit(solution)/shard_map/ppermute | solution.py:329
  84.7 1.8 %collective-permute-done.10.right = bf16[14,3,512]{2,1,0:T(4,128)(2,1)S(1)} collective-permute-done((bf16[14,3,512]{2,1,0:T(4,128)(2,1)S(1)}, bf16[14,3,512]{2,1,0:T(4,128)(2,1)S(1)}, u32[]{:S(2)}, u32[]{:S(2)}) %collective-permute-start.10) | collective-permute-done | bytes 43040 | tf_op jit(solution)/shard_map/ppermute | solution.py:329
  86.9 13.4 %all_to_all.15.chunks = bf16[8,16,512]{2,1,0:T(8,128)(2,1)S(1)} all-to-all(bf16[8,16,512]{2,1,0:T(8,128)(2,1)S(1)} %plane.1), channel_id=1, replica_groups=mesh['y'=4,'core'=2,'x'=4,'z'=8] {'z'}, dimensions={0} | all-to-all | bytes 262144 | tf_op jit(solution)/shard_map/all_to_all | solution.py:343
  100.2 0.7 line.1
  101.0 7.5 %all-to-all-start.2 = ((bf16[16,8,512]{2,1,0:T(8,128)(2,1)}), bf16[16,8,512]{2,1,0:T(8,128)(2,1)S(1)}, u32[]{:S(2)}, u32[]{:S(2)}) async-start(bf16[16,8,512]{2,1,0:T(8,128)(2,1)} %get-tuple-element.83), calls=%async_computation.2 | async-start | bytes 262144 | tf_op jit(solution)/shard_map/all_to_all | solution.py:343
  108.4 2.5 %features.1 = bf16[8,32,512]{2,1,0:T(8,128)(2,1)} custom-call(bf16[8,32,512]{2,1,0:T(8,128)(2,1)S(1)} %get-tuple-element.58.field, bf16[3,32,512]{2,1,0:T(8,128)(2,1)S(1)} %collective-permute-done.7.up, bf16[3,32,512]{2,1,0:T(8,128)(2,1)S(1)} %collective-permute-done.8.down, bf16[14,3,512]{2,1,0:T(4,128)(2,1)S(1)} %collective-permute-done.9.left, ...), custom_call_target="tpu_custom_call" | custom-call | tf_op jit(solution)/shard_map/features/pallas_call | solution.py:477
  110.9 4.1 %all-to-all-done.2.chunks = bf16[16,8,512]{2,1,0:T(8,128)(2,1)S(1)} async-done(((bf16[16,8,512]{2,1,0:T(8,128)(2,1)}), bf16[16,8,512]{2,1,0:T(8,128)(2,1)S(1)}, u32[]{:S(2)}, u32[]{:S(2)}) %all-to-all-start.2) | async-done | bytes 131104 | tf_op jit(solution)/shard_map/all_to_all | solution.py:343
  115.1 0.7 last.1
  (35 shorter events, 1.3 us)
Async XLA Ops:
  1.6 5.3 %collective-permute-start.1 = (bf16[3,32,512]{2,1,0:T(8,128)(2,1)S(1)}, bf16[3,32,512]{2,1,0:T(8,128)(2,1)S(1)}, u32[]{:S(2)}, u32[]{:S(2)}) collective-permute-start(bf16[3,32,512]{2,1,0:T(8,128)(2,1)S(1)} %get-tuple-element.96), channel_id=1, source_target_pairs={{32,0},{64,32},{96,64},{128,96},{160,128},{192,160},{224,192},{33,... | collective-permute-start | bytes 294920 | tf_op jit(solution)/shard_map/ppermute | solution.py:329
  2.9 4.0 %collective-permute-start = (bf16[3,32,512]{2,1,0:T(8,128)(2,1)S(1)}, bf16[3,32,512]{2,1,0:T(8,128)(2,1)S(1)}, u32[]{:S(2)}, u32[]{:S(2)}) collective-permute-start(bf16[3,32,512]{2,1,0:T(8,128)(2,1)S(1)} %get-tuple-element.97), channel_id=1, source_target_pairs={{0,32},{32,64},{64,96},{96,128},{128,160},{160,192},{192,224},{1,3... | collective-permute-start | bytes 294920 | tf_op jit(solution)/shard_map/ppermute | solution.py:329
  7.0 9.9 %collective-permute-start.2 = (bf16[14,3,512]{2,1,0:T(4,128)(2,1)S(1)}, bf16[14,3,512]{2,1,0:T(4,128)(2,1)S(1)}, u32[]{:S(2)}, u32[]{:S(2)}) collective-permute-start(bf16[14,3,512]{2,1,0:T(4,128)(2,1)S(1)} %pad_maximum_fusion), channel_id=1, source_target_pairs={{0,1},{1,2},{2,3},{3,4},{4,5},{5,6},{6,7},{7,8},{8,9},{9,10},{10,1... | collective-permute-start | bytes 129032 | tf_op jit(solution)/shard_map/ppermute | solution.py:329
  10.8 7.6 %collective-permute-start.3 = (bf16[14,3,512]{2,1,0:T(4,128)(2,1)S(1)}, bf16[14,3,512]{2,1,0:T(4,128)(2,1)S(1)}, u32[]{:S(2)}, u32[]{:S(2)}) collective-permute-start(bf16[14,3,512]{2,1,0:T(4,128)(2,1)S(1)} %pad_maximum_fusion.1), channel_id=1, source_target_pairs={{1,0},{2,1},{3,2},{4,3},{5,4},{6,5},{7,6},{8,7},{9,8},{10,9},{11,1... | collective-permute-start | bytes 129032 | tf_op jit(solution)/shard_map/ppermute | solution.py:329
  18.5 9.5 %copy-start = (bf16[512,2048]{1,0:T(8,128)(2,1)S(1)}, bf16[512,2048]{1,0:T(8,128)(2,1)}, u32[]{:S(2)}) copy-start(bf16[512,2048]{1,0:T(8,128)(2,1)} %expand.1) | copy-start | bytes 6291460
  26.8 5.8 %collective-permute-start.4 = (bf16[16,96,512]{2,1,0:T(8,128)(2,1)S(1)}, bf16[16,96,512]{2,1,0:T(8,128)(2,1)S(1)}, u32[]{:S(2)}, u32[]{:S(2)}) collective-permute-start(bf16[16,96,512]{2,1,0:T(8,128)(2,1)S(1)} %get-tuple-element.49), channel_id=1, source_target_pairs={{0,32},{32,0},{1,33},{33,1},{2,34},{34,2},{3,35},{35,3},{4,36},{36... | collective-permute-start | bytes 4718600 | tf_op jit(solution)/shard_map/ppermute | solution.py:401
  27.9 6.6 %collective-permute-start.6 = (bf16[8,8,8,512]{3,2,1,0:T(8,128)(2,1)S(1)}, bf16[8,8,8,512]{3,2,1,0:T(8,128)(2,1)S(1)}, u32[]{:S(2)}, u32[]{:S(2)}) collective-permute-start(bf16[8,8,8,512]{3,2,1,0:T(8,128)(2,1)S(1)} %get-tuple-element.57), channel_id=1, source_target_pairs={{0,32},{32,0},{1,33},{33,1},{2,34},{34,2},{3,35},{35,3},{4,36},{36... | collective-permute-start | bytes 1572872 | tf_op jit(solution)/shard_map/ppermute | solution.py:402
  31.1 1.5 %collective-permute-start.5 = (bf16[16,8,512]{2,1,0:T(8,128)(2,1)S(1)}, bf16[16,8,512]{2,1,0:T(8,128)(2,1)S(1)}, u32[]{:S(2)}, u32[]{:S(2)}) collective-permute-start(bf16[16,8,512]{2,1,0:T(8,128)(2,1)S(1)} %get-tuple-element.55.small), channel_id=1, source_target_pairs={{0,32},{32,0},{1,33},{33,1},{2,34},{34,2},{3,35},{35,3},{4,36},{36... | collective-permute-start | bytes 393224 | tf_op jit(solution)/shard_map/ppermute | solution.py:419
  34.5 52.0 %all-to-all-start = ((bf16[16,104,512]{2,1,0:T(8,128)(2,1)}), bf16[16,104,512]{2,1,0:T(8,128)(2,1)S(1)}, u32[]{:S(2)}, u32[]{:S(2)}) async-start(bf16[16,104,512]{2,1,0:T(8,128)(2,1)} %merge.1), calls=%async_computation | async-start | bytes 3407872 | tf_op jit(solution)/shard_map/all_to_all | solution.py:343
  44.0 10.9 %collective-permute-start.8 = (bf16[3,32,512]{2,1,0:T(8,128)(2,1)S(1)}, bf16[3,32,512]{2,1,0:T(8,128)(2,1)S(1)}, u32[]{:S(2)}, u32[]{:S(2)}) collective-permute-start(bf16[3,32,512]{2,1,0:T(8,128)(2,1)S(1)} %get-tuple-element.92), channel_id=1, source_target_pairs={{32,0},{64,32},{96,64},{128,96},{160,128},{192,160},{224,192},{33,... | collective-permute-start | bytes 294920 | tf_op jit(solution)/shard_map/ppermute | solution.py:329
  45.4 63.0 %copy-start.1 = (bf16[8,32,512]{2,1,0:T(8,128)(2,1)S(1)}, bf16[8,32,512]{2,1,0:T(8,128)(2,1)}, u32[]{:S(2)}) copy-start(bf16[8,32,512]{2,1,0:T(8,128)(2,1)} %cotangent.1) | copy-start | bytes 786436
  45.5 63.0 %copy-start.2 = (f32[7,7,512]{2,1,0:T(8,128)S(1)}, f32[7,7,512]{2,1,0:T(8,128)}, u32[]{:S(2)}) copy-start(f32[7,7,512]{2,1,0:T(8,128)} %taps.1) | copy-start | bytes 301060
  45.5 27.0 %collective-permute-start.11 = (bf16[8,8,512]{2,1,0:T(8,128)(2,1)S(1)}, bf16[8,8,512]{2,1,0:T(8,128)(2,1)S(1)}, u32[]{:S(2)}, u32[]{:S(2)}) collective-permute-start(bf16[8,8,512]{2,1,0:T(8,128)(2,1)S(1)} %get-tuple-element.63), channel_id=1, source_target_pairs={{0,1},{1,2},{2,3},{3,4},{4,5},{5,6},{6,7},{7,0},{8,9},{9,10},{10,1... | collective-permute-start | bytes 196616 | tf_op jit(solution)/shard_map/ppermute | solution.py:441
  45.9 30.6 %collective-permute-start.12 = (bf16[8,8,512]{2,1,0:T(8,128)(2,1)S(1)}, bf16[8,8,512]{2,1,0:T(8,128)(2,1)S(1)}, u32[]{:S(2)}, u32[]{:S(2)}) collective-permute-start(bf16[8,8,512]{2,1,0:T(8,128)(2,1)S(1)} %get-tuple-element.64), channel_id=1, source_target_pairs={{0,2},{1,3},{2,4},{3,5},{4,6},{5,7},{6,0},{7,1},{8,10},{9,11},{10,... | collective-permute-start | bytes 196616 | tf_op jit(solution)/shard_map/ppermute | solution.py:441
  51.5 24.9 %collective-permute-start.13 = (bf16[8,8,512]{2,1,0:T(8,128)(2,1)S(1)}, bf16[8,8,512]{2,1,0:T(8,128)(2,1)S(1)}, u32[]{:S(2)}, u32[]{:S(2)}) collective-permute-start(bf16[8,8,512]{2,1,0:T(8,128)(2,1)S(1)} %get-tuple-element.65), channel_id=1, source_target_pairs={{0,3},{1,4},{2,5},{3,6},{4,7},{5,0},{6,1},{7,2},{8,11},{9,12},{10,... | collective-permute-start | bytes 196616 | tf_op jit(solution)/shard_map/ppermute | solution.py:441
  52.3 28.2 %collective-permute-start.14 = (bf16[8,8,512]{2,1,0:T(8,128)(2,1)S(1)}, bf16[8,8,512]{2,1,0:T(8,128)(2,1)S(1)}, u32[]{:S(2)}, u32[]{:S(2)}) collective-permute-start(bf16[8,8,512]{2,1,0:T(8,128)(2,1)S(1)} %get-tuple-element.66), channel_id=1, source_target_pairs={{0,4},{1,5},{2,6},{3,7},{4,0},{5,1},{6,2},{7,3},{8,12},{9,13},{10,... | collective-permute-start | bytes 196616 | tf_op jit(solution)/shard_map/ppermute | solution.py:441
  54.8 13.3 %collective-permute-start.7 = (bf16[3,32,512]{2,1,0:T(8,128)(2,1)S(1)}, bf16[3,32,512]{2,1,0:T(8,128)(2,1)S(1)}, u32[]{:S(2)}, u32[]{:S(2)}) collective-permute-start(bf16[3,32,512]{2,1,0:T(8,128)(2,1)S(1)} %get-tuple-element.93), channel_id=1, source_target_pairs={{0,32},{32,64},{64,96},{96,128},{128,160},{160,192},{192,224},{1,3... | collective-permute-start | bytes 294920 | tf_op jit(solution)/shard_map/ppermute | solution.py:329
  68.2 16.3 %collective-permute-start.15 = (bf16[8,8,512]{2,1,0:T(8,128)(2,1)S(1)}, bf16[8,8,512]{2,1,0:T(8,128)(2,1)S(1)}, u32[]{:S(2)}, u32[]{:S(2)}) collective-permute-start(bf16[8,8,512]{2,1,0:T(8,128)(2,1)S(1)} %get-tuple-element.67), channel_id=1, source_target_pairs={{0,5},{1,6},{2,7},{3,0},{4,1},{5,2},{6,3},{7,4},{8,13},{9,14},{10,... | collective-permute-start | bytes 196616 | tf_op jit(solution)/shard_map/ppermute | solution.py:441
  72.5 12.0 %collective-permute-start.16 = (bf16[8,8,512]{2,1,0:T(8,128)(2,1)S(1)}, bf16[8,8,512]{2,1,0:T(8,128)(2,1)S(1)}, u32[]{:S(2)}, u32[]{:S(2)}) collective-permute-start(bf16[8,8,512]{2,1,0:T(8,128)(2,1)S(1)} %get-tuple-element.68), channel_id=1, source_target_pairs={{0,6},{1,7},{2,0},{3,1},{4,2},{5,3},{6,4},{7,5},{8,14},{9,15},{10,... | collective-permute-start | bytes 196616 | tf_op jit(solution)/shard_map/ppermute | solution.py:441
  76.4 8.1 %collective-permute-start.17 = (bf16[8,8,512]{2,1,0:T(8,128)(2,1)S(1)}, bf16[8,8,512]{2,1,0:T(8,128)(2,1)S(1)}, u32[]{:S(2)}, u32[]{:S(2)}) collective-permute-start(bf16[8,8,512]{2,1,0:T(8,128)(2,1)S(1)} %get-tuple-element.69), channel_id=1, source_target_pairs={{0,7},{1,0},{2,1},{3,2},{4,3},{5,4},{6,5},{7,6},{8,15},{9,8},{10,9... | collective-permute-start | bytes 196616 | tf_op jit(solution)/shard_map/ppermute | solution.py:441
  76.5 8.2 %collective-permute-start.9 = (bf16[14,3,512]{2,1,0:T(4,128)(2,1)S(1)}, bf16[14,3,512]{2,1,0:T(4,128)(2,1)S(1)}, u32[]{:S(2)}, u32[]{:S(2)}) collective-permute-start(bf16[14,3,512]{2,1,0:T(4,128)(2,1)S(1)} %pad_maximum_fusion.2), channel_id=1, source_target_pairs={{0,1},{1,2},{2,3},{3,4},{4,5},{5,6},{6,7},{7,8},{8,9},{9,10},{10,1... | collective-permute-start | bytes 129032 | tf_op jit(solution)/shard_map/ppermute | solution.py:329
  80.4 6.1 %collective-permute-start.10 = (bf16[14,3,512]{2,1,0:T(4,128)(2,1)S(1)}, bf16[14,3,512]{2,1,0:T(4,128)(2,1)S(1)}, u32[]{:S(2)}, u32[]{:S(2)}) collective-permute-start(bf16[14,3,512]{2,1,0:T(4,128)(2,1)S(1)} %pad_maximum_fusion.3), channel_id=1, source_target_pairs={{1,0},{2,1},{3,2},{4,3},{5,4},{6,5},{7,6},{8,7},{9,8},{10,9},{11,1... | collective-permute-start | bytes 129032 | tf_op jit(solution)/shard_map/ppermute | solution.py:329
  101.0 14.1 %all-to-all-start.2 = ((bf16[16,8,512]{2,1,0:T(8,128)(2,1)}), bf16[16,8,512]{2,1,0:T(8,128)(2,1)S(1)}, u32[]{:S(2)}, u32[]{:S(2)}) async-start(bf16[16,8,512]{2,1,0:T(8,128)(2,1)} %get-tuple-element.83), calls=%async_computation.2 | async-start | bytes 262144 | tf_op jit(solution)/shard_map/all_to_all | solution.py:343

commit v5 on v4

--- a/solution.py
+++ b/solution.py
@@ -316,7 +316,8 @@
 VMEM = pl.BlockSpec(memory_space=pltpu.VMEM)
 HBM = pl.BlockSpec(memory_space=pltpu.HBM)
 SMEM = pl.BlockSpec(memory_space=pltpu.SMEM)
-PARAMS = pltpu.CompilerParams(vmem_limit_bytes=24 << 20)
+PARAMS = pltpu.CompilerParams(vmem_limit_bytes=20 << 20)
+GLUE_PARAMS = pltpu.CompilerParams(vmem_limit_bytes=10 << 20)
 
 
 def in_hbm(value):
@@ -329,9 +330,11 @@
     return lax.ppermute(value, axes, pairs)
 
 
-def borders(field, reach):
-    up = shifted(field[-reach:], ROW, 1)
-    down = shifted(field[:reach], ROW, -1)
+def row_borders(field, reach):
+    return shifted(field[-reach:], ROW, 1), shifted(field[:reach], ROW, -1)
+
+
+def column_borders(field, up, down, reach):
     left, right = (
         jnp.concatenate([part[:, columns] for part in (up, field, down)])
         for columns in (slice(-reach, None), slice(0, reach))
@@ -393,7 +396,8 @@
         ],
         compiler_params=PARAMS,
     )(
-        core, in_hbm(features), *borders(features, reach), in_hbm(kernel), in_hbm(gain_row),
+        core, in_hbm(features),
+        *column_borders(features, *row_borders(features, reach), reach), in_hbm(kernel), in_hbm(gain_row),
         in_hbm(w_expand), in_hbm(w_reduce), in_hbm(scale_row), in_hbm(cotangent),
     )
 
@@ -426,23 +430,25 @@
         + [pl.BlockSpec((X, 2 * SMALL, channels), lambda i: (i, 0, 0))] * 2,
         out_specs=pl.BlockSpec((X, whole, channels), lambda i: (i, 0, 0)),
         out_shape=shape((places, whole, channels), bf16),
-        compiler_params=PARAMS,
+        compiler_params=GLUE_PARAMS,
     )(kept, came, small, small_came)
-    chip, dconv, came_z = lax.optimization_barrier((chip, dconv, came_z))
+    chip, dconv, came_z, rows_came = lax.optimization_barrier(
+        (chip, dconv, came_z, row_borders(dconv, reach))
+    )
     line = pl.pallas_call(
         join_kernel,
         name="join",
         in_specs=[SMEM] + [VMEM] * 2,
         out_specs=[VMEM] * Z,
         out_shape=[shape(kept_z.shape[1:], bf16)] * Z,
-        compiler_params=PARAMS,
+        compiler_params=GLUE_PARAMS,
     )(lax.axis_index("z").reshape(1), kept_z, came_z)
     line = [
         part if step == 0 else lax.ppermute(part, "z", [(i, (i + step) % Z) for i in range(Z)])
         for step, part in enumerate(line)
     ]
     chunks, edges, line = lax.optimization_barrier(
-        (exchanged(chip, ("y", "x")), borders(dconv, reach), line)
+        (exchanged(chip, ("y", "x")), column_borders(dconv, *rows_came, reach), line)
     )
     chunks = pl.pallas_call(
         plane_kernel,
@@ -451,7 +457,7 @@
         out_specs=VMEM,
         out_shape=shape((Z, 2 * each, channels), bf16),
         scratch_shapes=[pltpu.VMEM((whole, channels), f32)],
-        compiler_params=PARAMS,
+        compiler_params=GLUE_PARAMS,
     )(chunks)
     dexpand, half, chunks = pl.pallas_call(
         functools.partial(line_kernel, multiplier),
@@ -463,7 +469,7 @@
             shape((each, channels // 2), f32),
             shape((places, each, channels), bf16),
         ],
-        compiler_params=PARAMS,
+        compiler_params=GLUE_PARAMS,
     )(exchanged(chunks, "z"), *line)
     dreduce, dkernel, dgain, dscale = pl.pallas_call(
         functools.partial(last_kernel, multiplier),
@@ -472,7 +478,7 @@
         out_specs=[VMEM] * 4,
         out_shape=[shape((each, channels), f32), shape((side, side, channels), f32)]
         + [shape((1, channels), f32)] * 2,
-        compiler_params=PARAMS,
+        compiler_params=GLUE_PARAMS,
     )(exchanged(chunks, ("y", "x")), half)
     grad_features = pl.pallas_call(
         feature_kernel,
@@ -481,7 +487,7 @@
         out_specs=VMEM,
         out_shape=shape((height, width, channels), bf16),
         scratch_shapes=[pltpu.VMEM(padded_shape, f32)],
-        compiler_params=PARAMS,
+        compiler_params=GLUE_PARAMS,
     )(dconv, *edges, kernel, cotangent)
     return (
         grad_features,

time: 116 us -> 108 us (0.931)
  starting transfers between devices: 71.8 us -> 60.8 us
  waiting for transfers between devices: 9.86 us -> 12.1 us
    ppermute x8, starting transfers between devices: 35.6 us -> 25.1 us  [shifted(): return lax.ppermute(value, axes, pairs)]
    ppermute x7, waiting for transfers between devices: 0.02 us -> 6.15 us  [shards(): lax.ppermute(part, 'z', [(i, (i + step) % Z) for i in range(Z)])]
    ppermute x8, waiting for transfers between devices: 4.72 us -> 1.82 us  [shifted(): return lax.ppermute(value, axes, pairs)]
    ppermute x7, starting transfers between devices: 17.5 us -> 15.3 us  [shards(): lax.ppermute(part, 'z', [(i, (i + step) % Z) for i in range(Z)])]
    all_to_all x2, starting transfers between devices: 16.9 us -> 18.7 us  [exchanged(): return lax.all_to_all(chunks, axes, 0, 0, tiled=True)]
  transfers between devices with their start and end apart: 20 -> 20, of which waited for: 7 -> 5; matrix products, arithmetic and copies ran while one was open for 1% -> 1% of each run, Pallas kernels for 7% -> 7%
where the time goes in v5:
time: 108 us
  starting transfers between devices  60.8 us (56%)
  Pallas kernels  17.8 us (16%)
  blocking collectives  13.3 us (12%)
  waiting for transfers between devices  12.1 us (11%)
  local copies, waits for them, and re-layouts  2.6 us (2%)
    ppermute x8, starting transfers between devices, shifted(): return lax.ppermute(value, axes, pairs)  25.1 us
    all_to_all x2, starting transfers between devices, exchanged(): return lax.all_to_all(chunks, axes, 0, 0, tiled=True)  18.7 us
    ppermute x7, starting transfers between devices, shards(): lax.ppermute(part, 'z', [(i, (i + step) % Z) for i in range(Z)])  15.3 us
    all_to_all x1, blocking collectives, exchanged(): return lax.all_to_all(chunks, axes, 0, 0, tiled=True)  13.3 us
    pallas_call x1, Pallas kernels, shards(): pl.pallas_call(forward_kernel, name='forward', in_specs=[SMEM, HBM] + [VM...  8.35 us
    ppermute x7, waiting for transfers between devices, shards(): lax.ppermute(part, 'z', [(i, (i + step) % Z) for i in range(Z)])  6.15 us
    all_to_all x2, waiting for transfers between devices, exchanged(): return lax.all_to_all(chunks, axes, 0, 0, tiled=True)  4.12 us
    pallas_call x1, Pallas kernels, shards(): pl.pallas_call(functools.partial(backward_kernel, multiplier), name='back...  3.1 us
  transfers between devices with their start and end apart: 20, of which 5 were waited for; matrix products, arithmetic and copies ran while one was open for 1% of the time, Pallas kernels for 7%

profile of v5, /device:TPU:2, one launch (start us, length us, event | category | flops | bytes accessed | tf_op | source)
XLA Modules:
  0.0 107.7 jit_solution(16706258554294839839)
XLA Ops:
  0.6 1.0 fusion.3
  1.6 1.3 %collective-permute-start.1 = (bf16[3,32,512]{2,1,0:T(8,128)(2,1)S(1)}, bf16[3,32,512]{2,1,0:T(8,128)(2,1)S(1)}, u32[]{:S(2)}, u32[]{:S(2)}) collective-permute-start(bf16[3,32,512]{2,1,0:T(8,128)(2,1)S(1)} %get-tuple-element.100), channel_id=1, source_target_pairs={{32,0},{64,32},{96,64},{128,96},{160,128},{192,160},{224,192},{33,... | collective-permute-start | bytes 294920 | tf_op jit(solution)/shard_map/ppermute | solution.py:330
  2.9 3.0 %collective-permute-start = (bf16[3,32,512]{2,1,0:T(8,128)(2,1)S(1)}, bf16[3,32,512]{2,1,0:T(8,128)(2,1)S(1)}, u32[]{:S(2)}, u32[]{:S(2)}) collective-permute-start(bf16[3,32,512]{2,1,0:T(8,128)(2,1)S(1)} %get-tuple-element.101), channel_id=1, source_target_pairs={{0,32},{32,64},{64,96},{96,128},{128,160},{160,192},{192,224},{1,3... | collective-permute-start | bytes 294920 | tf_op jit(solution)/shard_map/ppermute | solution.py:330
  5.9 0.9 fusion.2
  7.0 3.8 %collective-permute-start.2 = (bf16[14,3,512]{2,1,0:T(4,128)(2,1)S(1)}, bf16[14,3,512]{2,1,0:T(4,128)(2,1)S(1)}, u32[]{:S(2)}, u32[]{:S(2)}) collective-permute-start(bf16[14,3,512]{2,1,0:T(4,128)(2,1)S(1)} %pad_maximum_fusion), channel_id=1, source_target_pairs={{0,1},{1,2},{2,3},{3,4},{4,5},{5,6},{6,7},{7,8},{8,9},{9,10},{10,1... | collective-permute-start | bytes 129032 | tf_op jit(solution)/shard_map/ppermute | solution.py:330
  10.8 5.8 %collective-permute-start.3 = (bf16[14,3,512]{2,1,0:T(4,128)(2,1)S(1)}, bf16[14,3,512]{2,1,0:T(4,128)(2,1)S(1)}, u32[]{:S(2)}, u32[]{:S(2)}) collective-permute-start(bf16[14,3,512]{2,1,0:T(4,128)(2,1)S(1)} %pad_maximum_fusion.1), channel_id=1, source_target_pairs={{1,0},{2,1},{3,2},{4,3},{5,4},{6,5},{7,6},{8,7},{9,8},{10,9},{11,1... | collective-permute-start | bytes 129032 | tf_op jit(solution)/shard_map/ppermute | solution.py:330
  16.8 1.6 %collective-permute-done.3.right = bf16[14,3,512]{2,1,0:T(4,128)(2,1)S(1)} collective-permute-done((bf16[14,3,512]{2,1,0:T(4,128)(2,1)S(1)}, bf16[14,3,512]{2,1,0:T(4,128)(2,1)S(1)}, u32[]{:S(2)}, u32[]{:S(2)}) %collective-permute-start.3) | collective-permute-done | bytes 43040 | tf_op jit(solution)/shard_map/ppermute | solution.py:330
  18.5 8.3 %forward.1 = (bf16[16,96,512]{2,1,0:T(8,128)(2,1)S(1)}, bf16[16,96,512]{2,1,0:T(8,128)(2,1)S(1)}, bf16[8,8,8,512]{3,2,1,0:T(8,128)(2,1)S(1)}, bf16[8,8,8,512]{3,...) custom-call(s32[1]{0:T(128)} %bitcast.core_ref, ...), custom_call_target="tpu_custom_call" | custom-call | tf_op jit(solution)/shard_map/forward/pallas_call | solution.py:368
  26.8 1.1 %collective-permute-start.4 = (bf16[16,96,512]{2,1,0:T(8,128)(2,1)S(1)}, bf16[16,96,512]{2,1,0:T(8,128)(2,1)S(1)}, u32[]{:S(2)}, u32[]{:S(2)}) collective-permute-start(bf16[16,96,512]{2,1,0:T(8,128)(2,1)S(1)} %get-tuple-element.51), channel_id=1, source_target_pairs={{0,32},{32,0},{1,33},{33,1},{2,34},{34,2},{3,35},{35,3},{4,36},{36... | collective-permute-start | bytes 4718600 | tf_op jit(solution)/shard_map/ppermute | solution.py:405
  28.0 3.1 %backward.1 = (bf16[8,32,512]{2,1,0:T(8,128)(2,1)S(1)}, bf16[16,8,512]{2,1,0:T(8,128)(2,1)S(1)}) custom-call(bf16[256,2048]{1,0:T(8,128)(2,1)S(1)} %get-tuple-element.52.dpre, bf16[512,2048]{1,0:T(8,128)(2,1)S(1)} %copy-done, f32[4,256,128]{2,1,0:T(8,128)S(1)} %get-tuple-element.53.xhat, f32[256,128]{1,0:T(8,128)S(1)} %get-tuple-element.54.rstd, ...), custom_call_target="tpu_custom_call" | custom-call | tf_op jit(solution)/shard_map/backward/pallas_call | solution.py:407
  31.1 0.5 collective-permute-start.5
  31.7 1.3 %collective-permute-start.8 = (bf16[3,32,512]{2,1,0:T(8,128)(2,1)S(1)}, bf16[3,32,512]{2,1,0:T(8,128)(2,1)S(1)}, u32[]{:S(2)}, u32[]{:S(2)}) collective-permute-start(bf16[3,32,512]{2,1,0:T(8,128)(2,1)S(1)} %get-tuple-element.96), channel_id=1, source_target_pairs={{32,0},{64,32},{96,64},{128,96},{160,128},{192,160},{224,192},{33,... | collective-permute-start | bytes 294920 | tf_op jit(solution)/shard_map/ppermute | solution.py:330
  33.0 3.0 %collective-permute-start.7 = (bf16[3,32,512]{2,1,0:T(8,128)(2,1)S(1)}, bf16[3,32,512]{2,1,0:T(8,128)(2,1)S(1)}, u32[]{:S(2)}, u32[]{:S(2)}) collective-permute-start(bf16[3,32,512]{2,1,0:T(8,128)(2,1)S(1)} %get-tuple-element.97), channel_id=1, source_target_pairs={{0,32},{32,64},{64,96},{96,128},{128,160},{160,192},{192,224},{1,3... | collective-permute-start | bytes 294920 | tf_op jit(solution)/shard_map/ppermute | solution.py:330
  36.0 1.9 %merge.1 = bf16[16,104,512]{2,1,0:T(8,128)(2,1)} custom-call(bf16[16,96,512]{2,1,0:T(8,128)(2,1)S(1)} %get-tuple-element.50.kept, bf16[16,96,512]{2,1,0:T(8,128)(2,1)S(1)} %collective-permute-done.4.came, bf16[16,8,512]{2,1,0:T(8,128)(2,1)S(1)} %get-tuple-element.57.small, bf16[16,8,512]{2,1,0:T(8,128)(2,1)S(1)} %collective-permute-done.5.small_came), custom_call_target="tpu_custom_call" | custom-call | tf_op jit(solution)/shard_map/merge/pallas_call | solution.py:425
  38.0 11.3 %all-to-all-start = ((bf16[16,104,512]{2,1,0:T(8,128)(2,1)}), bf16[16,104,512]{2,1,0:T(8,128)(2,1)S(1)}, u32[]{:S(2)}, u32[]{:S(2)}) async-start(bf16[16,104,512]{2,1,0:T(8,128)(2,1)} %merge.1), calls=%async_computation | async-start | bytes 3407872 | tf_op jit(solution)/shard_map/all_to_all | solution.py:346
  49.4 2.2 %collective-permute-start.9 = (bf16[14,3,512]{2,1,0:T(4,128)(2,1)S(1)}, bf16[14,3,512]{2,1,0:T(4,128)(2,1)S(1)}, u32[]{:S(2)}, u32[]{:S(2)}) collective-permute-start(bf16[14,3,512]{2,1,0:T(4,128)(2,1)S(1)} %pad_maximum_fusion.2), channel_id=1, source_target_pairs={{0,1},{1,2},{2,3},{3,4},{4,5},{5,6},{6,7},{7,8},{8,9},{9,10},{10,1... | collective-permute-start | bytes 129032 | tf_op jit(solution)/shard_map/ppermute | solution.py:330
  51.8 3.1 %collective-permute-start.11 = (bf16[8,8,512]{2,1,0:T(8,128)(2,1)S(1)}, bf16[8,8,512]{2,1,0:T(8,128)(2,1)S(1)}, u32[]{:S(2)}, u32[]{:S(2)}) collective-permute-start(bf16[8,8,512]{2,1,0:T(8,128)(2,1)S(1)} %get-tuple-element.67), channel_id=1, source_target_pairs={{0,1},{1,2},{2,3},{3,4},{4,5},{5,6},{6,7},{7,0},{8,9},{9,10},{10,1... | collective-permute-start | bytes 196616 | tf_op jit(solution)/shard_map/ppermute | solution.py:447
  54.9 2.7 %collective-permute-start.12 = (bf16[8,8,512]{2,1,0:T(8,128)(2,1)S(1)}, bf16[8,8,512]{2,1,0:T(8,128)(2,1)S(1)}, u32[]{:S(2)}, u32[]{:S(2)}) collective-permute-start(bf16[8,8,512]{2,1,0:T(8,128)(2,1)S(1)} %get-tuple-element.68), channel_id=1, source_target_pairs={{0,2},{1,3},{2,4},{3,5},{4,6},{5,7},{6,0},{7,1},{8,10},{9,11},{10,... | collective-permute-start | bytes 196616 | tf_op jit(solution)/shard_map/ppermute | solution.py:447
  57.7 4.6 %collective-permute-start.10 = (bf16[14,3,512]{2,1,0:T(4,128)(2,1)S(1)}, bf16[14,3,512]{2,1,0:T(4,128)(2,1)S(1)}, u32[]{:S(2)}, u32[]{:S(2)}) collective-permute-start(bf16[14,3,512]{2,1,0:T(4,128)(2,1)S(1)} %pad_maximum_fusion.3), channel_id=1, source_target_pairs={{1,0},{2,1},{3,2},{4,3},{5,4},{6,5},{7,6},{8,7},{9,8},{10,9},{11,1... | collective-permute-start | bytes 129032 | tf_op jit(solution)/shard_map/ppermute | solution.py:330
  62.4 0.6 copy-done.3
  63.1 3.7 %collective-permute-start.14 = (bf16[8,8,512]{2,1,0:T(8,128)(2,1)S(1)}, bf16[8,8,512]{2,1,0:T(8,128)(2,1)S(1)}, u32[]{:S(2)}, u32[]{:S(2)}) collective-permute-start(bf16[8,8,512]{2,1,0:T(8,128)(2,1)S(1)} %get-tuple-element.70), channel_id=1, source_target_pairs={{0,4},{1,5},{2,6},{3,7},{4,0},{5,1},{6,2},{7,3},{8,12},{9,13},{10,... | collective-permute-start | bytes 196616 | tf_op jit(solution)/shard_map/ppermute | solution.py:447
  66.7 4.0 %collective-permute-start.15 = (bf16[8,8,512]{2,1,0:T(8,128)(2,1)S(1)}, bf16[8,8,512]{2,1,0:T(8,128)(2,1)S(1)}, u32[]{:S(2)}, u32[]{:S(2)}) collective-permute-start(bf16[8,8,512]{2,1,0:T(8,128)(2,1)S(1)} %get-tuple-element.71), channel_id=1, source_target_pairs={{0,5},{1,6},{2,7},{3,0},{4,1},{5,2},{6,3},{7,4},{8,13},{9,14},{10,... | collective-permute-start | bytes 196616 | tf_op jit(solution)/shard_map/ppermute | solution.py:447
  71.1 1.3 %collective-permute-start.17 = (bf16[8,8,512]{2,1,0:T(8,128)(2,1)S(1)}, bf16[8,8,512]{2,1,0:T(8,128)(2,1)S(1)}, u32[]{:S(2)}, u32[]{:S(2)}) collective-permute-start(bf16[8,8,512]{2,1,0:T(8,128)(2,1)S(1)} %get-tuple-element.73), channel_id=1, source_target_pairs={{0,7},{1,0},{2,1},{3,2},{4,3},{5,4},{6,5},{7,6},{8,15},{9,8},{10,9... | collective-permute-start | bytes 196616 | tf_op jit(solution)/shard_map/ppermute | solution.py:447
  72.4 2.0 %collective-permute-done.15.refs_5_ = bf16[8,8,512]{2,1,0:T(8,128)(2,1)S(1)} collective-permute-done((bf16[8,8,512]{2,1,0:T(8,128)(2,1)S(1)}, bf16[8,8,512]{2,1,0:T(8,128)(2,1)S(1)}, u32[]{:S(2)}, u32[]{:S(2)}) %collective-permute-start.15) | collective-permute-done | bytes 65568 | tf_op jit(solution)/shard_map/ppermute | solution.py:447
  74.4 4.1 %collective-permute-done.16.refs_6_ = bf16[8,8,512]{2,1,0:T(8,128)(2,1)S(1)} collective-permute-done((bf16[8,8,512]{2,1,0:T(8,128)(2,1)S(1)}, bf16[8,8,512]{2,1,0:T(8,128)(2,1)S(1)}, u32[]{:S(2)}, u32[]{:S(2)}) %collective-permute-start.16) | collective-permute-done | bytes 65568 | tf_op jit(solution)/shard_map/ppermute | solution.py:447
  78.6 0.4 plane.1
  78.9 13.3 %all_to_all.15.chunks = bf16[8,16,512]{2,1,0:T(8,128)(2,1)S(1)} all-to-all(bf16[8,16,512]{2,1,0:T(8,128)(2,1)S(1)} %plane.1), channel_id=1, replica_groups=mesh['y'=4,'core'=2,'x'=4,'z'=8] {'z'}, dimensions={0} | all-to-all | bytes 262144 | tf_op jit(solution)/shard_map/all_to_all | solution.py:346
  92.2 0.7 line.1
  93.0 7.4 %all-to-all-start.2 = ((bf16[16,8,512]{2,1,0:T(8,128)(2,1)}), bf16[16,8,512]{2,1,0:T(8,128)(2,1)S(1)}, u32[]{:S(2)}, u32[]{:S(2)}) async-start(bf16[16,8,512]{2,1,0:T(8,128)(2,1)} %get-tuple-element.87), calls=%async_computation.2 | async-start | bytes 262144 | tf_op jit(solution)/shard_map/all_to_all | solution.py:346
  100.4 2.5 %features.1 = bf16[8,32,512]{2,1,0:T(8,128)(2,1)} custom-call(bf16[8,32,512]{2,1,0:T(8,128)(2,1)S(1)} %get-tuple-element.60.field, bf16[3,32,512]{2,1,0:T(8,128)(2,1)S(1)} %collective-permute-done.7.up, bf16[3,32,512]{2,1,0:T(8,128)(2,1)S(1)} %collective-permute-done.8.down, bf16[14,3,512]{2,1,0:T(4,128)(2,1)S(1)} %copy-done.4, ...), custom_call_target="tpu_custom_call" | custom-call | tf_op jit(solution)/shard_map/features/pallas_call | solution.py:483
  102.9 4.1 %all-to-all-done.2.chunks = bf16[16,8,512]{2,1,0:T(8,128)(2,1)S(1)} async-done(((bf16[16,8,512]{2,1,0:T(8,128)(2,1)}), bf16[16,8,512]{2,1,0:T(8,128)(2,1)S(1)}, u32[]{:S(2)}, u32[]{:S(2)}) %all-to-all-start.2) | async-done | bytes 131104 | tf_op jit(solution)/shard_map/all_to_all | solution.py:346
  107.0 0.7 last.1
  (38 shorter events, 1.2 us)
Async XLA Ops:
  1.6 5.3 %collective-permute-start.1 = (bf16[3,32,512]{2,1,0:T(8,128)(2,1)S(1)}, bf16[3,32,512]{2,1,0:T(8,128)(2,1)S(1)}, u32[]{:S(2)}, u32[]{:S(2)}) collective-permute-start(bf16[3,32,512]{2,1,0:T(8,128)(2,1)S(1)} %get-tuple-element.100), channel_id=1, source_target_pairs={{32,0},{64,32},{96,64},{128,96},{160,128},{192,160},{224,192},{33,... | collective-permute-start | bytes 294920 | tf_op jit(solution)/shard_map/ppermute | solution.py:330
  2.9 4.0 %collective-permute-start = (bf16[3,32,512]{2,1,0:T(8,128)(2,1)S(1)}, bf16[3,32,512]{2,1,0:T(8,128)(2,1)S(1)}, u32[]{:S(2)}, u32[]{:S(2)}) collective-permute-start(bf16[3,32,512]{2,1,0:T(8,128)(2,1)S(1)} %get-tuple-element.101), channel_id=1, source_target_pairs={{0,32},{32,64},{64,96},{96,128},{128,160},{160,192},{192,224},{1,3... | collective-permute-start | bytes 294920 | tf_op jit(solution)/shard_map/ppermute | solution.py:330
  7.0 9.9 %collective-permute-start.2 = (bf16[14,3,512]{2,1,0:T(4,128)(2,1)S(1)}, bf16[14,3,512]{2,1,0:T(4,128)(2,1)S(1)}, u32[]{:S(2)}, u32[]{:S(2)}) collective-permute-start(bf16[14,3,512]{2,1,0:T(4,128)(2,1)S(1)} %pad_maximum_fusion), channel_id=1, source_target_pairs={{0,1},{1,2},{2,3},{3,4},{4,5},{5,6},{6,7},{7,8},{8,9},{9,10},{10,1... | collective-permute-start | bytes 129032 | tf_op jit(solution)/shard_map/ppermute | solution.py:330
  10.8 7.6 %collective-permute-start.3 = (bf16[14,3,512]{2,1,0:T(4,128)(2,1)S(1)}, bf16[14,3,512]{2,1,0:T(4,128)(2,1)S(1)}, u32[]{:S(2)}, u32[]{:S(2)}) collective-permute-start(bf16[14,3,512]{2,1,0:T(4,128)(2,1)S(1)} %pad_maximum_fusion.1), channel_id=1, source_target_pairs={{1,0},{2,1},{3,2},{4,3},{5,4},{6,5},{7,6},{8,7},{9,8},{10,9},{11,1... | collective-permute-start | bytes 129032 | tf_op jit(solution)/shard_map/ppermute | solution.py:330
  18.5 9.5 %copy-start = (bf16[512,2048]{1,0:T(8,128)(2,1)S(1)}, bf16[512,2048]{1,0:T(8,128)(2,1)}, u32[]{:S(2)}) copy-start(bf16[512,2048]{1,0:T(8,128)(2,1)} %expand.1) | copy-start | bytes 6291460
  26.8 9.2 %collective-permute-start.4 = (bf16[16,96,512]{2,1,0:T(8,128)(2,1)S(1)}, bf16[16,96,512]{2,1,0:T(8,128)(2,1)S(1)}, u32[]{:S(2)}, u32[]{:S(2)}) collective-permute-start(bf16[16,96,512]{2,1,0:T(8,128)(2,1)S(1)} %get-tuple-element.51), channel_id=1, source_target_pairs={{0,32},{32,0},{1,33},{33,1},{2,34},{34,2},{3,35},{35,3},{4,36},{36... | collective-permute-start | bytes 4718600 | tf_op jit(solution)/shard_map/ppermute | solution.py:405
  27.9 10.0 %collective-permute-start.6 = (bf16[8,8,8,512]{3,2,1,0:T(8,128)(2,1)S(1)}, bf16[8,8,8,512]{3,2,1,0:T(8,128)(2,1)S(1)}, u32[]{:S(2)}, u32[]{:S(2)}) collective-permute-start(bf16[8,8,8,512]{3,2,1,0:T(8,128)(2,1)S(1)} %get-tuple-element.59), channel_id=1, source_target_pairs={{0,32},{32,0},{1,33},{33,1},{2,34},{34,2},{3,35},{35,3},{4,36},{36... | collective-permute-start | bytes 1572872 | tf_op jit(solution)/shard_map/ppermute | solution.py:406
  31.1 4.9 %collective-permute-start.5 = (bf16[16,8,512]{2,1,0:T(8,128)(2,1)S(1)}, bf16[16,8,512]{2,1,0:T(8,128)(2,1)S(1)}, u32[]{:S(2)}, u32[]{:S(2)}) collective-permute-start(bf16[16,8,512]{2,1,0:T(8,128)(2,1)S(1)} %get-tuple-element.57.small), channel_id=1, source_target_pairs={{0,32},{32,0},{1,33},{33,1},{2,34},{34,2},{3,35},{35,3},{4,36},{36... | collective-permute-start | bytes 393224 | tf_op jit(solution)/shard_map/ppermute | solution.py:423
  31.7 6.3 %collective-permute-start.8 = (bf16[3,32,512]{2,1,0:T(8,128)(2,1)S(1)}, bf16[3,32,512]{2,1,0:T(8,128)(2,1)S(1)}, u32[]{:S(2)}, u32[]{:S(2)}) collective-permute-start(bf16[3,32,512]{2,1,0:T(8,128)(2,1)S(1)} %get-tuple-element.96), channel_id=1, source_target_pairs={{32,0},{64,32},{96,64},{128,96},{160,128},{192,160},{224,192},{33,... | collective-permute-start | bytes 294920 | tf_op jit(solution)/shard_map/ppermute | solution.py:330
  33.0 5.0 %collective-permute-start.7 = (bf16[3,32,512]{2,1,0:T(8,128)(2,1)S(1)}, bf16[3,32,512]{2,1,0:T(8,128)(2,1)S(1)}, u32[]{:S(2)}, u32[]{:S(2)}) collective-permute-start(bf16[3,32,512]{2,1,0:T(8,128)(2,1)S(1)} %get-tuple-element.97), channel_id=1, source_target_pairs={{0,32},{32,64},{64,96},{96,128},{128,160},{160,192},{192,224},{1,3... | collective-permute-start | bytes 294920 | tf_op jit(solution)/shard_map/ppermute | solution.py:330
  38.0 40.6 %all-to-all-start = ((bf16[16,104,512]{2,1,0:T(8,128)(2,1)}), bf16[16,104,512]{2,1,0:T(8,128)(2,1)S(1)}, u32[]{:S(2)}, u32[]{:S(2)}) async-start(bf16[16,104,512]{2,1,0:T(8,128)(2,1)} %merge.1), calls=%async_computation | async-start | bytes 3407872 | tf_op jit(solution)/shard_map/all_to_all | solution.py:346
  49.4 13.1 %collective-permute-start.9 = (bf16[14,3,512]{2,1,0:T(4,128)(2,1)S(1)}, bf16[14,3,512]{2,1,0:T(4,128)(2,1)S(1)}, u32[]{:S(2)}, u32[]{:S(2)}) collective-permute-start(bf16[14,3,512]{2,1,0:T(4,128)(2,1)S(1)} %pad_maximum_fusion.2), channel_id=1, source_target_pairs={{0,1},{1,2},{2,3},{3,4},{4,5},{5,6},{6,7},{7,8},{8,9},{9,10},{10,1... | collective-permute-start | bytes 129032 | tf_op jit(solution)/shard_map/ppermute | solution.py:330
  51.7 48.6 %copy-start.1 = (bf16[8,32,512]{2,1,0:T(8,128)(2,1)S(1)}, bf16[8,32,512]{2,1,0:T(8,128)(2,1)}, u32[]{:S(2)}) copy-start(bf16[8,32,512]{2,1,0:T(8,128)(2,1)} %cotangent.1) | copy-start | bytes 786436
  51.8 48.6 %copy-start.2 = (f32[7,7,512]{2,1,0:T(8,128)S(1)}, f32[7,7,512]{2,1,0:T(8,128)}, u32[]{:S(2)}) copy-start(f32[7,7,512]{2,1,0:T(8,128)} %taps.1) | copy-start | bytes 301060
  51.8 19.0 %collective-permute-start.11 = (bf16[8,8,512]{2,1,0:T(8,128)(2,1)S(1)}, bf16[8,8,512]{2,1,0:T(8,128)(2,1)S(1)}, u32[]{:S(2)}, u32[]{:S(2)}) collective-permute-start(bf16[8,8,512]{2,1,0:T(8,128)(2,1)S(1)} %get-tuple-element.67), channel_id=1, source_target_pairs={{0,1},{1,2},{2,3},{3,4},{4,5},{5,6},{6,7},{7,0},{8,9},{9,10},{10,1... | collective-permute-start | bytes 196616 | tf_op jit(solution)/shard_map/ppermute | solution.py:447
  54.9 16.2 %collective-permute-start.12 = (bf16[8,8,512]{2,1,0:T(8,128)(2,1)S(1)}, bf16[8,8,512]{2,1,0:T(8,128)(2,1)S(1)}, u32[]{:S(2)}, u32[]{:S(2)}) collective-permute-start(bf16[8,8,512]{2,1,0:T(8,128)(2,1)S(1)} %get-tuple-element.68), channel_id=1, source_target_pairs={{0,2},{1,3},{2,4},{3,5},{4,6},{5,7},{6,0},{7,1},{8,10},{9,11},{10,... | collective-permute-start | bytes 196616 | tf_op jit(solution)/shard_map/ppermute | solution.py:447
  57.7 9.0 %collective-permute-start.10 = (bf16[14,3,512]{2,1,0:T(4,128)(2,1)S(1)}, bf16[14,3,512]{2,1,0:T(4,128)(2,1)S(1)}, u32[]{:S(2)}, u32[]{:S(2)}) collective-permute-start(bf16[14,3,512]{2,1,0:T(4,128)(2,1)S(1)} %pad_maximum_fusion.3), channel_id=1, source_target_pairs={{1,0},{2,1},{3,2},{4,3},{5,4},{6,5},{7,6},{8,7},{9,8},{10,9},{11,1... | collective-permute-start | bytes 129032 | tf_op jit(solution)/shard_map/ppermute | solution.py:330
  62.3 10.1 %collective-permute-start.13 = (bf16[8,8,512]{2,1,0:T(8,128)(2,1)S(1)}, bf16[8,8,512]{2,1,0:T(8,128)(2,1)S(1)}, u32[]{:S(2)}, u32[]{:S(2)}) collective-permute-start(bf16[8,8,512]{2,1,0:T(8,128)(2,1)S(1)} %get-tuple-element.69), channel_id=1, source_target_pairs={{0,3},{1,4},{2,5},{3,6},{4,7},{5,0},{6,1},{7,2},{8,11},{9,12},{10,... | collective-permute-start | bytes 196616 | tf_op jit(solution)/shard_map/ppermute | solution.py:447
  62.4 0.6 copy-start.3
  63.1 37.3 %copy-start.4 = (bf16[14,3,512]{2,1,0:T(4,128)(2,1)S(1)}, bf16[14,3,512]{2,1,0:T(4,128)(2,1)}, u32[]{:S(2)}) copy-start(bf16[14,3,512]{2,1,0:T(4,128)(2,1)} %copy-done.3) | copy-start | bytes 129028
  63.1 9.4 %collective-permute-start.14 = (bf16[8,8,512]{2,1,0:T(8,128)(2,1)S(1)}, bf16[8,8,512]{2,1,0:T(8,128)(2,1)S(1)}, u32[]{:S(2)}, u32[]{:S(2)}) collective-permute-start(bf16[8,8,512]{2,1,0:T(8,128)(2,1)S(1)} %get-tuple-element.70), channel_id=1, source_target_pairs={{0,4},{1,5},{2,6},{3,7},{4,0},{5,1},{6,2},{7,3},{8,12},{9,13},{10,... | collective-permute-start | bytes 196616 | tf_op jit(solution)/shard_map/ppermute | solution.py:447
  66.7 7.7 %collective-permute-start.15 = (bf16[8,8,512]{2,1,0:T(8,128)(2,1)S(1)}, bf16[8,8,512]{2,1,0:T(8,128)(2,1)S(1)}, u32[]{:S(2)}, u32[]{:S(2)}) collective-permute-start(bf16[8,8,512]{2,1,0:T(8,128)(2,1)S(1)} %get-tuple-element.71), channel_id=1, source_target_pairs={{0,5},{1,6},{2,7},{3,0},{4,1},{5,2},{6,3},{7,4},{8,13},{9,14},{10,... | collective-permute-start | bytes 196616 | tf_op jit(solution)/shard_map/ppermute | solution.py:447
  70.8 7.8 %collective-permute-start.16 = (bf16[8,8,512]{2,1,0:T(8,128)(2,1)S(1)}, bf16[8,8,512]{2,1,0:T(8,128)(2,1)S(1)}, u32[]{:S(2)}, u32[]{:S(2)}) collective-permute-start(bf16[8,8,512]{2,1,0:T(8,128)(2,1)S(1)} %get-tuple-element.72), channel_id=1, source_target_pairs={{0,6},{1,7},{2,0},{3,1},{4,2},{5,3},{6,4},{7,5},{8,14},{9,15},{10,... | collective-permute-start | bytes 196616 | tf_op jit(solution)/shard_map/ppermute | solution.py:447
  71.1 7.4 %collective-permute-start.17 = (bf16[8,8,512]{2,1,0:T(8,128)(2,1)S(1)}, bf16[8,8,512]{2,1,0:T(8,128)(2,1)S(1)}, u32[]{:S(2)}, u32[]{:S(2)}) collective-permute-start(bf16[8,8,512]{2,1,0:T(8,128)(2,1)S(1)} %get-tuple-element.73), channel_id=1, source_target_pairs={{0,7},{1,0},{2,1},{3,2},{4,3},{5,4},{6,5},{7,6},{8,15},{9,8},{10,9... | collective-permute-start | bytes 196616 | tf_op jit(solution)/shard_map/ppermute | solution.py:447
  93.0 14.0 %all-to-all-start.2 = ((bf16[16,8,512]{2,1,0:T(8,128)(2,1)}), bf16[16,8,512]{2,1,0:T(8,128)(2,1)S(1)}, u32[]{:S(2)}, u32[]{:S(2)}) async-start(bf16[16,8,512]{2,1,0:T(8,128)(2,1)} %get-tuple-element.87), calls=%async_computation.2 | async-start | bytes 262144 | tf_op jit(solution)/shard_map/all_to_all | solution.py:346

commit v6 on v5

--- a/solution.py
+++ b/solution.py
@@ -26,14 +26,19 @@
     return lax.dot_general(left, right, dims, preferred_element_type=jnp.float32)
 
 
-def fill(padded, field, up, down, left, right, reach):
+def fill_own(padded, field, up, down, reach):
     height, width, channels = field.shape
+    own = pl.ds(LEFT, width)
     for block in range(channels // LANES):
         lanes = pl.ds(block * LANES, LANES)
-        own = pl.ds(LEFT, width)
         padded[block, pl.ds(0, reach), own, :] = up[:, :, lanes].astype(jnp.float32)
         padded[block, pl.ds(reach, height), own, :] = field[:, :, lanes].astype(jnp.float32)
         padded[block, pl.ds(reach + height, reach), own, :] = down[:, :, lanes].astype(jnp.float32)
+
+
+def fill_sides(padded, left, right, width, reach):
+    for block in range(padded.shape[0]):
+        lanes = pl.ds(block * LANES, LANES)
         padded[block, :, pl.ds(LEFT - reach, reach), :] = left[:, :, lanes].astype(jnp.float32)
         padded[block, :, pl.ds(LEFT + width, reach), :] = right[:, :, lanes].astype(jnp.float32)
 
@@ -56,14 +61,22 @@
     return totals
 
 
-def forward_kernel(
-    core_ref, field_h, up, down, left, right, taps_h, gain_h, expand_h, reduce_h, scale_h,
-    cotangent_h,
-    sent, kept, sent_z, kept_z, dpre_out, xhat_out, rstd_out, padded, rows_out,
-    conv, normed, dbranch, turned, chosen, field, taps, gain, expand, reduce, scale, cotangent,
-    sems,
+def conv_columns(conv, padded, taps, height, width, starts):
+    def conv_block(block, _):
+        for first_col in starts:
+            totals = depthwise(padded, taps, block, first_col, height, taps.shape[0], False)
+            for row, total in enumerate(totals):
+                conv[block, pl.ds(row * width + first_col, 8), :] = total
+        return 0
+
+    lax.fori_loop(0, padded.shape[0], conv_block, 0)
+
+
+def prepare_kernel(
+    field_h, up, down, taps_h, gain_h, scale_h, cotangent_h, expand_h, reduce_h,
+    padded, conv, dbranch, dact, taps, rows_out, expand, reduce,
+    field, gain, scale, cotangent, sems,
 ):
-    core = core_ref[0]
     copies = [
         pltpu.make_async_copy(source, target, sems.at[i])
         for i, (source, target) in enumerate(
@@ -73,8 +86,8 @@
                 (gain_h, gain),
                 (scale_h, scale),
                 (cotangent_h, cotangent),
+                (reduce_h, reduce),
                 (expand_h, expand),
-                (reduce_h, reduce),
             )
         )
     ]
@@ -83,21 +96,39 @@
     for copy in copies[:2]:
         copy.wait()
     height, width, channels = field.shape
-    blocks = channels // LANES
-    side = 7
-    fill(padded, field, up, down, left, right, side // 2)
-
-    def conv_block(block, _):
-        for first_col in range(0, width, 8):
-            for row, total in enumerate(
-                depthwise(padded, taps, block, first_col, height, side, False)
-            ):
-                conv[block, pl.ds(row * width + first_col, 8), :] = total
+    fill_own(padded, field, up, down, taps.shape[0] // 2)
+    conv_columns(conv, padded, taps, height, width, range(8, width - 8, 8))
+    for copy in copies[2:]:
+        copy.wait()
+    rows_out[pl.ds(0, 8), :] = jnp.broadcast_to(gain[...], (8, channels))
+    rows_out[pl.ds(8, 8), :] = jnp.broadcast_to(scale[...], (8, channels))
+    for row in range(height):
+        value = cotangent[row].astype(jnp.float32) * scale[...]
+        dbranch[pl.ds(row * width, width), :] = value.astype(jnp.bfloat16)
+    step = 2 * LANES
+
+    def hidden_block(chunk, _):
+        hidden = pl.ds(pl.multiple_of(chunk * step, step), step)
+        dact[:, hidden] = product(dbranch[...], reduce[hidden, :], NT)
         return 0
 
-    lax.fori_loop(0, blocks, conv_block, 0)
-    for copy in copies[2:5]:
-        copy.wait()
+    lax.fori_loop(0, reduce.shape[0] // step, hidden_block, 0)
+
+
+def forward_kernel(
+    core_ref, left, right, padded_in, conv, dbranch, dact, taps, rows_in, expand, reduce,
+    sent, kept, sent_z, kept_z, dpre_out, xhat_out, rstd_out, padded, dscale_out,
+    normed, turned, chosen,
+):
+    core = core_ref[0]
+    del padded_in
+    blocks = padded.shape[0]
+    side = taps.shape[0]
+    height = padded.shape[1] - side + 1
+    width = conv.shape[1] // height
+    channels = blocks * LANES
+    fill_sides(padded, left, right, width, side // 2)
+    conv_columns(conv, padded, taps, height, width, (0, width - 8))
     for row in range(height):
         pixels = pl.ds(row * width, width)
         values = [conv[block, pixels, :] for block in range(blocks)]
@@ -110,8 +141,7 @@
             lanes = pl.ds(block * LANES, LANES)
             xhat = value * rstd
             xhat_out[block, pixels, :] = xhat
-            normed[pixels, lanes] = (xhat * gain[:, lanes]).astype(jnp.bfloat16)
-        dbranch[pixels, :] = (cotangent[row].astype(jnp.float32) * scale[...]).astype(jnp.bfloat16)
+            normed[pixels, lanes] = (xhat * rows_in[pl.ds(0, 1), lanes]).astype(jnp.bfloat16)
     turned[...] = normed[...].T
     part = channels // (Y * CORE)
     for y in range(Y):
@@ -120,11 +150,7 @@
             chosen[pl.ds((own * Y + y) * part, part), :] = turned[
                 pl.ds(pl.multiple_of((y * CORE + owner) * part, part), part), :
             ]
-    rows_out[pl.ds(0, 8), :] = jnp.zeros((8, channels), jnp.float32)
-    rows_out[pl.ds(8, 8), :] = jnp.broadcast_to(gain[...], (8, channels))
-    rows_out[pl.ds(16, 8), :] = jnp.broadcast_to(scale[...], (8, channels))
-    for copy in copies[5:]:
-        copy.wait()
+    dscale_out[...] = jnp.zeros_like(dscale_out)
     step = reduce.shape[0] // (Y * CORE)
     per_z = step // (X * Z)
     part_x = part // X
@@ -138,15 +164,14 @@
             chunk = y * CORE + owner
             hidden = pl.ds(pl.multiple_of(chunk * step, step), step)
             pre = product(normed[...], expand[:, hidden], NN)
-            dact = product(dbranch[...], reduce[hidden, :], NT)
             half = 0.5 * (1.0 + lax.erf(pre * INV_ROOT_TWO))
             slope = half + pre * jnp.exp(-0.5 * pre * pre) * INV_ROOT_TWO_PI
             act = (pre * half).astype(jnp.bfloat16)
-            dpre = (dact * slope).astype(jnp.bfloat16)
+            dpre = (dact[:, hidden] * slope).astype(jnp.bfloat16)
             dpre_out[:, hidden] = dpre
             share = product(act, dbranch[...], TN)
             weighed = share * reduce[hidden, :].astype(jnp.float32)
-            rows_out[pl.ds(0, 8), :] += jnp.sum(weighed.reshape(step // 8, 8, channels), axis=0)
+            dscale_out[...] += jnp.sum(weighed.reshape(step // 8, 8, channels), axis=0)
             share = share.astype(jnp.bfloat16)
             for place in range(X * Z):
                 x, z = place // Z, place % Z
@@ -170,7 +195,7 @@
 
 
 def backward_kernel(
-    multiplier, dpre, expand, xhat, rstd, padded, rows, dconv_out, out, dconv, small
+    multiplier, dpre, expand, xhat, rstd, padded, rows, dscale, dconv_out, out, dconv, small
 ):
     height, width, channels = dconv_out.shape
     blocks = channels // LANES
@@ -184,7 +209,7 @@
         grads = [dconv[block, pixels, :] for block in range(blocks)]
         hats = [xhat[block, pixels, :] for block in range(blocks)]
         sums = [total + grad * hat for total, grad, hat in zip(sums, grads, hats)]
-        grads = [grad * rows[pl.ds(8, 1), pl.ds(block * LANES, LANES)] for block, grad in enumerate(grads)]
+        grads = [grad * rows[pl.ds(0, 1), pl.ds(block * LANES, LANES)] for block, grad in enumerate(grads)]
         mean = jnp.sum(sum(grads), axis=-1, keepdims=True) / channels
         slant = sum(grad * hat for grad, hat in zip(grads, hats))
         slant = jnp.sum(slant, axis=-1, keepdims=True) / channels
@@ -199,8 +224,8 @@
         lanes = pl.ds(block * LANES, LANES)
         total = jnp.sum(sums[block], axis=0, keepdims=True)
         small[pl.ds(taps, 1), lanes] = total * multiplier
-        total = jnp.sum(rows[pl.ds(0, 8), lanes], axis=0, keepdims=True)
-        small[pl.ds(taps + 1, 1), lanes] = total / rows[pl.ds(16, 1), lanes] * multiplier
+        total = jnp.sum(dscale[:, lanes], axis=0, keepdims=True)
+        small[pl.ds(taps + 1, 1), lanes] = total / rows[pl.ds(8, 1), lanes] * multiplier
 
     def tap_block(block, _):
         lanes = pl.ds(pl.multiple_of(block * LANES, LANES), LANES)
@@ -229,7 +254,8 @@
 def feature_kernel(field, up, down, left, right, taps, cotangent, out, padded):
     height, width, channels = field.shape
     side = 7
-    fill(padded, field, up, down, left, right, side // 2)
+    fill_own(padded, field, up, down, side // 2)
+    fill_sides(padded, left, right, width, side // 2)
     for block in range(channels // LANES):
         lanes = pl.ds(block * LANES, LANES)
         for first_col in range(0, width, 8):
@@ -365,10 +391,39 @@
 
     each = rows // Z
     top = rows // 2
-    sent, kept, sent_z, kept_z, dpre, xhat, rstd, padded, row_sums = pl.pallas_call(
+    up, down = row_borders(features, reach)
+    left, right = column_borders(features, up, down, reach)[2:]
+    padded, conv, dbranch, dact, taps, params, expand, reduce = pl.pallas_call(
+        prepare_kernel,
+        name="prepare",
+        in_specs=[HBM] + [VMEM] * 2 + [HBM] * 6,
+        out_specs=[VMEM] * 8,
+        out_shape=[
+            shape(padded_shape, f32),
+            shape((blocks, pixels, LANES), f32),
+            shape((pixels, channels), bf16),
+            shape((pixels, hidden), f32),
+            shape(kernel.shape, f32),
+            shape((16, channels), f32),
+            shape(w_expand.shape, bf16),
+            shape(w_reduce.shape, bf16),
+        ],
+        scratch_shapes=[
+            pltpu.VMEM(features.shape, bf16),
+            pltpu.VMEM((1, channels), f32),
+            pltpu.VMEM((1, channels), f32),
+            pltpu.VMEM(cotangent.shape, bf16),
+            pltpu.SemaphoreType.DMA((7,)),
+        ],
+        compiler_params=PARAMS,
+    )(
+        in_hbm(features), up, down, in_hbm(kernel), in_hbm(gain_row), in_hbm(scale_row),
+        in_hbm(cotangent), in_hbm(w_expand), in_hbm(w_reduce),
+    )
+    sent, kept, sent_z, kept_z, dpre, xhat, rstd, padded, dscale = pl.pallas_call(
         forward_kernel,
         name="forward",
-        in_specs=[SMEM, HBM] + [VMEM] * 4 + [HBM] * 6,
+        in_specs=[SMEM] + [VMEM] * 10,
         out_specs=[VMEM] * 9,
         out_shape=[shape((places, top + rows, channels), bf16)] * 2
         + [shape((Z, places // 2, each, channels), bf16)] * 2
@@ -377,29 +432,16 @@
             shape((blocks, pixels, LANES), f32),
             shape((pixels, LANES), f32),
             shape(padded_shape, f32),
-            shape((24, channels), f32),
+            shape((8, channels), f32),
         ],
         scratch_shapes=[
-            pltpu.VMEM((blocks, pixels, LANES), f32),
-            pltpu.VMEM((pixels, channels), bf16),
             pltpu.VMEM((pixels, channels), bf16),
             pltpu.VMEM((channels, pixels), bf16),
             pltpu.VMEM((channels, pixels), bf16),
-            pltpu.VMEM(features.shape, bf16),
-            pltpu.VMEM(kernel.shape, f32),
-            pltpu.VMEM((1, channels), f32),
-            pltpu.VMEM((channels, hidden), bf16),
-            pltpu.VMEM((hidden, channels), bf16),
-            pltpu.VMEM((1, channels), f32),
-            pltpu.VMEM(cotangent.shape, bf16),
-            pltpu.SemaphoreType.DMA((7,)),
-        ],
+        ],
+        input_output_aliases={3: 7},
         compiler_params=PARAMS,
-    )(
-        core, in_hbm(features),
-        *column_borders(features, *row_borders(features, reach), reach), in_hbm(kernel), in_hbm(gain_row),
-        in_hbm(w_expand), in_hbm(w_reduce), in_hbm(scale_row), in_hbm(cotangent),
-    )
+    )(core, left, right, padded, conv, dbranch, dact, taps, params, expand, reduce)
 
     swap = [(0, 1), (1, 0)]
     came = lax.ppermute(sent, "core", swap)
@@ -407,7 +449,7 @@
     dconv, small = pl.pallas_call(
         functools.partial(backward_kernel, multiplier),
         name="backward",
-        in_specs=[VMEM] * 6,
+        in_specs=[VMEM] * 7,
         out_specs=[VMEM] * 2,
         out_shape=[
             shape((height, width, channels), bf16),
@@ -418,7 +460,7 @@
             pltpu.VMEM((places * SMALL, channels), f32),
         ],
         compiler_params=PARAMS,
-    )(dpre, w_expand, xhat, rstd, padded, row_sums)
+    )(dpre, expand, xhat, rstd, padded, params, dscale)
 
     small_came = lax.ppermute(small, "core", swap)
     whole = top + rows + 2 * SMALL

time: 108 us -> 108 us (level)
  Pallas kernels: 17.8 us -> 20.5 us
  starting transfers between devices: 60.8 us -> 58.6 us
  waiting for transfers between devices: 12.1 us -> 10.6 us
    ppermute x8, starting transfers between devices: 25.1 us -> 20.9 us  [shifted(): return lax.ppermute(value, axes, pairs)]
    pallas_call x1 -> x2, Pallas kernels: 8.35 us -> 11.1 us  [the longest x1 6.28 us: shards(): pl.pallas_call(forward_kernel, name='forward', in_specs=[SMEM] + [VMEM] *...]
    ppermute x7, starting transfers between devices: 15.3 us -> 17.6 us  [shards(): lax.ppermute(part, 'z', [(i, (i + step) % Z) for i in range(Z)])]
    all_to_all x2, starting transfers between devices: 18.7 us -> 16.4 us  [exchanged(): return lax.all_to_all(chunks, axes, 0, 0, tiled=True)]
    ppermute x1, starting transfers between devices: 1.09 us -> 3.1 us  [shards(): came = lax.ppermute(sent, 'core', swap)]
    ppermute x7, waiting for transfers between devices: 6.15 us -> 4.19 us  [shards(): lax.ppermute(part, 'z', [(i, (i + step) % Z) for i in range(Z)])]
  transfers between devices with their start and end apart: 20 -> 20, of which waited for: 5 -> 5; matrix products, arithmetic and copies ran while one was open for 1% -> 1% of each run, Pallas kernels for 7% -> 12%
where the time goes in v6:
time: 108 us; the launch traced here: 107 us
  starting transfers between devices  58.6 us (54%)
  Pallas kernels  20.5 us (19%)
  blocking collectives  13.6 us (13%)
  waiting for transfers between devices  10.6 us (10%)
  local copies, waits for them, and re-layouts  2.6 us (2%)
    ppermute x8, starting transfers between devices, shifted(): return lax.ppermute(value, axes, pairs)  20.9 us
    ppermute x7, starting transfers between devices, shards(): lax.ppermute(part, 'z', [(i, (i + step) % Z) for i in range(Z)])  17.6 us
    all_to_all x2, starting transfers between devices, exchanged(): return lax.all_to_all(chunks, axes, 0, 0, tiled=True)  16.4 us
    all_to_all x1, blocking collectives, exchanged(): return lax.all_to_all(chunks, axes, 0, 0, tiled=True)  13.6 us
    pallas_call x1, Pallas kernels, shards(): pl.pallas_call(forward_kernel, name='forward', in_specs=[SMEM] + [VMEM] *...  6.28 us
    pallas_call x1, Pallas kernels, shards(): pl.pallas_call(prepare_kernel, name='prepare', in_specs=[HBM] + [VMEM] *...  4.77 us
    ppermute x7, waiting for transfers between devices, shards(): lax.ppermute(part, 'z', [(i, (i + step) % Z) for i in range(Z)])  4.19 us
    all_to_all x2, waiting for transfers between devices, exchanged(): return lax.all_to_all(chunks, axes, 0, 0, tiled=True)  4.12 us
  transfers between devices with their start and end apart: 20, of which 5 were waited for; matrix products, arithmetic and copies ran while one was open for 1% of the time, Pallas kernels for 12%

profile of v6, /device:TPU:2, one launch (start us, length us, event | category | flops | bytes accessed | tf_op | source)
XLA Modules:
  0.0 107.0 jit_solution(8657104909905465937)
XLA Ops:
  0.6 1.0 fusion.3
  1.6 1.7 %collective-permute-start = (bf16[3,32,512]{2,1,0:T(8,128)(2,1)S(1)}, bf16[3,32,512]{2,1,0:T(8,128)(2,1)S(1)}, u32[]{:S(2)}, u32[]{:S(2)}) collective-permute-start(bf16[3,32,512]{2,1,0:T(8,128)(2,1)S(1)} %get-tuple-element.116), channel_id=1, source_target_pairs={{0,32},{32,64},{64,96},{96,128},{128,160},{160,192},{192,224},{1,3... | collective-permute-start | bytes 294920 | tf_op jit(solution)/shard_map/ppermute | solution.py:356
  3.3 1.3 %collective-permute-start.1 = (bf16[3,32,512]{2,1,0:T(8,128)(2,1)S(1)}, bf16[3,32,512]{2,1,0:T(8,128)(2,1)S(1)}, u32[]{:S(2)}, u32[]{:S(2)}) collective-permute-start(bf16[3,32,512]{2,1,0:T(8,128)(2,1)S(1)} %get-tuple-element.117), channel_id=1, source_target_pairs={{32,0},{64,32},{96,64},{128,96},{160,128},{192,160},{224,192},{33,... | collective-permute-start | bytes 294920 | tf_op jit(solution)/shard_map/ppermute | solution.py:356
  4.6 0.9 fusion.2
  5.6 2.3 %collective-permute-done.1.down = bf16[3,32,512]{2,1,0:T(8,128)(2,1)S(1)} collective-permute-done((bf16[3,32,512]{2,1,0:T(8,128)(2,1)S(1)}, bf16[3,32,512]{2,1,0:T(8,128)(2,1)S(1)}, u32[]{:S(2)}, u32[]{:S(2)}) %collective-permute-start.1) | collective-permute-done | bytes 98336 | tf_op jit(solution)/shard_map/ppermute | solution.py:356
  8.0 3.8 %collective-permute-start.2 = (bf16[14,3,512]{2,1,0:T(4,128)(2,1)S(1)}, bf16[14,3,512]{2,1,0:T(4,128)(2,1)S(1)}, u32[]{:S(2)}, u32[]{:S(2)}) collective-permute-start(bf16[14,3,512]{2,1,0:T(4,128)(2,1)S(1)} %pad_maximum_fusion), channel_id=1, source_target_pairs={{0,1},{1,2},{2,3},{3,4},{4,5},{5,6},{6,7},{7,8},{8,9},{9,10},{10,1... | collective-permute-start | bytes 129032 | tf_op jit(solution)/shard_map/ppermute | solution.py:356
  11.9 5.8 %collective-permute-start.3 = (bf16[14,3,512]{2,1,0:T(4,128)(2,1)S(1)}, bf16[14,3,512]{2,1,0:T(4,128)(2,1)S(1)}, u32[]{:S(2)}, u32[]{:S(2)}) collective-permute-start(bf16[14,3,512]{2,1,0:T(4,128)(2,1)S(1)} %pad_maximum_fusion.1), channel_id=1, source_target_pairs={{1,0},{2,1},{3,2},{4,3},{5,4},{6,5},{7,6},{8,7},{9,8},{10,9},{11,1... | collective-permute-start | bytes 129032 | tf_op jit(solution)/shard_map/ppermute | solution.py:356
  17.7 4.8 %prepare.1 = (f32[4,14,48,128]{3,2,1,0:T(8,128)S(1)}, f32[4,256,128]{2,1,0:T(8,128)S(1)}, bf16[256,512]{1,0:T(8,128)(2,1)S(1)}, f32[256,2048]{1,0:T(8,128)S(1)},...) custom-call(bf16[8,32,512]{2,1,0:T(8,128)(2,1)} %field_h.1, ...), custom_call_target="tpu_custom_call" | custom-call | tf_op jit(solution)/shard_map/prepare/pallas_call | solution.py:396
  22.5 6.3 %forward.1 = (bf16[16,96,512]{2,1,0:T(8,128)(2,1)S(1)}, bf16[16,96,512]{2,1,0:T(8,128)(2,1)S(1)}, bf16[8,8,8,512]{3,2,1,0:T(8,128)(2,1)S(1)}, bf16[8,8,8,512]{3,...) custom-call(s32[1]{0:T(128)} %bitcast.core_ref, ...), custom_call_target="tpu_custom_call", output_to_operand_aliasing={{7}: (3, {})} | custom-call | tf_op jit(solution)/shard_map/forward/pallas_call | solution.py:423
  28.8 3.1 %collective-permute-start.4 = (bf16[16,96,512]{2,1,0:T(8,128)(2,1)S(1)}, bf16[16,96,512]{2,1,0:T(8,128)(2,1)S(1)}, u32[]{:S(2)}, u32[]{:S(2)}) collective-permute-start(bf16[16,96,512]{2,1,0:T(8,128)(2,1)S(1)} %get-tuple-element.67), channel_id=1, source_target_pairs={{0,32},{32,0},{1,33},{33,1},{2,34},{34,2},{3,35},{35,3},{4,36},{36... | collective-permute-start | bytes 4718600 | tf_op jit(solution)/shard_map/ppermute | solution.py:447
  32.0 3.1 %backward.1 = (bf16[8,32,512]{2,1,0:T(8,128)(2,1)S(1)}, bf16[16,8,512]{2,1,0:T(8,128)(2,1)S(1)}) custom-call(bf16[256,2048]{1,0:T(8,128)(2,1)S(1)} %get-tuple-element.68.dpre, bf16[512,2048]{1,0:T(8,128)(2,1)S(1)} %get-tuple-element.64.expand, f32[4,256,128]{2,1,0:T(8,128)S(1)} %get-tuple-element.69.xhat, f32[256,128]{1,0:T(8,128)S(1)} %get-tuple-element.70.rstd, ...), custom_call_target="tpu_custom_call" | custom-call | tf_op jit(solution)/shard_map/backward/pallas_call | solution.py:449
  35.1 0.5 collective-permute-start.5
  35.6 1.3 %collective-permute-start.8 = (bf16[3,32,512]{2,1,0:T(8,128)(2,1)S(1)}, bf16[3,32,512]{2,1,0:T(8,128)(2,1)S(1)}, u32[]{:S(2)}, u32[]{:S(2)}) collective-permute-start(bf16[3,32,512]{2,1,0:T(8,128)(2,1)S(1)} %get-tuple-element.112), channel_id=1, source_target_pairs={{32,0},{64,32},{96,64},{128,96},{160,128},{192,160},{224,192},{33,... | collective-permute-start | bytes 294920 | tf_op jit(solution)/shard_map/ppermute | solution.py:356
  36.9 3.0 %collective-permute-start.7 = (bf16[3,32,512]{2,1,0:T(8,128)(2,1)S(1)}, bf16[3,32,512]{2,1,0:T(8,128)(2,1)S(1)}, u32[]{:S(2)}, u32[]{:S(2)}) collective-permute-start(bf16[3,32,512]{2,1,0:T(8,128)(2,1)S(1)} %get-tuple-element.113), channel_id=1, source_target_pairs={{0,32},{32,64},{64,96},{96,128},{128,160},{160,192},{192,224},{1,3... | collective-permute-start | bytes 294920 | tf_op jit(solution)/shard_map/ppermute | solution.py:356
  40.0 1.9 %merge.1 = bf16[16,104,512]{2,1,0:T(8,128)(2,1)} custom-call(bf16[16,96,512]{2,1,0:T(8,128)(2,1)S(1)} %get-tuple-element.66.kept, bf16[16,96,512]{2,1,0:T(8,128)(2,1)S(1)} %collective-permute-done.4.came, bf16[16,8,512]{2,1,0:T(8,128)(2,1)S(1)} %get-tuple-element.73.small, bf16[16,8,512]{2,1,0:T(8,128)(2,1)S(1)} %collective-permute-done.5.small_came), custom_call_target="tpu_custom_call" | custom-call | tf_op jit(solution)/shard_map/merge/pallas_call | solution.py:467
  41.9 9.2 %all-to-all-start = ((bf16[16,104,512]{2,1,0:T(8,128)(2,1)}), bf16[16,104,512]{2,1,0:T(8,128)(2,1)S(1)}, u32[]{:S(2)}, u32[]{:S(2)}) async-start(bf16[16,104,512]{2,1,0:T(8,128)(2,1)} %merge.1), calls=%async_computation | async-start | bytes 3407872 | tf_op jit(solution)/shard_map/all_to_all | solution.py:372
  51.2 1.9 %collective-permute-start.9 = (bf16[14,3,512]{2,1,0:T(4,128)(2,1)S(1)}, bf16[14,3,512]{2,1,0:T(4,128)(2,1)S(1)}, u32[]{:S(2)}, u32[]{:S(2)}) collective-permute-start(bf16[14,3,512]{2,1,0:T(4,128)(2,1)S(1)} %pad_maximum_fusion.2), channel_id=1, source_target_pairs={{0,1},{1,2},{2,3},{3,4},{4,5},{5,6},{6,7},{7,8},{8,9},{9,10},{10,1... | collective-permute-start | bytes 129032 | tf_op jit(solution)/shard_map/ppermute | solution.py:356
  53.4 5.4 %collective-permute-start.12 = (bf16[8,8,512]{2,1,0:T(8,128)(2,1)S(1)}, bf16[8,8,512]{2,1,0:T(8,128)(2,1)S(1)}, u32[]{:S(2)}, u32[]{:S(2)}) collective-permute-start(bf16[8,8,512]{2,1,0:T(8,128)(2,1)S(1)} %get-tuple-element.84), channel_id=1, source_target_pairs={{0,2},{1,3},{2,4},{3,5},{4,6},{5,7},{6,0},{7,1},{8,10},{9,11},{10,... | collective-permute-start | bytes 196616 | tf_op jit(solution)/shard_map/ppermute | solution.py:489
  58.8 1.9 %collective-permute-start.10 = (bf16[14,3,512]{2,1,0:T(4,128)(2,1)S(1)}, bf16[14,3,512]{2,1,0:T(4,128)(2,1)S(1)}, u32[]{:S(2)}, u32[]{:S(2)}) collective-permute-start(bf16[14,3,512]{2,1,0:T(4,128)(2,1)S(1)} %pad_maximum_fusion.3), channel_id=1, source_target_pairs={{1,0},{2,1},{3,2},{4,3},{5,4},{6,5},{7,6},{8,7},{9,8},{10,9},{11,1... | collective-permute-start | bytes 129032 | tf_op jit(solution)/shard_map/ppermute | solution.py:356
  60.8 1.8 %collective-permute-start.13 = (bf16[8,8,512]{2,1,0:T(8,128)(2,1)S(1)}, bf16[8,8,512]{2,1,0:T(8,128)(2,1)S(1)}, u32[]{:S(2)}, u32[]{:S(2)}) collective-permute-start(bf16[8,8,512]{2,1,0:T(8,128)(2,1)S(1)} %get-tuple-element.85), channel_id=1, source_target_pairs={{0,3},{1,4},{2,5},{3,6},{4,7},{5,0},{6,1},{7,2},{8,11},{9,12},{10,... | collective-permute-start | bytes 196616 | tf_op jit(solution)/shard_map/ppermute | solution.py:489
  62.6 0.6 copy-done.2
  63.2 2.3 %collective-permute-start.14 = (bf16[8,8,512]{2,1,0:T(8,128)(2,1)S(1)}, bf16[8,8,512]{2,1,0:T(8,128)(2,1)S(1)}, u32[]{:S(2)}, u32[]{:S(2)}) collective-permute-start(bf16[8,8,512]{2,1,0:T(8,128)(2,1)S(1)} %get-tuple-element.86), channel_id=1, source_target_pairs={{0,4},{1,5},{2,6},{3,7},{4,0},{5,1},{6,2},{7,3},{8,12},{9,13},{10,... | collective-permute-start | bytes 196616 | tf_op jit(solution)/shard_map/ppermute | solution.py:489
  65.5 4.4 %collective-permute-start.15 = (bf16[8,8,512]{2,1,0:T(8,128)(2,1)S(1)}, bf16[8,8,512]{2,1,0:T(8,128)(2,1)S(1)}, u32[]{:S(2)}, u32[]{:S(2)}) collective-permute-start(bf16[8,8,512]{2,1,0:T(8,128)(2,1)S(1)} %get-tuple-element.87), channel_id=1, source_target_pairs={{0,5},{1,6},{2,7},{3,0},{4,1},{5,2},{6,3},{7,4},{8,13},{9,14},{10,... | collective-permute-start | bytes 196616 | tf_op jit(solution)/shard_map/ppermute | solution.py:489
  69.9 1.7 %collective-permute-start.16 = (bf16[8,8,512]{2,1,0:T(8,128)(2,1)S(1)}, bf16[8,8,512]{2,1,0:T(8,128)(2,1)S(1)}, u32[]{:S(2)}, u32[]{:S(2)}) collective-permute-start(bf16[8,8,512]{2,1,0:T(8,128)(2,1)S(1)} %get-tuple-element.88), channel_id=1, source_target_pairs={{0,6},{1,7},{2,0},{3,1},{4,2},{5,3},{6,4},{7,5},{8,14},{9,15},{10,... | collective-permute-start | bytes 196616 | tf_op jit(solution)/shard_map/ppermute | solution.py:489
  71.6 1.9 %collective-permute-start.17 = (bf16[8,8,512]{2,1,0:T(8,128)(2,1)S(1)}, bf16[8,8,512]{2,1,0:T(8,128)(2,1)S(1)}, u32[]{:S(2)}, u32[]{:S(2)}) collective-permute-start(bf16[8,8,512]{2,1,0:T(8,128)(2,1)S(1)} %get-tuple-element.89), channel_id=1, source_target_pairs={{0,7},{1,0},{2,1},{3,2},{4,3},{5,4},{6,5},{7,6},{8,15},{9,8},{10,9... | collective-permute-start | bytes 196616 | tf_op jit(solution)/shard_map/ppermute | solution.py:489
  73.6 3.5 %collective-permute-done.15.refs_5_ = bf16[8,8,512]{2,1,0:T(8,128)(2,1)S(1)} collective-permute-done((bf16[8,8,512]{2,1,0:T(8,128)(2,1)S(1)}, bf16[8,8,512]{2,1,0:T(8,128)(2,1)S(1)}, u32[]{:S(2)}, u32[]{:S(2)}) %collective-permute-start.15) | collective-permute-done | bytes 65568 | tf_op jit(solution)/shard_map/ppermute | solution.py:489
  78.1 13.6 %all_to_all.15.chunks = bf16[8,16,512]{2,1,0:T(8,128)(2,1)S(1)} all-to-all(bf16[8,16,512]{2,1,0:T(8,128)(2,1)S(1)} %plane.1), channel_id=1, replica_groups=mesh['y'=4,'core'=2,'x'=4,'z'=8] {'z'}, dimensions={0} | all-to-all | bytes 262144 | tf_op jit(solution)/shard_map/all_to_all | solution.py:372
  91.8 0.7 line.1
  92.5 7.2 %all-to-all-start.2 = ((bf16[16,8,512]{2,1,0:T(8,128)(2,1)}), bf16[16,8,512]{2,1,0:T(8,128)(2,1)S(1)}, u32[]{:S(2)}, u32[]{:S(2)}) async-start(bf16[16,8,512]{2,1,0:T(8,128)(2,1)} %get-tuple-element.103), calls=%async_computation.2 | async-start | bytes 262144 | tf_op jit(solution)/shard_map/all_to_all | solution.py:372
  99.7 2.5 %features.1 = bf16[8,32,512]{2,1,0:T(8,128)(2,1)} custom-call(bf16[8,32,512]{2,1,0:T(8,128)(2,1)S(1)} %get-tuple-element.76.field, bf16[3,32,512]{2,1,0:T(8,128)(2,1)S(1)} %collective-permute-done.7.up, bf16[3,32,512]{2,1,0:T(8,128)(2,1)S(1)} %collective-permute-done.8.down, bf16[14,3,512]{2,1,0:T(4,128)(2,1)S(1)} %copy-done.3, ...), custom_call_target="tpu_custom_call" | custom-call | tf_op jit(solution)/shard_map/features/pallas_call | solution.py:525
  102.2 4.1 %all-to-all-done.2.chunks = bf16[16,8,512]{2,1,0:T(8,128)(2,1)S(1)} async-done(((bf16[16,8,512]{2,1,0:T(8,128)(2,1)}), bf16[16,8,512]{2,1,0:T(8,128)(2,1)S(1)}, u32[]{:S(2)}, u32[]{:S(2)}) %all-to-all-start.2) | async-done | bytes 131104 | tf_op jit(solution)/shard_map/all_to_all | solution.py:372
  106.3 0.7 last.1
  (37 shorter events, 1.7 us)
Async XLA Ops:
  1.6 4.0 %collective-permute-start = (bf16[3,32,512]{2,1,0:T(8,128)(2,1)S(1)}, bf16[3,32,512]{2,1,0:T(8,128)(2,1)S(1)}, u32[]{:S(2)}, u32[]{:S(2)}) collective-permute-start(bf16[3,32,512]{2,1,0:T(8,128)(2,1)S(1)} %get-tuple-element.116), channel_id=1, source_target_pairs={{0,32},{32,64},{64,96},{96,128},{128,160},{160,192},{192,224},{1,3... | collective-permute-start | bytes 294920 | tf_op jit(solution)/shard_map/ppermute | solution.py:356
  3.3 4.6 %collective-permute-start.1 = (bf16[3,32,512]{2,1,0:T(8,128)(2,1)S(1)}, bf16[3,32,512]{2,1,0:T(8,128)(2,1)S(1)}, u32[]{:S(2)}, u32[]{:S(2)}) collective-permute-start(bf16[3,32,512]{2,1,0:T(8,128)(2,1)S(1)} %get-tuple-element.117), channel_id=1, source_target_pairs={{32,0},{64,32},{96,64},{128,96},{160,128},{192,160},{224,192},{33,... | collective-permute-start | bytes 294920 | tf_op jit(solution)/shard_map/ppermute | solution.py:356
  8.0 14.5 %collective-permute-start.2 = (bf16[14,3,512]{2,1,0:T(4,128)(2,1)S(1)}, bf16[14,3,512]{2,1,0:T(4,128)(2,1)S(1)}, u32[]{:S(2)}, u32[]{:S(2)}) collective-permute-start(bf16[14,3,512]{2,1,0:T(4,128)(2,1)S(1)} %pad_maximum_fusion), channel_id=1, source_target_pairs={{0,1},{1,2},{2,3},{3,4},{4,5},{5,6},{6,7},{7,8},{8,9},{9,10},{10,1... | collective-permute-start | bytes 129032 | tf_op jit(solution)/shard_map/ppermute | solution.py:356
  11.9 10.6 %collective-permute-start.3 = (bf16[14,3,512]{2,1,0:T(4,128)(2,1)S(1)}, bf16[14,3,512]{2,1,0:T(4,128)(2,1)S(1)}, u32[]{:S(2)}, u32[]{:S(2)}) collective-permute-start(bf16[14,3,512]{2,1,0:T(4,128)(2,1)S(1)} %pad_maximum_fusion.1), channel_id=1, source_target_pairs={{1,0},{2,1},{3,2},{4,3},{5,4},{6,5},{7,6},{8,7},{9,8},{10,9},{11,1... | collective-permute-start | bytes 129032 | tf_op jit(solution)/shard_map/ppermute | solution.py:356
  28.8 11.2 %collective-permute-start.4 = (bf16[16,96,512]{2,1,0:T(8,128)(2,1)S(1)}, bf16[16,96,512]{2,1,0:T(8,128)(2,1)S(1)}, u32[]{:S(2)}, u32[]{:S(2)}) collective-permute-start(bf16[16,96,512]{2,1,0:T(8,128)(2,1)S(1)} %get-tuple-element.67), channel_id=1, source_target_pairs={{0,32},{32,0},{1,33},{33,1},{2,34},{34,2},{3,35},{35,3},{4,36},{36... | collective-permute-start | bytes 4718600 | tf_op jit(solution)/shard_map/ppermute | solution.py:447
  31.9 10.0 %collective-permute-start.6 = (bf16[8,8,8,512]{3,2,1,0:T(8,128)(2,1)S(1)}, bf16[8,8,8,512]{3,2,1,0:T(8,128)(2,1)S(1)}, u32[]{:S(2)}, u32[]{:S(2)}) collective-permute-start(bf16[8,8,8,512]{3,2,1,0:T(8,128)(2,1)S(1)} %get-tuple-element.75), channel_id=1, source_target_pairs={{0,32},{32,0},{1,33},{33,1},{2,34},{34,2},{3,35},{35,3},{4,36},{36... | collective-permute-start | bytes 1572872 | tf_op jit(solution)/shard_map/ppermute | solution.py:448
  35.1 4.9 %collective-permute-start.5 = (bf16[16,8,512]{2,1,0:T(8,128)(2,1)S(1)}, bf16[16,8,512]{2,1,0:T(8,128)(2,1)S(1)}, u32[]{:S(2)}, u32[]{:S(2)}) collective-permute-start(bf16[16,8,512]{2,1,0:T(8,128)(2,1)S(1)} %get-tuple-element.73.small), channel_id=1, source_target_pairs={{0,32},{32,0},{1,33},{33,1},{2,34},{34,2},{3,35},{35,3},{4,36},{36... | collective-permute-start | bytes 393224 | tf_op jit(solution)/shard_map/ppermute | solution.py:465
  35.6 6.3 %collective-permute-start.8 = (bf16[3,32,512]{2,1,0:T(8,128)(2,1)S(1)}, bf16[3,32,512]{2,1,0:T(8,128)(2,1)S(1)}, u32[]{:S(2)}, u32[]{:S(2)}) collective-permute-start(bf16[3,32,512]{2,1,0:T(8,128)(2,1)S(1)} %get-tuple-element.112), channel_id=1, source_target_pairs={{32,0},{64,32},{96,64},{128,96},{160,128},{192,160},{224,192},{33,... | collective-permute-start | bytes 294920 | tf_op jit(solution)/shard_map/ppermute | solution.py:356
  36.9 5.0 %collective-permute-start.7 = (bf16[3,32,512]{2,1,0:T(8,128)(2,1)S(1)}, bf16[3,32,512]{2,1,0:T(8,128)(2,1)S(1)}, u32[]{:S(2)}, u32[]{:S(2)}) collective-permute-start(bf16[3,32,512]{2,1,0:T(8,128)(2,1)S(1)} %get-tuple-element.113), channel_id=1, source_target_pairs={{0,32},{32,64},{64,96},{96,128},{128,160},{160,192},{192,224},{1,3... | collective-permute-start | bytes 294920 | tf_op jit(solution)/shard_map/ppermute | solution.py:356
  41.9 35.9 %all-to-all-start = ((bf16[16,104,512]{2,1,0:T(8,128)(2,1)}), bf16[16,104,512]{2,1,0:T(8,128)(2,1)S(1)}, u32[]{:S(2)}, u32[]{:S(2)}) async-start(bf16[16,104,512]{2,1,0:T(8,128)(2,1)} %merge.1), calls=%async_computation | async-start | bytes 3407872 | tf_op jit(solution)/shard_map/all_to_all | solution.py:372
  51.2 11.3 %collective-permute-start.9 = (bf16[14,3,512]{2,1,0:T(4,128)(2,1)S(1)}, bf16[14,3,512]{2,1,0:T(4,128)(2,1)S(1)}, u32[]{:S(2)}, u32[]{:S(2)}) collective-permute-start(bf16[14,3,512]{2,1,0:T(4,128)(2,1)S(1)} %pad_maximum_fusion.2), channel_id=1, source_target_pairs={{0,1},{1,2},{2,3},{3,4},{4,5},{5,6},{6,7},{7,8},{8,9},{9,10},{10,1... | collective-permute-start | bytes 129032 | tf_op jit(solution)/shard_map/ppermute | solution.py:356
  53.3 46.4 %copy-start = (bf16[8,32,512]{2,1,0:T(8,128)(2,1)S(1)}, bf16[8,32,512]{2,1,0:T(8,128)(2,1)}, u32[]{:S(2)}) copy-start(bf16[8,32,512]{2,1,0:T(8,128)(2,1)} %cotangent.1) | copy-start | bytes 786436
  53.3 46.4 %copy-start.1 = (f32[7,7,512]{2,1,0:T(8,128)S(1)}, f32[7,7,512]{2,1,0:T(8,128)}, u32[]{:S(2)}) copy-start(f32[7,7,512]{2,1,0:T(8,128)} %taps.1) | copy-start | bytes 301060
  53.3 16.6 %collective-permute-start.11 = (bf16[8,8,512]{2,1,0:T(8,128)(2,1)S(1)}, bf16[8,8,512]{2,1,0:T(8,128)(2,1)S(1)}, u32[]{:S(2)}, u32[]{:S(2)}) collective-permute-start(bf16[8,8,512]{2,1,0:T(8,128)(2,1)S(1)} %get-tuple-element.83), channel_id=1, source_target_pairs={{0,1},{1,2},{2,3},{3,4},{4,5},{5,6},{6,7},{7,0},{8,9},{9,10},{10,1... | collective-permute-start | bytes 196616 | tf_op jit(solution)/shard_map/ppermute | solution.py:489
  53.4 18.2 %collective-permute-start.12 = (bf16[8,8,512]{2,1,0:T(8,128)(2,1)S(1)}, bf16[8,8,512]{2,1,0:T(8,128)(2,1)S(1)}, u32[]{:S(2)}, u32[]{:S(2)}) collective-permute-start(bf16[8,8,512]{2,1,0:T(8,128)(2,1)S(1)} %get-tuple-element.84), channel_id=1, source_target_pairs={{0,2},{1,3},{2,4},{3,5},{4,6},{5,7},{6,0},{7,1},{8,10},{9,11},{10,... | collective-permute-start | bytes 196616 | tf_op jit(solution)/shard_map/ppermute | solution.py:489
  58.8 6.7 %collective-permute-start.10 = (bf16[14,3,512]{2,1,0:T(4,128)(2,1)S(1)}, bf16[14,3,512]{2,1,0:T(4,128)(2,1)S(1)}, u32[]{:S(2)}, u32[]{:S(2)}) collective-permute-start(bf16[14,3,512]{2,1,0:T(4,128)(2,1)S(1)} %pad_maximum_fusion.3), channel_id=1, source_target_pairs={{1,0},{2,1},{3,2},{4,3},{5,4},{6,5},{7,6},{8,7},{9,8},{10,9},{11,1... | collective-permute-start | bytes 129032 | tf_op jit(solution)/shard_map/ppermute | solution.py:356
  60.8 12.8 %collective-permute-start.13 = (bf16[8,8,512]{2,1,0:T(8,128)(2,1)S(1)}, bf16[8,8,512]{2,1,0:T(8,128)(2,1)S(1)}, u32[]{:S(2)}, u32[]{:S(2)}) collective-permute-start(bf16[8,8,512]{2,1,0:T(8,128)(2,1)S(1)} %get-tuple-element.85), channel_id=1, source_target_pairs={{0,3},{1,4},{2,5},{3,6},{4,7},{5,0},{6,1},{7,2},{8,11},{9,12},{10,... | collective-permute-start | bytes 196616 | tf_op jit(solution)/shard_map/ppermute | solution.py:489
  62.6 0.6 copy-start.2
  63.2 36.5 %copy-start.3 = (bf16[14,3,512]{2,1,0:T(4,128)(2,1)S(1)}, bf16[14,3,512]{2,1,0:T(4,128)(2,1)}, u32[]{:S(2)}) copy-start(bf16[14,3,512]{2,1,0:T(4,128)(2,1)} %copy-done.2) | copy-start | bytes 129028
  63.2 10.4 %collective-permute-start.14 = (bf16[8,8,512]{2,1,0:T(8,128)(2,1)S(1)}, bf16[8,8,512]{2,1,0:T(8,128)(2,1)S(1)}, u32[]{:S(2)}, u32[]{:S(2)}) collective-permute-start(bf16[8,8,512]{2,1,0:T(8,128)(2,1)S(1)} %get-tuple-element.86), channel_id=1, source_target_pairs={{0,4},{1,5},{2,6},{3,7},{4,0},{5,1},{6,2},{7,3},{8,12},{9,13},{10,... | collective-permute-start | bytes 196616 | tf_op jit(solution)/shard_map/ppermute | solution.py:489
  65.5 11.6 %collective-permute-start.15 = (bf16[8,8,512]{2,1,0:T(8,128)(2,1)S(1)}, bf16[8,8,512]{2,1,0:T(8,128)(2,1)S(1)}, u32[]{:S(2)}, u32[]{:S(2)}) collective-permute-start(bf16[8,8,512]{2,1,0:T(8,128)(2,1)S(1)} %get-tuple-element.87), channel_id=1, source_target_pairs={{0,5},{1,6},{2,7},{3,0},{4,1},{5,2},{6,3},{7,4},{8,13},{9,14},{10,... | collective-permute-start | bytes 196616 | tf_op jit(solution)/shard_map/ppermute | solution.py:489
  69.9 7.6 %collective-permute-start.16 = (bf16[8,8,512]{2,1,0:T(8,128)(2,1)S(1)}, bf16[8,8,512]{2,1,0:T(8,128)(2,1)S(1)}, u32[]{:S(2)}, u32[]{:S(2)}) collective-permute-start(bf16[8,8,512]{2,1,0:T(8,128)(2,1)S(1)} %get-tuple-element.88), channel_id=1, source_target_pairs={{0,6},{1,7},{2,0},{3,1},{4,2},{5,3},{6,4},{7,5},{8,14},{9,15},{10,... | collective-permute-start | bytes 196616 | tf_op jit(solution)/shard_map/ppermute | solution.py:489
  71.6 6.1 %collective-permute-start.17 = (bf16[8,8,512]{2,1,0:T(8,128)(2,1)S(1)}, bf16[8,8,512]{2,1,0:T(8,128)(2,1)S(1)}, u32[]{:S(2)}, u32[]{:S(2)}) collective-permute-start(bf16[8,8,512]{2,1,0:T(8,128)(2,1)S(1)} %get-tuple-element.89), channel_id=1, source_target_pairs={{0,7},{1,0},{2,1},{3,2},{4,3},{5,4},{6,5},{7,6},{8,15},{9,8},{10,9... | collective-permute-start | bytes 196616 | tf_op jit(solution)/shard_map/ppermute | solution.py:489
  92.5 13.9 %all-to-all-start.2 = ((bf16[16,8,512]{2,1,0:T(8,128)(2,1)}), bf16[16,8,512]{2,1,0:T(8,128)(2,1)S(1)}, u32[]{:S(2)}, u32[]{:S(2)}) async-start(bf16[16,8,512]{2,1,0:T(8,128)(2,1)} %get-tuple-element.103), calls=%async_computation.2 | async-start | bytes 262144 | tf_op jit(solution)/shard_map/all_to_all | solution.py:372

commit v7 on v6

--- a/solution.py
+++ b/solution.py
@@ -15,7 +15,7 @@
 INV_ROOT_TWO_PI = 1.0 / math.sqrt(2.0 * math.pi)
 LANES = 128
 LEFT = 8
-SMALL = 4
+SMALL = 32
 
 NN = (((1,), (0,)), ((), ()))
 NT = (((1,), (1,)), ((), ()))
@@ -73,7 +73,7 @@
 
 
 def prepare_kernel(
-    field_h, up, down, taps_h, gain_h, scale_h, cotangent_h, expand_h, reduce_h,
+    field_h, down, up, taps_h, gain_h, scale_h, cotangent_h, expand_h, reduce_h,
     padded, conv, dbranch, dact, taps, rows_out, expand, reduce,
     field, gain, scale, cotangent, sems,
 ):
@@ -117,7 +117,7 @@
 
 def forward_kernel(
     core_ref, left, right, padded_in, conv, dbranch, dact, taps, rows_in, expand, reduce,
-    sent, kept, sent_z, kept_z, dpre_out, xhat_out, rstd_out, padded, dscale_out,
+    sent, kept, dpre_out, xhat_out, rstd_out, padded, dscale_out,
     normed, turned, chosen,
 ):
     core = core_ref[0]
@@ -155,11 +155,10 @@
     per_z = step // (X * Z)
     part_x = part // X
     wide = channels // step
-    narrow = channels // 2
-    top = per_z * Z // 2
+    top = per_z * Z
 
     def hidden_block(y, _):
-        for own, target, target_z in ((0, sent, sent_z), (1, kept, kept_z)):
+        for own, target in ((0, sent), (1, kept)):
             owner = core if own else 1 - core
             chunk = y * CORE + owner
             hidden = pl.ds(pl.multiple_of(chunk * step, step), step)
@@ -173,15 +172,8 @@
             weighed = share * reduce[hidden, :].astype(jnp.float32)
             dscale_out[...] += jnp.sum(weighed.reshape(step // 8, 8, channels), axis=0)
             share = share.astype(jnp.bfloat16)
-            for place in range(X * Z):
-                x, z = place // Z, place % Z
-                mine = share[place * per_z : (place + 1) * per_z]
-                target[
-                    y * X + x, pl.ds(z // 2 * per_z, per_z), pl.ds(z % 2 * narrow, narrow)
-                ] = mine[:, :narrow]
-                target_z[
-                    z, y * (X // 2) + x // 2, :, pl.ds(x % 2 * narrow, narrow)
-                ] = mine[:, narrow:]
+            for x in range(X):
+                target[y * X + x, pl.ds(0, top), :] = share[x * top : (x + 1) * top]
             share = product(chosen[...], dpre, NN).astype(jnp.bfloat16)
             rows = pl.ds(pl.multiple_of(top + (chunk // wide) * part_x, part_x), part_x)
             lanes = pl.ds(pl.multiple_of((chunk % wide) * step, step), step)
@@ -195,7 +187,8 @@
 
 
 def backward_kernel(
-    multiplier, dpre, expand, xhat, rstd, padded, rows, dscale, dconv_out, out, dconv, small
+    multiplier, core_ref, dpre, expand, xhat, rstd, padded, rows, dscale,
+    dconv_out, sent, kept, dconv, small,
 ):
     height, width, channels = dconv_out.shape
     blocks = channels // LANES
@@ -246,9 +239,9 @@
         return 0
 
     lax.fori_loop(0, blocks, tap_block, 0)
-    for place in range(out.shape[0]):
-        part = small[pl.ds(place * SMALL, SMALL), :]
-        out[place] = jnp.concatenate([part, jnp.zeros_like(part)]).astype(jnp.bfloat16)
+    for out, core in ((sent, 1 - core_ref[0]), (kept, core_ref[0])):
+        half = small[pl.ds(pl.multiple_of(core * SMALL, SMALL), SMALL), :]
+        out[...] = half.astype(jnp.bfloat16)
 
 
 def feature_kernel(field, up, down, left, right, taps, cotangent, out, padded):
@@ -271,72 +264,41 @@
     return (left.astype(jnp.float32) + right.astype(jnp.float32)).astype(jnp.bfloat16)
 
 
-def merge_kernel(kept, came, small, small_came, out):
-    rows = kept.shape[1]
-    out[:, pl.ds(0, rows), :] = added(kept[...], came[...])
-    out[:, pl.ds(rows, small.shape[1]), :] = added(small[...], small_came[...])
-
-
-def join_kernel(z_ref, kept, came, *outs):
-    for step, out in enumerate(outs):
-        z = lax.rem(z_ref[0] + step, Z)
-        out[...] = added(kept[z], came[z])
+def merge_kernel(kept, came, out):
+    out[...] = added(kept[...], came[...])
 
 
 def plane_kernel(chunks, out, total):
     total[...] = jnp.sum(chunks[...].astype(jnp.float32), axis=0)
     each = out.shape[1] // 2
-    channels = out.shape[2]
-    narrow = channels // 2
-    top = each * Z // 2
-    small = total[pl.ds(total.shape[0] - 2 * SMALL, SMALL), :].astype(jnp.bfloat16)
-    small = jnp.concatenate([small[:, :narrow], small[:, narrow:]])
+    top = each * Z
     for z in range(Z):
-        parts = [total[pl.ds(top + q * 2 * Z + 2 * z, 2), :] for q in range(each // 2)]
-        out[z, pl.ds(0, each), :] = jnp.concatenate(parts).astype(jnp.bfloat16)
-        half = total[pl.ds(z // 2 * each, each), pl.ds(z % 2 * narrow, narrow)]
-        out[z, pl.ds(each, each), pl.ds(0, narrow)] = half.astype(jnp.bfloat16)
-        out[z, pl.ds(each, each), pl.ds(narrow, narrow)] = small
-
-
-def line_kernel(multiplier, chunks, *refs):
-    *came, dexpand, dreduce, out = refs
+        parts = [total[pl.ds(z * each, each), :]]
+        parts += [total[pl.ds(top + q * 2 * Z + 2 * z, 2), :] for q in range(each // 2)]
+        out[z] = jnp.concatenate(parts).astype(jnp.bfloat16)
+
+
+def line_kernel(multiplier, chunks, dreduce, dexpand):
     total = jnp.sum(chunks[...].astype(jnp.float32), axis=0)
-    each = total.shape[0] // 2
-    channels = total.shape[1]
-    narrow = channels // 2
+    each, channels = dreduce.shape
+    dreduce[...] = total[:each] * multiplier
     for q in range(each // 2):
-        dexpand[:, pl.ds(q * channels, channels)] = total[2 * q : 2 * q + 2] * multiplier
-    dreduce[...] = total[each:, :narrow] * multiplier
-    small = total[each:, narrow:].astype(jnp.bfloat16)
-    line = sum(ref[...].astype(jnp.float32) for ref in came).astype(jnp.bfloat16)
-    for place in range(out.shape[0]):
-        out[place, :, pl.ds(0, narrow)] = line[place // 2][
-            :, place % 2 * narrow : (place % 2 + 1) * narrow
-        ]
-        out[place, :, pl.ds(narrow, narrow)] = small
-
-
-def last_kernel(multiplier, chunks, half, dreduce, dkernel, dgain, dscale):
-    channels = dreduce.shape[1]
-    narrow = channels // 2
-    dreduce[:, pl.ds(0, narrow)] = half[...]
-    total = jnp.sum(chunks[:, :, pl.ds(0, narrow)].astype(jnp.float32), axis=0)
-    dreduce[:, pl.ds(narrow, narrow)] = total * multiplier
+        part = total[each + 2 * q : each + 2 * q + 2]
+        dexpand[:, pl.ds(q * channels, channels)] = part * multiplier
+
+
+def small_kernel(core_ref, own, other, dkernel, dgain, dscale, full):
+    full[core_ref[0]] = own[...].astype(jnp.float32)
+    full[1 - core_ref[0]] = other[...].astype(jnp.float32)
     side = dkernel.shape[0]
-    for place in range(chunks.shape[0]):
-        part = chunks[place, :, pl.ds(narrow, narrow)].astype(jnp.float32)
-        for row in range(SMALL):
-            tap = place * SMALL + row
-            for i in range(2):
-                lanes = pl.ds(i * narrow, narrow)
-                value = part[i * SMALL + row : i * SMALL + row + 1]
-                if tap < side * side:
-                    dkernel[tap // side, pl.ds(tap % side, 1), lanes] = value
-                elif tap == side * side:
-                    dgain[:, lanes] = value
-                elif tap == side * side + 1:
-                    dscale[:, lanes] = value
+    for tap in range(side * side + 2):
+        value = full[tap // SMALL, pl.ds(tap % SMALL, 1), :]
+        if tap < side * side:
+            dkernel[tap // side, pl.ds(tap % side, 1), :] = value
+        elif tap == side * side:
+            dgain[...] = value
+        else:
+            dscale[...] = value
 
 
 VMEM = pl.BlockSpec(memory_space=pltpu.VMEM)
@@ -357,7 +319,14 @@
 
 
 def row_borders(field, reach):
-    return shifted(field[-reach:], ROW, 1), shifted(field[:reach], ROW, -1)
+    down = shifted(field[:reach], ROW, -1)
+    return shifted(field[-reach:], ROW, 1), down
+
+
+def paired(value, axis, apart):
+    count = lax.axis_size(axis)
+    came = lax.ppermute(value, axis, [(i, i ^ apart) for i in range(count)])
+    return added(value, came)
 
 
 def column_borders(field, up, down, reach):
@@ -365,7 +334,8 @@
         jnp.concatenate([part[:, columns] for part in (up, field, down)])
         for columns in (slice(-reach, None), slice(0, reach))
     )
-    return up, down, shifted(left, COL, 1), shifted(right, COL, -1)
+    right = shifted(right, COL, -1)
+    return up, down, shifted(left, COL, 1), right
 
 
 def exchanged(chunks, axes):
@@ -390,7 +360,6 @@
     padded_shape = (blocks, height + side - 1, LEFT + width + 8, LANES)
 
     each = rows // Z
-    top = rows // 2
     up, down = row_borders(features, reach)
     left, right = column_borders(features, up, down, reach)[2:]
     padded, conv, dbranch, dact, taps, params, expand, reduce = pl.pallas_call(
@@ -417,16 +386,15 @@
         ],
         compiler_params=PARAMS,
     )(
-        in_hbm(features), up, down, in_hbm(kernel), in_hbm(gain_row), in_hbm(scale_row),
+        in_hbm(features), down, up, in_hbm(kernel), in_hbm(gain_row), in_hbm(scale_row),
         in_hbm(cotangent), in_hbm(w_expand), in_hbm(w_reduce),
     )
-    sent, kept, sent_z, kept_z, dpre, xhat, rstd, padded, dscale = pl.pallas_call(
+    sent, kept, dpre, xhat, rstd, padded, dscale = pl.pallas_call(
         forward_kernel,
         name="forward",
         in_specs=[SMEM] + [VMEM] * 10,
-        out_specs=[VMEM] * 9,
-        out_shape=[shape((places, top + rows, channels), bf16)] * 2
-        + [shape((Z, places // 2, each, channels), bf16)] * 2
+        out_specs=[VMEM] * 7,
+        out_shape=[shape((places, 2 * rows, channels), bf16)] * 2
         + [
             shape((pixels, hidden), bf16),
             shape((blocks, pixels, LANES), f32),
@@ -439,58 +407,48 @@
             pltpu.VMEM((channels, pixels), bf16),
             pltpu.VMEM((channels, pixels), bf16),
         ],
-        input_output_aliases={3: 7},
+        input_output_aliases={3: 5},
         compiler_params=PARAMS,
     )(core, left, right, padded, conv, dbranch, dact, taps, params, expand, reduce)
 
     swap = [(0, 1), (1, 0)]
     came = lax.ppermute(sent, "core", swap)
-    came_z = lax.ppermute(sent_z, "core", swap)
-    dconv, small = pl.pallas_call(
+    dconv, small_sent, small = pl.pallas_call(
         functools.partial(backward_kernel, multiplier),
         name="backward",
-        in_specs=[VMEM] * 7,
-        out_specs=[VMEM] * 2,
+        in_specs=[SMEM] + [VMEM] * 7,
+        out_specs=[VMEM] * 3,
         out_shape=[
             shape((height, width, channels), bf16),
-            shape((places, 2 * SMALL, channels), bf16),
+            shape((SMALL, channels), bf16),
+            shape((SMALL, channels), bf16),
         ],
         scratch_shapes=[
             pltpu.VMEM((blocks, pixels, LANES), f32),
-            pltpu.VMEM((places * SMALL, channels), f32),
+            pltpu.VMEM((CORE * SMALL, channels), f32),
         ],
         compiler_params=PARAMS,
-    )(dpre, expand, xhat, rstd, padded, params, dscale)
-
-    small_came = lax.ppermute(small, "core", swap)
-    whole = top + rows + 2 * SMALL
+    )(core, dpre, expand, xhat, rstd, padded, params, dscale)
+
+    small_came = lax.ppermute(small_sent, "core", swap)
+    block = pl.BlockSpec((X, 2 * rows, channels), lambda i: (i, 0, 0))
     chip = pl.pallas_call(
         merge_kernel,
         name="merge",
         grid=(Y,),
-        in_specs=[pl.BlockSpec((X, top + rows, channels), lambda i: (i, 0, 0))] * 2
-        + [pl.BlockSpec((X, 2 * SMALL, channels), lambda i: (i, 0, 0))] * 2,
-        out_specs=pl.BlockSpec((X, whole, channels), lambda i: (i, 0, 0)),
-        out_shape=shape((places, whole, channels), bf16),
+        in_specs=[block] * 2,
+        out_specs=block,
+        out_shape=shape((places, 2 * rows, channels), bf16),
         compiler_params=GLUE_PARAMS,
-    )(kept, came, small, small_came)
-    chip, dconv, came_z, rows_came = lax.optimization_barrier(
-        (chip, dconv, came_z, row_borders(dconv, reach))
+    )(kept, came)
+    chip, dconv, small, small_came, rows_came = lax.optimization_barrier(
+        (chip, dconv, small, small_came, row_borders(dconv, reach))
     )
-    line = pl.pallas_call(
-        join_kernel,
-        name="join",
-        in_specs=[SMEM] + [VMEM] * 2,
-        out_specs=[VMEM] * Z,
-        out_shape=[shape(kept_z.shape[1:], bf16)] * Z,
-        compiler_params=GLUE_PARAMS,
-    )(lax.axis_index("z").reshape(1), kept_z, came_z)
-    line = [
-        part if step == 0 else lax.ppermute(part, "z", [(i, (i + step) % Z) for i in range(Z)])
-        for step, part in enumerate(line)
-    ]
-    chunks, edges, line = lax.optimization_barrier(
-        (exchanged(chip, ("y", "x")), column_borders(dconv, *rows_came, reach), line)
+    small = added(small, small_came)
+    for axis, apart in (("z", 1), ("z", 2), ("z", 4), ("x", 1), ("x", 2)):
+        small = paired(small, axis, apart)
+    chunks, edges, small = lax.optimization_barrier(
+        (exchanged(chip, ("y", "x")), column_borders(dconv, *rows_came, reach), small)
     )
     chunks = pl.pallas_call(
         plane_kernel,
@@ -498,30 +456,32 @@
         in_specs=[VMEM],
         out_specs=VMEM,
         out_shape=shape((Z, 2 * each, channels), bf16),
-        scratch_shapes=[pltpu.VMEM((whole, channels), f32)],
+        scratch_shapes=[pltpu.VMEM((2 * rows, channels), f32)],
         compiler_params=GLUE_PARAMS,
     )(chunks)
-    dexpand, half, chunks = pl.pallas_call(
+    chunks, small = lax.optimization_barrier((chunks, small))
+    for apart in (1, 2):
+        small = paired(small, "y", apart)
+    dreduce, dexpand = pl.pallas_call(
         functools.partial(line_kernel, multiplier),
         name="line",
-        in_specs=[VMEM] * (1 + Z),
+        in_specs=[VMEM],
+        out_specs=[VMEM] * 2,
+        out_shape=[
+            shape((each, channels), f32),
+            shape((channels * each // hidden, hidden), f32),
+        ],
+        compiler_params=GLUE_PARAMS,
+    )(exchanged(chunks, "z"))
+    dkernel, dgain, dscale = pl.pallas_call(
+        small_kernel,
+        name="small",
+        in_specs=[SMEM] + [VMEM] * 2,
         out_specs=[VMEM] * 3,
-        out_shape=[
-            shape((channels * each // hidden, hidden), f32),
-            shape((each, channels // 2), f32),
-            shape((places, each, channels), bf16),
-        ],
+        out_shape=[shape((side, side, channels), f32)] + [shape((1, channels), f32)] * 2,
+        scratch_shapes=[pltpu.VMEM((CORE, SMALL, channels), f32)],
         compiler_params=GLUE_PARAMS,
-    )(exchanged(chunks, "z"), *line)
-    dreduce, dkernel, dgain, dscale = pl.pallas_call(
-        functools.partial(last_kernel, multiplier),
-        name="last",
-        in_specs=[VMEM] * 2,
-        out_specs=[VMEM] * 4,
-        out_shape=[shape((each, channels), f32), shape((side, side, channels), f32)]
-        + [shape((1, channels), f32)] * 2,
-        compiler_params=GLUE_PARAMS,
-    )(exchanged(chunks, ("y", "x")), half)
+    )(core, small, lax.ppermute(small, "core", swap))
     grad_features = pl.pallas_call(
         feature_kernel,
         name="features",

time: 108 us -> 110 us (1.019)
  waiting for transfers between devices: 10.6 us -> 35.7 us
  blocking collectives: 13.6 us -> 0 us
  starting transfers between devices: 58.6 us -> 49.6 us
    ppermute x9, waiting for transfers between devices: 4.19 us -> 23.7 us  [the longest x7 23.7 us: paired(): came = lax.ppermute(value, axis, [(i, i ^ apart) for i in range(count)])]
    all_to_all x1 -> x0, blocking collectives: 13.6 us -> none  [exchanged(): return lax.all_to_all(chunks, axes, 0, 0, tiled=True)]
    ppermute x9, starting transfers between devices: 18.2 us -> 13.1 us  [the longest x7 11.7 us: paired(): came = lax.ppermute(value, axis, [(i, i ^ apart) for i in range(count)])]
    all_to_all x2, starting transfers between devices: 16.4 us -> 12.3 us  [exchanged(): return lax.all_to_all(chunks, axes, 0, 0, tiled=True)]
    ppermute x8, waiting for transfers between devices: 2.33 us -> 6.24 us  [shifted(): return lax.ppermute(value, axes, pairs)]
    all_to_all x2, waiting for transfers between devices: 4.12 us -> 5.76 us  [exchanged(): return lax.all_to_all(chunks, axes, 0, 0, tiled=True)]
    pallas_call x3 -> x2, Pallas kernels: 2.74 us -> 2.71 us  [the longest x1 2.02 us: shards(): pl.pallas_call(merge_kernel, name='merge', grid=(Y,), in_specs=[block] *...]
  transfers between devices with their start and end apart: 20 -> 20, of which waited for: 5 -> 8; matrix products, arithmetic and copies ran while one was open for 1% -> 1% of each run, Pallas kernels for 12% -> 12%
where the time goes in v7:
time: 110 us; the launch traced here: 109 us
  starting transfers between devices  49.6 us (45%)
  waiting for transfers between devices  35.7 us (32%)
  Pallas kernels  21 us (19%)
  local copies, waits for them, and re-layouts  1.97 us (2%)
    ppermute x7, waiting for transfers between devices, paired(): came = lax.ppermute(value, axis, [(i, i ^ apart) for i in range(count)])  23.7 us
    ppermute x8, starting transfers between devices, shifted(): return lax.ppermute(value, axes, pairs)  21.1 us
    all_to_all x2, starting transfers between devices, exchanged(): return lax.all_to_all(chunks, axes, 0, 0, tiled=True)  12.3 us
    ppermute x7, starting transfers between devices, paired(): came = lax.ppermute(value, axis, [(i, i ^ apart) for i in range(count)])  11.7 us
    pallas_call x1, Pallas kernels, shards(): pl.pallas_call(forward_kernel, name='forward', in_specs=[SMEM] + [VMEM] *...  6.26 us
    ppermute x8, waiting for transfers between devices, shifted(): return lax.ppermute(value, axes, pairs)  6.24 us
    all_to_all x2, waiting for transfers between devices, exchanged(): return lax.all_to_all(chunks, axes, 0, 0, tiled=True)  5.76 us
    pallas_call x1, Pallas kernels, shards(): pl.pallas_call(prepare_kernel, name='prepare', in_specs=[HBM] + [VMEM] *...  4.74 us
  transfers between devices with their start and end apart: 20, of which 8 were waited for; matrix products, arithmetic and copies ran while one was open for 1% of the time, Pallas kernels for 12%

profile of v7, /device:TPU:2, one launch (start us, length us, event | category | flops | bytes accessed | tf_op | source)
XLA Modules:
  0.0 109.5 jit_solution(9104454560605611690)
XLA Ops:
  0.6 1.0 fusion.3
  1.6 1.7 %collective-permute-start = (bf16[3,32,512]{2,1,0:T(8,128)(2,1)S(1)}, bf16[3,32,512]{2,1,0:T(8,128)(2,1)S(1)}, u32[]{:S(2)}, u32[]{:S(2)}) collective-permute-start(bf16[3,32,512]{2,1,0:T(8,128)(2,1)S(1)} %get-tuple-element.86), channel_id=1, source_target_pairs={{0,32},{32,64},{64,96},{96,128},{128,160},{160,192},{192,224},{1,3... | collective-permute-start | bytes 294920 | tf_op jit(solution)/shard_map/ppermute | solution.py:318
  3.3 1.3 %collective-permute-start.1 = (bf16[3,32,512]{2,1,0:T(8,128)(2,1)S(1)}, bf16[3,32,512]{2,1,0:T(8,128)(2,1)S(1)}, u32[]{:S(2)}, u32[]{:S(2)}) collective-permute-start(bf16[3,32,512]{2,1,0:T(8,128)(2,1)S(1)} %get-tuple-element.87), channel_id=1, source_target_pairs={{32,0},{64,32},{96,64},{128,96},{160,128},{192,160},{224,192},{33,... | collective-permute-start | bytes 294920 | tf_op jit(solution)/shard_map/ppermute | solution.py:318
  4.6 0.9 fusion.2
  5.6 2.3 %collective-permute-done.1.down = bf16[3,32,512]{2,1,0:T(8,128)(2,1)S(1)} collective-permute-done((bf16[3,32,512]{2,1,0:T(8,128)(2,1)S(1)}, bf16[3,32,512]{2,1,0:T(8,128)(2,1)S(1)}, u32[]{:S(2)}, u32[]{:S(2)}) %collective-permute-start.1) | collective-permute-done | bytes 98336 | tf_op jit(solution)/shard_map/ppermute | solution.py:318
  8.0 3.8 %collective-permute-start.2 = (bf16[14,3,512]{2,1,0:T(4,128)(2,1)S(1)}, bf16[14,3,512]{2,1,0:T(4,128)(2,1)S(1)}, u32[]{:S(2)}, u32[]{:S(2)}) collective-permute-start(bf16[14,3,512]{2,1,0:T(4,128)(2,1)S(1)} %pad_maximum_fusion), channel_id=1, source_target_pairs={{0,1},{1,2},{2,3},{3,4},{4,5},{5,6},{6,7},{7,8},{8,9},{9,10},{10,1... | collective-permute-start | bytes 129032 | tf_op jit(solution)/shard_map/ppermute | solution.py:318
  11.9 5.8 %collective-permute-start.3 = (bf16[14,3,512]{2,1,0:T(4,128)(2,1)S(1)}, bf16[14,3,512]{2,1,0:T(4,128)(2,1)S(1)}, u32[]{:S(2)}, u32[]{:S(2)}) collective-permute-start(bf16[14,3,512]{2,1,0:T(4,128)(2,1)S(1)} %pad_maximum_fusion.1), channel_id=1, source_target_pairs={{1,0},{2,1},{3,2},{4,3},{5,4},{6,5},{7,6},{8,7},{9,8},{10,9},{11,1... | collective-permute-start | bytes 129032 | tf_op jit(solution)/shard_map/ppermute | solution.py:318
  17.7 4.7 %prepare.1 = (f32[4,14,48,128]{3,2,1,0:T(8,128)S(1)}, f32[4,256,128]{2,1,0:T(8,128)S(1)}, bf16[256,512]{1,0:T(8,128)(2,1)S(1)}, f32[256,2048]{1,0:T(8,128)S(1)},...) custom-call(bf16[8,32,512]{2,1,0:T(8,128)(2,1)} %field_h.1, ...), custom_call_target="tpu_custom_call" | custom-call | tf_op jit(solution)/shard_map/prepare/pallas_call | solution.py:365
  22.5 6.3 %forward.1 = (bf16[16,128,512]{2,1,0:T(8,128)(2,1)S(1)}, bf16[16,128,512]{2,1,0:T(8,128)(2,1)S(1)}, bf16[256,2048]{1,0:T(8,128)(2,1)S(1)}, f32[4,256,128]{2,1,0:...) custom-call(s32[1]{0:T(128)} %bitcast.core_ref, ...), custom_call_target="tpu_custom_call", output_to_operand_aliasing={{5}: (3, {})} | custom-call | tf_op jit(solution)/shard_map/forward/pallas_call | solution.py:392
  28.7 3.1 %collective-permute-start.4 = (bf16[16,128,512]{2,1,0:T(8,128)(2,1)S(1)}, bf16[16,128,512]{2,1,0:T(8,128)(2,1)S(1)}, u32[]{:S(2)}, u32[]{:S(2)}) collective-permute-start(bf16[16,128,512]{2,1,0:T(8,128)(2,1)S(1)} %get-tuple-element.52), channel_id=1, source_target_pairs={{0,32},{32,0},{1,33},{33,1},{2,34},{34,2},{3,35},{35,3},{4,36},{36... | collective-permute-start | bytes 6291464 | tf_op jit(solution)/shard_map/ppermute | solution.py:415
  31.8 3.1 %backward.1 = (bf16[8,32,512]{2,1,0:T(8,128)(2,1)S(1)}, bf16[32,512]{1,0:T(8,128)(2,1)S(1)}, bf16[32,512]{1,0:T(8,128)(2,1)S(1)}) custom-call(s32[1]{0:T(128)} %bitcast.core_ref, bf16[256,2048]{1,0:T(8,128)(2,1)S(1)} %get-tuple-element.53.dpre, bf16[512,2048]{1,0:T(8,128)(2,1)S(1)} %get-tuple-element.49.expand, f32[4,256,128]{2,1,0:T(8,128)S(1)} %get-tuple-element.54.xhat, ...), custom_call_target="tpu_custom_call" | custom-call | tf_op jit(solution)/shard_map/backward/pallas_call | solution.py:416
  34.9 1.3 %collective-permute-start.7 = (bf16[3,32,512]{2,1,0:T(8,128)(2,1)S(1)}, bf16[3,32,512]{2,1,0:T(8,128)(2,1)S(1)}, u32[]{:S(2)}, u32[]{:S(2)}) collective-permute-start(bf16[3,32,512]{2,1,0:T(8,128)(2,1)S(1)} %get-tuple-element.82), channel_id=1, source_target_pairs={{32,0},{64,32},{96,64},{128,96},{160,128},{192,160},{224,192},{33,... | collective-permute-start | bytes 294920 | tf_op jit(solution)/shard_map/ppermute | solution.py:318
  36.2 3.0 %collective-permute-start.6 = (bf16[3,32,512]{2,1,0:T(8,128)(2,1)S(1)}, bf16[3,32,512]{2,1,0:T(8,128)(2,1)S(1)}, u32[]{:S(2)}, u32[]{:S(2)}) collective-permute-start(bf16[3,32,512]{2,1,0:T(8,128)(2,1)S(1)} %get-tuple-element.83), channel_id=1, source_target_pairs={{0,32},{32,64},{64,96},{96,128},{128,160},{160,192},{192,224},{1,3... | collective-permute-start | bytes 294920 | tf_op jit(solution)/shard_map/ppermute | solution.py:318
  39.3 1.3 %collective-permute-start.5 = (bf16[32,512]{1,0:T(8,128)(2,1)S(1)}, bf16[32,512]{1,0:T(8,128)(2,1)S(1)}, u32[]{:S(2)}, u32[]{:S(2)}) collective-permute-start(bf16[32,512]{1,0:T(8,128)(2,1)S(1)} %get-tuple-element.60), channel_id=1, source_target_pairs={{0,32},{32,0},{1,33},{33,1},{2,34},{34,2},{3,35},{35,3},{4,36},{36... | collective-permute-start | bytes 98312 | tf_op jit(solution)/shard_map/ppermute | solution.py:433
  40.6 2.0 %merge.1 = bf16[16,128,512]{2,1,0:T(8,128)(2,1)} custom-call(bf16[16,128,512]{2,1,0:T(8,128)(2,1)S(1)} %get-tuple-element.51.kept, bf16[16,128,512]{2,1,0:T(8,128)(2,1)S(1)} %collective-permute-done.4.came), custom_call_target="tpu_custom_call" | custom-call | tf_op jit(solution)/shard_map/merge/pallas_call | solution.py:435
  42.7 7.7 %all-to-all-start = ((bf16[16,128,512]{2,1,0:T(8,128)(2,1)}), bf16[16,128,512]{2,1,0:T(8,128)(2,1)S(1)}, u32[]{:S(2)}, u32[]{:S(2)}) async-start(bf16[16,128,512]{2,1,0:T(8,128)(2,1)} %merge.1), calls=%async_computation | async-start | bytes 4194304 | tf_op jit(solution)/shard_map/all_to_all | solution.py:342
  50.5 3.9 %collective-permute-done.10 = bf16[32,512]{1,0:T(8,128)(2,1)S(1)} collective-permute-done((bf16[32,512]{1,0:T(8,128)(2,1)S(1)}, bf16[32,512]{1,0:T(8,128)(2,1)S(1)}, u32[]{:S(2)}, u32[]{:S(2)}) %collective-permute-start.10) | collective-permute-done | bytes 32800 | tf_op jit(solution)/shard_map/ppermute | solution.py:328
  55.0 4.3 %collective-permute-done.11 = bf16[32,512]{1,0:T(8,128)(2,1)S(1)} collective-permute-done((bf16[32,512]{1,0:T(8,128)(2,1)S(1)}, bf16[32,512]{1,0:T(8,128)(2,1)S(1)}, u32[]{:S(2)}, u32[]{:S(2)}) %collective-permute-start.11) | collective-permute-done | bytes 32800 | tf_op jit(solution)/shard_map/ppermute | solution.py:328
  59.4 4.4 %collective-permute-start.12 = (bf16[32,512]{1,0:T(8,128)(2,1)S(1)}, bf16[32,512]{1,0:T(8,128)(2,1)S(1)}, u32[]{:S(2)}, u32[]{:S(2)}) collective-permute-start(bf16[32,512]{1,0:T(8,128)(2,1)S(1)} %add_convert_fusion.5), channel_id=1, source_target_pairs={{0,4},{1,5},{2,6},{3,7},{4,0},{5,1},{6,2},{7,3},{8,12},{9,13},{10,... | collective-permute-start | bytes 98312 | tf_op jit(solution)/shard_map/ppermute | solution.py:328
  63.8 3.4 %collective-permute-done.12 = bf16[32,512]{1,0:T(8,128)(2,1)S(1)} collective-permute-done((bf16[32,512]{1,0:T(8,128)(2,1)S(1)}, bf16[32,512]{1,0:T(8,128)(2,1)S(1)}, u32[]{:S(2)}, u32[]{:S(2)}) %collective-permute-start.12) | collective-permute-done | bytes 32800 | tf_op jit(solution)/shard_map/ppermute | solution.py:328
  67.5 1.9 %collective-permute-start.8 = (bf16[14,3,512]{2,1,0:T(4,128)(2,1)S(1)}, bf16[14,3,512]{2,1,0:T(4,128)(2,1)S(1)}, u32[]{:S(2)}, u32[]{:S(2)}) collective-permute-start(bf16[14,3,512]{2,1,0:T(4,128)(2,1)S(1)} %pad_maximum_fusion.2), channel_id=1, source_target_pairs={{0,1},{1,2},{2,3},{3,4},{4,5},{5,6},{6,7},{7,8},{8,9},{9,10},{10,1... | collective-permute-start | bytes 129032 | tf_op jit(solution)/shard_map/ppermute | solution.py:318
  69.4 8.4 %collective-permute-done.13 = bf16[32,512]{1,0:T(8,128)(2,1)S(1)} collective-permute-done((bf16[32,512]{1,0:T(8,128)(2,1)S(1)}, bf16[32,512]{1,0:T(8,128)(2,1)S(1)}, u32[]{:S(2)}, u32[]{:S(2)}) %collective-permute-start.13) | collective-permute-done | bytes 32800 | tf_op jit(solution)/shard_map/ppermute | solution.py:328
  77.9 3.6 %collective-permute-start.14 = (bf16[32,512]{1,0:T(8,128)(2,1)S(1)}, bf16[32,512]{1,0:T(8,128)(2,1)S(1)}, u32[]{:S(2)}, u32[]{:S(2)}) collective-permute-start(bf16[32,512]{1,0:T(8,128)(2,1)S(1)} %add_convert_fusion.3), channel_id=1, source_target_pairs={{0,16},{8,24},{16,0},{24,8},{1,17},{9,25},{17,1},{25,9},{2,18},{10... | collective-permute-start | bytes 98312 | tf_op jit(solution)/shard_map/ppermute | solution.py:328
  81.5 2.1 %collective-permute-start.9 = (bf16[14,3,512]{2,1,0:T(4,128)(2,1)S(1)}, bf16[14,3,512]{2,1,0:T(4,128)(2,1)S(1)}, u32[]{:S(2)}, u32[]{:S(2)}) collective-permute-start(bf16[14,3,512]{2,1,0:T(4,128)(2,1)S(1)} %pad_maximum_fusion.3), channel_id=1, source_target_pairs={{1,0},{2,1},{3,2},{4,3},{5,4},{6,5},{7,6},{8,7},{9,8},{10,9},{11,1... | collective-permute-start | bytes 129032 | tf_op jit(solution)/shard_map/ppermute | solution.py:318
  83.6 3.9 %collective-permute-done.9.right = bf16[14,3,512]{2,1,0:T(4,128)(2,1)S(1)} collective-permute-done((bf16[14,3,512]{2,1,0:T(4,128)(2,1)S(1)}, bf16[14,3,512]{2,1,0:T(4,128)(2,1)S(1)}, u32[]{:S(2)}, u32[]{:S(2)}) %collective-permute-start.9) | collective-permute-done | bytes 43040 | tf_op jit(solution)/shard_map/ppermute | solution.py:318
  87.5 1.1 plane.1
  88.9 3.7 %collective-permute-done.15 = bf16[32,512]{1,0:T(8,128)(2,1)S(1)} collective-permute-done((bf16[32,512]{1,0:T(8,128)(2,1)S(1)}, bf16[32,512]{1,0:T(8,128)(2,1)S(1)}, u32[]{:S(2)}, u32[]{:S(2)}) %collective-permute-start.15) | collective-permute-done | bytes 32800 | tf_op jit(solution)/shard_map/ppermute | solution.py:328
  92.5 2.6 %collective-permute-start.16 = (bf16[32,512]{1,0:T(8,128)(2,1)S(1)}, bf16[32,512]{1,0:T(8,128)(2,1)S(1)}, u32[]{:S(2)}, u32[]{:S(2)}) collective-permute-start(bf16[32,512]{1,0:T(8,128)(2,1)S(1)} %add_convert_fusion.1), channel_id=1, source_target_pairs={{0,128},{64,192},{128,0},{192,64},{1,129},{65,193},{129,1},{193,65... | collective-permute-start | bytes 98312 | tf_op jit(solution)/shard_map/ppermute | solution.py:328
  95.1 4.6 %all-to-all-start.1 = ((bf16[8,16,512]{2,1,0:T(8,128)(2,1)}), bf16[8,16,512]{2,1,0:T(8,128)(2,1)S(1)}, u32[]{:S(2)}, u32[]{:S(2)}) async-start(bf16[8,16,512]{2,1,0:T(8,128)(2,1)} %plane.1), calls=%async_computation.1 | async-start | bytes 262144 | tf_op jit(solution)/shard_map/all_to_all | solution.py:342
  99.9 2.5 %features.1 = bf16[8,32,512]{2,1,0:T(8,128)(2,1)} custom-call(bf16[8,32,512]{2,1,0:T(8,128)(2,1)S(1)} %get-tuple-element.61.field, bf16[3,32,512]{2,1,0:T(8,128)(2,1)S(1)} %collective-permute-done.6.up, bf16[3,32,512]{2,1,0:T(8,128)(2,1)S(1)} %collective-permute-done.7.down, bf16[14,3,512]{2,1,0:T(4,128)(2,1)S(1)} %collective-permute-done.8.left, ...), custom_call_target="tpu_custom_call" | custom-call | tf_op jit(solution)/shard_map/features/pallas_call | solution.py:485
  102.4 0.7 small.1
  103.1 5.8 %all-to-all-done.1.chunks = bf16[8,16,512]{2,1,0:T(8,128)(2,1)S(1)} async-done(((bf16[8,16,512]{2,1,0:T(8,128)(2,1)}), bf16[8,16,512]{2,1,0:T(8,128)(2,1)S(1)}, u32[]{:S(2)}, u32[]{:S(2)}) %all-to-all-start.1) | async-done | bytes 131104 | tf_op jit(solution)/shard_map/all_to_all | solution.py:342
  (39 shorter events, 2.2 us)
Async XLA Ops:
  1.6 4.0 %collective-permute-start = (bf16[3,32,512]{2,1,0:T(8,128)(2,1)S(1)}, bf16[3,32,512]{2,1,0:T(8,128)(2,1)S(1)}, u32[]{:S(2)}, u32[]{:S(2)}) collective-permute-start(bf16[3,32,512]{2,1,0:T(8,128)(2,1)S(1)} %get-tuple-element.86), channel_id=1, source_target_pairs={{0,32},{32,64},{64,96},{96,128},{128,160},{160,192},{192,224},{1,3... | collective-permute-start | bytes 294920 | tf_op jit(solution)/shard_map/ppermute | solution.py:318
  3.3 4.6 %collective-permute-start.1 = (bf16[3,32,512]{2,1,0:T(8,128)(2,1)S(1)}, bf16[3,32,512]{2,1,0:T(8,128)(2,1)S(1)}, u32[]{:S(2)}, u32[]{:S(2)}) collective-permute-start(bf16[3,32,512]{2,1,0:T(8,128)(2,1)S(1)} %get-tuple-element.87), channel_id=1, source_target_pairs={{32,0},{64,32},{96,64},{128,96},{160,128},{192,160},{224,192},{33,... | collective-permute-start | bytes 294920 | tf_op jit(solution)/shard_map/ppermute | solution.py:318
  8.0 14.5 %collective-permute-start.2 = (bf16[14,3,512]{2,1,0:T(4,128)(2,1)S(1)}, bf16[14,3,512]{2,1,0:T(4,128)(2,1)S(1)}, u32[]{:S(2)}, u32[]{:S(2)}) collective-permute-start(bf16[14,3,512]{2,1,0:T(4,128)(2,1)S(1)} %pad_maximum_fusion), channel_id=1, source_target_pairs={{0,1},{1,2},{2,3},{3,4},{4,5},{5,6},{6,7},{7,8},{8,9},{9,10},{10,1... | collective-permute-start | bytes 129032 | tf_op jit(solution)/shard_map/ppermute | solution.py:318
  11.9 10.6 %collective-permute-start.3 = (bf16[14,3,512]{2,1,0:T(4,128)(2,1)S(1)}, bf16[14,3,512]{2,1,0:T(4,128)(2,1)S(1)}, u32[]{:S(2)}, u32[]{:S(2)}) collective-permute-start(bf16[14,3,512]{2,1,0:T(4,128)(2,1)S(1)} %pad_maximum_fusion.1), channel_id=1, source_target_pairs={{1,0},{2,1},{3,2},{4,3},{5,4},{6,5},{7,6},{8,7},{9,8},{10,9},{11,1... | collective-permute-start | bytes 129032 | tf_op jit(solution)/shard_map/ppermute | solution.py:318
  28.7 11.9 %collective-permute-start.4 = (bf16[16,128,512]{2,1,0:T(8,128)(2,1)S(1)}, bf16[16,128,512]{2,1,0:T(8,128)(2,1)S(1)}, u32[]{:S(2)}, u32[]{:S(2)}) collective-permute-start(bf16[16,128,512]{2,1,0:T(8,128)(2,1)S(1)} %get-tuple-element.52), channel_id=1, source_target_pairs={{0,32},{32,0},{1,33},{33,1},{2,34},{34,2},{3,35},{35,3},{4,36},{36... | collective-permute-start | bytes 6291464 | tf_op jit(solution)/shard_map/ppermute | solution.py:415
  34.9 7.7 %collective-permute-start.7 = (bf16[3,32,512]{2,1,0:T(8,128)(2,1)S(1)}, bf16[3,32,512]{2,1,0:T(8,128)(2,1)S(1)}, u32[]{:S(2)}, u32[]{:S(2)}) collective-permute-start(bf16[3,32,512]{2,1,0:T(8,128)(2,1)S(1)} %get-tuple-element.82), channel_id=1, source_target_pairs={{32,0},{64,32},{96,64},{128,96},{160,128},{192,160},{224,192},{33,... | collective-permute-start | bytes 294920 | tf_op jit(solution)/shard_map/ppermute | solution.py:318
  36.2 6.4 %collective-permute-start.6 = (bf16[3,32,512]{2,1,0:T(8,128)(2,1)S(1)}, bf16[3,32,512]{2,1,0:T(8,128)(2,1)S(1)}, u32[]{:S(2)}, u32[]{:S(2)}) collective-permute-start(bf16[3,32,512]{2,1,0:T(8,128)(2,1)S(1)} %get-tuple-element.83), channel_id=1, source_target_pairs={{0,32},{32,64},{64,96},{96,128},{128,160},{160,192},{192,224},{1,3... | collective-permute-start | bytes 294920 | tf_op jit(solution)/shard_map/ppermute | solution.py:318
  39.3 3.4 %collective-permute-start.5 = (bf16[32,512]{1,0:T(8,128)(2,1)S(1)}, bf16[32,512]{1,0:T(8,128)(2,1)S(1)}, u32[]{:S(2)}, u32[]{:S(2)}) collective-permute-start(bf16[32,512]{1,0:T(8,128)(2,1)S(1)} %get-tuple-element.60), channel_id=1, source_target_pairs={{0,32},{32,0},{1,33},{33,1},{2,34},{34,2},{3,35},{35,3},{4,36},{36... | collective-permute-start | bytes 98312 | tf_op jit(solution)/shard_map/ppermute | solution.py:433
  42.7 44.9 %all-to-all-start = ((bf16[16,128,512]{2,1,0:T(8,128)(2,1)}), bf16[16,128,512]{2,1,0:T(8,128)(2,1)S(1)}, u32[]{:S(2)}, u32[]{:S(2)}) async-start(bf16[16,128,512]{2,1,0:T(8,128)(2,1)} %merge.1), calls=%async_computation | async-start | bytes 4194304 | tf_op jit(solution)/shard_map/all_to_all | solution.py:342
  50.4 49.5 %copy-start = (bf16[8,32,512]{2,1,0:T(8,128)(2,1)S(1)}, bf16[8,32,512]{2,1,0:T(8,128)(2,1)}, u32[]{:S(2)}) copy-start(bf16[8,32,512]{2,1,0:T(8,128)(2,1)} %cotangent.1) | copy-start | bytes 786436
  50.4 49.5 %copy-start.1 = (f32[7,7,512]{2,1,0:T(8,128)S(1)}, f32[7,7,512]{2,1,0:T(8,128)}, u32[]{:S(2)}) copy-start(f32[7,7,512]{2,1,0:T(8,128)} %taps.1) | copy-start | bytes 301060
  50.4 4.0 %collective-permute-start.10 = (bf16[32,512]{1,0:T(8,128)(2,1)S(1)}, bf16[32,512]{1,0:T(8,128)(2,1)S(1)}, u32[]{:S(2)}, u32[]{:S(2)}) collective-permute-start(bf16[32,512]{1,0:T(8,128)(2,1)S(1)} %add_convert_fusion.7), channel_id=1, source_target_pairs={{0,1},{1,0},{2,3},{3,2},{4,5},{5,4},{6,7},{7,6},{8,9},{9,8},{10,11... | collective-permute-start | bytes 98312 | tf_op jit(solution)/shard_map/ppermute | solution.py:328
  54.4 4.9 %collective-permute-start.11 = (bf16[32,512]{1,0:T(8,128)(2,1)S(1)}, bf16[32,512]{1,0:T(8,128)(2,1)S(1)}, u32[]{:S(2)}, u32[]{:S(2)}) collective-permute-start(bf16[32,512]{1,0:T(8,128)(2,1)S(1)} %add_convert_fusion.6), channel_id=1, source_target_pairs={{0,2},{1,3},{2,0},{3,1},{4,6},{5,7},{6,4},{7,5},{8,10},{9,11},{10,... | collective-permute-start | bytes 98312 | tf_op jit(solution)/shard_map/ppermute | solution.py:328
  59.4 7.9 %collective-permute-start.12 = (bf16[32,512]{1,0:T(8,128)(2,1)S(1)}, bf16[32,512]{1,0:T(8,128)(2,1)S(1)}, u32[]{:S(2)}, u32[]{:S(2)}) collective-permute-start(bf16[32,512]{1,0:T(8,128)(2,1)S(1)} %add_convert_fusion.5), channel_id=1, source_target_pairs={{0,4},{1,5},{2,6},{3,7},{4,0},{5,1},{6,2},{7,3},{8,12},{9,13},{10,... | collective-permute-start | bytes 98312 | tf_op jit(solution)/shard_map/ppermute | solution.py:328
  67.3 10.6 %collective-permute-start.13 = (bf16[32,512]{1,0:T(8,128)(2,1)S(1)}, bf16[32,512]{1,0:T(8,128)(2,1)S(1)}, u32[]{:S(2)}, u32[]{:S(2)}) collective-permute-start(bf16[32,512]{1,0:T(8,128)(2,1)S(1)} %add_convert_fusion.4), channel_id=1, source_target_pairs={{0,8},{8,0},{16,24},{24,16},{1,9},{9,1},{17,25},{25,17},{2,10},{10... | collective-permute-start | bytes 98312 | tf_op jit(solution)/shard_map/ppermute | solution.py:328
  67.5 16.1 %collective-permute-start.8 = (bf16[14,3,512]{2,1,0:T(4,128)(2,1)S(1)}, bf16[14,3,512]{2,1,0:T(4,128)(2,1)S(1)}, u32[]{:S(2)}, u32[]{:S(2)}) collective-permute-start(bf16[14,3,512]{2,1,0:T(4,128)(2,1)S(1)} %pad_maximum_fusion.2), channel_id=1, source_target_pairs={{0,1},{1,2},{2,3},{3,4},{4,5},{5,6},{6,7},{7,8},{8,9},{9,10},{10,1... | collective-permute-start | bytes 129032 | tf_op jit(solution)/shard_map/ppermute | solution.py:318
  77.9 5.7 %collective-permute-start.14 = (bf16[32,512]{1,0:T(8,128)(2,1)S(1)}, bf16[32,512]{1,0:T(8,128)(2,1)S(1)}, u32[]{:S(2)}, u32[]{:S(2)}) collective-permute-start(bf16[32,512]{1,0:T(8,128)(2,1)S(1)} %add_convert_fusion.3), channel_id=1, source_target_pairs={{0,16},{8,24},{16,0},{24,8},{1,17},{9,25},{17,1},{25,9},{2,18},{10... | collective-permute-start | bytes 98312 | tf_op jit(solution)/shard_map/ppermute | solution.py:328
  81.5 6.1 %collective-permute-start.9 = (bf16[14,3,512]{2,1,0:T(4,128)(2,1)S(1)}, bf16[14,3,512]{2,1,0:T(4,128)(2,1)S(1)}, u32[]{:S(2)}, u32[]{:S(2)}) collective-permute-start(bf16[14,3,512]{2,1,0:T(4,128)(2,1)S(1)} %pad_maximum_fusion.3), channel_id=1, source_target_pairs={{1,0},{2,1},{3,2},{4,3},{5,4},{6,5},{7,6},{8,7},{9,8},{10,9},{11,1... | collective-permute-start | bytes 129032 | tf_op jit(solution)/shard_map/ppermute | solution.py:318
  88.6 3.9 %collective-permute-start.15 = (bf16[32,512]{1,0:T(8,128)(2,1)S(1)}, bf16[32,512]{1,0:T(8,128)(2,1)S(1)}, u32[]{:S(2)}, u32[]{:S(2)}) collective-permute-start(bf16[32,512]{1,0:T(8,128)(2,1)S(1)} %add_convert_fusion.2), channel_id=1, source_target_pairs={{0,64},{64,0},{128,192},{192,128},{1,65},{65,1},{129,193},{193,129... | collective-permute-start | bytes 98312 | tf_op jit(solution)/shard_map/ppermute | solution.py:328
  92.5 7.2 %collective-permute-start.16 = (bf16[32,512]{1,0:T(8,128)(2,1)S(1)}, bf16[32,512]{1,0:T(8,128)(2,1)S(1)}, u32[]{:S(2)}, u32[]{:S(2)}) collective-permute-start(bf16[32,512]{1,0:T(8,128)(2,1)S(1)} %add_convert_fusion.1), channel_id=1, source_target_pairs={{0,128},{64,192},{128,0},{192,64},{1,129},{65,193},{129,1},{193,65... | collective-permute-start | bytes 98312 | tf_op jit(solution)/shard_map/ppermute | solution.py:328
  95.1 13.7 %all-to-all-start.1 = ((bf16[8,16,512]{2,1,0:T(8,128)(2,1)}), bf16[8,16,512]{2,1,0:T(8,128)(2,1)S(1)}, u32[]{:S(2)}, u32[]{:S(2)}) async-start(bf16[8,16,512]{2,1,0:T(8,128)(2,1)} %plane.1), calls=%async_computation.1 | async-start | bytes 262144 | tf_op jit(solution)/shard_map/all_to_all | solution.py:342
  99.8 2.6 %collective-permute-start.17 = (bf16[32,512]{1,0:T(8,128)(2,1)S(1)}, bf16[32,512]{1,0:T(8,128)(2,1)S(1)}, u32[]{:S(2)}, u32[]{:S(2)}) collective-permute-start(bf16[32,512]{1,0:T(8,128)(2,1)S(1)} %add_convert_fusion.own), channel_id=1, source_target_pairs={{0,32},{32,0},{1,33},{33,1},{2,34},{34,2},{3,35},{35,3},{4,36},{36... | collective-permute-start | bytes 98312 | tf_op jit(solution)/shard_map/ppermute | solution.py:484

commit v8 on v7

--- a/solution.py
+++ b/solution.py
@@ -15,7 +15,7 @@
 INV_ROOT_TWO_PI = 1.0 / math.sqrt(2.0 * math.pi)
 LANES = 128
 LEFT = 8
-SMALL = 32
+SMALL = 4
 
 NN = (((1,), (0,)), ((), ()))
 NT = (((1,), (1,)), ((), ()))
@@ -37,10 +37,16 @@
 
 
 def fill_sides(padded, left, right, width, reach):
+    rows = padded.shape[1]
+    places = ((0, rows - reach, reach), (reach, reach, rows - 2 * reach), (rows - reach, 0, reach))
     for block in range(padded.shape[0]):
         lanes = pl.ds(block * LANES, LANES)
-        padded[block, :, pl.ds(LEFT - reach, reach), :] = left[:, :, lanes].astype(jnp.float32)
-        padded[block, :, pl.ds(LEFT + width, reach), :] = right[:, :, lanes].astype(jnp.float32)
+        for side, column in ((left, LEFT - reach), (right, LEFT + width)):
+            value = side[:, :, lanes].astype(jnp.float32)
+            for source, target, count in places:
+                padded[block, pl.ds(target, count), pl.ds(column, reach), :] = value[
+                    source : source + count
+                ]
 
 
 def depthwise(padded, taps, block, first_col, height, side, flip):
@@ -73,8 +79,8 @@
 
 
 def prepare_kernel(
-    field_h, down, up, taps_h, gain_h, scale_h, cotangent_h, expand_h, reduce_h,
-    padded, conv, dbranch, dact, taps, rows_out, expand, reduce,
+    field_h, up, down, taps_h, gain_h, scale_h, cotangent_h, expand_h, reduce_h,
+    padded, conv, dbranch, taps, rows_out, expand, reduce,
     field, gain, scale, cotangent, sems,
 ):
     copies = [
@@ -98,25 +104,19 @@
     height, width, channels = field.shape
     fill_own(padded, field, up, down, taps.shape[0] // 2)
     conv_columns(conv, padded, taps, height, width, range(8, width - 8, 8))
-    for copy in copies[2:]:
+    for copy in copies[2:5]:
         copy.wait()
     rows_out[pl.ds(0, 8), :] = jnp.broadcast_to(gain[...], (8, channels))
     rows_out[pl.ds(8, 8), :] = jnp.broadcast_to(scale[...], (8, channels))
     for row in range(height):
         value = cotangent[row].astype(jnp.float32) * scale[...]
         dbranch[pl.ds(row * width, width), :] = value.astype(jnp.bfloat16)
-    step = 2 * LANES
-
-    def hidden_block(chunk, _):
-        hidden = pl.ds(pl.multiple_of(chunk * step, step), step)
-        dact[:, hidden] = product(dbranch[...], reduce[hidden, :], NT)
-        return 0
-
-    lax.fori_loop(0, reduce.shape[0] // step, hidden_block, 0)
+    for copy in copies[5:]:
+        copy.wait()
 
 
 def forward_kernel(
-    core_ref, left, right, padded_in, conv, dbranch, dact, taps, rows_in, expand, reduce,
+    core_ref, left, right, padded_in, conv, dbranch, taps, rows_in, expand, reduce,
     sent, kept, dpre_out, xhat_out, rstd_out, padded, dscale_out,
     normed, turned, chosen,
 ):
@@ -163,10 +163,11 @@
             chunk = y * CORE + owner
             hidden = pl.ds(pl.multiple_of(chunk * step, step), step)
             pre = product(normed[...], expand[:, hidden], NN)
+            dact = product(dbranch[...], reduce[hidden, :], NT)
             half = 0.5 * (1.0 + lax.erf(pre * INV_ROOT_TWO))
             slope = half + pre * jnp.exp(-0.5 * pre * pre) * INV_ROOT_TWO_PI
             act = (pre * half).astype(jnp.bfloat16)
-            dpre = (dact[:, hidden] * slope).astype(jnp.bfloat16)
+            dpre = (dact * slope).astype(jnp.bfloat16)
             dpre_out[:, hidden] = dpre
             share = product(act, dbranch[...], TN)
             weighed = share * reduce[hidden, :].astype(jnp.float32)
@@ -187,8 +188,7 @@
 
 
 def backward_kernel(
-    multiplier, core_ref, dpre, expand, xhat, rstd, padded, rows, dscale,
-    dconv_out, sent, kept, dconv, small,
+    multiplier, dpre, expand, xhat, rstd, padded, rows, dscale, dconv_out, out, dconv, small
 ):
     height, width, channels = dconv_out.shape
     blocks = channels // LANES
@@ -239,9 +239,9 @@
         return 0
 
     lax.fori_loop(0, blocks, tap_block, 0)
-    for out, core in ((sent, 1 - core_ref[0]), (kept, core_ref[0])):
-        half = small[pl.ds(pl.multiple_of(core * SMALL, SMALL), SMALL), :]
-        out[...] = half.astype(jnp.bfloat16)
+    for place in range(out.shape[0]):
+        part = small[pl.ds(place * SMALL, SMALL), :]
+        out[place] = jnp.concatenate([part, jnp.zeros_like(part)]).astype(jnp.bfloat16)
 
 
 def feature_kernel(field, up, down, left, right, taps, cotangent, out, padded):
@@ -264,41 +264,48 @@
     return (left.astype(jnp.float32) + right.astype(jnp.float32)).astype(jnp.bfloat16)
 
 
-def merge_kernel(kept, came, out):
-    out[...] = added(kept[...], came[...])
+def merge_kernel(kept, came, small, small_came, out):
+    rows = kept.shape[1]
+    out[:, pl.ds(0, rows), :] = added(kept[...], came[...])
+    out[:, pl.ds(rows, small.shape[1]), :] = added(small[...], small_came[...])
 
 
 def plane_kernel(chunks, out, total):
     total[...] = jnp.sum(chunks[...].astype(jnp.float32), axis=0)
-    each = out.shape[1] // 2
+    each = (out.shape[1] - 2 * SMALL) // 2
     top = each * Z
+    small = total[pl.ds(2 * top, 2 * SMALL), :].astype(jnp.bfloat16)
     for z in range(Z):
         parts = [total[pl.ds(z * each, each), :]]
         parts += [total[pl.ds(top + q * 2 * Z + 2 * z, 2), :] for q in range(each // 2)]
-        out[z] = jnp.concatenate(parts).astype(jnp.bfloat16)
-
-
-def line_kernel(multiplier, chunks, dreduce, dexpand):
+        out[z, pl.ds(0, 2 * each), :] = jnp.concatenate(parts).astype(jnp.bfloat16)
+        out[z, pl.ds(2 * each, 2 * SMALL), :] = small
+
+
+def line_kernel(multiplier, chunks, dreduce, dexpand, out):
     total = jnp.sum(chunks[...].astype(jnp.float32), axis=0)
     each, channels = dreduce.shape
     dreduce[...] = total[:each] * multiplier
     for q in range(each // 2):
         part = total[each + 2 * q : each + 2 * q + 2]
         dexpand[:, pl.ds(q * channels, channels)] = part * multiplier
-
-
-def small_kernel(core_ref, own, other, dkernel, dgain, dscale, full):
-    full[core_ref[0]] = own[...].astype(jnp.float32)
-    full[1 - core_ref[0]] = other[...].astype(jnp.float32)
+    small = total[2 * each :].astype(jnp.bfloat16)
+    out[...] = jnp.broadcast_to(small[None], out.shape)
+
+
+def small_kernel(chunks, dkernel, dgain, dscale):
     side = dkernel.shape[0]
-    for tap in range(side * side + 2):
-        value = full[tap // SMALL, pl.ds(tap % SMALL, 1), :]
-        if tap < side * side:
-            dkernel[tap // side, pl.ds(tap % side, 1), :] = value
-        elif tap == side * side:
-            dgain[...] = value
-        else:
-            dscale[...] = value
+    for place in range(chunks.shape[0]):
+        part = chunks[place].astype(jnp.float32)
+        for row in range(SMALL):
+            tap = place * SMALL + row
+            value = part[row : row + 1]
+            if tap < side * side:
+                dkernel[tap // side, pl.ds(tap % side, 1), :] = value
+            elif tap == side * side:
+                dgain[...] = value
+            elif tap == side * side + 1:
+                dscale[...] = value
 
 
 VMEM = pl.BlockSpec(memory_space=pltpu.VMEM)
@@ -319,23 +326,15 @@
 
 
 def row_borders(field, reach):
-    down = shifted(field[:reach], ROW, -1)
-    return shifted(field[-reach:], ROW, 1), down
-
-
-def paired(value, axis, apart):
-    count = lax.axis_size(axis)
-    came = lax.ppermute(value, axis, [(i, i ^ apart) for i in range(count)])
-    return added(value, came)
+    return shifted(field[-reach:], ROW, 1), shifted(field[:reach], ROW, -1)
 
 
 def column_borders(field, up, down, reach):
     left, right = (
-        jnp.concatenate([part[:, columns] for part in (up, field, down)])
+        jnp.concatenate([part[:, columns] for part in (down, field, up)])
         for columns in (slice(-reach, None), slice(0, reach))
     )
-    right = shifted(right, COL, -1)
-    return up, down, shifted(left, COL, 1), right
+    return up, down, shifted(left, COL, 1), shifted(right, COL, -1)
 
 
 def exchanged(chunks, axes):
@@ -362,16 +361,15 @@
     each = rows // Z
     up, down = row_borders(features, reach)
     left, right = column_borders(features, up, down, reach)[2:]
-    padded, conv, dbranch, dact, taps, params, expand, reduce = pl.pallas_call(
+    padded, conv, dbranch, taps, params, expand, reduce = pl.pallas_call(
         prepare_kernel,
         name="prepare",
         in_specs=[HBM] + [VMEM] * 2 + [HBM] * 6,
-        out_specs=[VMEM] * 8,
+        out_specs=[VMEM] * 7,
         out_shape=[
             shape(padded_shape, f32),
             shape((blocks, pixels, LANES), f32),
             shape((pixels, channels), bf16),
-            shape((pixels, hidden), f32),
             shape(kernel.shape, f32),
             shape((16, channels), f32),
             shape(w_expand.shape, bf16),
@@ -386,13 +384,13 @@
         ],
         compiler_params=PARAMS,
     )(
-        in_hbm(features), down, up, in_hbm(kernel), in_hbm(gain_row), in_hbm(scale_row),
+        in_hbm(features), up, down, in_hbm(kernel), in_hbm(gain_row), in_hbm(scale_row),
         in_hbm(cotangent), in_hbm(w_expand), in_hbm(w_reduce),
     )
     sent, kept, dpre, xhat, rstd, padded, dscale = pl.pallas_call(
         forward_kernel,
         name="forward",
-        in_specs=[SMEM] + [VMEM] * 10,
+        in_specs=[SMEM] + [VMEM] * 9,
         out_specs=[VMEM] * 7,
         out_shape=[shape((places, 2 * rows, channels), bf16)] * 2
         + [
@@ -409,79 +407,40 @@
         ],
         input_output_aliases={3: 5},
         compiler_params=PARAMS,
-    )(core, left, right, padded, conv, dbranch, dact, taps, params, expand, reduce)
+    )(core, left, right, padded, conv, dbranch, taps, params, expand, reduce)
 
     swap = [(0, 1), (1, 0)]
     came = lax.ppermute(sent, "core", swap)
-    dconv, small_sent, small = pl.pallas_call(
+    dconv, small = pl.pallas_call(
         functools.partial(backward_kernel, multiplier),
         name="backward",
-        in_specs=[SMEM] + [VMEM] * 7,
-        out_specs=[VMEM] * 3,
+        in_specs=[VMEM] * 7,
+        out_specs=[VMEM] * 2,
         out_shape=[
             shape((height, width, channels), bf16),
-            shape((SMALL, channels), bf16),
-            shape((SMALL, channels), bf16),
+            shape((places, 2 * SMALL, channels), bf16),
         ],
         scratch_shapes=[
             pltpu.VMEM((blocks, pixels, LANES), f32),
-            pltpu.VMEM((CORE * SMALL, channels), f32),
+            pltpu.VMEM((places * SMALL, channels), f32),
         ],
         compiler_params=PARAMS,
-    )(core, dpre, expand, xhat, rstd, padded, params, dscale)
-
-    small_came = lax.ppermute(small_sent, "core", swap)
-    block = pl.BlockSpec((X, 2 * rows, channels), lambda i: (i, 0, 0))
+    )(dpre, expand, xhat, rstd, padded, params, dscale)
+
+    small_came = lax.ppermute(small, "core", swap)
+    whole = 2 * rows + 2 * SMALL
     chip = pl.pallas_call(
         merge_kernel,
         name="merge",
         grid=(Y,),
-        in_specs=[block] * 2,
-        out_specs=block,
-        out_shape=shape((places, 2 * rows, channels), bf16),
+        in_specs=[pl.BlockSpec((X, 2 * rows, channels), lambda i: (i, 0, 0))] * 2
+        + [pl.BlockSpec((X, 2 * SMALL, channels), lambda i: (i, 0, 0))] * 2,
+        out_specs=pl.BlockSpec((X, whole, channels), lambda i: (i, 0, 0)),
+        out_shape=shape((places, whole, channels), bf16),
         compiler_params=GLUE_PARAMS,
-    )(kept, came)
-    chip, dconv, small, small_came, rows_came = lax.optimization_barrier(
-        (chip, dconv, small, small_came, row_borders(dconv, reach))
-    )
-    small = added(small, small_came)
-    for axis, apart in (("z", 1), ("z", 2), ("z", 4), ("x", 1), ("x", 2)):
-        small = paired(small, axis, apart)
-    chunks, edges, small = lax.optimization_barrier(
-        (exchanged(chip, ("y", "x")), column_borders(dconv, *rows_came, reach), small)
-    )
-    chunks = pl.pallas_call(
-        plane_kernel,
-        name="plane",
-        in_specs=[VMEM],
-        out_specs=VMEM,
-        out_shape=shape((Z, 2 * each, channels), bf16),
-        scratch_shapes=[pltpu.VMEM((2 * rows, channels), f32)],
-        compiler_params=GLUE_PARAMS,
-    )(chunks)
-    chunks, small = lax.optimization_barrier((chunks, small))
-    for apart in (1, 2):
-        small = paired(small, "y", apart)
-    dreduce, dexpand = pl.pallas_call(
-        functools.partial(line_kernel, multiplier),
-        name="line",
-        in_specs=[VMEM],
-        out_specs=[VMEM] * 2,
-        out_shape=[
-            shape((each, channels), f32),
-            shape((channels * each // hidden, hidden), f32),
-        ],
-        compiler_params=GLUE_PARAMS,
-    )(exchanged(chunks, "z"))
-    dkernel, dgain, dscale = pl.pallas_call(
-        small_kernel,
-        name="small",
-        in_specs=[SMEM] + [VMEM] * 2,
-        out_specs=[VMEM] * 3,
-        out_shape=[shape((side, side, channels), f32)] + [shape((1, channels), f32)] * 2,
-        scratch_shapes=[pltpu.VMEM((CORE, SMALL, channels), f32)],
-        compiler_params=GLUE_PARAMS,
-    )(core, small, lax.ppermute(small, "core", swap))
+    )(kept, came, small, small_came)
+    chip, dconv, rows_came = lax.optimization_barrier((chip, dconv, row_borders(dconv, reach)))
+    edges = column_borders(dconv, *rows_came, reach)
     grad_features = pl.pallas_call(
         feature_kernel,
         name="features",
@@ -491,6 +450,36 @@
         scratch_shapes=[pltpu.VMEM(padded_shape, f32)],
         compiler_params=GLUE_PARAMS,
     )(dconv, *edges, kernel, cotangent)
+    chunks, grad_features = lax.optimization_barrier((exchanged(chip, ("y", "x")), grad_features))
+    chunks = pl.pallas_call(
+        plane_kernel,
+        name="plane",
+        in_specs=[VMEM],
+        out_specs=VMEM,
+        out_shape=shape((Z, 2 * each + 2 * SMALL, channels), bf16),
+        scratch_shapes=[pltpu.VMEM((whole, channels), f32)],
+        compiler_params=GLUE_PARAMS,
+    )(chunks)
+    dreduce, dexpand, chunks = pl.pallas_call(
+        functools.partial(line_kernel, multiplier),
+        name="line",
+        in_specs=[VMEM],
+        out_specs=[VMEM] * 3,
+        out_shape=[
+            shape((each, channels), f32),
+            shape((channels * each // hidden, hidden), f32),
+            shape((places, 2 * SMALL, channels), bf16),
+        ],
+        compiler_params=GLUE_PARAMS,
+    )(exchanged(chunks, "z"))
+    dkernel, dgain, dscale = pl.pallas_call(
+        small_kernel,
+        name="small",
+        in_specs=[VMEM],
+        out_specs=[VMEM] * 3,
+        out_shape=[shape((side, side, channels), f32)] + [shape((1, channels), f32)] * 2,
+        compiler_params=GLUE_PARAMS,
+    )(exchanged(chunks, ("y", "x")))
     return (
         grad_features,
         dkernel,

time: 110 us -> 109 us (level)
  blocking collectives: 0 us -> 31 us
  waiting for transfers between devices: 35.7 us -> 17.9 us
  starting transfers between devices: 49.6 us -> 38.6 us
  Pallas kernels: 21 us -> 17.8 us
    all_to_all x0 -> x2, blocking collectives: none -> 31 us  [exchanged(): return lax.all_to_all(chunks, axes, 0, 0, tiled=True)]
    ppermute x9 -> x1, waiting for transfers between devices: 23.7 us -> 0.01 us  [shards(): small_came = lax.ppermute(small, 'core', swap)]
    ppermute x9 -> x1, starting transfers between devices: 13.1 us -> 0.1 us  [shards(): small_came = lax.ppermute(small, 'core', swap)]
    all_to_all x2 -> x1, waiting for transfers between devices: 5.76 us -> 16.1 us  [exchanged(): return lax.all_to_all(chunks, axes, 0, 0, tiled=True)]
    ppermute x8, starting transfers between devices: 21.1 us -> 26.3 us  [shifted(): return lax.ppermute(value, axes, pairs)]
    ppermute x8, waiting for transfers between devices: 6.24 us -> 1.82 us  [shifted(): return lax.ppermute(value, axes, pairs)]
    pallas_call x1, Pallas kernels: 4.74 us -> 2.57 us  [shards(): pl.pallas_call(prepare_kernel, name='prepare', in_specs=[HBM] + [VMEM] *...]
    all_to_all x2 -> x1, starting transfers between devices: 12.3 us -> 10.5 us  [exchanged(): return lax.all_to_all(chunks, axes, 0, 0, tiled=True)]
  transfers between devices with their start and end apart: 20 -> 11, of which waited for: 8 -> 3; matrix products, arithmetic and copies ran while one was open for 1% -> 1% of each run, Pallas kernels for 12% -> 9%
where the time goes in v8:
time: 109 us; the launch traced here: 108 us
  starting transfers between devices  38.6 us (35%)
  blocking collectives  31 us (28%)
  waiting for transfers between devices  17.9 us (16%)
  Pallas kernels  17.8 us (16%)
  local copies, waits for them, and re-layouts  1.96 us (2%)
    all_to_all x2, blocking collectives, exchanged(): return lax.all_to_all(chunks, axes, 0, 0, tiled=True)  31 us
    ppermute x8, starting transfers between devices, shifted(): return lax.ppermute(value, axes, pairs)  26.3 us
    all_to_all x1, waiting for transfers between devices, exchanged(): return lax.all_to_all(chunks, axes, 0, 0, tiled=True)  16.1 us
    all_to_all x1, starting transfers between devices, exchanged(): return lax.all_to_all(chunks, axes, 0, 0, tiled=True)  10.5 us
    pallas_call x1, Pallas kernels, shards(): pl.pallas_call(forward_kernel, name='forward', in_specs=[SMEM] + [VMEM] *...  5.81 us
    pallas_call x1, Pallas kernels, shards(): pl.pallas_call(functools.partial(backward_kernel, multiplier), name='back...  3.1 us
    pallas_call x1, Pallas kernels, shards(): pl.pallas_call(prepare_kernel, name='prepare', in_specs=[HBM] + [VMEM] *...  2.57 us
    pallas_call x1, Pallas kernels, shards(): pl.pallas_call(feature_kernel, name='features', in_specs=[VMEM] * 7, out_...  2.48 us
  transfers between devices with their start and end apart: 11, of which 3 were waited for; matrix products, arithmetic and copies ran while one was open for 1% of the time, Pallas kernels for 9%

profile of v8, /device:TPU:2, one launch (start us, length us, event | category | flops | bytes accessed | tf_op | source)
XLA Modules:
  0.0 108.3 jit_solution(13468750975608040780)
XLA Ops:
  0.6 1.0 fusion.3
  1.6 1.3 %collective-permute-start = (bf16[3,32,512]{2,1,0:T(8,128)(2,1)S(1)}, bf16[3,32,512]{2,1,0:T(8,128)(2,1)S(1)}, u32[]{:S(2)}, u32[]{:S(2)}) collective-permute-start(bf16[3,32,512]{2,1,0:T(8,128)(2,1)S(1)} %get-tuple-element.68), channel_id=1, source_target_pairs={{32,0},{64,32},{96,64},{128,96},{160,128},{192,160},{224,192},{33,... | collective-permute-start | bytes 294920 | tf_op jit(solution)/shard_map/ppermute | solution.py:325
  2.9 3.0 %collective-permute-start.1 = (bf16[3,32,512]{2,1,0:T(8,128)(2,1)S(1)}, bf16[3,32,512]{2,1,0:T(8,128)(2,1)S(1)}, u32[]{:S(2)}, u32[]{:S(2)}) collective-permute-start(bf16[3,32,512]{2,1,0:T(8,128)(2,1)S(1)} %get-tuple-element.69), channel_id=1, source_target_pairs={{0,32},{32,64},{64,96},{96,128},{128,160},{160,192},{192,224},{1,3... | collective-permute-start | bytes 294920 | tf_op jit(solution)/shard_map/ppermute | solution.py:325
  5.9 0.9 fusion.2
  6.8 0.0 collective-permute-done.down
  7.0 3.8 %collective-permute-start.2 = (bf16[14,3,512]{2,1,0:T(4,128)(2,1)S(1)}, bf16[14,3,512]{2,1,0:T(4,128)(2,1)S(1)}, u32[]{:S(2)}, u32[]{:S(2)}) collective-permute-start(bf16[14,3,512]{2,1,0:T(4,128)(2,1)S(1)} %pad_maximum_fusion), channel_id=1, source_target_pairs={{0,1},{1,2},{2,3},{3,4},{4,5},{5,6},{6,7},{7,8},{8,9},{9,10},{10,1... | collective-permute-start | bytes 129032 | tf_op jit(solution)/shard_map/ppermute | solution.py:325
  10.8 5.8 %collective-permute-start.3 = (bf16[14,3,512]{2,1,0:T(4,128)(2,1)S(1)}, bf16[14,3,512]{2,1,0:T(4,128)(2,1)S(1)}, u32[]{:S(2)}, u32[]{:S(2)}) collective-permute-start(bf16[14,3,512]{2,1,0:T(4,128)(2,1)S(1)} %pad_maximum_fusion.1), channel_id=1, source_target_pairs={{1,0},{2,1},{3,2},{4,3},{5,4},{6,5},{7,6},{8,7},{9,8},{10,9},{11,1... | collective-permute-start | bytes 129032 | tf_op jit(solution)/shard_map/ppermute | solution.py:325
  16.7 2.6 %prepare.1 = (f32[4,14,48,128]{3,2,1,0:T(8,128)S(1)}, f32[4,256,128]{2,1,0:T(8,128)S(1)}, bf16[256,512]{1,0:T(8,128)(2,1)S(1)}, f32[7,7,512]{2,1,0:T(8,128)S(1)}...) custom-call(bf16[8,32,512]{2,1,0:T(8,128)(2,1)} %field_h.1, ...), custom_call_target="tpu_custom_call" | custom-call | tf_op jit(solution)/shard_map/prepare/pallas_call | solution.py:364
  19.3 0.0 collective-permute-done.2.left
  19.3 0.0 collective-permute-done.3.right
  19.3 5.8 %forward.1 = (bf16[16,128,512]{2,1,0:T(8,128)(2,1)S(1)}, bf16[16,128,512]{2,1,0:T(8,128)(2,1)S(1)}, bf16[256,2048]{1,0:T(8,128)(2,1)S(1)}, f32[4,256,128]{2,1,0:...) custom-call(s32[1]{0:T(128)} %bitcast.core_ref, ...), custom_call_target="tpu_custom_call", output_to_operand_aliasing={{5}: (3, {})} | custom-call | tf_op jit(solution)/shard_map/forward/pallas_call | solution.py:390
  25.1 1.7 %collective-permute-start.4 = (bf16[16,128,512]{2,1,0:T(8,128)(2,1)S(1)}, bf16[16,128,512]{2,1,0:T(8,128)(2,1)S(1)}, u32[]{:S(2)}, u32[]{:S(2)}) collective-permute-start(bf16[16,128,512]{2,1,0:T(8,128)(2,1)S(1)} %get-tuple-element.42), channel_id=1, source_target_pairs={{0,32},{32,0},{1,33},{33,1},{2,34},{34,2},{3,35},{35,3},{4,36},{36... | collective-permute-start | bytes 6291464 | tf_op jit(solution)/shard_map/ppermute | solution.py:413
  26.8 3.1 %backward.1 = (bf16[8,32,512]{2,1,0:T(8,128)(2,1)S(1)}, bf16[16,8,512]{2,1,0:T(8,128)(2,1)S(1)}) custom-call(bf16[256,2048]{1,0:T(8,128)(2,1)S(1)} %get-tuple-element.43.dpre, bf16[512,2048]{1,0:T(8,128)(2,1)S(1)} %get-tuple-element.39.expand, f32[4,256,128]{2,1,0:T(8,128)S(1)} %get-tuple-element.44.xhat, f32[256,128]{1,0:T(8,128)S(1)} %get-tuple-element.45.rstd, ...), custom_call_target="tpu_custom_call" | custom-call | tf_op jit(solution)/shard_map/backward/pallas_call | solution.py:414
  29.9 0.1 collective-permute-start.5
  30.0 1.3 %collective-permute-start.7 = (bf16[3,32,512]{2,1,0:T(8,128)(2,1)S(1)}, bf16[3,32,512]{2,1,0:T(8,128)(2,1)S(1)}, u32[]{:S(2)}, u32[]{:S(2)}) collective-permute-start(bf16[3,32,512]{2,1,0:T(8,128)(2,1)S(1)} %get-tuple-element.64), channel_id=1, source_target_pairs={{32,0},{64,32},{96,64},{128,96},{160,128},{192,160},{224,192},{33,... | collective-permute-start | bytes 294920 | tf_op jit(solution)/shard_map/ppermute | solution.py:325
  31.3 3.0 %collective-permute-start.6 = (bf16[3,32,512]{2,1,0:T(8,128)(2,1)S(1)}, bf16[3,32,512]{2,1,0:T(8,128)(2,1)S(1)}, u32[]{:S(2)}, u32[]{:S(2)}) collective-permute-start(bf16[3,32,512]{2,1,0:T(8,128)(2,1)S(1)} %get-tuple-element.65), channel_id=1, source_target_pairs={{0,32},{32,64},{64,96},{96,128},{128,160},{160,192},{192,224},{1,3... | collective-permute-start | bytes 294920 | tf_op jit(solution)/shard_map/ppermute | solution.py:325
  34.4 0.0 collective-permute-done.5.small_came
  34.4 2.1 %merge.1 = bf16[16,136,512]{2,1,0:T(8,128)(2,1)} custom-call(bf16[16,128,512]{2,1,0:T(8,128)(2,1)S(1)} %get-tuple-element.41.kept, bf16[16,128,512]{2,1,0:T(8,128)(2,1)S(1)} %collective-permute-done.4.came, bf16[16,8,512]{2,1,0:T(8,128)(2,1)S(1)} %get-tuple-element.48.small, bf16[16,8,512]{2,1,0:T(8,128)(2,1)S(1)} %collective-permute-done.5.small_came), custom_call_target="tpu_custom_call" | custom-call | tf_op jit(solution)/shard_map/merge/pallas_call | solution.py:432
  36.5 0.0 collective-permute-done.7.down
  36.5 0.0 collective-permute-done.6.up
  36.5 10.5 %all-to-all-start = ((bf16[16,136,512]{2,1,0:T(8,128)(2,1)}), bf16[16,136,512]{2,1,0:T(8,128)(2,1)S(1)}, u32[]{:S(2)}, u32[]{:S(2)}) async-start(bf16[16,136,512]{2,1,0:T(8,128)(2,1)} %merge.1), calls=%async_computation | async-start | bytes 4456448 | tf_op jit(solution)/shard_map/all_to_all | solution.py:341
  47.1 1.9 %collective-permute-start.8 = (bf16[14,3,512]{2,1,0:T(4,128)(2,1)S(1)}, bf16[14,3,512]{2,1,0:T(4,128)(2,1)S(1)}, u32[]{:S(2)}, u32[]{:S(2)}) collective-permute-start(bf16[14,3,512]{2,1,0:T(4,128)(2,1)S(1)} %pad_maximum_fusion.2), channel_id=1, source_target_pairs={{0,1},{1,2},{2,3},{3,4},{4,5},{5,6},{6,7},{7,8},{8,9},{9,10},{10,1... | collective-permute-start | bytes 129032 | tf_op jit(solution)/shard_map/ppermute | solution.py:325
  49.1 6.0 %collective-permute-start.9 = (bf16[14,3,512]{2,1,0:T(4,128)(2,1)S(1)}, bf16[14,3,512]{2,1,0:T(4,128)(2,1)S(1)}, u32[]{:S(2)}, u32[]{:S(2)}) collective-permute-start(bf16[14,3,512]{2,1,0:T(4,128)(2,1)S(1)} %pad_maximum_fusion.3), channel_id=1, source_target_pairs={{1,0},{2,1},{3,2},{4,3},{5,4},{6,5},{7,6},{8,7},{9,8},{10,9},{11,1... | collective-permute-start | bytes 129032 | tf_op jit(solution)/shard_map/ppermute | solution.py:325
  55.2 0.3 collective-permute-done.8.left
  55.4 1.5 %collective-permute-done.9.right = bf16[14,3,512]{2,1,0:T(4,128)(2,1)S(1)} collective-permute-done((bf16[14,3,512]{2,1,0:T(4,128)(2,1)S(1)}, bf16[14,3,512]{2,1,0:T(4,128)(2,1)S(1)}, u32[]{:S(2)}, u32[]{:S(2)}) %collective-permute-start.9) | collective-permute-done | bytes 43040 | tf_op jit(solution)/shard_map/ppermute | solution.py:325
  57.0 2.5 %features.1 = bf16[8,32,512]{2,1,0:T(8,128)(2,1)} custom-call(bf16[8,32,512]{2,1,0:T(8,128)(2,1)S(1)} %get-tuple-element.51.field, bf16[3,32,512]{2,1,0:T(8,128)(2,1)S(1)} %collective-permute-done.6.up, bf16[3,32,512]{2,1,0:T(8,128)(2,1)S(1)} %collective-permute-done.7.down, bf16[14,3,512]{2,1,0:T(4,128)(2,1)S(1)} %collective-permute-done.8.left, ...), custom_call_target="tpu_custom_call" | custom-call | tf_op jit(solution)/shard_map/features/pallas_call | solution.py:444
  59.5 16.1 %all-to-all-done.chunks = bf16[16,136,512]{2,1,0:T(8,128)(2,1)S(1)} async-done(((bf16[16,136,512]{2,1,0:T(8,128)(2,1)}), bf16[16,136,512]{2,1,0:T(8,128)(2,1)S(1)}, u32[]{:S(2)}, u32[]{:S(2)}) %all-to-all-start) | async-done | bytes 2228256 | tf_op jit(solution)/shard_map/all_to_all | solution.py:341
  75.6 0.4 plane.1
  76.0 16.9 %all_to_all.15.chunks = bf16[8,24,512]{2,1,0:T(8,128)(2,1)S(1)} all-to-all(bf16[8,24,512]{2,1,0:T(8,128)(2,1)S(1)} %plane.1), channel_id=1, replica_groups=mesh['y'=4,'core'=2,'x'=4,'z'=8] {'z'}, dimensions={0} | all-to-all | bytes 393216 | tf_op jit(solution)/shard_map/all_to_all | solution.py:341
  93.0 0.6 line.1
  93.6 14.0 %all_to_all.16.chunks = bf16[16,8,512]{2,1,0:T(8,128)(2,1)S(1)} all-to-all(bf16[16,8,512]{2,1,0:T(8,128)(2,1)S(1)} %get-tuple-element.56), channel_id=1, replica_groups=mesh['y'=4,'core'=2,'x'=4,'z'=8] {'y','x'}, dimensions={0} | all-to-all | bytes 262144 | tf_op jit(solution)/shard_map/all_to_all | solution.py:341
  107.6 0.7 small.1
  (15 shorter events, 0.3 us)
Async XLA Ops:
  1.6 5.3 %collective-permute-start = (bf16[3,32,512]{2,1,0:T(8,128)(2,1)S(1)}, bf16[3,32,512]{2,1,0:T(8,128)(2,1)S(1)}, u32[]{:S(2)}, u32[]{:S(2)}) collective-permute-start(bf16[3,32,512]{2,1,0:T(8,128)(2,1)S(1)} %get-tuple-element.68), channel_id=1, source_target_pairs={{32,0},{64,32},{96,64},{128,96},{160,128},{192,160},{224,192},{33,... | collective-permute-start | bytes 294920 | tf_op jit(solution)/shard_map/ppermute | solution.py:325
  2.9 4.0 %collective-permute-start.1 = (bf16[3,32,512]{2,1,0:T(8,128)(2,1)S(1)}, bf16[3,32,512]{2,1,0:T(8,128)(2,1)S(1)}, u32[]{:S(2)}, u32[]{:S(2)}) collective-permute-start(bf16[3,32,512]{2,1,0:T(8,128)(2,1)S(1)} %get-tuple-element.69), channel_id=1, source_target_pairs={{0,32},{32,64},{64,96},{96,128},{128,160},{160,192},{192,224},{1,3... | collective-permute-start | bytes 294920 | tf_op jit(solution)/shard_map/ppermute | solution.py:325
  7.0 12.3 %collective-permute-start.2 = (bf16[14,3,512]{2,1,0:T(4,128)(2,1)S(1)}, bf16[14,3,512]{2,1,0:T(4,128)(2,1)S(1)}, u32[]{:S(2)}, u32[]{:S(2)}) collective-permute-start(bf16[14,3,512]{2,1,0:T(4,128)(2,1)S(1)} %pad_maximum_fusion), channel_id=1, source_target_pairs={{0,1},{1,2},{2,3},{3,4},{4,5},{5,6},{6,7},{7,8},{8,9},{9,10},{10,1... | collective-permute-start | bytes 129032 | tf_op jit(solution)/shard_map/ppermute | solution.py:325
  10.8 8.4 %collective-permute-start.3 = (bf16[14,3,512]{2,1,0:T(4,128)(2,1)S(1)}, bf16[14,3,512]{2,1,0:T(4,128)(2,1)S(1)}, u32[]{:S(2)}, u32[]{:S(2)}) collective-permute-start(bf16[14,3,512]{2,1,0:T(4,128)(2,1)S(1)} %pad_maximum_fusion.1), channel_id=1, source_target_pairs={{1,0},{2,1},{3,2},{4,3},{5,4},{6,5},{7,6},{8,7},{9,8},{10,9},{11,1... | collective-permute-start | bytes 129032 | tf_op jit(solution)/shard_map/ppermute | solution.py:325
  25.1 9.3 %collective-permute-start.4 = (bf16[16,128,512]{2,1,0:T(8,128)(2,1)S(1)}, bf16[16,128,512]{2,1,0:T(8,128)(2,1)S(1)}, u32[]{:S(2)}, u32[]{:S(2)}) collective-permute-start(bf16[16,128,512]{2,1,0:T(8,128)(2,1)S(1)} %get-tuple-element.42), channel_id=1, source_target_pairs={{0,32},{32,0},{1,33},{33,1},{2,34},{34,2},{3,35},{35,3},{4,36},{36... | collective-permute-start | bytes 6291464 | tf_op jit(solution)/shard_map/ppermute | solution.py:413
  29.9 4.5 %collective-permute-start.5 = (bf16[16,8,512]{2,1,0:T(8,128)(2,1)S(1)}, bf16[16,8,512]{2,1,0:T(8,128)(2,1)S(1)}, u32[]{:S(2)}, u32[]{:S(2)}) collective-permute-start(bf16[16,8,512]{2,1,0:T(8,128)(2,1)S(1)} %get-tuple-element.48.small), channel_id=1, source_target_pairs={{0,32},{32,0},{1,33},{33,1},{2,34},{34,2},{3,35},{35,3},{4,36},{36... | collective-permute-start | bytes 393224 | tf_op jit(solution)/shard_map/ppermute | solution.py:430
  30.0 6.5 %collective-permute-start.7 = (bf16[3,32,512]{2,1,0:T(8,128)(2,1)S(1)}, bf16[3,32,512]{2,1,0:T(8,128)(2,1)S(1)}, u32[]{:S(2)}, u32[]{:S(2)}) collective-permute-start(bf16[3,32,512]{2,1,0:T(8,128)(2,1)S(1)} %get-tuple-element.64), channel_id=1, source_target_pairs={{32,0},{64,32},{96,64},{128,96},{160,128},{192,160},{224,192},{33,... | collective-permute-start | bytes 294920 | tf_op jit(solution)/shard_map/ppermute | solution.py:325
  31.3 5.2 %collective-permute-start.6 = (bf16[3,32,512]{2,1,0:T(8,128)(2,1)S(1)}, bf16[3,32,512]{2,1,0:T(8,128)(2,1)S(1)}, u32[]{:S(2)}, u32[]{:S(2)}) collective-permute-start(bf16[3,32,512]{2,1,0:T(8,128)(2,1)S(1)} %get-tuple-element.65), channel_id=1, source_target_pairs={{0,32},{32,64},{64,96},{96,128},{128,160},{160,192},{192,224},{1,3... | collective-permute-start | bytes 294920 | tf_op jit(solution)/shard_map/ppermute | solution.py:325
  36.5 20.5 %copy-start = (bf16[8,32,512]{2,1,0:T(8,128)(2,1)S(1)}, bf16[8,32,512]{2,1,0:T(8,128)(2,1)}, u32[]{:S(2)}) copy-start(bf16[8,32,512]{2,1,0:T(8,128)(2,1)} %cotangent.1) | copy-start | bytes 786436
  36.5 20.5 %copy-start.1 = (f32[7,7,512]{2,1,0:T(8,128)S(1)}, f32[7,7,512]{2,1,0:T(8,128)}, u32[]{:S(2)}) copy-start(f32[7,7,512]{2,1,0:T(8,128)} %taps.1) | copy-start | bytes 301060
  36.5 39.1 %all-to-all-start = ((bf16[16,136,512]{2,1,0:T(8,128)(2,1)}), bf16[16,136,512]{2,1,0:T(8,128)(2,1)S(1)}, u32[]{:S(2)}, u32[]{:S(2)}) async-start(bf16[16,136,512]{2,1,0:T(8,128)(2,1)} %merge.1), calls=%async_computation | async-start | bytes 4456448 | tf_op jit(solution)/shard_map/all_to_all | solution.py:341
  47.1 8.3 %collective-permute-start.8 = (bf16[14,3,512]{2,1,0:T(4,128)(2,1)S(1)}, bf16[14,3,512]{2,1,0:T(4,128)(2,1)S(1)}, u32[]{:S(2)}, u32[]{:S(2)}) collective-permute-start(bf16[14,3,512]{2,1,0:T(4,128)(2,1)S(1)} %pad_maximum_fusion.2), channel_id=1, source_target_pairs={{0,1},{1,2},{2,3},{3,4},{4,5},{5,6},{6,7},{7,8},{8,9},{9,10},{10,1... | collective-permute-start | bytes 129032 | tf_op jit(solution)/shard_map/ppermute | solution.py:325
  49.1 7.8 %collective-permute-start.9 = (bf16[14,3,512]{2,1,0:T(4,128)(2,1)S(1)}, bf16[14,3,512]{2,1,0:T(4,128)(2,1)S(1)}, u32[]{:S(2)}, u32[]{:S(2)}) collective-permute-start(bf16[14,3,512]{2,1,0:T(4,128)(2,1)S(1)} %pad_maximum_fusion.3), channel_id=1, source_target_pairs={{1,0},{2,1},{3,2},{4,3},{5,4},{6,5},{7,6},{8,7},{9,8},{10,9},{11,1... | collective-permute-start | bytes 129032 | tf_op jit(solution)/shard_map/ppermute | solution.py:325

commit v9 on v6

--- a/solution.py
+++ b/solution.py
@@ -14,6 +14,7 @@
 INV_ROOT_TWO = 1.0 / math.sqrt(2.0)
 INV_ROOT_TWO_PI = 1.0 / math.sqrt(2.0 * math.pi)
 LANES = 128
+ALONG = 128
 LEFT = 8
 SMALL = 4
 
@@ -37,10 +38,16 @@
 
 
 def fill_sides(padded, left, right, width, reach):
+    rows = padded.shape[1]
+    places = ((0, rows - reach, reach), (reach, reach, rows - 2 * reach), (rows - reach, 0, reach))
     for block in range(padded.shape[0]):
         lanes = pl.ds(block * LANES, LANES)
-        padded[block, :, pl.ds(LEFT - reach, reach), :] = left[:, :, lanes].astype(jnp.float32)
-        padded[block, :, pl.ds(LEFT + width, reach), :] = right[:, :, lanes].astype(jnp.float32)
+        for side, column in ((left, LEFT - reach), (right, LEFT + width)):
+            value = side[:, :, lanes].astype(jnp.float32)
+            for source, target, count in places:
+                padded[block, pl.ds(target, count), pl.ds(column, reach), :] = value[
+                    source : source + count
+                ]
 
 
 def depthwise(padded, taps, block, first_col, height, side, flip):
@@ -72,9 +79,14 @@
     lax.fori_loop(0, padded.shape[0], conv_block, 0)
 
 
+def slot(index, rows, channels):
+    across = channels // LANES
+    return pl.ds(index // across * rows, rows), pl.ds(index % across * LANES, LANES)
+
+
 def prepare_kernel(
     field_h, up, down, taps_h, gain_h, scale_h, cotangent_h, expand_h, reduce_h,
-    padded, conv, dbranch, dact, taps, rows_out, expand, reduce,
+    padded, conv, dbranch, taps, rows_out, expand, reduce,
     field, gain, scale, cotangent, sems,
 ):
     copies = [
@@ -98,25 +110,19 @@
     height, width, channels = field.shape
     fill_own(padded, field, up, down, taps.shape[0] // 2)
     conv_columns(conv, padded, taps, height, width, range(8, width - 8, 8))
-    for copy in copies[2:]:
+    for copy in copies[2:5]:
         copy.wait()
     rows_out[pl.ds(0, 8), :] = jnp.broadcast_to(gain[...], (8, channels))
     rows_out[pl.ds(8, 8), :] = jnp.broadcast_to(scale[...], (8, channels))
     for row in range(height):
         value = cotangent[row].astype(jnp.float32) * scale[...]
         dbranch[pl.ds(row * width, width), :] = value.astype(jnp.bfloat16)
-    step = 2 * LANES
-
-    def hidden_block(chunk, _):
-        hidden = pl.ds(pl.multiple_of(chunk * step, step), step)
-        dact[:, hidden] = product(dbranch[...], reduce[hidden, :], NT)
-        return 0
-
-    lax.fori_loop(0, reduce.shape[0] // step, hidden_block, 0)
+    for copy in copies[5:]:
+        copy.wait()
 
 
 def forward_kernel(
-    core_ref, left, right, padded_in, conv, dbranch, dact, taps, rows_in, expand, reduce,
+    core_ref, left, right, padded_in, conv, dbranch, taps, rows_in, expand, reduce,
     sent, kept, sent_z, kept_z, dpre_out, xhat_out, rstd_out, padded, dscale_out,
     normed, turned, chosen,
 ):
@@ -155,8 +161,8 @@
     per_z = step // (X * Z)
     part_x = part // X
     wide = channels // step
-    narrow = channels // 2
-    top = per_z * Z // 2
+    kept_blocks = (channels - ALONG) // LANES
+    top = per_z * Z * kept_blocks * LANES // channels
 
     def hidden_block(y, _):
         for own, target, target_z in ((0, sent, sent_z), (1, kept, kept_z)):
@@ -164,10 +170,11 @@
             chunk = y * CORE + owner
             hidden = pl.ds(pl.multiple_of(chunk * step, step), step)
             pre = product(normed[...], expand[:, hidden], NN)
+            dact = product(dbranch[...], reduce[hidden, :], NT)
             half = 0.5 * (1.0 + lax.erf(pre * INV_ROOT_TWO))
             slope = half + pre * jnp.exp(-0.5 * pre * pre) * INV_ROOT_TWO_PI
             act = (pre * half).astype(jnp.bfloat16)
-            dpre = (dact[:, hidden] * slope).astype(jnp.bfloat16)
+            dpre = (dact * slope).astype(jnp.bfloat16)
             dpre_out[:, hidden] = dpre
             share = product(act, dbranch[...], TN)
             weighed = share * reduce[hidden, :].astype(jnp.float32)
@@ -176,12 +183,12 @@
             for place in range(X * Z):
                 x, z = place // Z, place % Z
                 mine = share[place * per_z : (place + 1) * per_z]
-                target[
-                    y * X + x, pl.ds(z // 2 * per_z, per_z), pl.ds(z % 2 * narrow, narrow)
-                ] = mine[:, :narrow]
-                target_z[
-                    z, y * (X // 2) + x // 2, :, pl.ds(x % 2 * narrow, narrow)
-                ] = mine[:, narrow:]
+                for i in range(kept_blocks):
+                    slot_rows, slot_lanes = slot(z * kept_blocks + i, per_z, channels)
+                    target[y * X + x, slot_rows, slot_lanes] = mine[
+                        :, i * LANES : (i + 1) * LANES
+                    ]
+                target_z[z, y, :, pl.ds(x * ALONG, ALONG)] = mine[:, kept_blocks * LANES :]
             share = product(chosen[...], dpre, NN).astype(jnp.bfloat16)
             rows = pl.ds(pl.multiple_of(top + (chunk // wide) * part_x, part_x), part_x)
             lanes = pl.ds(pl.multiple_of((chunk % wide) * step, step), step)
@@ -285,52 +292,56 @@
 
 def plane_kernel(chunks, out, total):
     total[...] = jnp.sum(chunks[...].astype(jnp.float32), axis=0)
-    each = out.shape[1] // 2
+    each = (out.shape[1] - 2 * SMALL) // 2
     channels = out.shape[2]
-    narrow = channels // 2
-    top = each * Z // 2
-    small = total[pl.ds(total.shape[0] - 2 * SMALL, SMALL), :].astype(jnp.bfloat16)
-    small = jnp.concatenate([small[:, :narrow], small[:, narrow:]])
+    top = total.shape[0] - 2 * SMALL - each * Z
+    blocks = (channels - ALONG) // LANES
+    small = total[pl.ds(total.shape[0] - 2 * SMALL, 2 * SMALL), :].astype(jnp.bfloat16)
     for z in range(Z):
+        parts = [total[slot(z * blocks + i, each, channels)] for i in range(blocks)]
+        parts.append(jnp.zeros((each, ALONG), jnp.float32))
+        out[z, pl.ds(0, each), :] = jnp.concatenate(parts, axis=1).astype(jnp.bfloat16)
         parts = [total[pl.ds(top + q * 2 * Z + 2 * z, 2), :] for q in range(each // 2)]
-        out[z, pl.ds(0, each), :] = jnp.concatenate(parts).astype(jnp.bfloat16)
-        half = total[pl.ds(z // 2 * each, each), pl.ds(z % 2 * narrow, narrow)]
-        out[z, pl.ds(each, each), pl.ds(0, narrow)] = half.astype(jnp.bfloat16)
-        out[z, pl.ds(each, each), pl.ds(narrow, narrow)] = small
+        out[z, pl.ds(each, each), :] = jnp.concatenate(parts).astype(jnp.bfloat16)
+        out[z, pl.ds(2 * each, 2 * SMALL), :] = small
 
 
 def line_kernel(multiplier, chunks, *refs):
-    *came, dexpand, dreduce, out = refs
+    *came, part_out, dexpand, out = refs
     total = jnp.sum(chunks[...].astype(jnp.float32), axis=0)
-    each = total.shape[0] // 2
-    channels = total.shape[1]
-    narrow = channels // 2
+    each, channels = part_out.shape
+    part_out[...] = total[:each] * multiplier
     for q in range(each // 2):
-        dexpand[:, pl.ds(q * channels, channels)] = total[2 * q : 2 * q + 2] * multiplier
-    dreduce[...] = total[each:, :narrow] * multiplier
-    small = total[each:, narrow:].astype(jnp.bfloat16)
+        part = total[each + 2 * q : each + 2 * q + 2]
+        dexpand[:, pl.ds(q * channels, channels)] = part * multiplier
+    small = total[2 * each : 2 * each + SMALL]
+    half = channels // 2
+    small = jnp.concatenate([small[:, :half], small[:, half:]]).astype(jnp.bfloat16)
     line = sum(ref[...].astype(jnp.float32) for ref in came).astype(jnp.bfloat16)
     for place in range(out.shape[0]):
-        out[place, :, pl.ds(0, narrow)] = line[place // 2][
-            :, place % 2 * narrow : (place % 2 + 1) * narrow
-        ]
-        out[place, :, pl.ds(narrow, narrow)] = small
-
-
-def last_kernel(multiplier, chunks, half, dreduce, dkernel, dgain, dscale):
+        y, x = place // X, place % X
+        out[place, :, pl.ds(0, half)] = small
+        out[place, :, pl.ds(half, ALONG)] = line[y][:, x * ALONG : (x + 1) * ALONG]
+        out[place, :, pl.ds(half + ALONG, half - ALONG)] = jnp.zeros(
+            (each, half - ALONG), jnp.bfloat16
+        )
+
+
+def last_kernel(multiplier, chunks, part, dreduce, dkernel, dgain, dscale):
     channels = dreduce.shape[1]
-    narrow = channels // 2
-    dreduce[:, pl.ds(0, narrow)] = half[...]
-    total = jnp.sum(chunks[:, :, pl.ds(0, narrow)].astype(jnp.float32), axis=0)
-    dreduce[:, pl.ds(narrow, narrow)] = total * multiplier
+    half = channels // 2
+    own = channels - ALONG
+    dreduce[:, pl.ds(0, own)] = part[:, pl.ds(0, own)]
+    total = jnp.sum(chunks[:, :, pl.ds(half, ALONG)].astype(jnp.float32), axis=0)
+    dreduce[:, pl.ds(own, ALONG)] = total * multiplier
     side = dkernel.shape[0]
     for place in range(chunks.shape[0]):
-        part = chunks[place, :, pl.ds(narrow, narrow)].astype(jnp.float32)
+        small = chunks[place, :, pl.ds(0, half)].astype(jnp.float32)
         for row in range(SMALL):
             tap = place * SMALL + row
             for i in range(2):
-                lanes = pl.ds(i * narrow, narrow)
-                value = part[i * SMALL + row : i * SMALL + row + 1]
+                lanes = pl.ds(i * half, half)
+                value = small[i * SMALL + row : i * SMALL + row + 1]
                 if tap < side * side:
                     dkernel[tap // side, pl.ds(tap % side, 1), lanes] = value
                 elif tap == side * side:
@@ -362,7 +373,7 @@
 
 def column_borders(field, up, down, reach):
     left, right = (
-        jnp.concatenate([part[:, columns] for part in (up, field, down)])
+        jnp.concatenate([part[:, columns] for part in (down, field, up)])
         for columns in (slice(-reach, None), slice(0, reach))
     )
     return up, down, shifted(left, COL, 1), shifted(right, COL, -1)
@@ -390,19 +401,18 @@
     padded_shape = (blocks, height + side - 1, LEFT + width + 8, LANES)
 
     each = rows // Z
-    top = rows // 2
+    top = rows * (channels - ALONG) // channels
     up, down = row_borders(features, reach)
     left, right = column_borders(features, up, down, reach)[2:]
-    padded, conv, dbranch, dact, taps, params, expand, reduce = pl.pallas_call(
+    padded, conv, dbranch, taps, params, expand, reduce = pl.pallas_call(
         prepare_kernel,
         name="prepare",
         in_specs=[HBM] + [VMEM] * 2 + [HBM] * 6,
-        out_specs=[VMEM] * 8,
+        out_specs=[VMEM] * 7,
         out_shape=[
             shape(padded_shape, f32),
             shape((blocks, pixels, LANES), f32),
             shape((pixels, channels), bf16),
-            shape((pixels, hidden), f32),
             shape(kernel.shape, f32),
             shape((16, channels), f32),
             shape(w_expand.shape, bf16),
@@ -423,10 +433,10 @@
     sent, kept, sent_z, kept_z, dpre, xhat, rstd, padded, dscale = pl.pallas_call(
         forward_kernel,
         name="forward",
-        in_specs=[SMEM] + [VMEM] * 10,
+        in_specs=[SMEM] + [VMEM] * 9,
         out_specs=[VMEM] * 9,
         out_shape=[shape((places, top + rows, channels), bf16)] * 2
-        + [shape((Z, places // 2, each, channels), bf16)] * 2
+        + [shape((Z, Y, each, X * ALONG), bf16)] * 2
         + [
             shape((pixels, hidden), bf16),
             shape((blocks, pixels, LANES), f32),
@@ -441,7 +451,7 @@
         ],
         input_output_aliases={3: 7},
         compiler_params=PARAMS,
-    )(core, left, right, padded, conv, dbranch, dact, taps, params, expand, reduce)
+    )(core, left, right, padded, conv, dbranch, taps, params, expand, reduce)
 
     swap = [(0, 1), (1, 0)]
     came = lax.ppermute(sent, "core", swap)
@@ -497,18 +507,18 @@
         name="plane",
         in_specs=[VMEM],
         out_specs=VMEM,
-        out_shape=shape((Z, 2 * each, channels), bf16),
+        out_shape=shape((Z, 2 * each + 2 * SMALL, channels), bf16),
         scratch_shapes=[pltpu.VMEM((whole, channels), f32)],
         compiler_params=GLUE_PARAMS,
     )(chunks)
-    dexpand, half, chunks = pl.pallas_call(
+    part, dexpand, chunks = pl.pallas_call(
         functools.partial(line_kernel, multiplier),
         name="line",
         in_specs=[VMEM] * (1 + Z),
         out_specs=[VMEM] * 3,
         out_shape=[
+            shape((each, channels), f32),
             shape((channels * each // hidden, hidden), f32),
-            shape((each, channels // 2), f32),
             shape((places, each, channels), bf16),
         ],
         compiler_params=GLUE_PARAMS,
@@ -521,7 +531,7 @@
         out_shape=[shape((each, channels), f32), shape((side, side, channels), f32)]
         + [shape((1, channels), f32)] * 2,
         compiler_params=GLUE_PARAMS,
-    )(exchanged(chunks, ("y", "x")), half)
+    )(exchanged(chunks, ("y", "x")), part)
     grad_features = pl.pallas_call(
         feature_kernel,
         name="features",

time: 108 us -> 105 us (0.972)
  waiting for transfers between devices: 10.6 us -> 7.58 us
  Pallas kernels: 20.5 us -> 17.8 us
  blocking collectives: 13.6 us -> 15.7 us
  starting transfers between devices: 58.6 us -> 60.5 us
    ppermute x8, starting transfers between devices: 20.9 us -> 26.3 us  [shifted(): return lax.ppermute(value, axes, pairs)]
    ppermute x7, starting transfers between devices: 17.6 us -> 13.8 us  [shards(): lax.ppermute(part, 'z', [(i, (i + step) % Z) for i in range(Z)])]
    ppermute x8, waiting for transfers between devices: 2.33 us -> 0.02 us  [shifted(): return lax.ppermute(value, axes, pairs)]
    pallas_call x1, Pallas kernels: 4.77 us -> 2.57 us  [shards(): pl.pallas_call(prepare_kernel, name='prepare', in_specs=[HBM] + [VMEM] *...]
    all_to_all x1, blocking collectives: 13.6 us -> 15.7 us  [exchanged(): return lax.all_to_all(chunks, axes, 0, 0, tiled=True)]
    ppermute x7, waiting for transfers between devices: 4.19 us -> 2.24 us  [shards(): lax.ppermute(part, 'z', [(i, (i + step) % Z) for i in range(Z)])]
    all_to_all x2, starting transfers between devices: 16.4 us -> 18.1 us  [exchanged(): return lax.all_to_all(chunks, axes, 0, 0, tiled=True)]
    ppermute x1, starting transfers between devices: 3.1 us -> 1.68 us  [shards(): came = lax.ppermute(sent, 'core', swap)]
  transfers between devices with their start and end apart: 20 -> 20, of which waited for: 5 -> 5; matrix products, arithmetic and copies ran while one was open for 1% -> 1% of each run, Pallas kernels for 12% -> 10%
where the time goes in v9:
time: 105 us
  starting transfers between devices  60.5 us (58%)
  Pallas kernels  17.8 us (17%)
  blocking collectives  15.7 us (15%)
  waiting for transfers between devices  7.58 us (7%)
  local copies, waits for them, and re-layouts  1.97 us (2%)
    ppermute x8, starting transfers between devices, shifted(): return lax.ppermute(value, axes, pairs)  26.3 us
    all_to_all x2, starting transfers between devices, exchanged(): return lax.all_to_all(chunks, axes, 0, 0, tiled=True)  18.1 us
    all_to_all x1, blocking collectives, exchanged(): return lax.all_to_all(chunks, axes, 0, 0, tiled=True)  15.7 us
    ppermute x7, starting transfers between devices, shards(): lax.ppermute(part, 'z', [(i, (i + step) % Z) for i in range(Z)])  13.8 us
    pallas_call x1, Pallas kernels, shards(): pl.pallas_call(forward_kernel, name='forward', in_specs=[SMEM] + [VMEM] *...  5.83 us
    all_to_all x2, waiting for transfers between devices, exchanged(): return lax.all_to_all(chunks, axes, 0, 0, tiled=True)  5.31 us
    pallas_call x1, Pallas kernels, shards(): pl.pallas_call(functools.partial(backward_kernel, multiplier), name='back...  3.1 us
    pallas_call x1, Pallas kernels, shards(): pl.pallas_call(prepare_kernel, name='prepare', in_specs=[HBM] + [VMEM] *...  2.57 us
  transfers between devices with their start and end apart: 20, of which 5 were waited for; matrix products, arithmetic and copies ran while one was open for 1% of the time, Pallas kernels for 10%

profile of v9, /device:TPU:2, one launch (start us, length us, event | category | flops | bytes accessed | tf_op | source)
XLA Modules:
  0.0 104.6 jit_solution(78161402708132692)
XLA Ops:
  0.6 1.0 fusion.3
  1.6 1.3 %collective-permute-start = (bf16[3,32,512]{2,1,0:T(8,128)(2,1)S(1)}, bf16[3,32,512]{2,1,0:T(8,128)(2,1)S(1)}, u32[]{:S(2)}, u32[]{:S(2)}) collective-permute-start(bf16[3,32,512]{2,1,0:T(8,128)(2,1)S(1)} %get-tuple-element.114), channel_id=1, source_target_pairs={{32,0},{64,32},{96,64},{128,96},{160,128},{192,160},{224,192},{33,... | collective-permute-start | bytes 294920 | tf_op jit(solution)/shard_map/ppermute | solution.py:367
  2.9 3.0 %collective-permute-start.1 = (bf16[3,32,512]{2,1,0:T(8,128)(2,1)S(1)}, bf16[3,32,512]{2,1,0:T(8,128)(2,1)S(1)}, u32[]{:S(2)}, u32[]{:S(2)}) collective-permute-start(bf16[3,32,512]{2,1,0:T(8,128)(2,1)S(1)} %get-tuple-element.115), channel_id=1, source_target_pairs={{0,32},{32,64},{64,96},{96,128},{128,160},{160,192},{192,224},{1,3... | collective-permute-start | bytes 294920 | tf_op jit(solution)/shard_map/ppermute | solution.py:367
  5.9 0.9 fusion.2
  7.0 3.8 %collective-permute-start.2 = (bf16[14,3,512]{2,1,0:T(4,128)(2,1)S(1)}, bf16[14,3,512]{2,1,0:T(4,128)(2,1)S(1)}, u32[]{:S(2)}, u32[]{:S(2)}) collective-permute-start(bf16[14,3,512]{2,1,0:T(4,128)(2,1)S(1)} %pad_maximum_fusion), channel_id=1, source_target_pairs={{0,1},{1,2},{2,3},{3,4},{4,5},{5,6},{6,7},{7,8},{8,9},{9,10},{10,1... | collective-permute-start | bytes 129032 | tf_op jit(solution)/shard_map/ppermute | solution.py:367
  10.8 5.8 %collective-permute-start.3 = (bf16[14,3,512]{2,1,0:T(4,128)(2,1)S(1)}, bf16[14,3,512]{2,1,0:T(4,128)(2,1)S(1)}, u32[]{:S(2)}, u32[]{:S(2)}) collective-permute-start(bf16[14,3,512]{2,1,0:T(4,128)(2,1)S(1)} %pad_maximum_fusion.1), channel_id=1, source_target_pairs={{1,0},{2,1},{3,2},{4,3},{5,4},{6,5},{7,6},{8,7},{9,8},{10,9},{11,1... | collective-permute-start | bytes 129032 | tf_op jit(solution)/shard_map/ppermute | solution.py:367
  16.7 2.6 %prepare.1 = (f32[4,14,48,128]{3,2,1,0:T(8,128)S(1)}, f32[4,256,128]{2,1,0:T(8,128)S(1)}, bf16[256,512]{1,0:T(8,128)(2,1)S(1)}, f32[7,7,512]{2,1,0:T(8,128)S(1)}...) custom-call(bf16[8,32,512]{2,1,0:T(8,128)(2,1)} %field_h.1, ...), custom_call_target="tpu_custom_call" | custom-call | tf_op jit(solution)/shard_map/prepare/pallas_call | solution.py:407
  19.3 5.8 %forward.1 = (bf16[16,112,512]{2,1,0:T(8,128)(2,1)S(1)}, bf16[16,112,512]{2,1,0:T(8,128)(2,1)S(1)}, bf16[8,4,8,512]{3,2,1,0:T(8,128)(2,1)S(1)}, bf16[8,4,8,512]{...) custom-call(s32[1]{0:T(128)} %bitcast.core_ref, ...), custom_call_target="tpu_custom_call", output_to_operand_aliasing={{7}: (3, {})} | custom-call | tf_op jit(solution)/shard_map/forward/pallas_call | solution.py:433
  25.1 1.7 %collective-permute-start.4 = (bf16[16,112,512]{2,1,0:T(8,128)(2,1)S(1)}, bf16[16,112,512]{2,1,0:T(8,128)(2,1)S(1)}, u32[]{:S(2)}, u32[]{:S(2)}) collective-permute-start(bf16[16,112,512]{2,1,0:T(8,128)(2,1)S(1)} %get-tuple-element.65), channel_id=1, source_target_pairs={{0,32},{32,0},{1,33},{33,1},{2,34},{34,2},{3,35},{35,3},{4,36},{36... | collective-permute-start | bytes 5505032 | tf_op jit(solution)/shard_map/ppermute | solution.py:457
  26.8 3.1 %backward.1 = (bf16[8,32,512]{2,1,0:T(8,128)(2,1)S(1)}, bf16[16,8,512]{2,1,0:T(8,128)(2,1)S(1)}) custom-call(bf16[256,2048]{1,0:T(8,128)(2,1)S(1)} %get-tuple-element.66.dpre, bf16[512,2048]{1,0:T(8,128)(2,1)S(1)} %get-tuple-element.62.expand, f32[4,256,128]{2,1,0:T(8,128)S(1)} %get-tuple-element.67.xhat, f32[256,128]{1,0:T(8,128)S(1)} %get-tuple-element.68.rstd, ...), custom_call_target="tpu_custom_call" | custom-call | tf_op jit(solution)/shard_map/backward/pallas_call | solution.py:459
  30.5 1.3 %collective-permute-start.8 = (bf16[3,32,512]{2,1,0:T(8,128)(2,1)S(1)}, bf16[3,32,512]{2,1,0:T(8,128)(2,1)S(1)}, u32[]{:S(2)}, u32[]{:S(2)}) collective-permute-start(bf16[3,32,512]{2,1,0:T(8,128)(2,1)S(1)} %get-tuple-element.110), channel_id=1, source_target_pairs={{32,0},{64,32},{96,64},{128,96},{160,128},{192,160},{224,192},{33,... | collective-permute-start | bytes 294920 | tf_op jit(solution)/shard_map/ppermute | solution.py:367
  31.8 3.0 %collective-permute-start.7 = (bf16[3,32,512]{2,1,0:T(8,128)(2,1)S(1)}, bf16[3,32,512]{2,1,0:T(8,128)(2,1)S(1)}, u32[]{:S(2)}, u32[]{:S(2)}) collective-permute-start(bf16[3,32,512]{2,1,0:T(8,128)(2,1)S(1)} %get-tuple-element.111), channel_id=1, source_target_pairs={{0,32},{32,64},{64,96},{96,128},{128,160},{160,192},{192,224},{1,3... | collective-permute-start | bytes 294920 | tf_op jit(solution)/shard_map/ppermute | solution.py:367
  34.9 2.0 %merge.1 = bf16[16,120,512]{2,1,0:T(8,128)(2,1)} custom-call(bf16[16,112,512]{2,1,0:T(8,128)(2,1)S(1)} %get-tuple-element.64.kept, bf16[16,112,512]{2,1,0:T(8,128)(2,1)S(1)} %collective-permute-done.4.came, bf16[16,8,512]{2,1,0:T(8,128)(2,1)S(1)} %get-tuple-element.71.small, bf16[16,8,512]{2,1,0:T(8,128)(2,1)S(1)} %collective-permute-done.5.small_came), custom_call_target="tpu_custom_call" | custom-call | tf_op jit(solution)/shard_map/merge/pallas_call | solution.py:477
  36.9 10.6 %all-to-all-start = ((bf16[16,120,512]{2,1,0:T(8,128)(2,1)}), bf16[16,120,512]{2,1,0:T(8,128)(2,1)S(1)}, u32[]{:S(2)}, u32[]{:S(2)}) async-start(bf16[16,120,512]{2,1,0:T(8,128)(2,1)} %merge.1), calls=%async_computation | async-start | bytes 3932160 | tf_op jit(solution)/shard_map/all_to_all | solution.py:383
  47.7 5.2 %collective-permute-start.12 = (bf16[4,8,512]{2,1,0:T(8,128)(2,1)S(1)}, bf16[4,8,512]{2,1,0:T(8,128)(2,1)S(1)}, u32[]{:S(2)}, u32[]{:S(2)}) collective-permute-start(bf16[4,8,512]{2,1,0:T(8,128)(2,1)S(1)} %get-tuple-element.82), channel_id=1, source_target_pairs={{0,2},{1,3},{2,4},{3,5},{4,6},{5,7},{6,0},{7,1},{8,10},{9,11},{10,... | collective-permute-start | bytes 98312 | tf_op jit(solution)/shard_map/ppermute | solution.py:499
  52.9 0.7 collective-permute-start.13
  53.6 2.6 %collective-permute-start.14 = (bf16[4,8,512]{2,1,0:T(8,128)(2,1)S(1)}, bf16[4,8,512]{2,1,0:T(8,128)(2,1)S(1)}, u32[]{:S(2)}, u32[]{:S(2)}) collective-permute-start(bf16[4,8,512]{2,1,0:T(8,128)(2,1)S(1)} %get-tuple-element.84), channel_id=1, source_target_pairs={{0,4},{1,5},{2,6},{3,7},{4,0},{5,1},{6,2},{7,3},{8,12},{9,13},{10,... | collective-permute-start | bytes 98312 | tf_op jit(solution)/shard_map/ppermute | solution.py:499
  56.3 5.1 %collective-permute-start.9 = (bf16[14,3,512]{2,1,0:T(4,128)(2,1)S(1)}, bf16[14,3,512]{2,1,0:T(4,128)(2,1)S(1)}, u32[]{:S(2)}, u32[]{:S(2)}) collective-permute-start(bf16[14,3,512]{2,1,0:T(4,128)(2,1)S(1)} %pad_maximum_fusion.2), channel_id=1, source_target_pairs={{0,1},{1,2},{2,3},{3,4},{4,5},{5,6},{6,7},{7,8},{8,9},{9,10},{10,1... | collective-permute-start | bytes 129032 | tf_op jit(solution)/shard_map/ppermute | solution.py:367
  61.5 2.8 %collective-permute-start.10 = (bf16[14,3,512]{2,1,0:T(4,128)(2,1)S(1)}, bf16[14,3,512]{2,1,0:T(4,128)(2,1)S(1)}, u32[]{:S(2)}, u32[]{:S(2)}) collective-permute-start(bf16[14,3,512]{2,1,0:T(4,128)(2,1)S(1)} %pad_maximum_fusion.3), channel_id=1, source_target_pairs={{1,0},{2,1},{3,2},{4,3},{5,4},{6,5},{7,6},{8,7},{9,8},{10,9},{11,1... | collective-permute-start | bytes 129032 | tf_op jit(solution)/shard_map/ppermute | solution.py:367
  64.3 2.0 %collective-permute-start.15 = (bf16[4,8,512]{2,1,0:T(8,128)(2,1)S(1)}, bf16[4,8,512]{2,1,0:T(8,128)(2,1)S(1)}, u32[]{:S(2)}, u32[]{:S(2)}) collective-permute-start(bf16[4,8,512]{2,1,0:T(8,128)(2,1)S(1)} %get-tuple-element.85), channel_id=1, source_target_pairs={{0,5},{1,6},{2,7},{3,0},{4,1},{5,2},{6,3},{7,4},{8,13},{9,14},{10,... | collective-permute-start | bytes 98312 | tf_op jit(solution)/shard_map/ppermute | solution.py:499
  66.3 1.6 %collective-permute-start.16 = (bf16[4,8,512]{2,1,0:T(8,128)(2,1)S(1)}, bf16[4,8,512]{2,1,0:T(8,128)(2,1)S(1)}, u32[]{:S(2)}, u32[]{:S(2)}) collective-permute-start(bf16[4,8,512]{2,1,0:T(8,128)(2,1)S(1)} %get-tuple-element.86), channel_id=1, source_target_pairs={{0,6},{1,7},{2,0},{3,1},{4,2},{5,3},{6,4},{7,5},{8,14},{9,15},{10,... | collective-permute-start | bytes 98312 | tf_op jit(solution)/shard_map/ppermute | solution.py:499
  67.9 1.7 %collective-permute-start.17 = (bf16[4,8,512]{2,1,0:T(8,128)(2,1)S(1)}, bf16[4,8,512]{2,1,0:T(8,128)(2,1)S(1)}, u32[]{:S(2)}, u32[]{:S(2)}) collective-permute-start(bf16[4,8,512]{2,1,0:T(8,128)(2,1)S(1)} %get-tuple-element.87), channel_id=1, source_target_pairs={{0,7},{1,0},{2,1},{3,2},{4,3},{5,4},{6,5},{7,6},{8,15},{9,8},{10,9... | collective-permute-start | bytes 98312 | tf_op jit(solution)/shard_map/ppermute | solution.py:499
  69.6 0.6 collective-permute-done.15.refs_5_
  70.2 1.0 collective-permute-done.16.refs_6_
  71.2 0.7 collective-permute-done.17.refs_7_
  71.8 1.2 %all-to-all-done.chunks = bf16[16,120,512]{2,1,0:T(8,128)(2,1)S(1)} async-done(((bf16[16,120,512]{2,1,0:T(8,128)(2,1)}), bf16[16,120,512]{2,1,0:T(8,128)(2,1)S(1)}, u32[]{:S(2)}, u32[]{:S(2)}) %all-to-all-start) | async-done | bytes 1966112 | tf_op jit(solution)/shard_map/all_to_all | solution.py:383
  73.4 15.7 %all_to_all.15.chunks = bf16[8,24,512]{2,1,0:T(8,128)(2,1)S(1)} all-to-all(bf16[8,24,512]{2,1,0:T(8,128)(2,1)S(1)} %plane.1), channel_id=1, replica_groups=mesh['y'=4,'core'=2,'x'=4,'z'=8] {'z'}, dimensions={0} | all-to-all | bytes 393216 | tf_op jit(solution)/shard_map/all_to_all | solution.py:383
  89.1 0.7 line.1
  89.8 7.5 %all-to-all-start.2 = ((bf16[16,8,512]{2,1,0:T(8,128)(2,1)}), bf16[16,8,512]{2,1,0:T(8,128)(2,1)S(1)}, u32[]{:S(2)}, u32[]{:S(2)}) async-start(bf16[16,8,512]{2,1,0:T(8,128)(2,1)} %get-tuple-element.101), calls=%async_computation.2 | async-start | bytes 262144 | tf_op jit(solution)/shard_map/all_to_all | solution.py:383
  97.3 2.5 %features.1 = bf16[8,32,512]{2,1,0:T(8,128)(2,1)} custom-call(bf16[8,32,512]{2,1,0:T(8,128)(2,1)S(1)} %get-tuple-element.74.field, bf16[3,32,512]{2,1,0:T(8,128)(2,1)S(1)} %collective-permute-done.7.up, bf16[3,32,512]{2,1,0:T(8,128)(2,1)S(1)} %collective-permute-done.8.down, bf16[14,3,512]{2,1,0:T(4,128)(2,1)S(1)} %collective-permute-done.9.left, ...), custom_call_target="tpu_custom_call" | custom-call | tf_op jit(solution)/shard_map/features/pallas_call | solution.py:535
  99.8 4.1 %all-to-all-done.2.chunks = bf16[16,8,512]{2,1,0:T(8,128)(2,1)S(1)} async-done(((bf16[16,8,512]{2,1,0:T(8,128)(2,1)}), bf16[16,8,512]{2,1,0:T(8,128)(2,1)S(1)}, u32[]{:S(2)}, u32[]{:S(2)}) %all-to-all-start.2) | async-done | bytes 131104 | tf_op jit(solution)/shard_map/all_to_all | solution.py:383
  104.0 0.7 last.1
  (33 shorter events, 1.5 us)
Async XLA Ops:
  1.6 5.3 %collective-permute-start = (bf16[3,32,512]{2,1,0:T(8,128)(2,1)S(1)}, bf16[3,32,512]{2,1,0:T(8,128)(2,1)S(1)}, u32[]{:S(2)}, u32[]{:S(2)}) collective-permute-start(bf16[3,32,512]{2,1,0:T(8,128)(2,1)S(1)} %get-tuple-element.114), channel_id=1, source_target_pairs={{32,0},{64,32},{96,64},{128,96},{160,128},{192,160},{224,192},{33,... | collective-permute-start | bytes 294920 | tf_op jit(solution)/shard_map/ppermute | solution.py:367
  2.9 4.0 %collective-permute-start.1 = (bf16[3,32,512]{2,1,0:T(8,128)(2,1)S(1)}, bf16[3,32,512]{2,1,0:T(8,128)(2,1)S(1)}, u32[]{:S(2)}, u32[]{:S(2)}) collective-permute-start(bf16[3,32,512]{2,1,0:T(8,128)(2,1)S(1)} %get-tuple-element.115), channel_id=1, source_target_pairs={{0,32},{32,64},{64,96},{96,128},{128,160},{160,192},{192,224},{1,3... | collective-permute-start | bytes 294920 | tf_op jit(solution)/shard_map/ppermute | solution.py:367
  7.0 12.3 %collective-permute-start.2 = (bf16[14,3,512]{2,1,0:T(4,128)(2,1)S(1)}, bf16[14,3,512]{2,1,0:T(4,128)(2,1)S(1)}, u32[]{:S(2)}, u32[]{:S(2)}) collective-permute-start(bf16[14,3,512]{2,1,0:T(4,128)(2,1)S(1)} %pad_maximum_fusion), channel_id=1, source_target_pairs={{0,1},{1,2},{2,3},{3,4},{4,5},{5,6},{6,7},{7,8},{8,9},{9,10},{10,1... | collective-permute-start | bytes 129032 | tf_op jit(solution)/shard_map/ppermute | solution.py:367
  10.8 8.4 %collective-permute-start.3 = (bf16[14,3,512]{2,1,0:T(4,128)(2,1)S(1)}, bf16[14,3,512]{2,1,0:T(4,128)(2,1)S(1)}, u32[]{:S(2)}, u32[]{:S(2)}) collective-permute-start(bf16[14,3,512]{2,1,0:T(4,128)(2,1)S(1)} %pad_maximum_fusion.1), channel_id=1, source_target_pairs={{1,0},{2,1},{3,2},{4,3},{5,4},{6,5},{7,6},{8,7},{9,8},{10,9},{11,1... | collective-permute-start | bytes 129032 | tf_op jit(solution)/shard_map/ppermute | solution.py:367
  25.1 9.8 %collective-permute-start.4 = (bf16[16,112,512]{2,1,0:T(8,128)(2,1)S(1)}, bf16[16,112,512]{2,1,0:T(8,128)(2,1)S(1)}, u32[]{:S(2)}, u32[]{:S(2)}) collective-permute-start(bf16[16,112,512]{2,1,0:T(8,128)(2,1)S(1)} %get-tuple-element.65), channel_id=1, source_target_pairs={{0,32},{32,0},{1,33},{33,1},{2,34},{34,2},{3,35},{35,3},{4,36},{36... | collective-permute-start | bytes 5505032 | tf_op jit(solution)/shard_map/ppermute | solution.py:457
  29.9 5.0 %collective-permute-start.5 = (bf16[16,8,512]{2,1,0:T(8,128)(2,1)S(1)}, bf16[16,8,512]{2,1,0:T(8,128)(2,1)S(1)}, u32[]{:S(2)}, u32[]{:S(2)}) collective-permute-start(bf16[16,8,512]{2,1,0:T(8,128)(2,1)S(1)} %get-tuple-element.71.small), channel_id=1, source_target_pairs={{0,32},{32,0},{1,33},{33,1},{2,34},{34,2},{3,35},{35,3},{4,36},{36... | collective-permute-start | bytes 393224 | tf_op jit(solution)/shard_map/ppermute | solution.py:475
  30.0 6.9 %collective-permute-start.6 = (bf16[8,4,8,512]{3,2,1,0:T(8,128)(2,1)S(1)}, bf16[8,4,8,512]{3,2,1,0:T(8,128)(2,1)S(1)}, u32[]{:S(2)}, u32[]{:S(2)}) collective-permute-start(bf16[8,4,8,512]{3,2,1,0:T(8,128)(2,1)S(1)} %get-tuple-element.73), channel_id=1, source_target_pairs={{0,32},{32,0},{1,33},{33,1},{2,34},{34,2},{3,35},{35,3},{4,36},{36... | collective-permute-start | bytes 786440 | tf_op jit(solution)/shard_map/ppermute | solution.py:458
  30.5 6.4 %collective-permute-start.8 = (bf16[3,32,512]{2,1,0:T(8,128)(2,1)S(1)}, bf16[3,32,512]{2,1,0:T(8,128)(2,1)S(1)}, u32[]{:S(2)}, u32[]{:S(2)}) collective-permute-start(bf16[3,32,512]{2,1,0:T(8,128)(2,1)S(1)} %get-tuple-element.110), channel_id=1, source_target_pairs={{32,0},{64,32},{96,64},{128,96},{160,128},{192,160},{224,192},{33,... | collective-permute-start | bytes 294920 | tf_op jit(solution)/shard_map/ppermute | solution.py:367
  31.8 5.1 %collective-permute-start.7 = (bf16[3,32,512]{2,1,0:T(8,128)(2,1)S(1)}, bf16[3,32,512]{2,1,0:T(8,128)(2,1)S(1)}, u32[]{:S(2)}, u32[]{:S(2)}) collective-permute-start(bf16[3,32,512]{2,1,0:T(8,128)(2,1)S(1)} %get-tuple-element.111), channel_id=1, source_target_pairs={{0,32},{32,64},{64,96},{96,128},{128,160},{160,192},{192,224},{1,3... | collective-permute-start | bytes 294920 | tf_op jit(solution)/shard_map/ppermute | solution.py:367
  36.9 36.1 %all-to-all-start = ((bf16[16,120,512]{2,1,0:T(8,128)(2,1)}), bf16[16,120,512]{2,1,0:T(8,128)(2,1)S(1)}, u32[]{:S(2)}, u32[]{:S(2)}) async-start(bf16[16,120,512]{2,1,0:T(8,128)(2,1)} %merge.1), calls=%async_computation | async-start | bytes 3932160 | tf_op jit(solution)/shard_map/all_to_all | solution.py:383
  47.6 49.7 %copy-start = (bf16[8,32,512]{2,1,0:T(8,128)(2,1)S(1)}, bf16[8,32,512]{2,1,0:T(8,128)(2,1)}, u32[]{:S(2)}) copy-start(bf16[8,32,512]{2,1,0:T(8,128)(2,1)} %cotangent.1) | copy-start | bytes 786436
  47.6 49.7 %copy-start.1 = (f32[7,7,512]{2,1,0:T(8,128)S(1)}, f32[7,7,512]{2,1,0:T(8,128)}, u32[]{:S(2)}) copy-start(f32[7,7,512]{2,1,0:T(8,128)} %taps.1) | copy-start | bytes 301060
  47.6 13.9 %collective-permute-start.11 = (bf16[4,8,512]{2,1,0:T(8,128)(2,1)S(1)}, bf16[4,8,512]{2,1,0:T(8,128)(2,1)S(1)}, u32[]{:S(2)}, u32[]{:S(2)}) collective-permute-start(bf16[4,8,512]{2,1,0:T(8,128)(2,1)S(1)} %get-tuple-element.81), channel_id=1, source_target_pairs={{0,1},{1,2},{2,3},{3,4},{4,5},{5,6},{6,7},{7,0},{8,9},{9,10},{10,1... | collective-permute-start | bytes 98312 | tf_op jit(solution)/shard_map/ppermute | solution.py:499
  47.7 16.6 %collective-permute-start.12 = (bf16[4,8,512]{2,1,0:T(8,128)(2,1)S(1)}, bf16[4,8,512]{2,1,0:T(8,128)(2,1)S(1)}, u32[]{:S(2)}, u32[]{:S(2)}) collective-permute-start(bf16[4,8,512]{2,1,0:T(8,128)(2,1)S(1)} %get-tuple-element.82), channel_id=1, source_target_pairs={{0,2},{1,3},{2,4},{3,5},{4,6},{5,7},{6,0},{7,1},{8,10},{9,11},{10,... | collective-permute-start | bytes 98312 | tf_op jit(solution)/shard_map/ppermute | solution.py:499
  52.9 13.4 %collective-permute-start.13 = (bf16[4,8,512]{2,1,0:T(8,128)(2,1)S(1)}, bf16[4,8,512]{2,1,0:T(8,128)(2,1)S(1)}, u32[]{:S(2)}, u32[]{:S(2)}) collective-permute-start(bf16[4,8,512]{2,1,0:T(8,128)(2,1)S(1)} %get-tuple-element.83), channel_id=1, source_target_pairs={{0,3},{1,4},{2,5},{3,6},{4,7},{5,0},{6,1},{7,2},{8,11},{9,12},{10,... | collective-permute-start | bytes 98312 | tf_op jit(solution)/shard_map/ppermute | solution.py:499
  53.6 14.3 %collective-permute-start.14 = (bf16[4,8,512]{2,1,0:T(8,128)(2,1)S(1)}, bf16[4,8,512]{2,1,0:T(8,128)(2,1)S(1)}, u32[]{:S(2)}, u32[]{:S(2)}) collective-permute-start(bf16[4,8,512]{2,1,0:T(8,128)(2,1)S(1)} %get-tuple-element.84), channel_id=1, source_target_pairs={{0,4},{1,5},{2,6},{3,7},{4,0},{5,1},{6,2},{7,3},{8,12},{9,13},{10,... | collective-permute-start | bytes 98312 | tf_op jit(solution)/shard_map/ppermute | solution.py:499
  56.3 15.5 %collective-permute-start.9 = (bf16[14,3,512]{2,1,0:T(4,128)(2,1)S(1)}, bf16[14,3,512]{2,1,0:T(4,128)(2,1)S(1)}, u32[]{:S(2)}, u32[]{:S(2)}) collective-permute-start(bf16[14,3,512]{2,1,0:T(4,128)(2,1)S(1)} %pad_maximum_fusion.2), channel_id=1, source_target_pairs={{0,1},{1,2},{2,3},{3,4},{4,5},{5,6},{6,7},{7,8},{8,9},{9,10},{10,1... | collective-permute-start | bytes 129032 | tf_op jit(solution)/shard_map/ppermute | solution.py:367
  61.5 10.3 %collective-permute-start.10 = (bf16[14,3,512]{2,1,0:T(4,128)(2,1)S(1)}, bf16[14,3,512]{2,1,0:T(4,128)(2,1)S(1)}, u32[]{:S(2)}, u32[]{:S(2)}) collective-permute-start(bf16[14,3,512]{2,1,0:T(4,128)(2,1)S(1)} %pad_maximum_fusion.3), channel_id=1, source_target_pairs={{1,0},{2,1},{3,2},{4,3},{5,4},{6,5},{7,6},{8,7},{9,8},{10,9},{11,1... | collective-permute-start | bytes 129032 | tf_op jit(solution)/shard_map/ppermute | solution.py:367
  64.3 5.8 %collective-permute-start.15 = (bf16[4,8,512]{2,1,0:T(8,128)(2,1)S(1)}, bf16[4,8,512]{2,1,0:T(8,128)(2,1)S(1)}, u32[]{:S(2)}, u32[]{:S(2)}) collective-permute-start(bf16[4,8,512]{2,1,0:T(8,128)(2,1)S(1)} %get-tuple-element.85), channel_id=1, source_target_pairs={{0,5},{1,6},{2,7},{3,0},{4,1},{5,2},{6,3},{7,4},{8,13},{9,14},{10,... | collective-permute-start | bytes 98312 | tf_op jit(solution)/shard_map/ppermute | solution.py:499
  66.3 4.8 %collective-permute-start.16 = (bf16[4,8,512]{2,1,0:T(8,128)(2,1)S(1)}, bf16[4,8,512]{2,1,0:T(8,128)(2,1)S(1)}, u32[]{:S(2)}, u32[]{:S(2)}) collective-permute-start(bf16[4,8,512]{2,1,0:T(8,128)(2,1)S(1)} %get-tuple-element.86), channel_id=1, source_target_pairs={{0,6},{1,7},{2,0},{3,1},{4,2},{5,3},{6,4},{7,5},{8,14},{9,15},{10,... | collective-permute-start | bytes 98312 | tf_op jit(solution)/shard_map/ppermute | solution.py:499
  67.9 3.9 %collective-permute-start.17 = (bf16[4,8,512]{2,1,0:T(8,128)(2,1)S(1)}, bf16[4,8,512]{2,1,0:T(8,128)(2,1)S(1)}, u32[]{:S(2)}, u32[]{:S(2)}) collective-permute-start(bf16[4,8,512]{2,1,0:T(8,128)(2,1)S(1)} %get-tuple-element.87), channel_id=1, source_target_pairs={{0,7},{1,0},{2,1},{3,2},{4,3},{5,4},{6,5},{7,6},{8,15},{9,8},{10,9... | collective-permute-start | bytes 98312 | tf_op jit(solution)/shard_map/ppermute | solution.py:499
  89.8 14.1 %all-to-all-start.2 = ((bf16[16,8,512]{2,1,0:T(8,128)(2,1)}), bf16[16,8,512]{2,1,0:T(8,128)(2,1)S(1)}, u32[]{:S(2)}, u32[]{:S(2)}) async-start(bf16[16,8,512]{2,1,0:T(8,128)(2,1)} %get-tuple-element.101), calls=%async_computation.2 | async-start | bytes 262144 | tf_op jit(solution)/shard_map/all_to_all | solution.py:383

commit v10 on v9

--- a/solution.py
+++ b/solution.py
@@ -27,27 +27,40 @@
     return lax.dot_general(left, right, dims, preferred_element_type=jnp.float32)
 
 
-def fill_own(padded, field, up, down, reach):
+def in_order(first, inner, outer):
+    return jnp.where(first, outer, inner), jnp.where(first, inner, outer)
+
+
+def fill_own(padded, field, inner, outer, first_row, reach):
     height, width, channels = field.shape
     own = pl.ds(LEFT, width)
     for block in range(channels // LANES):
         lanes = pl.ds(block * LANES, LANES)
-        padded[block, pl.ds(0, reach), own, :] = up[:, :, lanes].astype(jnp.float32)
+        up, down = in_order(
+            first_row,
+            inner[:, :, lanes].astype(jnp.float32),
+            outer[:, :, lanes].astype(jnp.float32),
+        )
+        padded[block, pl.ds(0, reach), own, :] = up
         padded[block, pl.ds(reach, height), own, :] = field[:, :, lanes].astype(jnp.float32)
-        padded[block, pl.ds(reach + height, reach), own, :] = down[:, :, lanes].astype(jnp.float32)
-
-
-def fill_sides(padded, left, right, width, reach):
+        padded[block, pl.ds(reach + height, reach), own, :] = down
+
+
+def fill_sides(padded, inner, outer, first_row, first_column, width, reach):
     rows = padded.shape[1]
-    places = ((0, rows - reach, reach), (reach, reach, rows - 2 * reach), (rows - reach, 0, reach))
     for block in range(padded.shape[0]):
         lanes = pl.ds(block * LANES, LANES)
-        for side, column in ((left, LEFT - reach), (right, LEFT + width)):
-            value = side[:, :, lanes].astype(jnp.float32)
-            for source, target, count in places:
-                padded[block, pl.ds(target, count), pl.ds(column, reach), :] = value[
-                    source : source + count
-                ]
+        sides = in_order(
+            first_column,
+            inner[:, :, lanes].astype(jnp.float32),
+            outer[:, :, lanes].astype(jnp.float32),
+        )
+        for value, column in zip(sides, (LEFT - reach, LEFT + width)):
+            columns = pl.ds(column, reach)
+            up, down = in_order(first_row, value[:reach], value[rows - reach :])
+            padded[block, pl.ds(0, reach), columns, :] = up
+            padded[block, pl.ds(reach, rows - 2 * reach), columns, :] = value[reach : rows - reach]
+            padded[block, pl.ds(rows - reach, reach), columns, :] = down
 
 
 def depthwise(padded, taps, block, first_col, height, side, flip):
@@ -85,7 +98,7 @@
 
 
 def prepare_kernel(
-    field_h, up, down, taps_h, gain_h, scale_h, cotangent_h, expand_h, reduce_h,
+    place_ref, field_h, inner, outer, taps_h, gain_h, scale_h, cotangent_h, expand_h, reduce_h,
     padded, conv, dbranch, taps, rows_out, expand, reduce,
     field, gain, scale, cotangent, sems,
 ):
@@ -108,7 +121,7 @@
     for copy in copies[:2]:
         copy.wait()
     height, width, channels = field.shape
-    fill_own(padded, field, up, down, taps.shape[0] // 2)
+    fill_own(padded, field, inner, outer, place_ref[0] == 0, taps.shape[0] // 2)
     conv_columns(conv, padded, taps, height, width, range(8, width - 8, 8))
     for copy in copies[2:5]:
         copy.wait()
@@ -122,18 +135,19 @@
 
 
 def forward_kernel(
-    core_ref, left, right, padded_in, conv, dbranch, taps, rows_in, expand, reduce,
+    place_ref, inner, outer, padded_in, conv, dbranch, taps, rows_in, expand, reduce,
     sent, kept, sent_z, kept_z, dpre_out, xhat_out, rstd_out, padded, dscale_out,
     normed, turned, chosen,
 ):
-    core = core_ref[0]
+    core = place_ref[0]
+    first_column = lax.rem(place_ref[1], 2) == 0
     del padded_in
     blocks = padded.shape[0]
     side = taps.shape[0]
     height = padded.shape[1] - side + 1
     width = conv.shape[1] // height
     channels = blocks * LANES
-    fill_sides(padded, left, right, width, side // 2)
+    fill_sides(padded, inner, outer, core == 0, first_column, width, side // 2)
     conv_columns(conv, padded, taps, height, width, (0, width - 8))
     for row in range(height):
         pixels = pl.ds(row * width, width)
@@ -258,11 +272,15 @@
         out[place] = jnp.concatenate([part, jnp.zeros_like(part)]).astype(jnp.bfloat16)
 
 
-def feature_kernel(field, up, down, left, right, taps, cotangent, out, padded):
+def feature_kernel(
+    place_ref, field, row_inner, row_outer, inner, outer, taps, cotangent, out, padded
+):
     height, width, channels = field.shape
     side = 7
-    fill_own(padded, field, up, down, side // 2)
-    fill_sides(padded, left, right, width, side // 2)
+    first_row = place_ref[0] == 0
+    first_column = lax.rem(place_ref[1], 2) == 0
+    fill_own(padded, field, row_inner, row_outer, first_row, side // 2)
+    fill_sides(padded, inner, outer, first_row, first_column, width, side // 2)
     for block in range(channels // LANES):
         lanes = pl.ds(block * LANES, LANES)
         for first_col in range(0, width, 8):
@@ -284,9 +302,9 @@
     out[:, pl.ds(rows, small.shape[1]), :] = added(small[...], small_came[...])
 
 
-def join_kernel(z_ref, kept, came, *outs):
+def join_kernel(place_ref, kept, came, *outs):
     for step, out in enumerate(outs):
-        z = lax.rem(z_ref[0] + step, Z)
+        z = lax.rem(place_ref[1] + step, Z)
         out[...] = added(kept[z], came[z])
 
 
@@ -361,22 +379,26 @@
     return pltpu.with_memory_space_constraint(value, pltpu.HBM)
 
 
-def shifted(value, axes, by):
+def swapped(low, high, axes, first):
     count = lax.axis_size(axes)
-    pairs = [(i, i + by) for i in range(count) if 0 <= i + by < count]
-    return lax.ppermute(value, axes, pairs)
+    inner = [(i, i ^ 1) for i in range(count)]
+    outer = [(i, i + 1 if i % 2 else i - 1) for i in range(1, count - 1)]
+    return (
+        lax.ppermute(jnp.where(first, high, low), axes, inner),
+        lax.ppermute(jnp.where(first, low, high), axes, outer),
+    )
 
 
 def row_borders(field, reach):
-    return shifted(field[-reach:], ROW, 1), shifted(field[:reach], ROW, -1)
-
-
-def column_borders(field, up, down, reach):
-    left, right = (
-        jnp.concatenate([part[:, columns] for part in (down, field, up)])
-        for columns in (slice(-reach, None), slice(0, reach))
-    )
-    return up, down, shifted(left, COL, 1), shifted(right, COL, -1)
+    return swapped(field[:reach], field[-reach:], ROW, lax.axis_index("core") == 0)
+
+
+def column_borders(field, inner, outer, reach):
+    low, high = (
+        jnp.concatenate([part[:, columns] for part in (inner, field, outer)])
+        for columns in (slice(0, reach), slice(-reach, None))
+    )
+    return inner, outer, *swapped(low, high, COL, lax.axis_index("z") % 2 == 0)
 
 
 def exchanged(chunks, axes):
@@ -393,7 +415,7 @@
     multiplier = 1.0 / math.sqrt(pixels * lax.axis_size(ROW) * lax.axis_size(COL))
     gain_row = gain.reshape(1, channels)
     scale_row = layer_scale.reshape(1, channels)
-    core = lax.axis_index("core").reshape(1)
+    place = jnp.stack([lax.axis_index("core"), lax.axis_index("z")])
     places = Y * X
     rows = hidden // (Y * CORE * X)
     f32, bf16 = jnp.float32, jnp.bfloat16
@@ -402,12 +424,13 @@
 
     each = rows // Z
     top = rows * (channels - ALONG) // channels
-    up, down = row_borders(features, reach)
-    left, right = column_borders(features, up, down, reach)[2:]
+    row_inner, row_outer, inner, outer = column_borders(
+        features, *row_borders(features, reach), reach
+    )
     padded, conv, dbranch, taps, params, expand, reduce = pl.pallas_call(
         prepare_kernel,
         name="prepare",
-        in_specs=[HBM] + [VMEM] * 2 + [HBM] * 6,
+        in_specs=[SMEM, HBM] + [VMEM] * 2 + [HBM] * 6,
         out_specs=[VMEM] * 7,
         out_shape=[
             shape(padded_shape, f32),
@@ -427,8 +450,8 @@
         ],
         compiler_params=PARAMS,
     )(
-        in_hbm(features), up, down, in_hbm(kernel), in_hbm(gain_row), in_hbm(scale_row),
-        in_hbm(cotangent), in_hbm(w_expand), in_hbm(w_reduce),
+        place, in_hbm(features), row_inner, row_outer, in_hbm(kernel), in_hbm(gain_row),
+        in_hbm(scale_row), in_hbm(cotangent), in_hbm(w_expand), in_hbm(w_reduce),
     )
     sent, kept, sent_z, kept_z, dpre, xhat, rstd, padded, dscale = pl.pallas_call(
         forward_kernel,
@@ -451,7 +474,7 @@
         ],
         input_output_aliases={3: 7},
         compiler_params=PARAMS,
-    )(core, left, right, padded, conv, dbranch, taps, params, expand, reduce)
+    )(place, inner, outer, padded, conv, dbranch, taps, params, expand, reduce)
 
     swap = [(0, 1), (1, 0)]
     came = lax.ppermute(sent, "core", swap)
@@ -494,7 +517,7 @@
         out_specs=[VMEM] * Z,
         out_shape=[shape(kept_z.shape[1:], bf16)] * Z,
         compiler_params=GLUE_PARAMS,
-    )(lax.axis_index("z").reshape(1), kept_z, came_z)
+    )(place, kept_z, came_z)
     line = [
         part if step == 0 else lax.ppermute(part, "z", [(i, (i + step) % Z) for i in range(Z)])
         for step, part in enumerate(line)
@@ -535,12 +558,12 @@
     grad_features = pl.pallas_call(
         feature_kernel,
         name="features",
-        in_specs=[VMEM] * 7,
+        in_specs=[SMEM] + [VMEM] * 7,
         out_specs=VMEM,
         out_shape=shape((height, width, channels), bf16),
         scratch_shapes=[pltpu.VMEM(padded_shape, f32)],
         compiler_params=GLUE_PARAMS,
-    )(dconv, *edges, kernel, cotangent)
+    )(place, dconv, *edges, kernel, cotangent)
     return (
         grad_features,
         dkernel,

time: 105 us -> 102 us (0.971)
  starting transfers between devices: 60.5 us -> 51 us
  waiting for transfers between devices: 7.58 us -> 13.2 us
  Pallas kernels: 17.8 us -> 20 us
  blocking collectives: 15.7 us -> 13.9 us
  other arithmetic: 0.19 us -> 1.25 us
    ppermute x8, starting transfers between devices: 26.3 us -> 17.3 us  [the longest x4 12.8 us: swapped(): lax.ppermute(jnp.where(first, low, high), axes, outer)]
    all_to_all x2, waiting for transfers between devices: 5.31 us -> 9.32 us  [exchanged(): return lax.all_to_all(chunks, axes, 0, 0, tiled=True)]
    all_to_all x2, starting transfers between devices: 18.1 us -> 15.9 us  [exchanged(): return lax.all_to_all(chunks, axes, 0, 0, tiled=True)]
    ppermute x1, starting transfers between devices: 1.68 us -> 3.63 us  [shards(): came = lax.ppermute(sent, 'core', swap)]
    all_to_all x1, blocking collectives: 15.7 us -> 13.9 us  [exchanged(): return lax.all_to_all(chunks, axes, 0, 0, tiled=True)]
    select_n x0 -> x4, other arithmetic: none -> 1.17 us  [the longest x1 0.96 us: swapped(): jnp.where(first, high, low)]
    pallas_call x2, Pallas kernels: 5.05 us -> 6.14 us  [the longest x1 3.1 us: shards(): pl.pallas_call(prepare_kernel, name='prepare', in_specs=[SMEM, HBM] + [VM...]
  transfers between devices with their start and end apart: 20 -> 20, of which waited for: 5 -> 6; matrix products, arithmetic and copies ran while one was open for 1% -> 1% of each run, Pallas kernels for 10% -> 12%
where the time goes in v10:
time: 102 us; the launch traced here: 101 us
  starting transfers between devices  51 us (50%)
  Pallas kernels  20 us (20%)
  blocking collectives  13.9 us (14%)
  waiting for transfers between devices  13.2 us (13%)
  other arithmetic  1.25 us (1%)
    all_to_all x2, starting transfers between devices, exchanged(): return lax.all_to_all(chunks, axes, 0, 0, tiled=True)  15.9 us
    all_to_all x1, blocking collectives, exchanged(): return lax.all_to_all(chunks, axes, 0, 0, tiled=True)  13.9 us
    ppermute x7, starting transfers between devices, shards(): lax.ppermute(part, 'z', [(i, (i + step) % Z) for i in range(Z)])  13.5 us
    ppermute x4, starting transfers between devices, swapped(): lax.ppermute(jnp.where(first, low, high), axes, outer)  12.8 us
    all_to_all x2, waiting for transfers between devices, exchanged(): return lax.all_to_all(chunks, axes, 0, 0, tiled=True)  9.32 us
    pallas_call x1, Pallas kernels, shards(): pl.pallas_call(forward_kernel, name='forward', in_specs=[SMEM] + [VMEM] *...  6.43 us
    ppermute x4, starting transfers between devices, swapped(): lax.ppermute(jnp.where(first, high, low), axes, inner)  4.56 us
    ppermute x1, starting transfers between devices, shards(): came = lax.ppermute(sent, 'core', swap)  3.63 us
  transfers between devices with their start and end apart: 20, of which 6 were waited for; matrix products, arithmetic and copies ran while one was open for 1% of the time, Pallas kernels for 12%

profile of v10, /device:TPU:2, one launch (start us, length us, event | category | flops | bytes accessed | tf_op | source)
XLA Modules:
  0.0 101.2 jit_solution(14253619815844810554)
XLA Ops:
  0.6 1.0 broadcast_select_fusion.3
  1.7 0.7 collective-permute-start.1
  2.4 0.9 fusion.1
  3.5 7.7 %collective-permute-start.3 = (bf16[14,3,512]{2,1,0:T(4,128)(2,1)S(1)}, bf16[14,3,512]{2,1,0:T(4,128)(2,1)S(1)}, u32[]{:S(2)}, u32[]{:S(2)}) collective-permute-start(bf16[14,3,512]{2,1,0:T(4,128)(2,1)S(1)} %get-tuple-element.118), channel_id=1, source_target_pairs={{1,2},{2,1},{3,4},{4,3},{5,6},{6,5},{7,8},{8,7},{9,10},{10,9},{11,... | collective-permute-start | bytes 129032 | tf_op jit(solution)/shard_map/ppermute | solution.py:388
  11.4 3.1 %prepare.1 = (f32[4,14,48,128]{3,2,1,0:T(8,128)S(1)}, f32[4,256,128]{2,1,0:T(8,128)S(1)}, bf16[256,512]{1,0:T(8,128)(2,1)S(1)}, f32[7,7,512]{2,1,0:T(8,128)S(1)}...) custom-call(s32[2]{0:T(128)S(1)} %pad_add_fusion.place_ref, ...), custom_call_target="tpu_custom_call" | custom-call | tf_op jit(solution)/shard_map/prepare/pallas_call | solution.py:430
  14.5 1.0 collective-permute-done.2.inner
  15.5 6.4 %forward.1 = (bf16[16,112,512]{2,1,0:T(8,128)(2,1)S(1)}, bf16[16,112,512]{2,1,0:T(8,128)(2,1)S(1)}, bf16[8,4,8,512]{3,2,1,0:T(8,128)(2,1)S(1)}, bf16[8,4,8,512]{...) custom-call(s32[2]{0:T(128)S(1)} %pad_add_fusion.place_ref, ...), custom_call_target="tpu_custom_call", output_to_operand_aliasing={{7}: (3, {})} | custom-call | tf_op jit(solution)/shard_map/forward/pallas_call | solution.py:456
  21.9 3.6 %collective-permute-start.4 = (bf16[16,112,512]{2,1,0:T(8,128)(2,1)S(1)}, bf16[16,112,512]{2,1,0:T(8,128)(2,1)S(1)}, u32[]{:S(2)}, u32[]{:S(2)}) collective-permute-start(bf16[16,112,512]{2,1,0:T(8,128)(2,1)S(1)} %get-tuple-element.65), channel_id=1, source_target_pairs={{0,32},{32,0},{1,33},{33,1},{2,34},{34,2},{3,35},{35,3},{4,36},{36... | collective-permute-start | bytes 5505032 | tf_op jit(solution)/shard_map/ppermute | solution.py:480
  25.5 3.1 %backward.1 = (bf16[8,32,512]{2,1,0:T(8,128)(2,1)S(1)}, bf16[16,8,512]{2,1,0:T(8,128)(2,1)S(1)}) custom-call(bf16[256,2048]{1,0:T(8,128)(2,1)S(1)} %get-tuple-element.66.dpre, bf16[512,2048]{1,0:T(8,128)(2,1)S(1)} %get-tuple-element.62.expand, f32[4,256,128]{2,1,0:T(8,128)S(1)} %get-tuple-element.67.xhat, f32[256,128]{1,0:T(8,128)S(1)} %get-tuple-element.68.rstd, ...), custom_call_target="tpu_custom_call" | custom-call | tf_op jit(solution)/shard_map/backward/pallas_call | solution.py:482
  29.3 0.7 collective-permute-start.8
  29.9 3.9 %collective-permute-start.7 = (bf16[3,32,512]{2,1,0:T(8,128)(2,1)S(1)}, bf16[3,32,512]{2,1,0:T(8,128)(2,1)S(1)}, u32[]{:S(2)}, u32[]{:S(2)}) collective-permute-start(bf16[3,32,512]{2,1,0:T(8,128)(2,1)S(1)} %get-tuple-element.111), channel_id=1, source_target_pairs={{0,32},{32,0},{64,96},{96,64},{128,160},{160,128},{192,224},{224,1... | collective-permute-start | bytes 294920 | tf_op jit(solution)/shard_map/ppermute | solution.py:387
  33.8 2.0 %merge.1 = bf16[16,120,512]{2,1,0:T(8,128)(2,1)} custom-call(bf16[16,112,512]{2,1,0:T(8,128)(2,1)S(1)} %get-tuple-element.64.kept, bf16[16,112,512]{2,1,0:T(8,128)(2,1)S(1)} %collective-permute-done.4.came, bf16[16,8,512]{2,1,0:T(8,128)(2,1)S(1)} %get-tuple-element.71.small, bf16[16,8,512]{2,1,0:T(8,128)(2,1)S(1)} %collective-permute-done.5.small_came), custom_call_target="tpu_custom_call" | custom-call | tf_op jit(solution)/shard_map/merge/pallas_call | solution.py:500
  35.8 7.8 %all-to-all-start = ((bf16[16,120,512]{2,1,0:T(8,128)(2,1)}), bf16[16,120,512]{2,1,0:T(8,128)(2,1)S(1)}, u32[]{:S(2)}, u32[]{:S(2)}) async-start(bf16[16,120,512]{2,1,0:T(8,128)(2,1)} %merge.1), calls=%async_computation | async-start | bytes 3932160 | tf_op jit(solution)/shard_map/all_to_all | solution.py:405
  43.6 0.6 join.1
  44.2 1.1 %collective-permute-start.11 = (bf16[4,8,512]{2,1,0:T(8,128)(2,1)S(1)}, bf16[4,8,512]{2,1,0:T(8,128)(2,1)S(1)}, u32[]{:S(2)}, u32[]{:S(2)}) collective-permute-start(bf16[4,8,512]{2,1,0:T(8,128)(2,1)S(1)} %get-tuple-element.81), channel_id=1, source_target_pairs={{0,1},{1,2},{2,3},{3,4},{4,5},{5,6},{6,7},{7,0},{8,9},{9,10},{10,1... | collective-permute-start | bytes 98312 | tf_op jit(solution)/shard_map/ppermute | solution.py:522
  45.4 1.4 %collective-permute-start.12 = (bf16[4,8,512]{2,1,0:T(8,128)(2,1)S(1)}, bf16[4,8,512]{2,1,0:T(8,128)(2,1)S(1)}, u32[]{:S(2)}, u32[]{:S(2)}) collective-permute-start(bf16[4,8,512]{2,1,0:T(8,128)(2,1)S(1)} %get-tuple-element.82), channel_id=1, source_target_pairs={{0,2},{1,3},{2,4},{3,5},{4,6},{5,7},{6,0},{7,1},{8,10},{9,11},{10,... | collective-permute-start | bytes 98312 | tf_op jit(solution)/shard_map/ppermute | solution.py:522
  46.7 1.9 %collective-permute-start.13 = (bf16[4,8,512]{2,1,0:T(8,128)(2,1)S(1)}, bf16[4,8,512]{2,1,0:T(8,128)(2,1)S(1)}, u32[]{:S(2)}, u32[]{:S(2)}) collective-permute-start(bf16[4,8,512]{2,1,0:T(8,128)(2,1)S(1)} %get-tuple-element.83), channel_id=1, source_target_pairs={{0,3},{1,4},{2,5},{3,6},{4,7},{5,0},{6,1},{7,2},{8,11},{9,12},{10,... | collective-permute-start | bytes 98312 | tf_op jit(solution)/shard_map/ppermute | solution.py:522
  48.7 3.6 %collective-permute-start.14 = (bf16[4,8,512]{2,1,0:T(8,128)(2,1)S(1)}, bf16[4,8,512]{2,1,0:T(8,128)(2,1)S(1)}, u32[]{:S(2)}, u32[]{:S(2)}) collective-permute-start(bf16[4,8,512]{2,1,0:T(8,128)(2,1)S(1)} %get-tuple-element.84), channel_id=1, source_target_pairs={{0,4},{1,5},{2,6},{3,7},{4,0},{5,1},{6,2},{7,3},{8,12},{9,13},{10,... | collective-permute-start | bytes 98312 | tf_op jit(solution)/shard_map/ppermute | solution.py:522
  52.4 3.7 %collective-permute-start.10 = (bf16[14,3,512]{2,1,0:T(4,128)(2,1)S(1)}, bf16[14,3,512]{2,1,0:T(4,128)(2,1)S(1)}, u32[]{:S(2)}, u32[]{:S(2)}) collective-permute-start(bf16[14,3,512]{2,1,0:T(4,128)(2,1)S(1)} %get-tuple-element.116), channel_id=1, source_target_pairs={{1,2},{2,1},{3,4},{4,3},{5,6},{6,5},{7,8},{8,7},{9,10},{10,9},{11,... | collective-permute-start | bytes 129032 | tf_op jit(solution)/shard_map/ppermute | solution.py:388
  56.2 0.5 collective-permute-start.9
  56.7 2.9 %collective-permute-start.15 = (bf16[4,8,512]{2,1,0:T(8,128)(2,1)S(1)}, bf16[4,8,512]{2,1,0:T(8,128)(2,1)S(1)}, u32[]{:S(2)}, u32[]{:S(2)}) collective-permute-start(bf16[4,8,512]{2,1,0:T(8,128)(2,1)S(1)} %get-tuple-element.85), channel_id=1, source_target_pairs={{0,5},{1,6},{2,7},{3,0},{4,1},{5,2},{6,3},{7,4},{8,13},{9,14},{10,... | collective-permute-start | bytes 98312 | tf_op jit(solution)/shard_map/ppermute | solution.py:522
  59.6 1.4 %collective-permute-start.16 = (bf16[4,8,512]{2,1,0:T(8,128)(2,1)S(1)}, bf16[4,8,512]{2,1,0:T(8,128)(2,1)S(1)}, u32[]{:S(2)}, u32[]{:S(2)}) collective-permute-start(bf16[4,8,512]{2,1,0:T(8,128)(2,1)S(1)} %get-tuple-element.86), channel_id=1, source_target_pairs={{0,6},{1,7},{2,0},{3,1},{4,2},{5,3},{6,4},{7,5},{8,14},{9,15},{10,... | collective-permute-start | bytes 98312 | tf_op jit(solution)/shard_map/ppermute | solution.py:522
  61.0 1.0 %collective-permute-start.17 = (bf16[4,8,512]{2,1,0:T(8,128)(2,1)S(1)}, bf16[4,8,512]{2,1,0:T(8,128)(2,1)S(1)}, u32[]{:S(2)}, u32[]{:S(2)}) collective-permute-start(bf16[4,8,512]{2,1,0:T(8,128)(2,1)S(1)} %get-tuple-element.87), channel_id=1, source_target_pairs={{0,7},{1,0},{2,1},{3,2},{4,3},{5,4},{6,5},{7,6},{8,15},{9,8},{10,9... | collective-permute-start | bytes 98312 | tf_op jit(solution)/shard_map/ppermute | solution.py:522
  62.0 0.9 collective-permute-done.15.refs_5_
  62.9 1.7 %collective-permute-done.16.refs_6_ = bf16[4,8,512]{2,1,0:T(8,128)(2,1)S(1)} collective-permute-done((bf16[4,8,512]{2,1,0:T(8,128)(2,1)S(1)}, bf16[4,8,512]{2,1,0:T(8,128)(2,1)S(1)}, u32[]{:S(2)}, u32[]{:S(2)}) %collective-permute-start.16) | collective-permute-done | bytes 32800 | tf_op jit(solution)/shard_map/ppermute | solution.py:522
  65.0 5.8 %all-to-all-done.chunks = bf16[16,120,512]{2,1,0:T(8,128)(2,1)S(1)} async-done(((bf16[16,120,512]{2,1,0:T(8,128)(2,1)}), bf16[16,120,512]{2,1,0:T(8,128)(2,1)S(1)}, u32[]{:S(2)}, u32[]{:S(2)}) %all-to-all-start) | async-done | bytes 1966112 | tf_op jit(solution)/shard_map/all_to_all | solution.py:405
  71.1 13.9 %all_to_all.15.chunks = bf16[8,24,512]{2,1,0:T(8,128)(2,1)S(1)} all-to-all(bf16[8,24,512]{2,1,0:T(8,128)(2,1)S(1)} %plane.1), channel_id=1, replica_groups=mesh['y'=4,'core'=2,'x'=4,'z'=8] {'z'}, dimensions={0} | all-to-all | bytes 393216 | tf_op jit(solution)/shard_map/all_to_all | solution.py:405
  85.0 0.7 line.1
  85.7 8.2 %all-to-all-start.2 = ((bf16[16,8,512]{2,1,0:T(8,128)(2,1)}), bf16[16,8,512]{2,1,0:T(8,128)(2,1)S(1)}, u32[]{:S(2)}, u32[]{:S(2)}) async-start(bf16[16,8,512]{2,1,0:T(8,128)(2,1)} %get-tuple-element.101), calls=%async_computation.2 | async-start | bytes 262144 | tf_op jit(solution)/shard_map/all_to_all | solution.py:405
  93.9 3.0 %features.1 = bf16[8,32,512]{2,1,0:T(8,128)(2,1)} custom-call(s32[2]{0:T(128)S(1)} %pad_add_fusion.place_ref, bf16[8,32,512]{2,1,0:T(8,128)(2,1)S(1)} %get-tuple-element.74.field, bf16[3,32,512]{2,1,0:T(8,128)(2,1)S(1)} %collective-permute-done.7.row_inner, bf16[3,32,512]{2,1,0:T(8,128)(2,1)S(1)} %collective-permute-done.8.row_outer, ...), custom_call_target="tpu_custom_call" | custom-call | tf_op jit(solution)/shard_map/features/pallas_call | solution.py:558
  97.0 3.6 %all-to-all-done.2.chunks = bf16[16,8,512]{2,1,0:T(8,128)(2,1)S(1)} async-done(((bf16[16,8,512]{2,1,0:T(8,128)(2,1)}), bf16[16,8,512]{2,1,0:T(8,128)(2,1)S(1)}, u32[]{:S(2)}, u32[]{:S(2)}) %all-to-all-start.2) | async-done | bytes 131104 | tf_op jit(solution)/shard_map/all_to_all | solution.py:405
  100.5 0.7 last.1
  (32 shorter events, 1.9 us)
Async XLA Ops:
  1.6 1.7 %collective-permute-start = (bf16[3,32,512]{2,1,0:T(8,128)(2,1)S(1)}, bf16[3,32,512]{2,1,0:T(8,128)(2,1)S(1)}, u32[]{:S(2)}, u32[]{:S(2)}) collective-permute-start(bf16[3,32,512]{2,1,0:T(8,128)(2,1)S(1)} %get-tuple-element.114), channel_id=1, source_target_pairs={{0,32},{32,0},{64,96},{96,64},{128,160},{160,128},{192,224},{224,1... | collective-permute-start | bytes 294920 | tf_op jit(solution)/shard_map/ppermute | solution.py:387
  1.7 1.6 %collective-permute-start.1 = (bf16[3,32,512]{2,1,0:T(8,128)(2,1)S(1)}, bf16[3,32,512]{2,1,0:T(8,128)(2,1)S(1)}, u32[]{:S(2)}, u32[]{:S(2)}) collective-permute-start(bf16[3,32,512]{2,1,0:T(8,128)(2,1)S(1)} %get-tuple-element.115), channel_id=1, source_target_pairs={{32,64},{64,32},{96,128},{128,96},{160,192},{192,160},{33,65},{65,... | collective-permute-start | bytes 294920 | tf_op jit(solution)/shard_map/ppermute | solution.py:388
  3.5 11.0 %collective-permute-start.3 = (bf16[14,3,512]{2,1,0:T(4,128)(2,1)S(1)}, bf16[14,3,512]{2,1,0:T(4,128)(2,1)S(1)}, u32[]{:S(2)}, u32[]{:S(2)}) collective-permute-start(bf16[14,3,512]{2,1,0:T(4,128)(2,1)S(1)} %get-tuple-element.118), channel_id=1, source_target_pairs={{1,2},{2,1},{3,4},{4,3},{5,6},{6,5},{7,8},{8,7},{9,10},{10,9},{11,... | collective-permute-start | bytes 129032 | tf_op jit(solution)/shard_map/ppermute | solution.py:388
  11.2 4.3 %collective-permute-start.2 = (bf16[14,3,512]{2,1,0:T(4,128)(2,1)S(1)}, bf16[14,3,512]{2,1,0:T(4,128)(2,1)S(1)}, u32[]{:S(2)}, u32[]{:S(2)}) collective-permute-start(bf16[14,3,512]{2,1,0:T(4,128)(2,1)S(1)} %get-tuple-element.119), channel_id=1, source_target_pairs={{0,1},{1,0},{2,3},{3,2},{4,5},{5,4},{6,7},{7,6},{8,9},{9,8},{10,11... | collective-permute-start | bytes 129032 | tf_op jit(solution)/shard_map/ppermute | solution.py:387
  21.9 11.9 %collective-permute-start.4 = (bf16[16,112,512]{2,1,0:T(8,128)(2,1)S(1)}, bf16[16,112,512]{2,1,0:T(8,128)(2,1)S(1)}, u32[]{:S(2)}, u32[]{:S(2)}) collective-permute-start(bf16[16,112,512]{2,1,0:T(8,128)(2,1)S(1)} %get-tuple-element.65), channel_id=1, source_target_pairs={{0,32},{32,0},{1,33},{33,1},{2,34},{34,2},{3,35},{35,3},{4,36},{36... | collective-permute-start | bytes 5505032 | tf_op jit(solution)/shard_map/ppermute | solution.py:480
  28.6 5.2 %collective-permute-start.5 = (bf16[16,8,512]{2,1,0:T(8,128)(2,1)S(1)}, bf16[16,8,512]{2,1,0:T(8,128)(2,1)S(1)}, u32[]{:S(2)}, u32[]{:S(2)}) collective-permute-start(bf16[16,8,512]{2,1,0:T(8,128)(2,1)S(1)} %get-tuple-element.71.small), channel_id=1, source_target_pairs={{0,32},{32,0},{1,33},{33,1},{2,34},{34,2},{3,35},{35,3},{4,36},{36... | collective-permute-start | bytes 393224 | tf_op jit(solution)/shard_map/ppermute | solution.py:498
  28.8 7.1 %collective-permute-start.6 = (bf16[8,4,8,512]{3,2,1,0:T(8,128)(2,1)S(1)}, bf16[8,4,8,512]{3,2,1,0:T(8,128)(2,1)S(1)}, u32[]{:S(2)}, u32[]{:S(2)}) collective-permute-start(bf16[8,4,8,512]{3,2,1,0:T(8,128)(2,1)S(1)} %get-tuple-element.73), channel_id=1, source_target_pairs={{0,32},{32,0},{1,33},{33,1},{2,34},{34,2},{3,35},{35,3},{4,36},{36... | collective-permute-start | bytes 786440 | tf_op jit(solution)/shard_map/ppermute | solution.py:481
  29.3 6.5 %collective-permute-start.8 = (bf16[3,32,512]{2,1,0:T(8,128)(2,1)S(1)}, bf16[3,32,512]{2,1,0:T(8,128)(2,1)S(1)}, u32[]{:S(2)}, u32[]{:S(2)}) collective-permute-start(bf16[3,32,512]{2,1,0:T(8,128)(2,1)S(1)} %get-tuple-element.110), channel_id=1, source_target_pairs={{32,64},{64,32},{96,128},{128,96},{160,192},{192,160},{33,65},{65,... | collective-permute-start | bytes 294920 | tf_op jit(solution)/shard_map/ppermute | solution.py:388
  29.9 5.9 %collective-permute-start.7 = (bf16[3,32,512]{2,1,0:T(8,128)(2,1)S(1)}, bf16[3,32,512]{2,1,0:T(8,128)(2,1)S(1)}, u32[]{:S(2)}, u32[]{:S(2)}) collective-permute-start(bf16[3,32,512]{2,1,0:T(8,128)(2,1)S(1)} %get-tuple-element.111), channel_id=1, source_target_pairs={{0,32},{32,0},{64,96},{96,64},{128,160},{160,128},{192,224},{224,1... | collective-permute-start | bytes 294920 | tf_op jit(solution)/shard_map/ppermute | solution.py:387
  35.8 34.9 %all-to-all-start = ((bf16[16,120,512]{2,1,0:T(8,128)(2,1)}), bf16[16,120,512]{2,1,0:T(8,128)(2,1)S(1)}, u32[]{:S(2)}, u32[]{:S(2)}) async-start(bf16[16,120,512]{2,1,0:T(8,128)(2,1)} %merge.1), calls=%async_computation | async-start | bytes 3932160 | tf_op jit(solution)/shard_map/all_to_all | solution.py:405
  44.2 49.7 %copy-start = (bf16[8,32,512]{2,1,0:T(8,128)(2,1)S(1)}, bf16[8,32,512]{2,1,0:T(8,128)(2,1)}, u32[]{:S(2)}) copy-start(bf16[8,32,512]{2,1,0:T(8,128)(2,1)} %cotangent.1) | copy-start | bytes 786436
  44.2 49.7 %copy-start.1 = (f32[7,7,512]{2,1,0:T(8,128)S(1)}, f32[7,7,512]{2,1,0:T(8,128)}, u32[]{:S(2)}) copy-start(f32[7,7,512]{2,1,0:T(8,128)} %taps.1) | copy-start | bytes 301060
  44.2 11.9 %collective-permute-start.11 = (bf16[4,8,512]{2,1,0:T(8,128)(2,1)S(1)}, bf16[4,8,512]{2,1,0:T(8,128)(2,1)S(1)}, u32[]{:S(2)}, u32[]{:S(2)}) collective-permute-start(bf16[4,8,512]{2,1,0:T(8,128)(2,1)S(1)} %get-tuple-element.81), channel_id=1, source_target_pairs={{0,1},{1,2},{2,3},{3,4},{4,5},{5,6},{6,7},{7,0},{8,9},{9,10},{10,1... | collective-permute-start | bytes 98312 | tf_op jit(solution)/shard_map/ppermute | solution.py:522
  45.4 11.3 %collective-permute-start.12 = (bf16[4,8,512]{2,1,0:T(8,128)(2,1)S(1)}, bf16[4,8,512]{2,1,0:T(8,128)(2,1)S(1)}, u32[]{:S(2)}, u32[]{:S(2)}) collective-permute-start(bf16[4,8,512]{2,1,0:T(8,128)(2,1)S(1)} %get-tuple-element.82), channel_id=1, source_target_pairs={{0,2},{1,3},{2,4},{3,5},{4,6},{5,7},{6,0},{7,1},{8,10},{9,11},{10,... | collective-permute-start | bytes 98312 | tf_op jit(solution)/shard_map/ppermute | solution.py:522
  46.7 12.8 %collective-permute-start.13 = (bf16[4,8,512]{2,1,0:T(8,128)(2,1)S(1)}, bf16[4,8,512]{2,1,0:T(8,128)(2,1)S(1)}, u32[]{:S(2)}, u32[]{:S(2)}) collective-permute-start(bf16[4,8,512]{2,1,0:T(8,128)(2,1)S(1)} %get-tuple-element.83), channel_id=1, source_target_pairs={{0,3},{1,4},{2,5},{3,6},{4,7},{5,0},{6,1},{7,2},{8,11},{9,12},{10,... | collective-permute-start | bytes 98312 | tf_op jit(solution)/shard_map/ppermute | solution.py:522
  48.7 12.4 %collective-permute-start.14 = (bf16[4,8,512]{2,1,0:T(8,128)(2,1)S(1)}, bf16[4,8,512]{2,1,0:T(8,128)(2,1)S(1)}, u32[]{:S(2)}, u32[]{:S(2)}) collective-permute-start(bf16[4,8,512]{2,1,0:T(8,128)(2,1)S(1)} %get-tuple-element.84), channel_id=1, source_target_pairs={{0,4},{1,5},{2,6},{3,7},{4,0},{5,1},{6,2},{7,3},{8,12},{9,13},{10,... | collective-permute-start | bytes 98312 | tf_op jit(solution)/shard_map/ppermute | solution.py:522
  52.4 12.5 %collective-permute-start.10 = (bf16[14,3,512]{2,1,0:T(4,128)(2,1)S(1)}, bf16[14,3,512]{2,1,0:T(4,128)(2,1)S(1)}, u32[]{:S(2)}, u32[]{:S(2)}) collective-permute-start(bf16[14,3,512]{2,1,0:T(4,128)(2,1)S(1)} %get-tuple-element.116), channel_id=1, source_target_pairs={{1,2},{2,1},{3,4},{4,3},{5,6},{6,5},{7,8},{8,7},{9,10},{10,9},{11,... | collective-permute-start | bytes 129032 | tf_op jit(solution)/shard_map/ppermute | solution.py:388
  56.2 8.8 %collective-permute-start.9 = (bf16[14,3,512]{2,1,0:T(4,128)(2,1)S(1)}, bf16[14,3,512]{2,1,0:T(4,128)(2,1)S(1)}, u32[]{:S(2)}, u32[]{:S(2)}) collective-permute-start(bf16[14,3,512]{2,1,0:T(4,128)(2,1)S(1)} %get-tuple-element.117), channel_id=1, source_target_pairs={{0,1},{1,0},{2,3},{3,2},{4,5},{5,4},{6,7},{7,6},{8,9},{9,8},{10,11... | collective-permute-start | bytes 129032 | tf_op jit(solution)/shard_map/ppermute | solution.py:387
  56.7 6.3 %collective-permute-start.15 = (bf16[4,8,512]{2,1,0:T(8,128)(2,1)S(1)}, bf16[4,8,512]{2,1,0:T(8,128)(2,1)S(1)}, u32[]{:S(2)}, u32[]{:S(2)}) collective-permute-start(bf16[4,8,512]{2,1,0:T(8,128)(2,1)S(1)} %get-tuple-element.85), channel_id=1, source_target_pairs={{0,5},{1,6},{2,7},{3,0},{4,1},{5,2},{6,3},{7,4},{8,13},{9,14},{10,... | collective-permute-start | bytes 98312 | tf_op jit(solution)/shard_map/ppermute | solution.py:522
  59.6 5.1 %collective-permute-start.16 = (bf16[4,8,512]{2,1,0:T(8,128)(2,1)S(1)}, bf16[4,8,512]{2,1,0:T(8,128)(2,1)S(1)}, u32[]{:S(2)}, u32[]{:S(2)}) collective-permute-start(bf16[4,8,512]{2,1,0:T(8,128)(2,1)S(1)} %get-tuple-element.86), channel_id=1, source_target_pairs={{0,6},{1,7},{2,0},{3,1},{4,2},{5,3},{6,4},{7,5},{8,14},{9,15},{10,... | collective-permute-start | bytes 98312 | tf_op jit(solution)/shard_map/ppermute | solution.py:522
  61.0 3.9 %collective-permute-start.17 = (bf16[4,8,512]{2,1,0:T(8,128)(2,1)S(1)}, bf16[4,8,512]{2,1,0:T(8,128)(2,1)S(1)}, u32[]{:S(2)}, u32[]{:S(2)}) collective-permute-start(bf16[4,8,512]{2,1,0:T(8,128)(2,1)S(1)} %get-tuple-element.87), channel_id=1, source_target_pairs={{0,7},{1,0},{2,1},{3,2},{4,3},{5,4},{6,5},{7,6},{8,15},{9,8},{10,9... | collective-permute-start | bytes 98312 | tf_op jit(solution)/shard_map/ppermute | solution.py:522
  85.7 14.8 %all-to-all-start.2 = ((bf16[16,8,512]{2,1,0:T(8,128)(2,1)}), bf16[16,8,512]{2,1,0:T(8,128)(2,1)S(1)}, u32[]{:S(2)}, u32[]{:S(2)}) async-start(bf16[16,8,512]{2,1,0:T(8,128)(2,1)} %get-tuple-element.101), calls=%async_computation.2 | async-start | bytes 262144 | tf_op jit(solution)/shard_map/all_to_all | solution.py:405

commit v11 on v10

--- a/solution.py
+++ b/solution.py
@@ -14,7 +14,7 @@
 INV_ROOT_TWO = 1.0 / math.sqrt(2.0)
 INV_ROOT_TWO_PI = 1.0 / math.sqrt(2.0 * math.pi)
 LANES = 128
-ALONG = 128
+ALONG = 256
 LEFT = 8
 SMALL = 4
 
@@ -27,40 +27,44 @@
     return lax.dot_general(left, right, dims, preferred_element_type=jnp.float32)
 
 
-def in_order(first, inner, outer):
-    return jnp.where(first, outer, inner), jnp.where(first, inner, outer)
+def border_rows(first, rows, reach):
+    return jnp.where(first, rows - reach, 0), jnp.where(first, 0, rows - reach)
 
 
 def fill_own(padded, field, inner, outer, first_row, reach):
     height, width, channels = field.shape
     own = pl.ds(LEFT, width)
+    starts = border_rows(first_row, height + 2 * reach, reach)
     for block in range(channels // LANES):
         lanes = pl.ds(block * LANES, LANES)
-        up, down = in_order(
-            first_row,
-            inner[:, :, lanes].astype(jnp.float32),
-            outer[:, :, lanes].astype(jnp.float32),
-        )
-        padded[block, pl.ds(0, reach), own, :] = up
         padded[block, pl.ds(reach, height), own, :] = field[:, :, lanes].astype(jnp.float32)
-        padded[block, pl.ds(reach + height, reach), own, :] = down
+        for border, start in zip((inner, outer), starts):
+            padded[block, pl.ds(start, reach), own, :] = border[:, :, lanes].astype(jnp.float32)
 
 
 def fill_sides(padded, inner, outer, first_row, first_column, width, reach):
     rows = padded.shape[1]
-    for block in range(padded.shape[0]):
-        lanes = pl.ds(block * LANES, LANES)
-        sides = in_order(
-            first_column,
-            inner[:, :, lanes].astype(jnp.float32),
-            outer[:, :, lanes].astype(jnp.float32),
-        )
-        for value, column in zip(sides, (LEFT - reach, LEFT + width)):
-            columns = pl.ds(column, reach)
-            up, down = in_order(first_row, value[:reach], value[rows - reach :])
-            padded[block, pl.ds(0, reach), columns, :] = up
-            padded[block, pl.ds(reach, rows - 2 * reach), columns, :] = value[reach : rows - reach]
-            padded[block, pl.ds(rows - reach, reach), columns, :] = down
+    before, after = border_rows(first_row, rows, reach)
+
+    def fill(left, right):
+        for block in range(padded.shape[0]):
+            lanes = pl.ds(block * LANES, LANES)
+            for side, column in ((left, LEFT - reach), (right, LEFT + width)):
+                value = side[:, :, lanes].astype(jnp.float32)
+                columns = pl.ds(column, reach)
+                padded[block, pl.ds(before, reach), columns, :] = value[:reach]
+                padded[block, pl.ds(reach, rows - 2 * reach), columns, :] = value[
+                    reach : rows - reach
+                ]
+                padded[block, pl.ds(after, reach), columns, :] = value[rows - reach :]
+
+    @pl.when(first_column)
+    def _():
+        fill(outer, inner)
+
+    @pl.when(jnp.logical_not(first_column))
+    def _():
+        fill(inner, outer)
 
 
 def depthwise(padded, taps, block, first_col, height, side, flip):
@@ -304,7 +308,7 @@
 
 def join_kernel(place_ref, kept, came, *outs):
     for step, out in enumerate(outs):
-        z = lax.rem(place_ref[1] + step, Z)
+        z = place_ref[1] ^ step
         out[...] = added(kept[z], came[z])
 
 
@@ -340,9 +344,6 @@
         y, x = place // X, place % X
         out[place, :, pl.ds(0, half)] = small
         out[place, :, pl.ds(half, ALONG)] = line[y][:, x * ALONG : (x + 1) * ALONG]
-        out[place, :, pl.ds(half + ALONG, half - ALONG)] = jnp.zeros(
-            (each, half - ALONG), jnp.bfloat16
-        )
 
 
 def last_kernel(multiplier, chunks, part, dreduce, dkernel, dgain, dscale):
@@ -519,7 +520,7 @@
         compiler_params=GLUE_PARAMS,
     )(place, kept_z, came_z)
     line = [
-        part if step == 0 else lax.ppermute(part, "z", [(i, (i + step) % Z) for i in range(Z)])
+        part if step == 0 else lax.ppermute(part, "z", [(i, i ^ step) for i in range(Z)])
         for step, part in enumerate(line)
     ]
     chunks, edges, line = lax.optimization_barrier(

time: 102 us -> 100 us (0.980)
  waiting for transfers between devices: 13.2 us -> 11.7 us
    all_to_all x2, waiting for transfers between devices: 9.32 us -> 3.33 us  [exchanged(): return lax.all_to_all(chunks, axes, 0, 0, tiled=True)]
    ppermute x7, waiting for transfers between devices: 2.91 us -> 5.29 us  [shards(): lax.ppermute(part, 'z', [(i, i ^ step) for i in range(Z)])]
    ppermute x4, waiting for transfers between devices: 0.01 us -> 2.13 us  [swapped(): lax.ppermute(jnp.where(first, low, high), axes, outer)]
    all_to_all x2, starting transfers between devices: 15.9 us -> 14.9 us  [exchanged(): return lax.all_to_all(chunks, axes, 0, 0, tiled=True)]
where the time goes in v11:
time: 100 us; the launch traced here: 99.8 us
  starting transfers between devices  50.3 us (50%)
  Pallas kernels  20.2 us (20%)
  blocking collectives  14.5 us (14%)
  waiting for transfers between devices  11.7 us (12%)
  other arithmetic  1.25 us (1%)
  local copies, waits for them, and re-layouts  1 us (1%)
    all_to_all x2, starting transfers between devices, exchanged(): return lax.all_to_all(chunks, axes, 0, 0, tiled=True)  14.9 us
    all_to_all x1, blocking collectives, exchanged(): return lax.all_to_all(chunks, axes, 0, 0, tiled=True)  14.5 us
    ppermute x7, starting transfers between devices, shards(): lax.ppermute(part, 'z', [(i, i ^ step) for i in range(Z)])  13.7 us
    ppermute x4, starting transfers between devices, swapped(): lax.ppermute(jnp.where(first, low, high), axes, outer)  11.9 us
    pallas_call x1, Pallas kernels, shards(): pl.pallas_call(forward_kernel, name='forward', in_specs=[SMEM] + [VMEM] *...  6.4 us
    ppermute x4, starting transfers between devices, swapped(): lax.ppermute(jnp.where(first, high, low), axes, inner)  5.42 us
    ppermute x7, waiting for transfers between devices, shards(): lax.ppermute(part, 'z', [(i, i ^ step) for i in range(Z)])  5.29 us
    ppermute x1, starting transfers between devices, shards(): came = lax.ppermute(sent, 'core', swap)  3.69 us
  transfers between devices with their start and end apart: 20, of which 6 were waited for; matrix products, arithmetic and copies ran while one was open for 1% of the time, Pallas kernels for 12%

profile of v11, /device:TPU:2, one launch (start us, length us, event | category | flops | bytes accessed | tf_op | source)
XLA Modules:
  0.0 99.8 jit_solution(11653643790206045934)
XLA Ops:
  0.6 1.0 broadcast_select_fusion.3
  1.7 0.7 collective-permute-start.1
  2.4 0.9 fusion.1
  3.5 7.7 %collective-permute-start.3 = (bf16[14,3,512]{2,1,0:T(4,128)(2,1)S(1)}, bf16[14,3,512]{2,1,0:T(4,128)(2,1)S(1)}, u32[]{:S(2)}, u32[]{:S(2)}) collective-permute-start(bf16[14,3,512]{2,1,0:T(4,128)(2,1)S(1)} %get-tuple-element.118), channel_id=1, source_target_pairs={{1,2},{2,1},{3,4},{4,3},{5,6},{6,5},{7,8},{8,7},{9,10},{10,9},{11,... | collective-permute-start | bytes 129032 | tf_op jit(solution)/shard_map/ppermute | solution.py:389
  11.4 3.1 %prepare.1 = (f32[4,14,48,128]{3,2,1,0:T(8,128)S(1)}, f32[4,256,128]{2,1,0:T(8,128)S(1)}, bf16[256,512]{1,0:T(8,128)(2,1)S(1)}, f32[7,7,512]{2,1,0:T(8,128)S(1)}...) custom-call(s32[2]{0:T(128)S(1)} %pad_add_fusion.place_ref, ...), custom_call_target="tpu_custom_call" | custom-call | tf_op jit(solution)/shard_map/prepare/pallas_call | solution.py:431
  14.5 1.0 collective-permute-done.2.inner
  15.5 6.4 %forward.1 = (bf16[16,96,512]{2,1,0:T(8,128)(2,1)S(1)}, bf16[16,96,512]{2,1,0:T(8,128)(2,1)S(1)}, bf16[8,4,8,1024]{3,2,1,0:T(8,128)(2,1)S(1)}, bf16[8,4,8,1024]{...) custom-call(s32[2]{0:T(128)S(1)} %pad_add_fusion.place_ref, ...), custom_call_target="tpu_custom_call", output_to_operand_aliasing={{7}: (3, {})} | custom-call | tf_op jit(solution)/shard_map/forward/pallas_call | solution.py:457
  21.9 3.7 %collective-permute-start.4 = (bf16[16,96,512]{2,1,0:T(8,128)(2,1)S(1)}, bf16[16,96,512]{2,1,0:T(8,128)(2,1)S(1)}, u32[]{:S(2)}, u32[]{:S(2)}) collective-permute-start(bf16[16,96,512]{2,1,0:T(8,128)(2,1)S(1)} %get-tuple-element.65), channel_id=1, source_target_pairs={{0,32},{32,0},{1,33},{33,1},{2,34},{34,2},{3,35},{35,3},{4,36},{36... | collective-permute-start | bytes 4718600 | tf_op jit(solution)/shard_map/ppermute | solution.py:481
  25.7 3.1 %backward.1 = (bf16[8,32,512]{2,1,0:T(8,128)(2,1)S(1)}, bf16[16,8,512]{2,1,0:T(8,128)(2,1)S(1)}) custom-call(bf16[256,2048]{1,0:T(8,128)(2,1)S(1)} %get-tuple-element.66.dpre, bf16[512,2048]{1,0:T(8,128)(2,1)S(1)} %get-tuple-element.62.expand, f32[4,256,128]{2,1,0:T(8,128)S(1)} %get-tuple-element.67.xhat, f32[256,128]{1,0:T(8,128)S(1)} %get-tuple-element.68.rstd, ...), custom_call_target="tpu_custom_call" | custom-call | tf_op jit(solution)/shard_map/backward/pallas_call | solution.py:483
  29.3 0.7 collective-permute-start.8
  30.0 3.8 %collective-permute-start.7 = (bf16[3,32,512]{2,1,0:T(8,128)(2,1)S(1)}, bf16[3,32,512]{2,1,0:T(8,128)(2,1)S(1)}, u32[]{:S(2)}, u32[]{:S(2)}) collective-permute-start(bf16[3,32,512]{2,1,0:T(8,128)(2,1)S(1)} %get-tuple-element.111), channel_id=1, source_target_pairs={{0,32},{32,0},{64,96},{96,64},{128,160},{160,128},{192,224},{224,1... | collective-permute-start | bytes 294920 | tf_op jit(solution)/shard_map/ppermute | solution.py:388
  33.8 1.9 %merge.1 = bf16[16,104,512]{2,1,0:T(8,128)(2,1)} custom-call(bf16[16,96,512]{2,1,0:T(8,128)(2,1)S(1)} %get-tuple-element.64.kept, bf16[16,96,512]{2,1,0:T(8,128)(2,1)S(1)} %collective-permute-done.4.came, bf16[16,8,512]{2,1,0:T(8,128)(2,1)S(1)} %get-tuple-element.71.small, bf16[16,8,512]{2,1,0:T(8,128)(2,1)S(1)} %collective-permute-done.5.small_came), custom_call_target="tpu_custom_call" | custom-call | tf_op jit(solution)/shard_map/merge/pallas_call | solution.py:501
  35.7 7.8 %all-to-all-start = ((bf16[16,104,512]{2,1,0:T(8,128)(2,1)}), bf16[16,104,512]{2,1,0:T(8,128)(2,1)S(1)}, u32[]{:S(2)}, u32[]{:S(2)}) async-start(bf16[16,104,512]{2,1,0:T(8,128)(2,1)} %merge.1), calls=%async_computation | async-start | bytes 3407872 | tf_op jit(solution)/shard_map/all_to_all | solution.py:406
  44.2 1.2 %collective-permute-start.11 = (bf16[4,8,1024]{2,1,0:T(8,128)(2,1)S(1)}, bf16[4,8,1024]{2,1,0:T(8,128)(2,1)S(1)}, u32[]{:S(2)}, u32[]{:S(2)}) collective-permute-start(bf16[4,8,1024]{2,1,0:T(8,128)(2,1)S(1)} %get-tuple-element.81), channel_id=1, source_target_pairs={{0,1},{1,0},{2,3},{3,2},{4,5},{5,4},{6,7},{7,6},{8,9},{9,8},{10,11... | collective-permute-start | bytes 196616 | tf_op jit(solution)/shard_map/ppermute | solution.py:523
  45.4 1.4 %collective-permute-start.12 = (bf16[4,8,1024]{2,1,0:T(8,128)(2,1)S(1)}, bf16[4,8,1024]{2,1,0:T(8,128)(2,1)S(1)}, u32[]{:S(2)}, u32[]{:S(2)}) collective-permute-start(bf16[4,8,1024]{2,1,0:T(8,128)(2,1)S(1)} %get-tuple-element.82), channel_id=1, source_target_pairs={{0,2},{1,3},{2,0},{3,1},{4,6},{5,7},{6,4},{7,5},{8,10},{9,11},{10,... | collective-permute-start | bytes 196616 | tf_op jit(solution)/shard_map/ppermute | solution.py:523
  46.9 2.8 %collective-permute-start.10 = (bf16[14,3,512]{2,1,0:T(4,128)(2,1)S(1)}, bf16[14,3,512]{2,1,0:T(4,128)(2,1)S(1)}, u32[]{:S(2)}, u32[]{:S(2)}) collective-permute-start(bf16[14,3,512]{2,1,0:T(4,128)(2,1)S(1)} %get-tuple-element.116), channel_id=1, source_target_pairs={{1,2},{2,1},{3,4},{4,3},{5,6},{6,5},{7,8},{8,7},{9,10},{10,9},{11,... | collective-permute-start | bytes 129032 | tf_op jit(solution)/shard_map/ppermute | solution.py:389
  49.8 1.4 %collective-permute-start.9 = (bf16[14,3,512]{2,1,0:T(4,128)(2,1)S(1)}, bf16[14,3,512]{2,1,0:T(4,128)(2,1)S(1)}, u32[]{:S(2)}, u32[]{:S(2)}) collective-permute-start(bf16[14,3,512]{2,1,0:T(4,128)(2,1)S(1)} %get-tuple-element.117), channel_id=1, source_target_pairs={{0,1},{1,0},{2,3},{3,2},{4,5},{5,4},{6,7},{7,6},{8,9},{9,8},{10,11... | collective-permute-start | bytes 129032 | tf_op jit(solution)/shard_map/ppermute | solution.py:388
  51.2 2.0 %collective-permute-start.13 = (bf16[4,8,1024]{2,1,0:T(8,128)(2,1)S(1)}, bf16[4,8,1024]{2,1,0:T(8,128)(2,1)S(1)}, u32[]{:S(2)}, u32[]{:S(2)}) collective-permute-start(bf16[4,8,1024]{2,1,0:T(8,128)(2,1)S(1)} %get-tuple-element.83), channel_id=1, source_target_pairs={{0,3},{1,2},{2,1},{3,0},{4,7},{5,6},{6,5},{7,4},{8,11},{9,10},{10,... | collective-permute-start | bytes 196616 | tf_op jit(solution)/shard_map/ppermute | solution.py:523
  53.2 2.1 %collective-permute-done.10.outer = bf16[14,3,512]{2,1,0:T(4,128)(2,1)S(1)} collective-permute-done((bf16[14,3,512]{2,1,0:T(4,128)(2,1)S(1)}, bf16[14,3,512]{2,1,0:T(4,128)(2,1)S(1)}, u32[]{:S(2)}, u32[]{:S(2)}) %collective-permute-start.10) | collective-permute-done | bytes 43040 | tf_op jit(solution)/shard_map/ppermute | solution.py:389
  55.4 2.5 %collective-permute-start.14 = (bf16[4,8,1024]{2,1,0:T(8,128)(2,1)S(1)}, bf16[4,8,1024]{2,1,0:T(8,128)(2,1)S(1)}, u32[]{:S(2)}, u32[]{:S(2)}) collective-permute-start(bf16[4,8,1024]{2,1,0:T(8,128)(2,1)S(1)} %get-tuple-element.84), channel_id=1, source_target_pairs={{0,4},{1,5},{2,6},{3,7},{4,0},{5,1},{6,2},{7,3},{8,12},{9,13},{10,... | collective-permute-start | bytes 196616 | tf_op jit(solution)/shard_map/ppermute | solution.py:523
  57.9 1.2 %collective-permute-start.15 = (bf16[4,8,1024]{2,1,0:T(8,128)(2,1)S(1)}, bf16[4,8,1024]{2,1,0:T(8,128)(2,1)S(1)}, u32[]{:S(2)}, u32[]{:S(2)}) collective-permute-start(bf16[4,8,1024]{2,1,0:T(8,128)(2,1)S(1)} %get-tuple-element.85), channel_id=1, source_target_pairs={{0,5},{1,4},{2,7},{3,6},{4,1},{5,0},{6,3},{7,2},{8,13},{9,12},{10,... | collective-permute-start | bytes 196616 | tf_op jit(solution)/shard_map/ppermute | solution.py:523
  59.0 3.7 %collective-permute-start.16 = (bf16[4,8,1024]{2,1,0:T(8,128)(2,1)S(1)}, bf16[4,8,1024]{2,1,0:T(8,128)(2,1)S(1)}, u32[]{:S(2)}, u32[]{:S(2)}) collective-permute-start(bf16[4,8,1024]{2,1,0:T(8,128)(2,1)S(1)} %get-tuple-element.86), channel_id=1, source_target_pairs={{0,6},{1,7},{2,4},{3,5},{4,2},{5,3},{6,0},{7,1},{8,14},{9,15},{10,... | collective-permute-start | bytes 196616 | tf_op jit(solution)/shard_map/ppermute | solution.py:523
  62.8 1.8 %collective-permute-start.17 = (bf16[4,8,1024]{2,1,0:T(8,128)(2,1)S(1)}, bf16[4,8,1024]{2,1,0:T(8,128)(2,1)S(1)}, u32[]{:S(2)}, u32[]{:S(2)}) collective-permute-start(bf16[4,8,1024]{2,1,0:T(8,128)(2,1)S(1)} %get-tuple-element.87), channel_id=1, source_target_pairs={{0,7},{1,6},{2,5},{3,4},{4,3},{5,2},{6,1},{7,0},{8,15},{9,14},{10,... | collective-permute-start | bytes 196616 | tf_op jit(solution)/shard_map/ppermute | solution.py:523
  64.5 0.8 collective-permute-done.15.refs_5_
  65.3 1.7 %collective-permute-done.16.refs_6_ = bf16[4,8,1024]{2,1,0:T(8,128)(2,1)S(1)} collective-permute-done((bf16[4,8,1024]{2,1,0:T(8,128)(2,1)S(1)}, bf16[4,8,1024]{2,1,0:T(8,128)(2,1)S(1)}, u32[]{:S(2)}, u32[]{:S(2)}) %collective-permute-start.16) | collective-permute-done | bytes 65568 | tf_op jit(solution)/shard_map/ppermute | solution.py:523
  67.0 2.8 %collective-permute-done.17.refs_7_ = bf16[4,8,1024]{2,1,0:T(8,128)(2,1)S(1)} collective-permute-done((bf16[4,8,1024]{2,1,0:T(8,128)(2,1)S(1)}, bf16[4,8,1024]{2,1,0:T(8,128)(2,1)S(1)}, u32[]{:S(2)}, u32[]{:S(2)}) %collective-permute-start.17) | collective-permute-done | bytes 65568 | tf_op jit(solution)/shard_map/ppermute | solution.py:523
  70.2 14.5 %all_to_all.15.chunks = bf16[8,24,512]{2,1,0:T(8,128)(2,1)S(1)} all-to-all(bf16[8,24,512]{2,1,0:T(8,128)(2,1)S(1)} %plane.1), channel_id=1, replica_groups=mesh['y'=4,'core'=2,'x'=4,'z'=8] {'z'}, dimensions={0} | all-to-all | bytes 393216 | tf_op jit(solution)/shard_map/all_to_all | solution.py:406
  84.6 0.7 line.1
  85.4 7.1 %all-to-all-start.2 = ((bf16[16,8,512]{2,1,0:T(8,128)(2,1)}), bf16[16,8,512]{2,1,0:T(8,128)(2,1)S(1)}, u32[]{:S(2)}, u32[]{:S(2)}) async-start(bf16[16,8,512]{2,1,0:T(8,128)(2,1)} %get-tuple-element.101), calls=%async_computation.2 | async-start | bytes 262144 | tf_op jit(solution)/shard_map/all_to_all | solution.py:406
  92.5 3.3 %features.1 = bf16[8,32,512]{2,1,0:T(8,128)(2,1)} custom-call(s32[2]{0:T(128)S(1)} %pad_add_fusion.place_ref, bf16[8,32,512]{2,1,0:T(8,128)(2,1)S(1)} %get-tuple-element.74.field, bf16[3,32,512]{2,1,0:T(8,128)(2,1)S(1)} %collective-permute-done.7.row_inner, bf16[3,32,512]{2,1,0:T(8,128)(2,1)S(1)} %collective-permute-done.8.row_outer, ...), custom_call_target="tpu_custom_call" | custom-call | tf_op jit(solution)/shard_map/features/pallas_call | solution.py:559
  95.7 3.3 %all-to-all-done.2.chunks = bf16[16,8,512]{2,1,0:T(8,128)(2,1)S(1)} async-done(((bf16[16,8,512]{2,1,0:T(8,128)(2,1)}), bf16[16,8,512]{2,1,0:T(8,128)(2,1)S(1)}, u32[]{:S(2)}, u32[]{:S(2)}) %all-to-all-start.2) | async-done | bytes 131104 | tf_op jit(solution)/shard_map/all_to_all | solution.py:406
  99.1 0.7 last.1
  (32 shorter events, 2.2 us)
Async XLA Ops:
  1.6 1.7 %collective-permute-start = (bf16[3,32,512]{2,1,0:T(8,128)(2,1)S(1)}, bf16[3,32,512]{2,1,0:T(8,128)(2,1)S(1)}, u32[]{:S(2)}, u32[]{:S(2)}) collective-permute-start(bf16[3,32,512]{2,1,0:T(8,128)(2,1)S(1)} %get-tuple-element.114), channel_id=1, source_target_pairs={{0,32},{32,0},{64,96},{96,64},{128,160},{160,128},{192,224},{224,1... | collective-permute-start | bytes 294920 | tf_op jit(solution)/shard_map/ppermute | solution.py:388
  1.7 1.6 %collective-permute-start.1 = (bf16[3,32,512]{2,1,0:T(8,128)(2,1)S(1)}, bf16[3,32,512]{2,1,0:T(8,128)(2,1)S(1)}, u32[]{:S(2)}, u32[]{:S(2)}) collective-permute-start(bf16[3,32,512]{2,1,0:T(8,128)(2,1)S(1)} %get-tuple-element.115), channel_id=1, source_target_pairs={{32,64},{64,32},{96,128},{128,96},{160,192},{192,160},{33,65},{65,... | collective-permute-start | bytes 294920 | tf_op jit(solution)/shard_map/ppermute | solution.py:389
  3.5 11.0 %collective-permute-start.3 = (bf16[14,3,512]{2,1,0:T(4,128)(2,1)S(1)}, bf16[14,3,512]{2,1,0:T(4,128)(2,1)S(1)}, u32[]{:S(2)}, u32[]{:S(2)}) collective-permute-start(bf16[14,3,512]{2,1,0:T(4,128)(2,1)S(1)} %get-tuple-element.118), channel_id=1, source_target_pairs={{1,2},{2,1},{3,4},{4,3},{5,6},{6,5},{7,8},{8,7},{9,10},{10,9},{11,... | collective-permute-start | bytes 129032 | tf_op jit(solution)/shard_map/ppermute | solution.py:389
  11.2 4.3 %collective-permute-start.2 = (bf16[14,3,512]{2,1,0:T(4,128)(2,1)S(1)}, bf16[14,3,512]{2,1,0:T(4,128)(2,1)S(1)}, u32[]{:S(2)}, u32[]{:S(2)}) collective-permute-start(bf16[14,3,512]{2,1,0:T(4,128)(2,1)S(1)} %get-tuple-element.119), channel_id=1, source_target_pairs={{0,1},{1,0},{2,3},{3,2},{4,5},{5,4},{6,7},{7,6},{8,9},{9,8},{10,11... | collective-permute-start | bytes 129032 | tf_op jit(solution)/shard_map/ppermute | solution.py:388
  21.9 11.9 %collective-permute-start.4 = (bf16[16,96,512]{2,1,0:T(8,128)(2,1)S(1)}, bf16[16,96,512]{2,1,0:T(8,128)(2,1)S(1)}, u32[]{:S(2)}, u32[]{:S(2)}) collective-permute-start(bf16[16,96,512]{2,1,0:T(8,128)(2,1)S(1)} %get-tuple-element.65), channel_id=1, source_target_pairs={{0,32},{32,0},{1,33},{33,1},{2,34},{34,2},{3,35},{35,3},{4,36},{36... | collective-permute-start | bytes 4718600 | tf_op jit(solution)/shard_map/ppermute | solution.py:481
  25.6 10.1 %collective-permute-start.6 = (bf16[8,4,8,1024]{3,2,1,0:T(8,128)(2,1)S(1)}, bf16[8,4,8,1024]{3,2,1,0:T(8,128)(2,1)S(1)}, u32[]{:S(2)}, u32[]{:S(2)}) collective-permute-start(bf16[8,4,8,1024]{3,2,1,0:T(8,128)(2,1)S(1)} %get-tuple-element.73), channel_id=1, source_target_pairs={{0,32},{32,0},{1,33},{33,1},{2,34},{34,2},{3,35},{35,3},{4,36},{36... | collective-permute-start | bytes 1572872 | tf_op jit(solution)/shard_map/ppermute | solution.py:482
  28.8 5.0 %collective-permute-start.5 = (bf16[16,8,512]{2,1,0:T(8,128)(2,1)S(1)}, bf16[16,8,512]{2,1,0:T(8,128)(2,1)S(1)}, u32[]{:S(2)}, u32[]{:S(2)}) collective-permute-start(bf16[16,8,512]{2,1,0:T(8,128)(2,1)S(1)} %get-tuple-element.71.small), channel_id=1, source_target_pairs={{0,32},{32,0},{1,33},{33,1},{2,34},{34,2},{3,35},{35,3},{4,36},{36... | collective-permute-start | bytes 393224 | tf_op jit(solution)/shard_map/ppermute | solution.py:499
  29.3 6.4 %collective-permute-start.8 = (bf16[3,32,512]{2,1,0:T(8,128)(2,1)S(1)}, bf16[3,32,512]{2,1,0:T(8,128)(2,1)S(1)}, u32[]{:S(2)}, u32[]{:S(2)}) collective-permute-start(bf16[3,32,512]{2,1,0:T(8,128)(2,1)S(1)} %get-tuple-element.110), channel_id=1, source_target_pairs={{32,64},{64,32},{96,128},{128,96},{160,192},{192,160},{33,65},{65,... | collective-permute-start | bytes 294920 | tf_op jit(solution)/shard_map/ppermute | solution.py:389
  30.0 5.7 %collective-permute-start.7 = (bf16[3,32,512]{2,1,0:T(8,128)(2,1)S(1)}, bf16[3,32,512]{2,1,0:T(8,128)(2,1)S(1)}, u32[]{:S(2)}, u32[]{:S(2)}) collective-permute-start(bf16[3,32,512]{2,1,0:T(8,128)(2,1)S(1)} %get-tuple-element.111), channel_id=1, source_target_pairs={{0,32},{32,0},{64,96},{96,64},{128,160},{160,128},{192,224},{224,1... | collective-permute-start | bytes 294920 | tf_op jit(solution)/shard_map/ppermute | solution.py:388
  35.7 34.1 %all-to-all-start = ((bf16[16,104,512]{2,1,0:T(8,128)(2,1)}), bf16[16,104,512]{2,1,0:T(8,128)(2,1)S(1)}, u32[]{:S(2)}, u32[]{:S(2)}) async-start(bf16[16,104,512]{2,1,0:T(8,128)(2,1)} %merge.1), calls=%async_computation | async-start | bytes 3407872 | tf_op jit(solution)/shard_map/all_to_all | solution.py:406
  44.2 14.8 %collective-permute-start.11 = (bf16[4,8,1024]{2,1,0:T(8,128)(2,1)S(1)}, bf16[4,8,1024]{2,1,0:T(8,128)(2,1)S(1)}, u32[]{:S(2)}, u32[]{:S(2)}) collective-permute-start(bf16[4,8,1024]{2,1,0:T(8,128)(2,1)S(1)} %get-tuple-element.81), channel_id=1, source_target_pairs={{0,1},{1,0},{2,3},{3,2},{4,5},{5,4},{6,7},{7,6},{8,9},{9,8},{10,11... | collective-permute-start | bytes 196616 | tf_op jit(solution)/shard_map/ppermute | solution.py:523
  45.4 17.4 %collective-permute-start.12 = (bf16[4,8,1024]{2,1,0:T(8,128)(2,1)S(1)}, bf16[4,8,1024]{2,1,0:T(8,128)(2,1)S(1)}, u32[]{:S(2)}, u32[]{:S(2)}) collective-permute-start(bf16[4,8,1024]{2,1,0:T(8,128)(2,1)S(1)} %get-tuple-element.82), channel_id=1, source_target_pairs={{0,2},{1,3},{2,0},{3,1},{4,6},{5,7},{6,4},{7,5},{8,10},{9,11},{10,... | collective-permute-start | bytes 196616 | tf_op jit(solution)/shard_map/ppermute | solution.py:523
  46.9 45.5 %copy-start = (bf16[8,32,512]{2,1,0:T(8,128)(2,1)S(1)}, bf16[8,32,512]{2,1,0:T(8,128)(2,1)}, u32[]{:S(2)}) copy-start(bf16[8,32,512]{2,1,0:T(8,128)(2,1)} %cotangent.1) | copy-start | bytes 786436
  46.9 45.5 %copy-start.1 = (f32[7,7,512]{2,1,0:T(8,128)S(1)}, f32[7,7,512]{2,1,0:T(8,128)}, u32[]{:S(2)}) copy-start(f32[7,7,512]{2,1,0:T(8,128)} %taps.1) | copy-start | bytes 301060
  46.9 8.4 %collective-permute-start.10 = (bf16[14,3,512]{2,1,0:T(4,128)(2,1)S(1)}, bf16[14,3,512]{2,1,0:T(4,128)(2,1)S(1)}, u32[]{:S(2)}, u32[]{:S(2)}) collective-permute-start(bf16[14,3,512]{2,1,0:T(4,128)(2,1)S(1)} %get-tuple-element.116), channel_id=1, source_target_pairs={{1,2},{2,1},{3,4},{4,3},{5,6},{6,5},{7,8},{8,7},{9,10},{10,9},{11,... | collective-permute-start | bytes 129032 | tf_op jit(solution)/shard_map/ppermute | solution.py:389
  49.8 8.1 %collective-permute-start.9 = (bf16[14,3,512]{2,1,0:T(4,128)(2,1)S(1)}, bf16[14,3,512]{2,1,0:T(4,128)(2,1)S(1)}, u32[]{:S(2)}, u32[]{:S(2)}) collective-permute-start(bf16[14,3,512]{2,1,0:T(4,128)(2,1)S(1)} %get-tuple-element.117), channel_id=1, source_target_pairs={{0,1},{1,0},{2,3},{3,2},{4,5},{5,4},{6,7},{7,6},{8,9},{9,8},{10,11... | collective-permute-start | bytes 129032 | tf_op jit(solution)/shard_map/ppermute | solution.py:388
  51.2 13.3 %collective-permute-start.13 = (bf16[4,8,1024]{2,1,0:T(8,128)(2,1)S(1)}, bf16[4,8,1024]{2,1,0:T(8,128)(2,1)S(1)}, u32[]{:S(2)}, u32[]{:S(2)}) collective-permute-start(bf16[4,8,1024]{2,1,0:T(8,128)(2,1)S(1)} %get-tuple-element.83), channel_id=1, source_target_pairs={{0,3},{1,2},{2,1},{3,0},{4,7},{5,6},{6,5},{7,4},{8,11},{9,10},{10,... | collective-permute-start | bytes 196616 | tf_op jit(solution)/shard_map/ppermute | solution.py:523
  55.4 9.2 %collective-permute-start.14 = (bf16[4,8,1024]{2,1,0:T(8,128)(2,1)S(1)}, bf16[4,8,1024]{2,1,0:T(8,128)(2,1)S(1)}, u32[]{:S(2)}, u32[]{:S(2)}) collective-permute-start(bf16[4,8,1024]{2,1,0:T(8,128)(2,1)S(1)} %get-tuple-element.84), channel_id=1, source_target_pairs={{0,4},{1,5},{2,6},{3,7},{4,0},{5,1},{6,2},{7,3},{8,12},{9,13},{10,... | collective-permute-start | bytes 196616 | tf_op jit(solution)/shard_map/ppermute | solution.py:523
  57.9 7.5 %collective-permute-start.15 = (bf16[4,8,1024]{2,1,0:T(8,128)(2,1)S(1)}, bf16[4,8,1024]{2,1,0:T(8,128)(2,1)S(1)}, u32[]{:S(2)}, u32[]{:S(2)}) collective-permute-start(bf16[4,8,1024]{2,1,0:T(8,128)(2,1)S(1)} %get-tuple-element.85), channel_id=1, source_target_pairs={{0,5},{1,4},{2,7},{3,6},{4,1},{5,0},{6,3},{7,2},{8,13},{9,12},{10,... | collective-permute-start | bytes 196616 | tf_op jit(solution)/shard_map/ppermute | solution.py:523
  59.0 8.0 %collective-permute-start.16 = (bf16[4,8,1024]{2,1,0:T(8,128)(2,1)S(1)}, bf16[4,8,1024]{2,1,0:T(8,128)(2,1)S(1)}, u32[]{:S(2)}, u32[]{:S(2)}) collective-permute-start(bf16[4,8,1024]{2,1,0:T(8,128)(2,1)S(1)} %get-tuple-element.86), channel_id=1, source_target_pairs={{0,6},{1,7},{2,4},{3,5},{4,2},{5,3},{6,0},{7,1},{8,14},{9,15},{10,... | collective-permute-start | bytes 196616 | tf_op jit(solution)/shard_map/ppermute | solution.py:523
  62.8 7.1 %collective-permute-start.17 = (bf16[4,8,1024]{2,1,0:T(8,128)(2,1)S(1)}, bf16[4,8,1024]{2,1,0:T(8,128)(2,1)S(1)}, u32[]{:S(2)}, u32[]{:S(2)}) collective-permute-start(bf16[4,8,1024]{2,1,0:T(8,128)(2,1)S(1)} %get-tuple-element.87), channel_id=1, source_target_pairs={{0,7},{1,6},{2,5},{3,4},{4,3},{5,2},{6,1},{7,0},{8,15},{9,14},{10,... | collective-permute-start | bytes 196616 | tf_op jit(solution)/shard_map/ppermute | solution.py:523
  85.4 13.7 %all-to-all-start.2 = ((bf16[16,8,512]{2,1,0:T(8,128)(2,1)}), bf16[16,8,512]{2,1,0:T(8,128)(2,1)S(1)}, u32[]{:S(2)}, u32[]{:S(2)}) async-start(bf16[16,8,512]{2,1,0:T(8,128)(2,1)} %get-tuple-element.101), calls=%async_computation.2 | async-start | bytes 262144 | tf_op jit(solution)/shard_map/all_to_all | solution.py:406

commit v12 on v11

--- a/solution.py
+++ b/solution.py
@@ -312,10 +312,11 @@
         out[...] = added(kept[z], came[z])
 
 
-def plane_kernel(chunks, out, total):
+def plane_kernel(place_ref, chunks, *refs):
+    *outs, out, total = refs
     total[...] = jnp.sum(chunks[...].astype(jnp.float32), axis=0)
     each = (out.shape[1] - 2 * SMALL) // 2
-    channels = out.shape[2]
+    channels = total.shape[1]
     top = total.shape[0] - 2 * SMALL - each * Z
     blocks = (channels - ALONG) // LANES
     small = total[pl.ds(total.shape[0] - 2 * SMALL, 2 * SMALL), :].astype(jnp.bfloat16)
@@ -326,11 +327,14 @@
         parts = [total[pl.ds(top + q * 2 * Z + 2 * z, 2), :] for q in range(each // 2)]
         out[z, pl.ds(each, each), :] = jnp.concatenate(parts).astype(jnp.bfloat16)
         out[z, pl.ds(2 * each, 2 * SMALL), :] = small
-
-
-def line_kernel(multiplier, chunks, *refs):
+    for step, target in enumerate(outs):
+        target[...] = out[place_ref[1] ^ step]
+
+
+def line_kernel(multiplier, *refs):
     *came, part_out, dexpand, out = refs
-    total = jnp.sum(chunks[...].astype(jnp.float32), axis=0)
+    chunks, came = came[:Z], came[Z:]
+    total = sum(ref[...].astype(jnp.float32) for ref in chunks)
     each, channels = part_out.shape
     part_out[...] = total[:each] * multiplier
     for q in range(each // 2):
@@ -402,6 +406,13 @@
     return inner, outer, *swapped(low, high, COL, lax.axis_index("z") % 2 == 0)
 
 
+def along_z(parts):
+    return [
+        part if step == 0 else lax.ppermute(part, "z", [(i, i ^ step) for i in range(Z)])
+        for step, part in enumerate(parts)
+    ]
+
+
 def exchanged(chunks, axes):
     return lax.all_to_all(chunks, axes, 0, 0, tiled=True)
 
@@ -519,26 +530,27 @@
         out_shape=[shape(kept_z.shape[1:], bf16)] * Z,
         compiler_params=GLUE_PARAMS,
     )(place, kept_z, came_z)
-    line = [
-        part if step == 0 else lax.ppermute(part, "z", [(i, i ^ step) for i in range(Z)])
-        for step, part in enumerate(line)
-    ]
+    line = along_z(line)
     chunks, edges, line = lax.optimization_barrier(
         (exchanged(chip, ("y", "x")), column_borders(dconv, *rows_came, reach), line)
     )
+    per_z = 2 * each + 2 * SMALL
     chunks = pl.pallas_call(
         plane_kernel,
         name="plane",
-        in_specs=[VMEM],
-        out_specs=VMEM,
-        out_shape=shape((Z, 2 * each + 2 * SMALL, channels), bf16),
-        scratch_shapes=[pltpu.VMEM((whole, channels), f32)],
+        in_specs=[SMEM, VMEM],
+        out_specs=[VMEM] * Z,
+        out_shape=[shape((per_z, channels), bf16)] * Z,
+        scratch_shapes=[
+            pltpu.VMEM((Z, per_z, channels), bf16),
+            pltpu.VMEM((whole, channels), f32),
+        ],
         compiler_params=GLUE_PARAMS,
-    )(chunks)
+    )(place, chunks)
     part, dexpand, chunks = pl.pallas_call(
         functools.partial(line_kernel, multiplier),
         name="line",
-        in_specs=[VMEM] * (1 + Z),
+        in_specs=[VMEM] * (2 * Z),
         out_specs=[VMEM] * 3,
         out_shape=[
             shape((each, channels), f32),
@@ -546,7 +558,7 @@
             shape((places, each, channels), bf16),
         ],
         compiler_params=GLUE_PARAMS,
-    )(exchanged(chunks, "z"), *line)
+    )(*along_z(chunks), *line)
     dreduce, dkernel, dgain, dscale = pl.pallas_call(
         functools.partial(last_kernel, multiplier),
         name="last",

time: 100 us -> 104 us (1.040)
  blocking collectives: 14.5 us -> 0 us
  starting transfers between devices: 50.3 us -> 63.6 us
  waiting for transfers between devices: 11.7 us -> 15.8 us
    all_to_all x1 -> x0, blocking collectives: 14.5 us -> none  [exchanged(): return lax.all_to_all(chunks, axes, 0, 0, tiled=True)]
    ppermute x7 -> x14, starting transfers between devices: 13.7 us -> 27.4 us  [along_z(): lax.ppermute(part, 'z', [(i, i ^ step) for i in range(Z)])]
    ppermute x7 -> x14, waiting for transfers between devices: 5.29 us -> 9.31 us  [along_z(): lax.ppermute(part, 'z', [(i, i ^ step) for i in range(Z)])]
  transfers between devices with their start and end apart: 20 -> 27, of which waited for: 6 -> 8; matrix products, arithmetic and copies ran while one was open for 1% -> 1% of each run, Pallas kernels for 12% -> 12%
where the time goes in v12:
time: 104 us; the launch traced here: 103 us
  starting transfers between devices  63.6 us (61%)
  Pallas kernels  20.8 us (20%)
  waiting for transfers between devices  15.8 us (15%)
  other arithmetic  1.25 us (1%)
    ppermute x14, starting transfers between devices, along_z(): lax.ppermute(part, 'z', [(i, i ^ step) for i in range(Z)])  27.4 us
    all_to_all x2, starting transfers between devices, exchanged(): return lax.all_to_all(chunks, axes, 0, 0, tiled=True)  14.7 us
    ppermute x4, starting transfers between devices, swapped(): lax.ppermute(jnp.where(first, low, high), axes, outer)  11.8 us
    ppermute x14, waiting for transfers between devices, along_z(): lax.ppermute(part, 'z', [(i, i ^ step) for i in range(Z)])  9.31 us
    pallas_call x1, Pallas kernels, shards(): pl.pallas_call(forward_kernel, name='forward', in_specs=[SMEM] + [VMEM] *...  6.4 us
    ppermute x4, starting transfers between devices, swapped(): lax.ppermute(jnp.where(first, high, low), axes, inner)  5.42 us
    ppermute x1, starting transfers between devices, shards(): came = lax.ppermute(sent, 'core', swap)  3.69 us
    all_to_all x2, waiting for transfers between devices, exchanged(): return lax.all_to_all(chunks, axes, 0, 0, tiled=True)  3.33 us
  transfers between devices with their start and end apart: 27, of which 8 were waited for; matrix products, arithmetic and copies ran while one was open for 1% of the time, Pallas kernels for 12%

profile of v12, /device:TPU:2, one launch (start us, length us, event | category | flops | bytes accessed | tf_op | source)
XLA Modules:
  0.0 103.2 jit_solution(12443345959905430830)
XLA Ops:
  0.6 1.0 broadcast_select_fusion.3
  3.5 7.7 %collective-permute-start.3 = (bf16[14,3,512]{2,1,0:T(4,128)(2,1)S(1)}, bf16[14,3,512]{2,1,0:T(4,128)(2,1)S(1)}, u32[]{:S(2)}, u32[]{:S(2)}) collective-permute-start(bf16[14,3,512]{2,1,0:T(4,128)(2,1)S(1)} %get-tuple-element.134), channel_id=1, source_target_pairs={{1,2},{2,1},{3,4},{4,3},{5,6},{6,5},{7,8},{8,7},{9,10},{10,9},{11,... | collective-permute-start | bytes 129032 | tf_op jit(solution)/shard_map/ppermute | solution.py:393
  11.4 3.1 %prepare.1 = (f32[4,14,48,128]{3,2,1,0:T(8,128)S(1)}, f32[4,256,128]{2,1,0:T(8,128)S(1)}, bf16[256,512]{1,0:T(8,128)(2,1)S(1)}, f32[7,7,512]{2,1,0:T(8,128)S(1)}...) custom-call(s32[2]{0:T(128)S(1)} %pad_add_fusion.place_ref, ...), custom_call_target="tpu_custom_call" | custom-call | tf_op jit(solution)/shard_map/prepare/pallas_call | solution.py:442
  14.5 1.0 collective-permute-done.2.inner
  15.5 6.4 %forward.1 = (bf16[16,96,512]{2,1,0:T(8,128)(2,1)S(1)}, bf16[16,96,512]{2,1,0:T(8,128)(2,1)S(1)}, bf16[8,4,8,1024]{3,2,1,0:T(8,128)(2,1)S(1)}, bf16[8,4,8,1024]{...) custom-call(s32[2]{0:T(128)S(1)} %pad_add_fusion.place_ref, ...), custom_call_target="tpu_custom_call", output_to_operand_aliasing={{7}: (3, {})} | custom-call | tf_op jit(solution)/shard_map/forward/pallas_call | solution.py:468
  21.9 3.7 %collective-permute-start.4 = (bf16[16,96,512]{2,1,0:T(8,128)(2,1)S(1)}, bf16[16,96,512]{2,1,0:T(8,128)(2,1)S(1)}, u32[]{:S(2)}, u32[]{:S(2)}) collective-permute-start(bf16[16,96,512]{2,1,0:T(8,128)(2,1)S(1)} %get-tuple-element.73), channel_id=1, source_target_pairs={{0,32},{32,0},{1,33},{33,1},{2,34},{34,2},{3,35},{35,3},{4,36},{36... | collective-permute-start | bytes 4718600 | tf_op jit(solution)/shard_map/ppermute | solution.py:492
  25.7 3.1 %backward.1 = (bf16[8,32,512]{2,1,0:T(8,128)(2,1)S(1)}, bf16[16,8,512]{2,1,0:T(8,128)(2,1)S(1)}) custom-call(bf16[256,2048]{1,0:T(8,128)(2,1)S(1)} %get-tuple-element.74.dpre, bf16[512,2048]{1,0:T(8,128)(2,1)S(1)} %get-tuple-element.70.expand, f32[4,256,128]{2,1,0:T(8,128)S(1)} %get-tuple-element.75.xhat, f32[256,128]{1,0:T(8,128)S(1)} %get-tuple-element.76.rstd, ...), custom_call_target="tpu_custom_call" | custom-call | tf_op jit(solution)/shard_map/backward/pallas_call | solution.py:494
  30.0 3.8 %collective-permute-start.7 = (bf16[3,32,512]{2,1,0:T(8,128)(2,1)S(1)}, bf16[3,32,512]{2,1,0:T(8,128)(2,1)S(1)}, u32[]{:S(2)}, u32[]{:S(2)}) collective-permute-start(bf16[3,32,512]{2,1,0:T(8,128)(2,1)S(1)} %get-tuple-element.127), channel_id=1, source_target_pairs={{0,32},{32,0},{64,96},{96,64},{128,160},{160,128},{192,224},{224,1... | collective-permute-start | bytes 294920 | tf_op jit(solution)/shard_map/ppermute | solution.py:392
  33.8 1.9 %merge.1 = bf16[16,104,512]{2,1,0:T(8,128)(2,1)} custom-call(bf16[16,96,512]{2,1,0:T(8,128)(2,1)S(1)} %get-tuple-element.72.kept, bf16[16,96,512]{2,1,0:T(8,128)(2,1)S(1)} %collective-permute-done.4.came, bf16[16,8,512]{2,1,0:T(8,128)(2,1)S(1)} %get-tuple-element.79.small, bf16[16,8,512]{2,1,0:T(8,128)(2,1)S(1)} %collective-permute-done.5.small_came), custom_call_target="tpu_custom_call" | custom-call | tf_op jit(solution)/shard_map/merge/pallas_call | solution.py:512
  35.7 7.8 %all-to-all-start = ((bf16[16,104,512]{2,1,0:T(8,128)(2,1)}), bf16[16,104,512]{2,1,0:T(8,128)(2,1)S(1)}, u32[]{:S(2)}, u32[]{:S(2)}) async-start(bf16[16,104,512]{2,1,0:T(8,128)(2,1)} %merge.1), calls=%async_computation | async-start | bytes 3407872 | tf_op jit(solution)/shard_map/all_to_all | solution.py:417
  44.2 1.2 %collective-permute-start.11 = (bf16[4,8,1024]{2,1,0:T(8,128)(2,1)S(1)}, bf16[4,8,1024]{2,1,0:T(8,128)(2,1)S(1)}, u32[]{:S(2)}, u32[]{:S(2)}) collective-permute-start(bf16[4,8,1024]{2,1,0:T(8,128)(2,1)S(1)} %get-tuple-element.89), channel_id=1, source_target_pairs={{0,1},{1,0},{2,3},{3,2},{4,5},{5,4},{6,7},{7,6},{8,9},{9,8},{10,11... | collective-permute-start | bytes 196616 | tf_op jit(solution)/shard_map/ppermute | solution.py:411
  45.4 1.4 %collective-permute-start.12 = (bf16[4,8,1024]{2,1,0:T(8,128)(2,1)S(1)}, bf16[4,8,1024]{2,1,0:T(8,128)(2,1)S(1)}, u32[]{:S(2)}, u32[]{:S(2)}) collective-permute-start(bf16[4,8,1024]{2,1,0:T(8,128)(2,1)S(1)} %get-tuple-element.90), channel_id=1, source_target_pairs={{0,2},{1,3},{2,0},{3,1},{4,6},{5,7},{6,4},{7,5},{8,10},{9,11},{10,... | collective-permute-start | bytes 196616 | tf_op jit(solution)/shard_map/ppermute | solution.py:411
  46.9 2.7 %collective-permute-start.10 = (bf16[14,3,512]{2,1,0:T(4,128)(2,1)S(1)}, bf16[14,3,512]{2,1,0:T(4,128)(2,1)S(1)}, u32[]{:S(2)}, u32[]{:S(2)}) collective-permute-start(bf16[14,3,512]{2,1,0:T(4,128)(2,1)S(1)} %get-tuple-element.132), channel_id=1, source_target_pairs={{1,2},{2,1},{3,4},{4,3},{5,6},{6,5},{7,8},{8,7},{9,10},{10,9},{11,... | collective-permute-start | bytes 129032 | tf_op jit(solution)/shard_map/ppermute | solution.py:393
  49.6 1.4 %collective-permute-start.9 = (bf16[14,3,512]{2,1,0:T(4,128)(2,1)S(1)}, bf16[14,3,512]{2,1,0:T(4,128)(2,1)S(1)}, u32[]{:S(2)}, u32[]{:S(2)}) collective-permute-start(bf16[14,3,512]{2,1,0:T(4,128)(2,1)S(1)} %get-tuple-element.133), channel_id=1, source_target_pairs={{0,1},{1,0},{2,3},{3,2},{4,5},{5,4},{6,7},{7,6},{8,9},{9,8},{10,11... | collective-permute-start | bytes 129032 | tf_op jit(solution)/shard_map/ppermute | solution.py:392
  51.1 2.0 %collective-permute-start.13 = (bf16[4,8,1024]{2,1,0:T(8,128)(2,1)S(1)}, bf16[4,8,1024]{2,1,0:T(8,128)(2,1)S(1)}, u32[]{:S(2)}, u32[]{:S(2)}) collective-permute-start(bf16[4,8,1024]{2,1,0:T(8,128)(2,1)S(1)} %get-tuple-element.91), channel_id=1, source_target_pairs={{0,3},{1,2},{2,1},{3,0},{4,7},{5,6},{6,5},{7,4},{8,11},{9,10},{10,... | collective-permute-start | bytes 196616 | tf_op jit(solution)/shard_map/ppermute | solution.py:411
  53.1 2.1 %collective-permute-done.10.outer = bf16[14,3,512]{2,1,0:T(4,128)(2,1)S(1)} collective-permute-done((bf16[14,3,512]{2,1,0:T(4,128)(2,1)S(1)}, bf16[14,3,512]{2,1,0:T(4,128)(2,1)S(1)}, u32[]{:S(2)}, u32[]{:S(2)}) %collective-permute-start.10) | collective-permute-done | bytes 43040 | tf_op jit(solution)/shard_map/ppermute | solution.py:393
  55.2 2.5 %collective-permute-start.14 = (bf16[4,8,1024]{2,1,0:T(8,128)(2,1)S(1)}, bf16[4,8,1024]{2,1,0:T(8,128)(2,1)S(1)}, u32[]{:S(2)}, u32[]{:S(2)}) collective-permute-start(bf16[4,8,1024]{2,1,0:T(8,128)(2,1)S(1)} %get-tuple-element.92), channel_id=1, source_target_pairs={{0,4},{1,5},{2,6},{3,7},{4,0},{5,1},{6,2},{7,3},{8,12},{9,13},{10,... | collective-permute-start | bytes 196616 | tf_op jit(solution)/shard_map/ppermute | solution.py:411
  57.7 1.2 %collective-permute-start.15 = (bf16[4,8,1024]{2,1,0:T(8,128)(2,1)S(1)}, bf16[4,8,1024]{2,1,0:T(8,128)(2,1)S(1)}, u32[]{:S(2)}, u32[]{:S(2)}) collective-permute-start(bf16[4,8,1024]{2,1,0:T(8,128)(2,1)S(1)} %get-tuple-element.93), channel_id=1, source_target_pairs={{0,5},{1,4},{2,7},{3,6},{4,1},{5,0},{6,3},{7,2},{8,13},{9,12},{10,... | collective-permute-start | bytes 196616 | tf_op jit(solution)/shard_map/ppermute | solution.py:411
  58.9 3.7 %collective-permute-start.16 = (bf16[4,8,1024]{2,1,0:T(8,128)(2,1)S(1)}, bf16[4,8,1024]{2,1,0:T(8,128)(2,1)S(1)}, u32[]{:S(2)}, u32[]{:S(2)}) collective-permute-start(bf16[4,8,1024]{2,1,0:T(8,128)(2,1)S(1)} %get-tuple-element.94), channel_id=1, source_target_pairs={{0,6},{1,7},{2,4},{3,5},{4,2},{5,3},{6,0},{7,1},{8,14},{9,15},{10,... | collective-permute-start | bytes 196616 | tf_op jit(solution)/shard_map/ppermute | solution.py:411
  62.6 1.8 %collective-permute-start.17 = (bf16[4,8,1024]{2,1,0:T(8,128)(2,1)S(1)}, bf16[4,8,1024]{2,1,0:T(8,128)(2,1)S(1)}, u32[]{:S(2)}, u32[]{:S(2)}) collective-permute-start(bf16[4,8,1024]{2,1,0:T(8,128)(2,1)S(1)} %get-tuple-element.95), channel_id=1, source_target_pairs={{0,7},{1,6},{2,5},{3,4},{4,3},{5,2},{6,1},{7,0},{8,15},{9,14},{10,... | collective-permute-start | bytes 196616 | tf_op jit(solution)/shard_map/ppermute | solution.py:411
  65.2 1.7 %collective-permute-done.16.refs_14_ = bf16[4,8,1024]{2,1,0:T(8,128)(2,1)S(1)} collective-permute-done((bf16[4,8,1024]{2,1,0:T(8,128)(2,1)S(1)}, bf16[4,8,1024]{2,1,0:T(8,128)(2,1)S(1)}, u32[]{:S(2)}, u32[]{:S(2)}) %collective-permute-start.16) | collective-permute-done | bytes 65568 | tf_op jit(solution)/shard_map/ppermute | solution.py:411
  66.9 2.8 %collective-permute-done.17.refs_15_ = bf16[4,8,1024]{2,1,0:T(8,128)(2,1)S(1)} collective-permute-done((bf16[4,8,1024]{2,1,0:T(8,128)(2,1)S(1)}, bf16[4,8,1024]{2,1,0:T(8,128)(2,1)S(1)}, u32[]{:S(2)}, u32[]{:S(2)}) %collective-permute-start.17) | collective-permute-done | bytes 65568 | tf_op jit(solution)/shard_map/ppermute | solution.py:411
  71.3 1.9 %collective-permute-start.19 = (bf16[24,512]{1,0:T(8,128)(2,1)S(1)}, bf16[24,512]{1,0:T(8,128)(2,1)S(1)}, u32[]{:S(2)}, u32[]{:S(2)}) collective-permute-start(bf16[24,512]{1,0:T(8,128)(2,1)S(1)} %get-tuple-element.103), channel_id=1, source_target_pairs={{0,2},{1,3},{2,0},{3,1},{4,6},{5,7},{6,4},{7,5},{8,10},{9,11},{10,... | collective-permute-start | bytes 73736 | tf_op jit(solution)/shard_map/ppermute | solution.py:411
  73.3 1.8 %collective-permute-start.20 = (bf16[24,512]{1,0:T(8,128)(2,1)S(1)}, bf16[24,512]{1,0:T(8,128)(2,1)S(1)}, u32[]{:S(2)}, u32[]{:S(2)}) collective-permute-start(bf16[24,512]{1,0:T(8,128)(2,1)S(1)} %get-tuple-element.104), channel_id=1, source_target_pairs={{0,3},{1,2},{2,1},{3,0},{4,7},{5,6},{6,5},{7,4},{8,11},{9,10},{10,... | collective-permute-start | bytes 73736 | tf_op jit(solution)/shard_map/ppermute | solution.py:411
  75.1 3.3 %collective-permute-start.21 = (bf16[24,512]{1,0:T(8,128)(2,1)S(1)}, bf16[24,512]{1,0:T(8,128)(2,1)S(1)}, u32[]{:S(2)}, u32[]{:S(2)}) collective-permute-start(bf16[24,512]{1,0:T(8,128)(2,1)S(1)} %get-tuple-element.105), channel_id=1, source_target_pairs={{0,4},{1,5},{2,6},{3,7},{4,0},{5,1},{6,2},{7,3},{8,12},{9,13},{10,... | collective-permute-start | bytes 73736 | tf_op jit(solution)/shard_map/ppermute | solution.py:411
  79.3 3.7 %collective-permute-start.23 = (bf16[24,512]{1,0:T(8,128)(2,1)S(1)}, bf16[24,512]{1,0:T(8,128)(2,1)S(1)}, u32[]{:S(2)}, u32[]{:S(2)}) collective-permute-start(bf16[24,512]{1,0:T(8,128)(2,1)S(1)} %get-tuple-element.107), channel_id=1, source_target_pairs={{0,6},{1,7},{2,4},{3,5},{4,2},{5,3},{6,0},{7,1},{8,14},{9,15},{10,... | collective-permute-start | bytes 73736 | tf_op jit(solution)/shard_map/ppermute | solution.py:411
  83.0 1.2 %collective-permute-start.24 = (bf16[24,512]{1,0:T(8,128)(2,1)S(1)}, bf16[24,512]{1,0:T(8,128)(2,1)S(1)}, u32[]{:S(2)}, u32[]{:S(2)}) collective-permute-start(bf16[24,512]{1,0:T(8,128)(2,1)S(1)} %get-tuple-element.108), channel_id=1, source_target_pairs={{0,7},{1,6},{2,5},{3,4},{4,3},{5,2},{6,1},{7,0},{8,15},{9,14},{10,... | collective-permute-start | bytes 73736 | tf_op jit(solution)/shard_map/ppermute | solution.py:411
  84.3 1.2 %collective-permute-done.22.refs_5_ = bf16[24,512]{1,0:T(8,128)(2,1)S(1)} collective-permute-done((bf16[24,512]{1,0:T(8,128)(2,1)S(1)}, bf16[24,512]{1,0:T(8,128)(2,1)S(1)}, u32[]{:S(2)}, u32[]{:S(2)}) %collective-permute-start.22) | collective-permute-done | bytes 24608 | tf_op jit(solution)/shard_map/ppermute | solution.py:411
  85.5 2.8 %collective-permute-done.24.refs_7_ = bf16[24,512]{1,0:T(8,128)(2,1)S(1)} collective-permute-done((bf16[24,512]{1,0:T(8,128)(2,1)S(1)}, bf16[24,512]{1,0:T(8,128)(2,1)S(1)}, u32[]{:S(2)}, u32[]{:S(2)}) %collective-permute-start.24) | collective-permute-done | bytes 24608 | tf_op jit(solution)/shard_map/ppermute | solution.py:411
  89.0 6.9 %all-to-all-start.1 = ((bf16[16,8,512]{2,1,0:T(8,128)(2,1)}), bf16[16,8,512]{2,1,0:T(8,128)(2,1)S(1)}, u32[]{:S(2)}, u32[]{:S(2)}) async-start(bf16[16,8,512]{2,1,0:T(8,128)(2,1)} %get-tuple-element.117), calls=%async_computation.1 | async-start | bytes 262144 | tf_op jit(solution)/shard_map/all_to_all | solution.py:417
  95.9 3.3 %features.1 = bf16[8,32,512]{2,1,0:T(8,128)(2,1)} custom-call(s32[2]{0:T(128)S(1)} %pad_add_fusion.place_ref, bf16[8,32,512]{2,1,0:T(8,128)(2,1)S(1)} %get-tuple-element.82.field, bf16[3,32,512]{2,1,0:T(8,128)(2,1)S(1)} %collective-permute-done.7.row_inner, bf16[3,32,512]{2,1,0:T(8,128)(2,1)S(1)} %collective-permute-done.8.row_outer, ...), custom_call_target="tpu_custom_call" | custom-call | tf_op jit(solution)/shard_map/features/pallas_call | solution.py:571
  99.2 3.3 %all-to-all-done.1.chunks = bf16[16,8,512]{2,1,0:T(8,128)(2,1)S(1)} async-done(((bf16[16,8,512]{2,1,0:T(8,128)(2,1)}), bf16[16,8,512]{2,1,0:T(8,128)(2,1)S(1)}, u32[]{:S(2)}, u32[]{:S(2)}) %all-to-all-start.1) | async-done | bytes 131104 | tf_op jit(solution)/shard_map/all_to_all | solution.py:417
  (45 shorter events, 8.8 us)
Async XLA Ops:
  1.6 1.7 %collective-permute-start = (bf16[3,32,512]{2,1,0:T(8,128)(2,1)S(1)}, bf16[3,32,512]{2,1,0:T(8,128)(2,1)S(1)}, u32[]{:S(2)}, u32[]{:S(2)}) collective-permute-start(bf16[3,32,512]{2,1,0:T(8,128)(2,1)S(1)} %get-tuple-element.130), channel_id=1, source_target_pairs={{0,32},{32,0},{64,96},{96,64},{128,160},{160,128},{192,224},{224,1... | collective-permute-start | bytes 294920 | tf_op jit(solution)/shard_map/ppermute | solution.py:392
  1.7 1.6 %collective-permute-start.1 = (bf16[3,32,512]{2,1,0:T(8,128)(2,1)S(1)}, bf16[3,32,512]{2,1,0:T(8,128)(2,1)S(1)}, u32[]{:S(2)}, u32[]{:S(2)}) collective-permute-start(bf16[3,32,512]{2,1,0:T(8,128)(2,1)S(1)} %get-tuple-element.131), channel_id=1, source_target_pairs={{32,64},{64,32},{96,128},{128,96},{160,192},{192,160},{33,65},{65,... | collective-permute-start | bytes 294920 | tf_op jit(solution)/shard_map/ppermute | solution.py:393
  3.5 11.0 %collective-permute-start.3 = (bf16[14,3,512]{2,1,0:T(4,128)(2,1)S(1)}, bf16[14,3,512]{2,1,0:T(4,128)(2,1)S(1)}, u32[]{:S(2)}, u32[]{:S(2)}) collective-permute-start(bf16[14,3,512]{2,1,0:T(4,128)(2,1)S(1)} %get-tuple-element.134), channel_id=1, source_target_pairs={{1,2},{2,1},{3,4},{4,3},{5,6},{6,5},{7,8},{8,7},{9,10},{10,9},{11,... | collective-permute-start | bytes 129032 | tf_op jit(solution)/shard_map/ppermute | solution.py:393
  11.2 4.3 %collective-permute-start.2 = (bf16[14,3,512]{2,1,0:T(4,128)(2,1)S(1)}, bf16[14,3,512]{2,1,0:T(4,128)(2,1)S(1)}, u32[]{:S(2)}, u32[]{:S(2)}) collective-permute-start(bf16[14,3,512]{2,1,0:T(4,128)(2,1)S(1)} %get-tuple-element.135), channel_id=1, source_target_pairs={{0,1},{1,0},{2,3},{3,2},{4,5},{5,4},{6,7},{7,6},{8,9},{9,8},{10,11... | collective-permute-start | bytes 129032 | tf_op jit(solution)/shard_map/ppermute | solution.py:392
  21.9 11.9 %collective-permute-start.4 = (bf16[16,96,512]{2,1,0:T(8,128)(2,1)S(1)}, bf16[16,96,512]{2,1,0:T(8,128)(2,1)S(1)}, u32[]{:S(2)}, u32[]{:S(2)}) collective-permute-start(bf16[16,96,512]{2,1,0:T(8,128)(2,1)S(1)} %get-tuple-element.73), channel_id=1, source_target_pairs={{0,32},{32,0},{1,33},{33,1},{2,34},{34,2},{3,35},{35,3},{4,36},{36... | collective-permute-start | bytes 4718600 | tf_op jit(solution)/shard_map/ppermute | solution.py:492
  25.6 10.1 %collective-permute-start.6 = (bf16[8,4,8,1024]{3,2,1,0:T(8,128)(2,1)S(1)}, bf16[8,4,8,1024]{3,2,1,0:T(8,128)(2,1)S(1)}, u32[]{:S(2)}, u32[]{:S(2)}) collective-permute-start(bf16[8,4,8,1024]{3,2,1,0:T(8,128)(2,1)S(1)} %get-tuple-element.81), channel_id=1, source_target_pairs={{0,32},{32,0},{1,33},{33,1},{2,34},{34,2},{3,35},{35,3},{4,36},{36... | collective-permute-start | bytes 1572872 | tf_op jit(solution)/shard_map/ppermute | solution.py:493
  28.8 5.0 %collective-permute-start.5 = (bf16[16,8,512]{2,1,0:T(8,128)(2,1)S(1)}, bf16[16,8,512]{2,1,0:T(8,128)(2,1)S(1)}, u32[]{:S(2)}, u32[]{:S(2)}) collective-permute-start(bf16[16,8,512]{2,1,0:T(8,128)(2,1)S(1)} %get-tuple-element.79.small), channel_id=1, source_target_pairs={{0,32},{32,0},{1,33},{33,1},{2,34},{34,2},{3,35},{35,3},{4,36},{36... | collective-permute-start | bytes 393224 | tf_op jit(solution)/shard_map/ppermute | solution.py:510
  29.3 6.4 %collective-permute-start.8 = (bf16[3,32,512]{2,1,0:T(8,128)(2,1)S(1)}, bf16[3,32,512]{2,1,0:T(8,128)(2,1)S(1)}, u32[]{:S(2)}, u32[]{:S(2)}) collective-permute-start(bf16[3,32,512]{2,1,0:T(8,128)(2,1)S(1)} %get-tuple-element.126), channel_id=1, source_target_pairs={{32,64},{64,32},{96,128},{128,96},{160,192},{192,160},{33,65},{65,... | collective-permute-start | bytes 294920 | tf_op jit(solution)/shard_map/ppermute | solution.py:393
  30.0 5.7 %collective-permute-start.7 = (bf16[3,32,512]{2,1,0:T(8,128)(2,1)S(1)}, bf16[3,32,512]{2,1,0:T(8,128)(2,1)S(1)}, u32[]{:S(2)}, u32[]{:S(2)}) collective-permute-start(bf16[3,32,512]{2,1,0:T(8,128)(2,1)S(1)} %get-tuple-element.127), channel_id=1, source_target_pairs={{0,32},{32,0},{64,96},{96,64},{128,160},{160,128},{192,224},{224,1... | collective-permute-start | bytes 294920 | tf_op jit(solution)/shard_map/ppermute | solution.py:392
  35.7 34.0 %all-to-all-start = ((bf16[16,104,512]{2,1,0:T(8,128)(2,1)}), bf16[16,104,512]{2,1,0:T(8,128)(2,1)S(1)}, u32[]{:S(2)}, u32[]{:S(2)}) async-start(bf16[16,104,512]{2,1,0:T(8,128)(2,1)} %merge.1), calls=%async_computation | async-start | bytes 3407872 | tf_op jit(solution)/shard_map/all_to_all | solution.py:417
  44.2 51.7 %copy-start = (bf16[8,32,512]{2,1,0:T(8,128)(2,1)S(1)}, bf16[8,32,512]{2,1,0:T(8,128)(2,1)}, u32[]{:S(2)}) copy-start(bf16[8,32,512]{2,1,0:T(8,128)(2,1)} %cotangent.1) | copy-start | bytes 786436
  44.2 51.7 %copy-start.1 = (f32[7,7,512]{2,1,0:T(8,128)S(1)}, f32[7,7,512]{2,1,0:T(8,128)}, u32[]{:S(2)}) copy-start(f32[7,7,512]{2,1,0:T(8,128)} %taps.1) | copy-start | bytes 301060
  44.2 14.7 %collective-permute-start.11 = (bf16[4,8,1024]{2,1,0:T(8,128)(2,1)S(1)}, bf16[4,8,1024]{2,1,0:T(8,128)(2,1)S(1)}, u32[]{:S(2)}, u32[]{:S(2)}) collective-permute-start(bf16[4,8,1024]{2,1,0:T(8,128)(2,1)S(1)} %get-tuple-element.89), channel_id=1, source_target_pairs={{0,1},{1,0},{2,3},{3,2},{4,5},{5,4},{6,7},{7,6},{8,9},{9,8},{10,11... | collective-permute-start | bytes 196616 | tf_op jit(solution)/shard_map/ppermute | solution.py:411
  45.4 17.2 %collective-permute-start.12 = (bf16[4,8,1024]{2,1,0:T(8,128)(2,1)S(1)}, bf16[4,8,1024]{2,1,0:T(8,128)(2,1)S(1)}, u32[]{:S(2)}, u32[]{:S(2)}) collective-permute-start(bf16[4,8,1024]{2,1,0:T(8,128)(2,1)S(1)} %get-tuple-element.90), channel_id=1, source_target_pairs={{0,2},{1,3},{2,0},{3,1},{4,6},{5,7},{6,4},{7,5},{8,10},{9,11},{10,... | collective-permute-start | bytes 196616 | tf_op jit(solution)/shard_map/ppermute | solution.py:411
  46.9 8.3 %collective-permute-start.10 = (bf16[14,3,512]{2,1,0:T(4,128)(2,1)S(1)}, bf16[14,3,512]{2,1,0:T(4,128)(2,1)S(1)}, u32[]{:S(2)}, u32[]{:S(2)}) collective-permute-start(bf16[14,3,512]{2,1,0:T(4,128)(2,1)S(1)} %get-tuple-element.132), channel_id=1, source_target_pairs={{1,2},{2,1},{3,4},{4,3},{5,6},{6,5},{7,8},{8,7},{9,10},{10,9},{11,... | collective-permute-start | bytes 129032 | tf_op jit(solution)/shard_map/ppermute | solution.py:393
  49.6 8.1 %collective-permute-start.9 = (bf16[14,3,512]{2,1,0:T(4,128)(2,1)S(1)}, bf16[14,3,512]{2,1,0:T(4,128)(2,1)S(1)}, u32[]{:S(2)}, u32[]{:S(2)}) collective-permute-start(bf16[14,3,512]{2,1,0:T(4,128)(2,1)S(1)} %get-tuple-element.133), channel_id=1, source_target_pairs={{0,1},{1,0},{2,3},{3,2},{4,5},{5,4},{6,7},{7,6},{8,9},{9,8},{10,11... | collective-permute-start | bytes 129032 | tf_op jit(solution)/shard_map/ppermute | solution.py:392
  51.1 13.3 %collective-permute-start.13 = (bf16[4,8,1024]{2,1,0:T(8,128)(2,1)S(1)}, bf16[4,8,1024]{2,1,0:T(8,128)(2,1)S(1)}, u32[]{:S(2)}, u32[]{:S(2)}) collective-permute-start(bf16[4,8,1024]{2,1,0:T(8,128)(2,1)S(1)} %get-tuple-element.91), channel_id=1, source_target_pairs={{0,3},{1,2},{2,1},{3,0},{4,7},{5,6},{6,5},{7,4},{8,11},{9,10},{10,... | collective-permute-start | bytes 196616 | tf_op jit(solution)/shard_map/ppermute | solution.py:411
  55.2 9.2 %collective-permute-start.14 = (bf16[4,8,1024]{2,1,0:T(8,128)(2,1)S(1)}, bf16[4,8,1024]{2,1,0:T(8,128)(2,1)S(1)}, u32[]{:S(2)}, u32[]{:S(2)}) collective-permute-start(bf16[4,8,1024]{2,1,0:T(8,128)(2,1)S(1)} %get-tuple-element.92), channel_id=1, source_target_pairs={{0,4},{1,5},{2,6},{3,7},{4,0},{5,1},{6,2},{7,3},{8,12},{9,13},{10,... | collective-permute-start | bytes 196616 | tf_op jit(solution)/shard_map/ppermute | solution.py:411
  57.7 7.4 %collective-permute-start.15 = (bf16[4,8,1024]{2,1,0:T(8,128)(2,1)S(1)}, bf16[4,8,1024]{2,1,0:T(8,128)(2,1)S(1)}, u32[]{:S(2)}, u32[]{:S(2)}) collective-permute-start(bf16[4,8,1024]{2,1,0:T(8,128)(2,1)S(1)} %get-tuple-element.93), channel_id=1, source_target_pairs={{0,5},{1,4},{2,7},{3,6},{4,1},{5,0},{6,3},{7,2},{8,13},{9,12},{10,... | collective-permute-start | bytes 196616 | tf_op jit(solution)/shard_map/ppermute | solution.py:411
  58.9 8.0 %collective-permute-start.16 = (bf16[4,8,1024]{2,1,0:T(8,128)(2,1)S(1)}, bf16[4,8,1024]{2,1,0:T(8,128)(2,1)S(1)}, u32[]{:S(2)}, u32[]{:S(2)}) collective-permute-start(bf16[4,8,1024]{2,1,0:T(8,128)(2,1)S(1)} %get-tuple-element.94), channel_id=1, source_target_pairs={{0,6},{1,7},{2,4},{3,5},{4,2},{5,3},{6,0},{7,1},{8,14},{9,15},{10,... | collective-permute-start | bytes 196616 | tf_op jit(solution)/shard_map/ppermute | solution.py:411
  62.6 7.1 %collective-permute-start.17 = (bf16[4,8,1024]{2,1,0:T(8,128)(2,1)S(1)}, bf16[4,8,1024]{2,1,0:T(8,128)(2,1)S(1)}, u32[]{:S(2)}, u32[]{:S(2)}) collective-permute-start(bf16[4,8,1024]{2,1,0:T(8,128)(2,1)S(1)} %get-tuple-element.95), channel_id=1, source_target_pairs={{0,7},{1,6},{2,5},{3,4},{4,3},{5,2},{6,1},{7,0},{8,15},{9,14},{10,... | collective-permute-start | bytes 196616 | tf_op jit(solution)/shard_map/ppermute | solution.py:411
  70.6 8.7 %collective-permute-start.18 = (bf16[24,512]{1,0:T(8,128)(2,1)S(1)}, bf16[24,512]{1,0:T(8,128)(2,1)S(1)}, u32[]{:S(2)}, u32[]{:S(2)}) collective-permute-start(bf16[24,512]{1,0:T(8,128)(2,1)S(1)} %get-tuple-element.102), channel_id=1, source_target_pairs={{0,1},{1,0},{2,3},{3,2},{4,5},{5,4},{6,7},{7,6},{8,9},{9,8},{10,11... | collective-permute-start | bytes 73736 | tf_op jit(solution)/shard_map/ppermute | solution.py:411
  71.3 11.7 %collective-permute-start.19 = (bf16[24,512]{1,0:T(8,128)(2,1)S(1)}, bf16[24,512]{1,0:T(8,128)(2,1)S(1)}, u32[]{:S(2)}, u32[]{:S(2)}) collective-permute-start(bf16[24,512]{1,0:T(8,128)(2,1)S(1)} %get-tuple-element.103), channel_id=1, source_target_pairs={{0,2},{1,3},{2,0},{3,1},{4,6},{5,7},{6,4},{7,5},{8,10},{9,11},{10,... | collective-permute-start | bytes 73736 | tf_op jit(solution)/shard_map/ppermute | solution.py:411
  73.3 11.0 %collective-permute-start.20 = (bf16[24,512]{1,0:T(8,128)(2,1)S(1)}, bf16[24,512]{1,0:T(8,128)(2,1)S(1)}, u32[]{:S(2)}, u32[]{:S(2)}) collective-permute-start(bf16[24,512]{1,0:T(8,128)(2,1)S(1)} %get-tuple-element.104), channel_id=1, source_target_pairs={{0,3},{1,2},{2,1},{3,0},{4,7},{5,6},{6,5},{7,4},{8,11},{9,10},{10,... | collective-permute-start | bytes 73736 | tf_op jit(solution)/shard_map/ppermute | solution.py:411
  75.1 9.2 %collective-permute-start.21 = (bf16[24,512]{1,0:T(8,128)(2,1)S(1)}, bf16[24,512]{1,0:T(8,128)(2,1)S(1)}, u32[]{:S(2)}, u32[]{:S(2)}) collective-permute-start(bf16[24,512]{1,0:T(8,128)(2,1)S(1)} %get-tuple-element.105), channel_id=1, source_target_pairs={{0,4},{1,5},{2,6},{3,7},{4,0},{5,1},{6,2},{7,3},{8,12},{9,13},{10,... | collective-permute-start | bytes 73736 | tf_op jit(solution)/shard_map/ppermute | solution.py:411
  78.4 7.1 %collective-permute-start.22 = (bf16[24,512]{1,0:T(8,128)(2,1)S(1)}, bf16[24,512]{1,0:T(8,128)(2,1)S(1)}, u32[]{:S(2)}, u32[]{:S(2)}) collective-permute-start(bf16[24,512]{1,0:T(8,128)(2,1)S(1)} %get-tuple-element.106), channel_id=1, source_target_pairs={{0,5},{1,4},{2,7},{3,6},{4,1},{5,0},{6,3},{7,2},{8,13},{9,12},{10,... | collective-permute-start | bytes 73736 | tf_op jit(solution)/shard_map/ppermute | solution.py:411
  79.3 6.2 %collective-permute-start.23 = (bf16[24,512]{1,0:T(8,128)(2,1)S(1)}, bf16[24,512]{1,0:T(8,128)(2,1)S(1)}, u32[]{:S(2)}, u32[]{:S(2)}) collective-permute-start(bf16[24,512]{1,0:T(8,128)(2,1)S(1)} %get-tuple-element.107), channel_id=1, source_target_pairs={{0,6},{1,7},{2,4},{3,5},{4,2},{5,3},{6,0},{7,1},{8,14},{9,15},{10,... | collective-permute-start | bytes 73736 | tf_op jit(solution)/shard_map/ppermute | solution.py:411
  83.0 5.3 %collective-permute-start.24 = (bf16[24,512]{1,0:T(8,128)(2,1)S(1)}, bf16[24,512]{1,0:T(8,128)(2,1)S(1)}, u32[]{:S(2)}, u32[]{:S(2)}) collective-permute-start(bf16[24,512]{1,0:T(8,128)(2,1)S(1)} %get-tuple-element.108), channel_id=1, source_target_pairs={{0,7},{1,6},{2,5},{3,4},{4,3},{5,2},{6,1},{7,0},{8,15},{9,14},{10,... | collective-permute-start | bytes 73736 | tf_op jit(solution)/shard_map/ppermute | solution.py:411
  89.0 13.5 %all-to-all-start.1 = ((bf16[16,8,512]{2,1,0:T(8,128)(2,1)}), bf16[16,8,512]{2,1,0:T(8,128)(2,1)S(1)}, u32[]{:S(2)}, u32[]{:S(2)}) async-start(bf16[16,8,512]{2,1,0:T(8,128)(2,1)} %get-tuple-element.117), calls=%async_computation.1 | async-start | bytes 262144 | tf_op jit(solution)/shard_map/all_to_all | solution.py:417

commit v13 on v11

--- a/solution.py
+++ b/solution.py
@@ -102,7 +102,7 @@
 
 
 def prepare_kernel(
-    place_ref, field_h, inner, outer, taps_h, gain_h, scale_h, cotangent_h, expand_h, reduce_h,
+    field_h, inner, outer, taps_h, gain_h, scale_h, cotangent_h, expand_h, reduce_h,
     padded, conv, dbranch, taps, rows_out, expand, reduce,
     field, gain, scale, cotangent, sems,
 ):
@@ -125,7 +125,7 @@
     for copy in copies[:2]:
         copy.wait()
     height, width, channels = field.shape
-    fill_own(padded, field, inner, outer, place_ref[0] == 0, taps.shape[0] // 2)
+    fill_own(padded, field, inner, outer, lax.axis_index("core") == 0, taps.shape[0] // 2)
     conv_columns(conv, padded, taps, height, width, range(8, width - 8, 8))
     for copy in copies[2:5]:
         copy.wait()
@@ -139,12 +139,12 @@
 
 
 def forward_kernel(
-    place_ref, inner, outer, padded_in, conv, dbranch, taps, rows_in, expand, reduce,
+    inner, outer, padded_in, conv, dbranch, taps, rows_in, expand, reduce,
     sent, kept, sent_z, kept_z, dpre_out, xhat_out, rstd_out, padded, dscale_out,
     normed, turned, chosen,
 ):
-    core = place_ref[0]
-    first_column = lax.rem(place_ref[1], 2) == 0
+    core = lax.axis_index("core")
+    first_column = lax.rem(lax.axis_index("z"), 2) == 0
     del padded_in
     blocks = padded.shape[0]
     side = taps.shape[0]
@@ -277,12 +277,12 @@
 
 
 def feature_kernel(
-    place_ref, field, row_inner, row_outer, inner, outer, taps, cotangent, out, padded
+    field, row_inner, row_outer, inner, outer, taps, cotangent, out, padded
 ):
     height, width, channels = field.shape
     side = 7
-    first_row = place_ref[0] == 0
-    first_column = lax.rem(place_ref[1], 2) == 0
+    first_row = lax.axis_index("core") == 0
+    first_column = lax.rem(lax.axis_index("z"), 2) == 0
     fill_own(padded, field, row_inner, row_outer, first_row, side // 2)
     fill_sides(padded, inner, outer, first_row, first_column, width, side // 2)
     for block in range(channels // LANES):
@@ -306,9 +306,9 @@
     out[:, pl.ds(rows, small.shape[1]), :] = added(small[...], small_came[...])
 
 
-def join_kernel(place_ref, kept, came, *outs):
+def join_kernel(kept, came, *outs):
     for step, out in enumerate(outs):
-        z = place_ref[1] ^ step
+        z = lax.axis_index("z") ^ step
         out[...] = added(kept[z], came[z])
 
 
@@ -371,7 +371,6 @@
 
 VMEM = pl.BlockSpec(memory_space=pltpu.VMEM)
 HBM = pl.BlockSpec(memory_space=pltpu.HBM)
-SMEM = pl.BlockSpec(memory_space=pltpu.SMEM)
 PARAMS = pltpu.CompilerParams(vmem_limit_bytes=20 << 20)
 GLUE_PARAMS = pltpu.CompilerParams(vmem_limit_bytes=10 << 20)
 
@@ -416,7 +415,6 @@
     multiplier = 1.0 / math.sqrt(pixels * lax.axis_size(ROW) * lax.axis_size(COL))
     gain_row = gain.reshape(1, channels)
     scale_row = layer_scale.reshape(1, channels)
-    place = jnp.stack([lax.axis_index("core"), lax.axis_index("z")])
     places = Y * X
     rows = hidden // (Y * CORE * X)
     f32, bf16 = jnp.float32, jnp.bfloat16
@@ -431,7 +429,7 @@
     padded, conv, dbranch, taps, params, expand, reduce = pl.pallas_call(
         prepare_kernel,
         name="prepare",
-        in_specs=[SMEM, HBM] + [VMEM] * 2 + [HBM] * 6,
+        in_specs=[HBM] + [VMEM] * 2 + [HBM] * 6,
         out_specs=[VMEM] * 7,
         out_shape=[
             shape(padded_shape, f32),
@@ -451,13 +449,13 @@
         ],
         compiler_params=PARAMS,
     )(
-        place, in_hbm(features), row_inner, row_outer, in_hbm(kernel), in_hbm(gain_row),
+        in_hbm(features), row_inner, row_outer, in_hbm(kernel), in_hbm(gain_row),
         in_hbm(scale_row), in_hbm(cotangent), in_hbm(w_expand), in_hbm(w_reduce),
     )
     sent, kept, sent_z, kept_z, dpre, xhat, rstd, padded, dscale = pl.pallas_call(
         forward_kernel,
         name="forward",
-        in_specs=[SMEM] + [VMEM] * 9,
+        in_specs=[VMEM] * 9,
         out_specs=[VMEM] * 9,
         out_shape=[shape((places, top + rows, channels), bf16)] * 2
         + [shape((Z, Y, each, X * ALONG), bf16)] * 2
@@ -473,9 +471,9 @@
             pltpu.VMEM((channels, pixels), bf16),
             pltpu.VMEM((channels, pixels), bf16),
         ],
-        input_output_aliases={3: 7},
+        input_output_aliases={2: 7},
         compiler_params=PARAMS,
-    )(place, inner, outer, padded, conv, dbranch, taps, params, expand, reduce)
+    )(inner, outer, padded, conv, dbranch, taps, params, expand, reduce)
 
     swap = [(0, 1), (1, 0)]
     came = lax.ppermute(sent, "core", swap)
@@ -514,11 +512,11 @@
     line = pl.pallas_call(
         join_kernel,
         name="join",
-        in_specs=[SMEM] + [VMEM] * 2,
+        in_specs=[VMEM] * 2,
         out_specs=[VMEM] * Z,
         out_shape=[shape(kept_z.shape[1:], bf16)] * Z,
         compiler_params=GLUE_PARAMS,
-    )(place, kept_z, came_z)
+    )(kept_z, came_z)
     line = [
         part if step == 0 else lax.ppermute(part, "z", [(i, i ^ step) for i in range(Z)])
         for step, part in enumerate(line)
@@ -559,12 +557,12 @@
     grad_features = pl.pallas_call(
         feature_kernel,
         name="features",
-        in_specs=[SMEM] + [VMEM] * 7,
+        in_specs=[VMEM] * 7,
         out_specs=VMEM,
         out_shape=shape((height, width, channels), bf16),
         scratch_shapes=[pltpu.VMEM(padded_shape, f32)],
         compiler_params=GLUE_PARAMS,
-    )(place, dconv, *edges, kernel, cotangent)
+    )(dconv, *edges, kernel, cotangent)
     return (
         grad_features,
         dkernel,

time: 100 us -> 98.9 us (0.989)
  Pallas kernels: 20.2 us -> 17.7 us
  waiting for transfers between devices: 11.7 us -> 12.9 us
    pallas_call x4, Pallas kernels: 13.4 us -> 11.2 us  [the longest x1 5.74 us: shards(): pl.pallas_call(forward_kernel, name='forward', in_specs=[VMEM] * 9, out_s...]
  transfers between devices with their start and end apart: 20 -> 20, of which waited for: 6 -> 6; matrix products, arithmetic and copies ran while one was open for 1% -> 1% of each run, Pallas kernels for 12% -> 10%
where the time goes in v13:
time: 98.9 us; the launch traced here: 98.4 us
  starting transfers between devices  50.4 us (51%)
  Pallas kernels  17.7 us (18%)
  blocking collectives  14.4 us (15%)
  waiting for transfers between devices  12.9 us (13%)
  other arithmetic  1.17 us (1%)
  local copies, waits for them, and re-layouts  1 us (1%)
    all_to_all x2, starting transfers between devices, exchanged(): return lax.all_to_all(chunks, axes, 0, 0, tiled=True)  15 us
    all_to_all x1, blocking collectives, exchanged(): return lax.all_to_all(chunks, axes, 0, 0, tiled=True)  14.4 us
    ppermute x7, starting transfers between devices, shards(): lax.ppermute(part, 'z', [(i, i ^ step) for i in range(Z)])  14.4 us
    ppermute x4, starting transfers between devices, swapped(): lax.ppermute(jnp.where(first, low, high), axes, outer)  11.9 us
    pallas_call x1, Pallas kernels, shards(): pl.pallas_call(forward_kernel, name='forward', in_specs=[VMEM] * 9, out_s...  5.74 us
    ppermute x7, waiting for transfers between devices, shards(): lax.ppermute(part, 'z', [(i, i ^ step) for i in range(Z)])  5.27 us
    ppermute x4, starting transfers between devices, swapped(): lax.ppermute(jnp.where(first, high, low), axes, inner)  5.07 us
    all_to_all x2, waiting for transfers between devices, exchanged(): return lax.all_to_all(chunks, axes, 0, 0, tiled=True)  3.87 us
  transfers between devices with their start and end apart: 20, of which 6 were waited for; matrix products, arithmetic and copies ran while one was open for 1% of the time, Pallas kernels for 10%

profile of v13, /device:TPU:2, one launch (start us, length us, event | category | flops | bytes accessed | tf_op | source)
XLA Modules:
  0.0 98.4 jit_solution(7699535977939131847)
XLA Ops:
  0.6 1.0 broadcast_select_fusion.3
  1.7 0.7 collective-permute-start.1
  2.4 0.9 fusion.1
  3.5 7.7 %collective-permute-start.3 = (bf16[14,3,512]{2,1,0:T(4,128)(2,1)S(1)}, bf16[14,3,512]{2,1,0:T(4,128)(2,1)S(1)}, u32[]{:S(2)}, u32[]{:S(2)}) collective-permute-start(bf16[14,3,512]{2,1,0:T(4,128)(2,1)S(1)} %get-tuple-element.118), channel_id=1, source_target_pairs={{1,2},{2,1},{3,4},{4,3},{5,6},{6,5},{7,8},{8,7},{9,10},{10,9},{11,... | collective-permute-start | bytes 129032 | tf_op jit(solution)/shard_map/ppermute | solution.py:388
  11.3 2.6 %prepare.1 = (f32[4,14,48,128]{3,2,1,0:T(8,128)S(1)}, f32[4,256,128]{2,1,0:T(8,128)S(1)}, bf16[256,512]{1,0:T(8,128)(2,1)S(1)}, f32[7,7,512]{2,1,0:T(8,128)S(1)}...) custom-call(bf16[8,32,512]{2,1,0:T(8,128)(2,1)} %field_h.1, ...), custom_call_target="tpu_custom_call" | custom-call | tf_op jit(solution)/shard_map/prepare/pallas_call | solution.py:429
  13.9 1.6 %collective-permute-done.2.inner = bf16[14,3,512]{2,1,0:T(4,128)(2,1)S(1)} collective-permute-done((bf16[14,3,512]{2,1,0:T(4,128)(2,1)S(1)}, bf16[14,3,512]{2,1,0:T(4,128)(2,1)S(1)}, u32[]{:S(2)}, u32[]{:S(2)}) %collective-permute-start.2) | collective-permute-done | bytes 43040 | tf_op jit(solution)/shard_map/ppermute | solution.py:387
  15.5 5.7 %forward.1 = (bf16[16,96,512]{2,1,0:T(8,128)(2,1)S(1)}, bf16[16,96,512]{2,1,0:T(8,128)(2,1)S(1)}, bf16[8,4,8,1024]{3,2,1,0:T(8,128)(2,1)S(1)}, bf16[8,4,8,1024]{...) custom-call(bf16[14,3,512]{2,1,0:T(4,128)(2,1)S(1)} %collective-perm, ...), custom_call_target="tpu_custom_call", output_to_operand_aliasing={{7}: (2, {})} | custom-call | tf_op jit(solution)/shard_map/forward/pallas_call | solution.py:455
  21.2 3.4 %collective-permute-start.4 = (bf16[16,96,512]{2,1,0:T(8,128)(2,1)S(1)}, bf16[16,96,512]{2,1,0:T(8,128)(2,1)S(1)}, u32[]{:S(2)}, u32[]{:S(2)}) collective-permute-start(bf16[16,96,512]{2,1,0:T(8,128)(2,1)S(1)} %get-tuple-element.65), channel_id=1, source_target_pairs={{0,32},{32,0},{1,33},{33,1},{2,34},{34,2},{3,35},{35,3},{4,36},{36... | collective-permute-start | bytes 4718600 | tf_op jit(solution)/shard_map/ppermute | solution.py:479
  24.7 2.8 %backward.1 = (bf16[8,32,512]{2,1,0:T(8,128)(2,1)S(1)}, bf16[16,8,512]{2,1,0:T(8,128)(2,1)S(1)}) custom-call(bf16[256,2048]{1,0:T(8,128)(2,1)S(1)} %get-tuple-element.66.dpre, bf16[512,2048]{1,0:T(8,128)(2,1)S(1)} %get-tuple-element.62.expand, f32[4,256,128]{2,1,0:T(8,128)S(1)} %get-tuple-element.67.xhat, f32[256,128]{1,0:T(8,128)S(1)} %get-tuple-element.68.rstd, ...), custom_call_target="tpu_custom_call" | custom-call | tf_op jit(solution)/shard_map/backward/pallas_call | solution.py:481
  28.1 0.7 collective-permute-start.8
  28.8 4.1 %collective-permute-start.7 = (bf16[3,32,512]{2,1,0:T(8,128)(2,1)S(1)}, bf16[3,32,512]{2,1,0:T(8,128)(2,1)S(1)}, u32[]{:S(2)}, u32[]{:S(2)}) collective-permute-start(bf16[3,32,512]{2,1,0:T(8,128)(2,1)S(1)} %get-tuple-element.111), channel_id=1, source_target_pairs={{0,32},{32,0},{64,96},{96,64},{128,160},{160,128},{192,224},{224,1... | collective-permute-start | bytes 294920 | tf_op jit(solution)/shard_map/ppermute | solution.py:387
  32.9 1.9 %merge.1 = bf16[16,104,512]{2,1,0:T(8,128)(2,1)} custom-call(bf16[16,96,512]{2,1,0:T(8,128)(2,1)S(1)} %get-tuple-element.64.kept, bf16[16,96,512]{2,1,0:T(8,128)(2,1)S(1)} %collective-permute-done.4.came, bf16[16,8,512]{2,1,0:T(8,128)(2,1)S(1)} %get-tuple-element.71.small, bf16[16,8,512]{2,1,0:T(8,128)(2,1)S(1)} %collective-permute-done.5.small_came), custom_call_target="tpu_custom_call" | custom-call | tf_op jit(solution)/shard_map/merge/pallas_call | solution.py:499
  34.8 7.8 %all-to-all-start = ((bf16[16,104,512]{2,1,0:T(8,128)(2,1)}), bf16[16,104,512]{2,1,0:T(8,128)(2,1)S(1)}, u32[]{:S(2)}, u32[]{:S(2)}) async-start(bf16[16,104,512]{2,1,0:T(8,128)(2,1)} %merge.1), calls=%async_computation | async-start | bytes 3407872 | tf_op jit(solution)/shard_map/all_to_all | solution.py:405
  42.7 0.6 collective-permute-start.11
  43.3 2.0 %collective-permute-start.12 = (bf16[4,8,1024]{2,1,0:T(8,128)(2,1)S(1)}, bf16[4,8,1024]{2,1,0:T(8,128)(2,1)S(1)}, u32[]{:S(2)}, u32[]{:S(2)}) collective-permute-start(bf16[4,8,1024]{2,1,0:T(8,128)(2,1)S(1)} %get-tuple-element.82), channel_id=1, source_target_pairs={{0,2},{1,3},{2,0},{3,1},{4,6},{5,7},{6,4},{7,5},{8,10},{9,11},{10,... | collective-permute-start | bytes 196616 | tf_op jit(solution)/shard_map/ppermute | solution.py:521
  45.5 2.8 %collective-permute-start.10 = (bf16[14,3,512]{2,1,0:T(4,128)(2,1)S(1)}, bf16[14,3,512]{2,1,0:T(4,128)(2,1)S(1)}, u32[]{:S(2)}, u32[]{:S(2)}) collective-permute-start(bf16[14,3,512]{2,1,0:T(4,128)(2,1)S(1)} %get-tuple-element.116), channel_id=1, source_target_pairs={{1,2},{2,1},{3,4},{4,3},{5,6},{6,5},{7,8},{8,7},{9,10},{10,9},{11,... | collective-permute-start | bytes 129032 | tf_op jit(solution)/shard_map/ppermute | solution.py:388
  48.3 0.8 collective-permute-start.9
  49.1 2.7 %collective-permute-start.13 = (bf16[4,8,1024]{2,1,0:T(8,128)(2,1)S(1)}, bf16[4,8,1024]{2,1,0:T(8,128)(2,1)S(1)}, u32[]{:S(2)}, u32[]{:S(2)}) collective-permute-start(bf16[4,8,1024]{2,1,0:T(8,128)(2,1)S(1)} %get-tuple-element.83), channel_id=1, source_target_pairs={{0,3},{1,2},{2,1},{3,0},{4,7},{5,6},{6,5},{7,4},{8,11},{9,10},{10,... | collective-permute-start | bytes 196616 | tf_op jit(solution)/shard_map/ppermute | solution.py:521
  51.8 2.1 %collective-permute-done.10.outer = bf16[14,3,512]{2,1,0:T(4,128)(2,1)S(1)} collective-permute-done((bf16[14,3,512]{2,1,0:T(4,128)(2,1)S(1)}, bf16[14,3,512]{2,1,0:T(4,128)(2,1)S(1)}, u32[]{:S(2)}, u32[]{:S(2)}) %collective-permute-start.10) | collective-permute-done | bytes 43040 | tf_op jit(solution)/shard_map/ppermute | solution.py:388
  53.9 2.5 %collective-permute-start.14 = (bf16[4,8,1024]{2,1,0:T(8,128)(2,1)S(1)}, bf16[4,8,1024]{2,1,0:T(8,128)(2,1)S(1)}, u32[]{:S(2)}, u32[]{:S(2)}) collective-permute-start(bf16[4,8,1024]{2,1,0:T(8,128)(2,1)S(1)} %get-tuple-element.84), channel_id=1, source_target_pairs={{0,4},{1,5},{2,6},{3,7},{4,0},{5,1},{6,2},{7,3},{8,12},{9,13},{10,... | collective-permute-start | bytes 196616 | tf_op jit(solution)/shard_map/ppermute | solution.py:521
  56.4 0.9 collective-permute-start.15
  57.3 4.2 %collective-permute-start.16 = (bf16[4,8,1024]{2,1,0:T(8,128)(2,1)S(1)}, bf16[4,8,1024]{2,1,0:T(8,128)(2,1)S(1)}, u32[]{:S(2)}, u32[]{:S(2)}) collective-permute-start(bf16[4,8,1024]{2,1,0:T(8,128)(2,1)S(1)} %get-tuple-element.86), channel_id=1, source_target_pairs={{0,6},{1,7},{2,4},{3,5},{4,2},{5,3},{6,0},{7,1},{8,14},{9,15},{10,... | collective-permute-start | bytes 196616 | tf_op jit(solution)/shard_map/ppermute | solution.py:521
  61.5 1.6 %collective-permute-start.17 = (bf16[4,8,1024]{2,1,0:T(8,128)(2,1)S(1)}, bf16[4,8,1024]{2,1,0:T(8,128)(2,1)S(1)}, u32[]{:S(2)}, u32[]{:S(2)}) collective-permute-start(bf16[4,8,1024]{2,1,0:T(8,128)(2,1)S(1)} %get-tuple-element.87), channel_id=1, source_target_pairs={{0,7},{1,6},{2,5},{3,4},{4,3},{5,2},{6,1},{7,0},{8,15},{9,14},{10,... | collective-permute-start | bytes 196616 | tf_op jit(solution)/shard_map/ppermute | solution.py:521
  63.1 0.7 collective-permute-done.15.refs_5_
  63.8 1.8 %collective-permute-done.16.refs_6_ = bf16[4,8,1024]{2,1,0:T(8,128)(2,1)S(1)} collective-permute-done((bf16[4,8,1024]{2,1,0:T(8,128)(2,1)S(1)}, bf16[4,8,1024]{2,1,0:T(8,128)(2,1)S(1)}, u32[]{:S(2)}, u32[]{:S(2)}) %collective-permute-start.16) | collective-permute-done | bytes 65568 | tf_op jit(solution)/shard_map/ppermute | solution.py:521
  65.6 2.8 %collective-permute-done.17.refs_7_ = bf16[4,8,1024]{2,1,0:T(8,128)(2,1)S(1)} collective-permute-done((bf16[4,8,1024]{2,1,0:T(8,128)(2,1)S(1)}, bf16[4,8,1024]{2,1,0:T(8,128)(2,1)S(1)}, u32[]{:S(2)}, u32[]{:S(2)}) %collective-permute-start.17) | collective-permute-done | bytes 65568 | tf_op jit(solution)/shard_map/ppermute | solution.py:521
  68.7 14.4 %all_to_all.15.chunks = bf16[8,24,512]{2,1,0:T(8,128)(2,1)S(1)} all-to-all(bf16[8,24,512]{2,1,0:T(8,128)(2,1)S(1)} %plane.1), channel_id=1, replica_groups=mesh['y'=4,'core'=2,'x'=4,'z'=8] {'z'}, dimensions={0} | all-to-all | bytes 393216 | tf_op jit(solution)/shard_map/all_to_all | solution.py:405
  83.1 0.7 line.1
  83.9 7.2 %all-to-all-start.2 = ((bf16[16,8,512]{2,1,0:T(8,128)(2,1)}), bf16[16,8,512]{2,1,0:T(8,128)(2,1)S(1)}, u32[]{:S(2)}, u32[]{:S(2)}) async-start(bf16[16,8,512]{2,1,0:T(8,128)(2,1)} %get-tuple-element.101), calls=%async_computation.2 | async-start | bytes 262144 | tf_op jit(solution)/shard_map/all_to_all | solution.py:405
  91.1 2.7 %features.1 = bf16[8,32,512]{2,1,0:T(8,128)(2,1)} custom-call(bf16[8,32,512]{2,1,0:T(8,128)(2,1)S(1)} %get-tuple-element.74.field, bf16[3,32,512]{2,1,0:T(8,128)(2,1)S(1)} %collective-permute-done.7.row_inner, bf16[3,32,512]{2,1,0:T(8,128)(2,1)S(1)} %collective-permute-done.8.row_outer, bf16[14,3,512]{2,1,0:T(4,128)(2,1)S(1)} %collective-permute-done.9.inner, ...), custom_call_target="tpu_custom_call" | custom-call | tf_op jit(solution)/shard_map/features/pallas_call | solution.py:557
  93.8 3.9 %all-to-all-done.2.chunks = bf16[16,8,512]{2,1,0:T(8,128)(2,1)S(1)} async-done(((bf16[16,8,512]{2,1,0:T(8,128)(2,1)}), bf16[16,8,512]{2,1,0:T(8,128)(2,1)S(1)}, u32[]{:S(2)}, u32[]{:S(2)}) %all-to-all-start.2) | async-done | bytes 131104 | tf_op jit(solution)/shard_map/all_to_all | solution.py:405
  97.7 0.7 last.1
  (31 shorter events, 1.6 us)
Async XLA Ops:
  1.6 1.7 %collective-permute-start = (bf16[3,32,512]{2,1,0:T(8,128)(2,1)S(1)}, bf16[3,32,512]{2,1,0:T(8,128)(2,1)S(1)}, u32[]{:S(2)}, u32[]{:S(2)}) collective-permute-start(bf16[3,32,512]{2,1,0:T(8,128)(2,1)S(1)} %get-tuple-element.114), channel_id=1, source_target_pairs={{0,32},{32,0},{64,96},{96,64},{128,160},{160,128},{192,224},{224,1... | collective-permute-start | bytes 294920 | tf_op jit(solution)/shard_map/ppermute | solution.py:387
  1.7 1.6 %collective-permute-start.1 = (bf16[3,32,512]{2,1,0:T(8,128)(2,1)S(1)}, bf16[3,32,512]{2,1,0:T(8,128)(2,1)S(1)}, u32[]{:S(2)}, u32[]{:S(2)}) collective-permute-start(bf16[3,32,512]{2,1,0:T(8,128)(2,1)S(1)} %get-tuple-element.115), channel_id=1, source_target_pairs={{32,64},{64,32},{96,128},{128,96},{160,192},{192,160},{33,65},{65,... | collective-permute-start | bytes 294920 | tf_op jit(solution)/shard_map/ppermute | solution.py:388
  3.5 10.4 %collective-permute-start.3 = (bf16[14,3,512]{2,1,0:T(4,128)(2,1)S(1)}, bf16[14,3,512]{2,1,0:T(4,128)(2,1)S(1)}, u32[]{:S(2)}, u32[]{:S(2)}) collective-permute-start(bf16[14,3,512]{2,1,0:T(4,128)(2,1)S(1)} %get-tuple-element.118), channel_id=1, source_target_pairs={{1,2},{2,1},{3,4},{4,3},{5,6},{6,5},{7,8},{8,7},{9,10},{10,9},{11,... | collective-permute-start | bytes 129032 | tf_op jit(solution)/shard_map/ppermute | solution.py:388
  11.2 4.3 %collective-permute-start.2 = (bf16[14,3,512]{2,1,0:T(4,128)(2,1)S(1)}, bf16[14,3,512]{2,1,0:T(4,128)(2,1)S(1)}, u32[]{:S(2)}, u32[]{:S(2)}) collective-permute-start(bf16[14,3,512]{2,1,0:T(4,128)(2,1)S(1)} %get-tuple-element.119), channel_id=1, source_target_pairs={{0,1},{1,0},{2,3},{3,2},{4,5},{5,4},{6,7},{7,6},{8,9},{9,8},{10,11... | collective-permute-start | bytes 129032 | tf_op jit(solution)/shard_map/ppermute | solution.py:387
  21.2 11.7 %collective-permute-start.4 = (bf16[16,96,512]{2,1,0:T(8,128)(2,1)S(1)}, bf16[16,96,512]{2,1,0:T(8,128)(2,1)S(1)}, u32[]{:S(2)}, u32[]{:S(2)}) collective-permute-start(bf16[16,96,512]{2,1,0:T(8,128)(2,1)S(1)} %get-tuple-element.65), channel_id=1, source_target_pairs={{0,32},{32,0},{1,33},{33,1},{2,34},{34,2},{3,35},{35,3},{4,36},{36... | collective-permute-start | bytes 4718600 | tf_op jit(solution)/shard_map/ppermute | solution.py:479
  24.6 10.2 %collective-permute-start.6 = (bf16[8,4,8,1024]{3,2,1,0:T(8,128)(2,1)S(1)}, bf16[8,4,8,1024]{3,2,1,0:T(8,128)(2,1)S(1)}, u32[]{:S(2)}, u32[]{:S(2)}) collective-permute-start(bf16[8,4,8,1024]{3,2,1,0:T(8,128)(2,1)S(1)} %get-tuple-element.73), channel_id=1, source_target_pairs={{0,32},{32,0},{1,33},{33,1},{2,34},{34,2},{3,35},{35,3},{4,36},{36... | collective-permute-start | bytes 1572872 | tf_op jit(solution)/shard_map/ppermute | solution.py:480
  27.6 5.3 %collective-permute-start.5 = (bf16[16,8,512]{2,1,0:T(8,128)(2,1)S(1)}, bf16[16,8,512]{2,1,0:T(8,128)(2,1)S(1)}, u32[]{:S(2)}, u32[]{:S(2)}) collective-permute-start(bf16[16,8,512]{2,1,0:T(8,128)(2,1)S(1)} %get-tuple-element.71.small), channel_id=1, source_target_pairs={{0,32},{32,0},{1,33},{33,1},{2,34},{34,2},{3,35},{35,3},{4,36},{36... | collective-permute-start | bytes 393224 | tf_op jit(solution)/shard_map/ppermute | solution.py:497
  28.1 6.7 %collective-permute-start.8 = (bf16[3,32,512]{2,1,0:T(8,128)(2,1)S(1)}, bf16[3,32,512]{2,1,0:T(8,128)(2,1)S(1)}, u32[]{:S(2)}, u32[]{:S(2)}) collective-permute-start(bf16[3,32,512]{2,1,0:T(8,128)(2,1)S(1)} %get-tuple-element.110), channel_id=1, source_target_pairs={{32,64},{64,32},{96,128},{128,96},{160,192},{192,160},{33,65},{65,... | collective-permute-start | bytes 294920 | tf_op jit(solution)/shard_map/ppermute | solution.py:388
  28.8 6.0 %collective-permute-start.7 = (bf16[3,32,512]{2,1,0:T(8,128)(2,1)S(1)}, bf16[3,32,512]{2,1,0:T(8,128)(2,1)S(1)}, u32[]{:S(2)}, u32[]{:S(2)}) collective-permute-start(bf16[3,32,512]{2,1,0:T(8,128)(2,1)S(1)} %get-tuple-element.111), channel_id=1, source_target_pairs={{0,32},{32,0},{64,96},{96,64},{128,160},{160,128},{192,224},{224,1... | collective-permute-start | bytes 294920 | tf_op jit(solution)/shard_map/ppermute | solution.py:387
  34.8 33.6 %all-to-all-start = ((bf16[16,104,512]{2,1,0:T(8,128)(2,1)}), bf16[16,104,512]{2,1,0:T(8,128)(2,1)S(1)}, u32[]{:S(2)}, u32[]{:S(2)}) async-start(bf16[16,104,512]{2,1,0:T(8,128)(2,1)} %merge.1), calls=%async_computation | async-start | bytes 3407872 | tf_op jit(solution)/shard_map/all_to_all | solution.py:405
  42.7 14.5 %collective-permute-start.11 = (bf16[4,8,1024]{2,1,0:T(8,128)(2,1)S(1)}, bf16[4,8,1024]{2,1,0:T(8,128)(2,1)S(1)}, u32[]{:S(2)}, u32[]{:S(2)}) collective-permute-start(bf16[4,8,1024]{2,1,0:T(8,128)(2,1)S(1)} %get-tuple-element.81), channel_id=1, source_target_pairs={{0,1},{1,0},{2,3},{3,2},{4,5},{5,4},{6,7},{7,6},{8,9},{9,8},{10,11... | collective-permute-start | bytes 196616 | tf_op jit(solution)/shard_map/ppermute | solution.py:521
  43.3 18.2 %collective-permute-start.12 = (bf16[4,8,1024]{2,1,0:T(8,128)(2,1)S(1)}, bf16[4,8,1024]{2,1,0:T(8,128)(2,1)S(1)}, u32[]{:S(2)}, u32[]{:S(2)}) collective-permute-start(bf16[4,8,1024]{2,1,0:T(8,128)(2,1)S(1)} %get-tuple-element.82), channel_id=1, source_target_pairs={{0,2},{1,3},{2,0},{3,1},{4,6},{5,7},{6,4},{7,5},{8,10},{9,11},{10,... | collective-permute-start | bytes 196616 | tf_op jit(solution)/shard_map/ppermute | solution.py:521
  45.5 45.6 %copy-start = (bf16[8,32,512]{2,1,0:T(8,128)(2,1)S(1)}, bf16[8,32,512]{2,1,0:T(8,128)(2,1)}, u32[]{:S(2)}) copy-start(bf16[8,32,512]{2,1,0:T(8,128)(2,1)} %cotangent.1) | copy-start | bytes 786436
  45.5 45.6 %copy-start.1 = (f32[7,7,512]{2,1,0:T(8,128)S(1)}, f32[7,7,512]{2,1,0:T(8,128)}, u32[]{:S(2)}) copy-start(f32[7,7,512]{2,1,0:T(8,128)} %taps.1) | copy-start | bytes 301060
  45.5 8.4 %collective-permute-start.10 = (bf16[14,3,512]{2,1,0:T(4,128)(2,1)S(1)}, bf16[14,3,512]{2,1,0:T(4,128)(2,1)S(1)}, u32[]{:S(2)}, u32[]{:S(2)}) collective-permute-start(bf16[14,3,512]{2,1,0:T(4,128)(2,1)S(1)} %get-tuple-element.116), channel_id=1, source_target_pairs={{1,2},{2,1},{3,4},{4,3},{5,6},{6,5},{7,8},{8,7},{9,10},{10,9},{11,... | collective-permute-start | bytes 129032 | tf_op jit(solution)/shard_map/ppermute | solution.py:388
  48.3 8.1 %collective-permute-start.9 = (bf16[14,3,512]{2,1,0:T(4,128)(2,1)S(1)}, bf16[14,3,512]{2,1,0:T(4,128)(2,1)S(1)}, u32[]{:S(2)}, u32[]{:S(2)}) collective-permute-start(bf16[14,3,512]{2,1,0:T(4,128)(2,1)S(1)} %get-tuple-element.117), channel_id=1, source_target_pairs={{0,1},{1,0},{2,3},{3,2},{4,5},{5,4},{6,7},{7,6},{8,9},{9,8},{10,11... | collective-permute-start | bytes 129032 | tf_op jit(solution)/shard_map/ppermute | solution.py:387
  49.1 14.0 %collective-permute-start.13 = (bf16[4,8,1024]{2,1,0:T(8,128)(2,1)S(1)}, bf16[4,8,1024]{2,1,0:T(8,128)(2,1)S(1)}, u32[]{:S(2)}, u32[]{:S(2)}) collective-permute-start(bf16[4,8,1024]{2,1,0:T(8,128)(2,1)S(1)} %get-tuple-element.83), channel_id=1, source_target_pairs={{0,3},{1,2},{2,1},{3,0},{4,7},{5,6},{6,5},{7,4},{8,11},{9,10},{10,... | collective-permute-start | bytes 196616 | tf_op jit(solution)/shard_map/ppermute | solution.py:521
  53.9 9.2 %collective-permute-start.14 = (bf16[4,8,1024]{2,1,0:T(8,128)(2,1)S(1)}, bf16[4,8,1024]{2,1,0:T(8,128)(2,1)S(1)}, u32[]{:S(2)}, u32[]{:S(2)}) collective-permute-start(bf16[4,8,1024]{2,1,0:T(8,128)(2,1)S(1)} %get-tuple-element.84), channel_id=1, source_target_pairs={{0,4},{1,5},{2,6},{3,7},{4,0},{5,1},{6,2},{7,3},{8,12},{9,13},{10,... | collective-permute-start | bytes 196616 | tf_op jit(solution)/shard_map/ppermute | solution.py:521
  56.4 7.4 %collective-permute-start.15 = (bf16[4,8,1024]{2,1,0:T(8,128)(2,1)S(1)}, bf16[4,8,1024]{2,1,0:T(8,128)(2,1)S(1)}, u32[]{:S(2)}, u32[]{:S(2)}) collective-permute-start(bf16[4,8,1024]{2,1,0:T(8,128)(2,1)S(1)} %get-tuple-element.85), channel_id=1, source_target_pairs={{0,5},{1,4},{2,7},{3,6},{4,1},{5,0},{6,3},{7,2},{8,13},{9,12},{10,... | collective-permute-start | bytes 196616 | tf_op jit(solution)/shard_map/ppermute | solution.py:521
  57.3 8.3 %collective-permute-start.16 = (bf16[4,8,1024]{2,1,0:T(8,128)(2,1)S(1)}, bf16[4,8,1024]{2,1,0:T(8,128)(2,1)S(1)}, u32[]{:S(2)}, u32[]{:S(2)}) collective-permute-start(bf16[4,8,1024]{2,1,0:T(8,128)(2,1)S(1)} %get-tuple-element.86), channel_id=1, source_target_pairs={{0,6},{1,7},{2,4},{3,5},{4,2},{5,3},{6,0},{7,1},{8,14},{9,15},{10,... | collective-permute-start | bytes 196616 | tf_op jit(solution)/shard_map/ppermute | solution.py:521
  61.5 6.9 %collective-permute-start.17 = (bf16[4,8,1024]{2,1,0:T(8,128)(2,1)S(1)}, bf16[4,8,1024]{2,1,0:T(8,128)(2,1)S(1)}, u32[]{:S(2)}, u32[]{:S(2)}) collective-permute-start(bf16[4,8,1024]{2,1,0:T(8,128)(2,1)S(1)} %get-tuple-element.87), channel_id=1, source_target_pairs={{0,7},{1,6},{2,5},{3,4},{4,3},{5,2},{6,1},{7,0},{8,15},{9,14},{10,... | collective-permute-start | bytes 196616 | tf_op jit(solution)/shard_map/ppermute | solution.py:521
  83.9 13.8 %all-to-all-start.2 = ((bf16[16,8,512]{2,1,0:T(8,128)(2,1)}), bf16[16,8,512]{2,1,0:T(8,128)(2,1)S(1)}, u32[]{:S(2)}, u32[]{:S(2)}) async-start(bf16[16,8,512]{2,1,0:T(8,128)(2,1)} %get-tuple-element.101), calls=%async_computation.2 | async-start | bytes 262144 | tf_op jit(solution)/shard_map/all_to_all | solution.py:405

commit v14 on v13

--- a/solution.py
+++ b/solution.py
@@ -314,18 +314,18 @@
 
 def plane_kernel(chunks, out, total):
     total[...] = jnp.sum(chunks[...].astype(jnp.float32), axis=0)
-    each = (out.shape[1] - 2 * SMALL) // 2
+    each = out.shape[1] // 2
     channels = out.shape[2]
     top = total.shape[0] - 2 * SMALL - each * Z
     blocks = (channels - ALONG) // LANES
-    small = total[pl.ds(total.shape[0] - 2 * SMALL, 2 * SMALL), :].astype(jnp.bfloat16)
+    small = total[pl.ds(total.shape[0] - 2 * SMALL, SMALL), :]
+    small = jnp.concatenate([small[:, :ALONG], small[:, ALONG:]])
     for z in range(Z):
         parts = [total[slot(z * blocks + i, each, channels)] for i in range(blocks)]
-        parts.append(jnp.zeros((each, ALONG), jnp.float32))
+        parts.append(small)
         out[z, pl.ds(0, each), :] = jnp.concatenate(parts, axis=1).astype(jnp.bfloat16)
         parts = [total[pl.ds(top + q * 2 * Z + 2 * z, 2), :] for q in range(each // 2)]
         out[z, pl.ds(each, each), :] = jnp.concatenate(parts).astype(jnp.bfloat16)
-        out[z, pl.ds(2 * each, 2 * SMALL), :] = small
 
 
 def line_kernel(multiplier, chunks, *refs):
@@ -336,9 +336,8 @@
     for q in range(each // 2):
         part = total[each + 2 * q : each + 2 * q + 2]
         dexpand[:, pl.ds(q * channels, channels)] = part * multiplier
-    small = total[2 * each : 2 * each + SMALL]
     half = channels // 2
-    small = jnp.concatenate([small[:, :half], small[:, half:]]).astype(jnp.bfloat16)
+    small = total[:each, half:].astype(jnp.bfloat16)
     line = sum(ref[...].astype(jnp.float32) for ref in came).astype(jnp.bfloat16)
     for place in range(out.shape[0]):
         y, x = place // X, place % X
@@ -529,7 +528,7 @@
         name="plane",
         in_specs=[VMEM],
         out_specs=VMEM,
-        out_shape=shape((Z, 2 * each + 2 * SMALL, channels), bf16),
+        out_shape=shape((Z, 2 * each, channels), bf16),
         scratch_shapes=[pltpu.VMEM((whole, channels), f32)],
         compiler_params=GLUE_PARAMS,
     )(chunks)

time: 98.9 us -> 97.3 us (0.984)
  blocking collectives: 14.4 us -> 13.3 us
    all_to_all x1, blocking collectives: 14.4 us -> 13.3 us  [exchanged(): return lax.all_to_all(chunks, axes, 0, 0, tiled=True)]
where the time goes in v14:
time: 97.3 us; the launch traced here: 96.9 us
  starting transfers between devices  50 us (51%)
  Pallas kernels  17.7 us (18%)
  blocking collectives  13.3 us (14%)
  waiting for transfers between devices  12.9 us (13%)
  other arithmetic  1.17 us (1%)
  local copies, waits for them, and re-layouts  1 us (1%)
    all_to_all x2, starting transfers between devices, exchanged(): return lax.all_to_all(chunks, axes, 0, 0, tiled=True)  14.8 us
    ppermute x7, starting transfers between devices, shards(): lax.ppermute(part, 'z', [(i, i ^ step) for i in range(Z)])  14.4 us
    all_to_all x1, blocking collectives, exchanged(): return lax.all_to_all(chunks, axes, 0, 0, tiled=True)  13.3 us
    ppermute x4, starting transfers between devices, swapped(): lax.ppermute(jnp.where(first, low, high), axes, outer)  11.8 us
    pallas_call x1, Pallas kernels, shards(): pl.pallas_call(forward_kernel, name='forward', in_specs=[VMEM] * 9, out_s...  5.74 us
    ppermute x7, waiting for transfers between devices, shards(): lax.ppermute(part, 'z', [(i, i ^ step) for i in range(Z)])  5.27 us
    ppermute x4, starting transfers between devices, swapped(): lax.ppermute(jnp.where(first, high, low), axes, inner)  5.07 us
    all_to_all x2, waiting for transfers between devices, exchanged(): return lax.all_to_all(chunks, axes, 0, 0, tiled=True)  3.87 us
  transfers between devices with their start and end apart: 20, of which 6 were waited for; matrix products, arithmetic and copies ran while one was open for 1% of the time, Pallas kernels for 10%

profile of v14, /device:TPU:2, one launch (start us, length us, event | category | flops | bytes accessed | tf_op | source)
XLA Modules:
  0.0 96.9 jit_solution(13271305821496697605)
XLA Ops:
  0.6 1.0 broadcast_select_fusion.3
  1.7 0.7 collective-permute-start.1
  2.4 0.9 fusion.1
  3.5 7.7 %collective-permute-start.3 = (bf16[14,3,512]{2,1,0:T(4,128)(2,1)S(1)}, bf16[14,3,512]{2,1,0:T(4,128)(2,1)S(1)}, u32[]{:S(2)}, u32[]{:S(2)}) collective-permute-start(bf16[14,3,512]{2,1,0:T(4,128)(2,1)S(1)} %get-tuple-element.118), channel_id=1, source_target_pairs={{1,2},{2,1},{3,4},{4,3},{5,6},{6,5},{7,8},{8,7},{9,10},{10,9},{11,... | collective-permute-start | bytes 129032 | tf_op jit(solution)/shard_map/ppermute | solution.py:387
  11.3 2.6 %prepare.1 = (f32[4,14,48,128]{3,2,1,0:T(8,128)S(1)}, f32[4,256,128]{2,1,0:T(8,128)S(1)}, bf16[256,512]{1,0:T(8,128)(2,1)S(1)}, f32[7,7,512]{2,1,0:T(8,128)S(1)}...) custom-call(bf16[8,32,512]{2,1,0:T(8,128)(2,1)} %field_h.1, ...), custom_call_target="tpu_custom_call" | custom-call | tf_op jit(solution)/shard_map/prepare/pallas_call | solution.py:428
  13.9 1.6 %collective-permute-done.2.inner = bf16[14,3,512]{2,1,0:T(4,128)(2,1)S(1)} collective-permute-done((bf16[14,3,512]{2,1,0:T(4,128)(2,1)S(1)}, bf16[14,3,512]{2,1,0:T(4,128)(2,1)S(1)}, u32[]{:S(2)}, u32[]{:S(2)}) %collective-permute-start.2) | collective-permute-done | bytes 43040 | tf_op jit(solution)/shard_map/ppermute | solution.py:386
  15.5 5.7 %forward.1 = (bf16[16,96,512]{2,1,0:T(8,128)(2,1)S(1)}, bf16[16,96,512]{2,1,0:T(8,128)(2,1)S(1)}, bf16[8,4,8,1024]{3,2,1,0:T(8,128)(2,1)S(1)}, bf16[8,4,8,1024]{...) custom-call(bf16[14,3,512]{2,1,0:T(4,128)(2,1)S(1)} %collective-perm, ...), custom_call_target="tpu_custom_call", output_to_operand_aliasing={{7}: (2, {})} | custom-call | tf_op jit(solution)/shard_map/forward/pallas_call | solution.py:454
  21.2 3.4 %collective-permute-start.4 = (bf16[16,96,512]{2,1,0:T(8,128)(2,1)S(1)}, bf16[16,96,512]{2,1,0:T(8,128)(2,1)S(1)}, u32[]{:S(2)}, u32[]{:S(2)}) collective-permute-start(bf16[16,96,512]{2,1,0:T(8,128)(2,1)S(1)} %get-tuple-element.65), channel_id=1, source_target_pairs={{0,32},{32,0},{1,33},{33,1},{2,34},{34,2},{3,35},{35,3},{4,36},{36... | collective-permute-start | bytes 4718600 | tf_op jit(solution)/shard_map/ppermute | solution.py:478
  24.7 2.8 %backward.1 = (bf16[8,32,512]{2,1,0:T(8,128)(2,1)S(1)}, bf16[16,8,512]{2,1,0:T(8,128)(2,1)S(1)}) custom-call(bf16[256,2048]{1,0:T(8,128)(2,1)S(1)} %get-tuple-element.66.dpre, bf16[512,2048]{1,0:T(8,128)(2,1)S(1)} %get-tuple-element.62.expand, f32[4,256,128]{2,1,0:T(8,128)S(1)} %get-tuple-element.67.xhat, f32[256,128]{1,0:T(8,128)S(1)} %get-tuple-element.68.rstd, ...), custom_call_target="tpu_custom_call" | custom-call | tf_op jit(solution)/shard_map/backward/pallas_call | solution.py:480
  28.1 0.7 collective-permute-start.8
  28.8 4.1 %collective-permute-start.7 = (bf16[3,32,512]{2,1,0:T(8,128)(2,1)S(1)}, bf16[3,32,512]{2,1,0:T(8,128)(2,1)S(1)}, u32[]{:S(2)}, u32[]{:S(2)}) collective-permute-start(bf16[3,32,512]{2,1,0:T(8,128)(2,1)S(1)} %get-tuple-element.111), channel_id=1, source_target_pairs={{0,32},{32,0},{64,96},{96,64},{128,160},{160,128},{192,224},{224,1... | collective-permute-start | bytes 294920 | tf_op jit(solution)/shard_map/ppermute | solution.py:386
  32.9 1.9 %merge.1 = bf16[16,104,512]{2,1,0:T(8,128)(2,1)} custom-call(bf16[16,96,512]{2,1,0:T(8,128)(2,1)S(1)} %get-tuple-element.64.kept, bf16[16,96,512]{2,1,0:T(8,128)(2,1)S(1)} %collective-permute-done.4.came, bf16[16,8,512]{2,1,0:T(8,128)(2,1)S(1)} %get-tuple-element.71.small, bf16[16,8,512]{2,1,0:T(8,128)(2,1)S(1)} %collective-permute-done.5.small_came), custom_call_target="tpu_custom_call" | custom-call | tf_op jit(solution)/shard_map/merge/pallas_call | solution.py:498
  34.8 7.8 %all-to-all-start = ((bf16[16,104,512]{2,1,0:T(8,128)(2,1)}), bf16[16,104,512]{2,1,0:T(8,128)(2,1)S(1)}, u32[]{:S(2)}, u32[]{:S(2)}) async-start(bf16[16,104,512]{2,1,0:T(8,128)(2,1)} %merge.1), calls=%async_computation | async-start | bytes 3407872 | tf_op jit(solution)/shard_map/all_to_all | solution.py:404
  42.7 0.6 collective-permute-start.11
  43.3 2.0 %collective-permute-start.12 = (bf16[4,8,1024]{2,1,0:T(8,128)(2,1)S(1)}, bf16[4,8,1024]{2,1,0:T(8,128)(2,1)S(1)}, u32[]{:S(2)}, u32[]{:S(2)}) collective-permute-start(bf16[4,8,1024]{2,1,0:T(8,128)(2,1)S(1)} %get-tuple-element.82), channel_id=1, source_target_pairs={{0,2},{1,3},{2,0},{3,1},{4,6},{5,7},{6,4},{7,5},{8,10},{9,11},{10,... | collective-permute-start | bytes 196616 | tf_op jit(solution)/shard_map/ppermute | solution.py:520
  45.5 2.7 %collective-permute-start.10 = (bf16[14,3,512]{2,1,0:T(4,128)(2,1)S(1)}, bf16[14,3,512]{2,1,0:T(4,128)(2,1)S(1)}, u32[]{:S(2)}, u32[]{:S(2)}) collective-permute-start(bf16[14,3,512]{2,1,0:T(4,128)(2,1)S(1)} %get-tuple-element.116), channel_id=1, source_target_pairs={{1,2},{2,1},{3,4},{4,3},{5,6},{6,5},{7,8},{8,7},{9,10},{10,9},{11,... | collective-permute-start | bytes 129032 | tf_op jit(solution)/shard_map/ppermute | solution.py:387
  48.2 0.8 collective-permute-start.9
  49.0 2.7 %collective-permute-start.13 = (bf16[4,8,1024]{2,1,0:T(8,128)(2,1)S(1)}, bf16[4,8,1024]{2,1,0:T(8,128)(2,1)S(1)}, u32[]{:S(2)}, u32[]{:S(2)}) collective-permute-start(bf16[4,8,1024]{2,1,0:T(8,128)(2,1)S(1)} %get-tuple-element.83), channel_id=1, source_target_pairs={{0,3},{1,2},{2,1},{3,0},{4,7},{5,6},{6,5},{7,4},{8,11},{9,10},{10,... | collective-permute-start | bytes 196616 | tf_op jit(solution)/shard_map/ppermute | solution.py:520
  51.6 2.1 %collective-permute-done.10.outer = bf16[14,3,512]{2,1,0:T(4,128)(2,1)S(1)} collective-permute-done((bf16[14,3,512]{2,1,0:T(4,128)(2,1)S(1)}, bf16[14,3,512]{2,1,0:T(4,128)(2,1)S(1)}, u32[]{:S(2)}, u32[]{:S(2)}) %collective-permute-start.10) | collective-permute-done | bytes 43040 | tf_op jit(solution)/shard_map/ppermute | solution.py:387
  53.8 2.5 %collective-permute-start.14 = (bf16[4,8,1024]{2,1,0:T(8,128)(2,1)S(1)}, bf16[4,8,1024]{2,1,0:T(8,128)(2,1)S(1)}, u32[]{:S(2)}, u32[]{:S(2)}) collective-permute-start(bf16[4,8,1024]{2,1,0:T(8,128)(2,1)S(1)} %get-tuple-element.84), channel_id=1, source_target_pairs={{0,4},{1,5},{2,6},{3,7},{4,0},{5,1},{6,2},{7,3},{8,12},{9,13},{10,... | collective-permute-start | bytes 196616 | tf_op jit(solution)/shard_map/ppermute | solution.py:520
  56.3 0.9 collective-permute-start.15
  57.2 4.2 %collective-permute-start.16 = (bf16[4,8,1024]{2,1,0:T(8,128)(2,1)S(1)}, bf16[4,8,1024]{2,1,0:T(8,128)(2,1)S(1)}, u32[]{:S(2)}, u32[]{:S(2)}) collective-permute-start(bf16[4,8,1024]{2,1,0:T(8,128)(2,1)S(1)} %get-tuple-element.86), channel_id=1, source_target_pairs={{0,6},{1,7},{2,4},{3,5},{4,2},{5,3},{6,0},{7,1},{8,14},{9,15},{10,... | collective-permute-start | bytes 196616 | tf_op jit(solution)/shard_map/ppermute | solution.py:520
  61.4 1.5 %collective-permute-start.17 = (bf16[4,8,1024]{2,1,0:T(8,128)(2,1)S(1)}, bf16[4,8,1024]{2,1,0:T(8,128)(2,1)S(1)}, u32[]{:S(2)}, u32[]{:S(2)}) collective-permute-start(bf16[4,8,1024]{2,1,0:T(8,128)(2,1)S(1)} %get-tuple-element.87), channel_id=1, source_target_pairs={{0,7},{1,6},{2,5},{3,4},{4,3},{5,2},{6,1},{7,0},{8,15},{9,14},{10,... | collective-permute-start | bytes 196616 | tf_op jit(solution)/shard_map/ppermute | solution.py:520
  63.0 0.7 collective-permute-done.15.refs_5_
  63.7 1.8 %collective-permute-done.16.refs_6_ = bf16[4,8,1024]{2,1,0:T(8,128)(2,1)S(1)} collective-permute-done((bf16[4,8,1024]{2,1,0:T(8,128)(2,1)S(1)}, bf16[4,8,1024]{2,1,0:T(8,128)(2,1)S(1)}, u32[]{:S(2)}, u32[]{:S(2)}) %collective-permute-start.16) | collective-permute-done | bytes 65568 | tf_op jit(solution)/shard_map/ppermute | solution.py:520
  65.4 2.8 %collective-permute-done.17.refs_7_ = bf16[4,8,1024]{2,1,0:T(8,128)(2,1)S(1)} collective-permute-done((bf16[4,8,1024]{2,1,0:T(8,128)(2,1)S(1)}, bf16[4,8,1024]{2,1,0:T(8,128)(2,1)S(1)}, u32[]{:S(2)}, u32[]{:S(2)}) %collective-permute-start.17) | collective-permute-done | bytes 65568 | tf_op jit(solution)/shard_map/ppermute | solution.py:520
  68.6 13.3 %all_to_all.15.chunks = bf16[8,16,512]{2,1,0:T(8,128)(2,1)S(1)} all-to-all(bf16[8,16,512]{2,1,0:T(8,128)(2,1)S(1)} %plane.1), channel_id=1, replica_groups=mesh['y'=4,'core'=2,'x'=4,'z'=8] {'z'}, dimensions={0} | all-to-all | bytes 262144 | tf_op jit(solution)/shard_map/all_to_all | solution.py:404
  81.9 0.7 line.1
  82.6 7.0 %all-to-all-start.2 = ((bf16[16,8,512]{2,1,0:T(8,128)(2,1)}), bf16[16,8,512]{2,1,0:T(8,128)(2,1)S(1)}, u32[]{:S(2)}, u32[]{:S(2)}) async-start(bf16[16,8,512]{2,1,0:T(8,128)(2,1)} %get-tuple-element.101), calls=%async_computation.2 | async-start | bytes 262144 | tf_op jit(solution)/shard_map/all_to_all | solution.py:404
  89.6 2.7 %features.1 = bf16[8,32,512]{2,1,0:T(8,128)(2,1)} custom-call(bf16[8,32,512]{2,1,0:T(8,128)(2,1)S(1)} %get-tuple-element.74.field, bf16[3,32,512]{2,1,0:T(8,128)(2,1)S(1)} %collective-permute-done.7.row_inner, bf16[3,32,512]{2,1,0:T(8,128)(2,1)S(1)} %collective-permute-done.8.row_outer, bf16[14,3,512]{2,1,0:T(4,128)(2,1)S(1)} %collective-permute-done.9.inner, ...), custom_call_target="tpu_custom_call" | custom-call | tf_op jit(solution)/shard_map/features/pallas_call | solution.py:556
  92.3 3.9 %all-to-all-done.2.chunks = bf16[16,8,512]{2,1,0:T(8,128)(2,1)S(1)} async-done(((bf16[16,8,512]{2,1,0:T(8,128)(2,1)}), bf16[16,8,512]{2,1,0:T(8,128)(2,1)S(1)}, u32[]{:S(2)}, u32[]{:S(2)}) %all-to-all-start.2) | async-done | bytes 131104 | tf_op jit(solution)/shard_map/all_to_all | solution.py:404
  96.2 0.7 last.1
  (31 shorter events, 1.6 us)
Async XLA Ops:
  1.6 1.7 %collective-permute-start = (bf16[3,32,512]{2,1,0:T(8,128)(2,1)S(1)}, bf16[3,32,512]{2,1,0:T(8,128)(2,1)S(1)}, u32[]{:S(2)}, u32[]{:S(2)}) collective-permute-start(bf16[3,32,512]{2,1,0:T(8,128)(2,1)S(1)} %get-tuple-element.114), channel_id=1, source_target_pairs={{0,32},{32,0},{64,96},{96,64},{128,160},{160,128},{192,224},{224,1... | collective-permute-start | bytes 294920 | tf_op jit(solution)/shard_map/ppermute | solution.py:386
  1.7 1.6 %collective-permute-start.1 = (bf16[3,32,512]{2,1,0:T(8,128)(2,1)S(1)}, bf16[3,32,512]{2,1,0:T(8,128)(2,1)S(1)}, u32[]{:S(2)}, u32[]{:S(2)}) collective-permute-start(bf16[3,32,512]{2,1,0:T(8,128)(2,1)S(1)} %get-tuple-element.115), channel_id=1, source_target_pairs={{32,64},{64,32},{96,128},{128,96},{160,192},{192,160},{33,65},{65,... | collective-permute-start | bytes 294920 | tf_op jit(solution)/shard_map/ppermute | solution.py:387
  3.5 10.4 %collective-permute-start.3 = (bf16[14,3,512]{2,1,0:T(4,128)(2,1)S(1)}, bf16[14,3,512]{2,1,0:T(4,128)(2,1)S(1)}, u32[]{:S(2)}, u32[]{:S(2)}) collective-permute-start(bf16[14,3,512]{2,1,0:T(4,128)(2,1)S(1)} %get-tuple-element.118), channel_id=1, source_target_pairs={{1,2},{2,1},{3,4},{4,3},{5,6},{6,5},{7,8},{8,7},{9,10},{10,9},{11,... | collective-permute-start | bytes 129032 | tf_op jit(solution)/shard_map/ppermute | solution.py:387
  11.2 4.3 %collective-permute-start.2 = (bf16[14,3,512]{2,1,0:T(4,128)(2,1)S(1)}, bf16[14,3,512]{2,1,0:T(4,128)(2,1)S(1)}, u32[]{:S(2)}, u32[]{:S(2)}) collective-permute-start(bf16[14,3,512]{2,1,0:T(4,128)(2,1)S(1)} %get-tuple-element.119), channel_id=1, source_target_pairs={{0,1},{1,0},{2,3},{3,2},{4,5},{5,4},{6,7},{7,6},{8,9},{9,8},{10,11... | collective-permute-start | bytes 129032 | tf_op jit(solution)/shard_map/ppermute | solution.py:386
  21.2 11.7 %collective-permute-start.4 = (bf16[16,96,512]{2,1,0:T(8,128)(2,1)S(1)}, bf16[16,96,512]{2,1,0:T(8,128)(2,1)S(1)}, u32[]{:S(2)}, u32[]{:S(2)}) collective-permute-start(bf16[16,96,512]{2,1,0:T(8,128)(2,1)S(1)} %get-tuple-element.65), channel_id=1, source_target_pairs={{0,32},{32,0},{1,33},{33,1},{2,34},{34,2},{3,35},{35,3},{4,36},{36... | collective-permute-start | bytes 4718600 | tf_op jit(solution)/shard_map/ppermute | solution.py:478
  24.6 10.2 %collective-permute-start.6 = (bf16[8,4,8,1024]{3,2,1,0:T(8,128)(2,1)S(1)}, bf16[8,4,8,1024]{3,2,1,0:T(8,128)(2,1)S(1)}, u32[]{:S(2)}, u32[]{:S(2)}) collective-permute-start(bf16[8,4,8,1024]{3,2,1,0:T(8,128)(2,1)S(1)} %get-tuple-element.73), channel_id=1, source_target_pairs={{0,32},{32,0},{1,33},{33,1},{2,34},{34,2},{3,35},{35,3},{4,36},{36... | collective-permute-start | bytes 1572872 | tf_op jit(solution)/shard_map/ppermute | solution.py:479
  27.6 5.3 %collective-permute-start.5 = (bf16[16,8,512]{2,1,0:T(8,128)(2,1)S(1)}, bf16[16,8,512]{2,1,0:T(8,128)(2,1)S(1)}, u32[]{:S(2)}, u32[]{:S(2)}) collective-permute-start(bf16[16,8,512]{2,1,0:T(8,128)(2,1)S(1)} %get-tuple-element.71.small), channel_id=1, source_target_pairs={{0,32},{32,0},{1,33},{33,1},{2,34},{34,2},{3,35},{35,3},{4,36},{36... | collective-permute-start | bytes 393224 | tf_op jit(solution)/shard_map/ppermute | solution.py:496
  28.1 6.7 %collective-permute-start.8 = (bf16[3,32,512]{2,1,0:T(8,128)(2,1)S(1)}, bf16[3,32,512]{2,1,0:T(8,128)(2,1)S(1)}, u32[]{:S(2)}, u32[]{:S(2)}) collective-permute-start(bf16[3,32,512]{2,1,0:T(8,128)(2,1)S(1)} %get-tuple-element.110), channel_id=1, source_target_pairs={{32,64},{64,32},{96,128},{128,96},{160,192},{192,160},{33,65},{65,... | collective-permute-start | bytes 294920 | tf_op jit(solution)/shard_map/ppermute | solution.py:387
  28.8 6.0 %collective-permute-start.7 = (bf16[3,32,512]{2,1,0:T(8,128)(2,1)S(1)}, bf16[3,32,512]{2,1,0:T(8,128)(2,1)S(1)}, u32[]{:S(2)}, u32[]{:S(2)}) collective-permute-start(bf16[3,32,512]{2,1,0:T(8,128)(2,1)S(1)} %get-tuple-element.111), channel_id=1, source_target_pairs={{0,32},{32,0},{64,96},{96,64},{128,160},{160,128},{192,224},{224,1... | collective-permute-start | bytes 294920 | tf_op jit(solution)/shard_map/ppermute | solution.py:386
  34.8 33.4 %all-to-all-start = ((bf16[16,104,512]{2,1,0:T(8,128)(2,1)}), bf16[16,104,512]{2,1,0:T(8,128)(2,1)S(1)}, u32[]{:S(2)}, u32[]{:S(2)}) async-start(bf16[16,104,512]{2,1,0:T(8,128)(2,1)} %merge.1), calls=%async_computation | async-start | bytes 3407872 | tf_op jit(solution)/shard_map/all_to_all | solution.py:404
  42.7 14.4 %collective-permute-start.11 = (bf16[4,8,1024]{2,1,0:T(8,128)(2,1)S(1)}, bf16[4,8,1024]{2,1,0:T(8,128)(2,1)S(1)}, u32[]{:S(2)}, u32[]{:S(2)}) collective-permute-start(bf16[4,8,1024]{2,1,0:T(8,128)(2,1)S(1)} %get-tuple-element.81), channel_id=1, source_target_pairs={{0,1},{1,0},{2,3},{3,2},{4,5},{5,4},{6,7},{7,6},{8,9},{9,8},{10,11... | collective-permute-start | bytes 196616 | tf_op jit(solution)/shard_map/ppermute | solution.py:520
  43.3 18.1 %collective-permute-start.12 = (bf16[4,8,1024]{2,1,0:T(8,128)(2,1)S(1)}, bf16[4,8,1024]{2,1,0:T(8,128)(2,1)S(1)}, u32[]{:S(2)}, u32[]{:S(2)}) collective-permute-start(bf16[4,8,1024]{2,1,0:T(8,128)(2,1)S(1)} %get-tuple-element.82), channel_id=1, source_target_pairs={{0,2},{1,3},{2,0},{3,1},{4,6},{5,7},{6,4},{7,5},{8,10},{9,11},{10,... | collective-permute-start | bytes 196616 | tf_op jit(solution)/shard_map/ppermute | solution.py:520
  45.3 44.3 %copy-start = (bf16[8,32,512]{2,1,0:T(8,128)(2,1)S(1)}, bf16[8,32,512]{2,1,0:T(8,128)(2,1)}, u32[]{:S(2)}) copy-start(bf16[8,32,512]{2,1,0:T(8,128)(2,1)} %cotangent.1) | copy-start | bytes 786436
  45.3 44.3 %copy-start.1 = (f32[7,7,512]{2,1,0:T(8,128)S(1)}, f32[7,7,512]{2,1,0:T(8,128)}, u32[]{:S(2)}) copy-start(f32[7,7,512]{2,1,0:T(8,128)} %taps.1) | copy-start | bytes 301060
  45.5 8.3 %collective-permute-start.10 = (bf16[14,3,512]{2,1,0:T(4,128)(2,1)S(1)}, bf16[14,3,512]{2,1,0:T(4,128)(2,1)S(1)}, u32[]{:S(2)}, u32[]{:S(2)}) collective-permute-start(bf16[14,3,512]{2,1,0:T(4,128)(2,1)S(1)} %get-tuple-element.116), channel_id=1, source_target_pairs={{1,2},{2,1},{3,4},{4,3},{5,6},{6,5},{7,8},{8,7},{9,10},{10,9},{11,... | collective-permute-start | bytes 129032 | tf_op jit(solution)/shard_map/ppermute | solution.py:387
  48.2 8.1 %collective-permute-start.9 = (bf16[14,3,512]{2,1,0:T(4,128)(2,1)S(1)}, bf16[14,3,512]{2,1,0:T(4,128)(2,1)S(1)}, u32[]{:S(2)}, u32[]{:S(2)}) collective-permute-start(bf16[14,3,512]{2,1,0:T(4,128)(2,1)S(1)} %get-tuple-element.117), channel_id=1, source_target_pairs={{0,1},{1,0},{2,3},{3,2},{4,5},{5,4},{6,7},{7,6},{8,9},{9,8},{10,11... | collective-permute-start | bytes 129032 | tf_op jit(solution)/shard_map/ppermute | solution.py:386
  49.0 14.0 %collective-permute-start.13 = (bf16[4,8,1024]{2,1,0:T(8,128)(2,1)S(1)}, bf16[4,8,1024]{2,1,0:T(8,128)(2,1)S(1)}, u32[]{:S(2)}, u32[]{:S(2)}) collective-permute-start(bf16[4,8,1024]{2,1,0:T(8,128)(2,1)S(1)} %get-tuple-element.83), channel_id=1, source_target_pairs={{0,3},{1,2},{2,1},{3,0},{4,7},{5,6},{6,5},{7,4},{8,11},{9,10},{10,... | collective-permute-start | bytes 196616 | tf_op jit(solution)/shard_map/ppermute | solution.py:520
  53.8 9.2 %collective-permute-start.14 = (bf16[4,8,1024]{2,1,0:T(8,128)(2,1)S(1)}, bf16[4,8,1024]{2,1,0:T(8,128)(2,1)S(1)}, u32[]{:S(2)}, u32[]{:S(2)}) collective-permute-start(bf16[4,8,1024]{2,1,0:T(8,128)(2,1)S(1)} %get-tuple-element.84), channel_id=1, source_target_pairs={{0,4},{1,5},{2,6},{3,7},{4,0},{5,1},{6,2},{7,3},{8,12},{9,13},{10,... | collective-permute-start | bytes 196616 | tf_op jit(solution)/shard_map/ppermute | solution.py:520
  56.3 7.4 %collective-permute-start.15 = (bf16[4,8,1024]{2,1,0:T(8,128)(2,1)S(1)}, bf16[4,8,1024]{2,1,0:T(8,128)(2,1)S(1)}, u32[]{:S(2)}, u32[]{:S(2)}) collective-permute-start(bf16[4,8,1024]{2,1,0:T(8,128)(2,1)S(1)} %get-tuple-element.85), channel_id=1, source_target_pairs={{0,5},{1,4},{2,7},{3,6},{4,1},{5,0},{6,3},{7,2},{8,13},{9,12},{10,... | collective-permute-start | bytes 196616 | tf_op jit(solution)/shard_map/ppermute | solution.py:520
  57.2 8.3 %collective-permute-start.16 = (bf16[4,8,1024]{2,1,0:T(8,128)(2,1)S(1)}, bf16[4,8,1024]{2,1,0:T(8,128)(2,1)S(1)}, u32[]{:S(2)}, u32[]{:S(2)}) collective-permute-start(bf16[4,8,1024]{2,1,0:T(8,128)(2,1)S(1)} %get-tuple-element.86), channel_id=1, source_target_pairs={{0,6},{1,7},{2,4},{3,5},{4,2},{5,3},{6,0},{7,1},{8,14},{9,15},{10,... | collective-permute-start | bytes 196616 | tf_op jit(solution)/shard_map/ppermute | solution.py:520
  61.4 6.8 %collective-permute-start.17 = (bf16[4,8,1024]{2,1,0:T(8,128)(2,1)S(1)}, bf16[4,8,1024]{2,1,0:T(8,128)(2,1)S(1)}, u32[]{:S(2)}, u32[]{:S(2)}) collective-permute-start(bf16[4,8,1024]{2,1,0:T(8,128)(2,1)S(1)} %get-tuple-element.87), channel_id=1, source_target_pairs={{0,7},{1,6},{2,5},{3,4},{4,3},{5,2},{6,1},{7,0},{8,15},{9,14},{10,... | collective-permute-start | bytes 196616 | tf_op jit(solution)/shard_map/ppermute | solution.py:520
  82.6 13.6 %all-to-all-start.2 = ((bf16[16,8,512]{2,1,0:T(8,128)(2,1)}), bf16[16,8,512]{2,1,0:T(8,128)(2,1)S(1)}, u32[]{:S(2)}, u32[]{:S(2)}) async-start(bf16[16,8,512]{2,1,0:T(8,128)(2,1)} %get-tuple-element.101), calls=%async_computation.2 | async-start | bytes 262144 | tf_op jit(solution)/shard_map/all_to_all | solution.py:404
